TPU v7x, 32 devices: a whole 2x2x4 slice. The times are simulated.
32 devices in a mesh: gx: 4 (over z), gy: 8 (over y, x, core).
Axes of the slice: x: 2, y: 2, z: 4, core: 2. Of those that a mesh axis runs over, the one named last changes fastest.
Arguments:
- tokens: bfloat16 [4096, 2048], P(('gx', 'gy')), may hold values from -6 to 6
- cotangent: bfloat16 [4096, 2048], P(('gx', 'gy')), may hold values from -6 to 6
- expert_ids: int32 [4096, 8], P(('gx', 'gy')), may hold values from 0 to 15, all different within a row; in each aligned block of 128 rows (0 to 127, 128 to 255, ...) at most 96 rows name the same one
- doc_ids: int32 [4096], P('gx'), may hold values from 0 to 7, never falling along the last dimension, each value on 1 to 1024 neighbouring positions
- clip_rank: int32 [1], replicated, may hold values from 2 to 13
- attn_gain: float32 [2048], replicated, may hold values from 0.5 to 1.5
- moe_gain: float32 [2048], replicated, may hold values from 0.5 to 1.5
- query_gain: float32 [128], replicated, may hold values from 0.25 to 1.75
- key_gain: float32 [128], replicated, may hold values from 0.25 to 1.75
- query_weight: bfloat16 [2048, 2048], P('gx', 'gy')
- key_weight: bfloat16 [2048, 2048], P('gx', 'gy')
- value_weight: bfloat16 [2048, 2048], P('gx', 'gy'), may hold values from -0.125 to 0.125
- out_weight: bfloat16 [2048, 2048], P('gy', 'gx'), may hold values from -2 to 2
- router_weight: bfloat16 [2048, 16], replicated, may hold values from -0.0625 to 0.0625
- gate_weight: bfloat16 [32, 2048, 512], P(('gx', 'gy')), may hold values from -0.125 to 0.125
- up_weight: bfloat16 [32, 2048, 512], P(('gx', 'gy')), may hold values from -0.125 to 0.125
- down_weight: bfloat16 [32, 512, 2048], P(('gx', 'gy')), may hold values from -0.75 to 0.75
Outputs:
- output: bfloat16 [4096, 2048], P(('gx', 'gy'))
- input_grad: float32 [4096, 2048], P(('gx', 'gy'))
- attn_gain_grad: float32 [2048], replicated
- moe_gain_grad: float32 [2048], replicated
- query_gain_grad: float32 [128], replicated
- key_gain_grad: float32 [128], replicated
- query_grad: float32 [2048, 2048], P('gx', 'gy')
- key_grad: float32 [2048, 2048], P('gx', 'gy')
- value_grad: float32 [2048, 2048], P('gx', 'gy')
- out_grad: float32 [2048, 2048], P('gy', 'gx')
- router_grad: float32 [2048, 16], replicated
- gate_grad: float32 [32, 2048, 512], P(('gx', 'gy'))
- up_grad: float32 [32, 2048, 512], P(('gx', 'gy'))
- down_grad: float32 [32, 512, 2048], P(('gx', 'gy'))
- query_clipped: bfloat16 [2048, 2048], P('gx', 'gy')
- key_clipped: bfloat16 [2048, 2048], P('gx', 'gy')
- clip_factors: float32 [16], replicated
Inputs may be any that keep to these rules, and one draw needn't show every extreme that they name: `expert_ids`: each row names 8 different experts. Among the 128 rows of one device no expert is named more than 96 times, and in every draw some device names some expert exactly 96 times. `doc_ids`: never falls from one token to the next; each value covers 1 to 1024 consecutive tokens, and one covers exactly 1024.
All inputs are finite; a program needn't handle non-finite values.
Results may differ from a plain program's by a relative error of at most 0.015.
Values may be sent and summed in bfloat16 or wider, within the bound.
A program may use at most 256 MiB of HBM per device.

v0:
```python
from functools import partial

import jax
import jax.numpy as jnp
from jax import lax
from jax.sharding import PartitionSpec as P

NH = 16
HD = 128
TOP = 8


EPSILON = 1e-06
NEGATIVE = -1e30


def norm_rows(values, gain_row):
    return (
        values * lax.rsqrt(jnp.mean(values * values, axis=-1, keepdims=True) + EPSILON) * gain_row
    )


def rotary(values):
    length = values.shape[0]
    halfway = values.shape[-1] // 2
    positions = jnp.arange(length, dtype=jnp.float32)
    frequency = jnp.exp(
        jnp.arange(halfway, dtype=jnp.float32) * (-2.0 * jnp.log(10000.0) / values.shape[-1])
    )
    angles = (positions[:, None] * frequency[None, :])[:, None, :]
    cosine = jnp.cos(angles)
    sine_table = jnp.sin(angles)
    first_half = values[..., :halfway]
    second = values[..., halfway:]
    return jnp.concatenate(
        [first_half * cosine - second * sine_table, second * cosine + first_half * sine_table],
        axis=-1,
    )


def prepare_heads(raw_heads, gain_row):
    return rotary(norm_rows(raw_heads, gain_row))


def route_gates(id_table, logits):
    shares = jax.nn.softmax(logits, axis=-1)
    experts = logits.shape[-1]
    matches = id_table[:, :, None] == jnp.arange(experts, dtype=jnp.int32)[None, None, :]
    chosen = jnp.sum(jnp.where(matches, shares[:, None, :], 0.0), axis=-1)
    return chosen / jnp.sum(chosen, axis=-1, keepdims=True)


def contract_rows(left_side, right_side):
    return lax.dot_general(
        left_side, right_side, (((0,), (0,)), ((), ())), preferred_element_type=jnp.float32
    )


def contract_cols(left_side, right_side):
    return lax.dot_general(
        left_side, right_side, (((1,), (1,)), ((), ())), preferred_element_type=jnp.float32
    )


def local(
    tokens,
    cotangent,
    expert_ids,
    doc_ids,
    clip_rank,
    attn_gain,
    moe_gain,
    query_gain,
    key_gain,
    query_weight,
    key_weight,
    value_weight,
    out_weight,
    router_weight,
    gate_weight,
    up_weight,
    down_weight,
):
    tok_rows = tokens.shape[0]
    inputs = tokens.astype(jnp.float32)
    acts_float, norm_pull = jax.vjp(norm_rows, inputs, attn_gain)
    acts_low = acts_float.astype(jnp.bfloat16)
    seq_acts = lax.all_gather(acts_low, "gy", axis=0, tiled=True)
    full_query, full_key, full_value, out_rows = (
        lax.all_gather(query_weight, "gx", axis=0, tiled=True),
        lax.all_gather(key_weight, "gx", axis=0, tiled=True),
        lax.all_gather(value_weight, "gx", axis=0, tiled=True),
        lax.all_gather(out_weight, "gx", axis=1, tiled=True),
    )
    length = seq_acts.shape[0]
    local_width = full_query.shape[1]
    local_heads = local_width // HD
    queries = jnp.dot(seq_acts, full_query, preferred_element_type=jnp.float32)
    key_raw = jnp.dot(seq_acts, full_key, preferred_element_type=jnp.float32)
    value_ready = (
        jnp.dot(seq_acts, full_value, preferred_element_type=jnp.float32)
        .astype(jnp.bfloat16)
        .reshape(length, local_heads, HD)
    )
    query_float, query_pull = jax.vjp(
        prepare_heads, queries.reshape(length, local_heads, HD), query_gain
    )
    key_float, key_pull = jax.vjp(prepare_heads, key_raw.reshape(length, local_heads, HD), key_gain)
    query_ready = query_float.astype(jnp.bfloat16)
    key_ready = key_float.astype(jnp.bfloat16)
    block_rows = min(512, length)
    block_count = length // block_rows
    score_scale = HD ** (-0.5)
    query_blocks = query_ready.reshape(block_count, block_rows, local_heads, HD)
    doc_blocks = doc_ids.reshape(block_count, block_rows)

    def block_scores(query_block, doc_block):
        scores = (
            jnp.einsum("qhd,khd->hqk", query_block, key_ready, preferred_element_type=jnp.float32)
            * score_scale
        )
        same_doc = doc_block[:, None] == doc_ids[None, :]
        return jnp.where(same_doc[None], scores, NEGATIVE)

    def forward_block(pieces):
        scores = block_scores(pieces[0], pieces[1])
        highest = jnp.max(scores, axis=-1, keepdims=True)
        weights = jnp.exp(scores - highest)
        totals = jnp.sum(weights, axis=-1, keepdims=True)
        shares = (weights / totals).astype(jnp.bfloat16)
        mixed_heads = jnp.einsum(
            "hqk,khd->qhd", shares, value_ready, preferred_element_type=jnp.float32
        )
        return (
            mixed_heads.astype(jnp.bfloat16),
            highest[..., 0] + jnp.log(totals[..., 0]),
            jnp.max(highest[..., 0], axis=-1),
        )

    mixed_blocks, log_totals, peak_blocks = lax.map(forward_block, (query_blocks, doc_blocks))
    mixed_seq = mixed_blocks.reshape(length, local_width)
    start_head = lax.axis_index("gy") * local_heads
    peak_local = lax.dynamic_update_slice(
        jnp.full((NH,), NEGATIVE, jnp.float32), jnp.max(peak_blocks, axis=0), (start_head,)
    )
    peak_global = lax.pmax(peak_local, ("gx", "gy"))
    attended = lax.psum_scatter(
        jnp.dot(mixed_seq, out_rows, preferred_element_type=jnp.float32),
        "gy",
        scatter_dimension=0,
        tiled=True,
    )
    residual = inputs + attended
    moe_float, moe_pull = jax.vjp(norm_rows, residual, moe_gain)
    moe_in = moe_float.astype(jnp.bfloat16)
    logits = jnp.dot(moe_in, router_weight, preferred_element_type=jnp.float32)
    gate_share, gate_pull = jax.vjp(partial(route_gates, expert_ids), logits)
    experts = router_weight.shape[1]
    width_all = moe_in.shape[1]
    capacity = tok_rows * TOP * 3 // (2 * experts)
    route_count = tok_rows * TOP
    flat_ids = expert_ids.reshape(route_count)
    onehot = (flat_ids[:, None] == jnp.arange(experts, dtype=jnp.int32)[None, :]).astype(jnp.int32)
    earlier = jnp.cumsum(onehot, axis=0) - onehot
    slot_index = jnp.sum(earlier * onehot, axis=1)
    target = flat_ids * capacity + slot_index
    source = (
        jnp.full((experts * capacity,), tok_rows, jnp.int32)
        .at[target]
        .set(jnp.arange(route_count, dtype=jnp.int32) // TOP)
    )
    padded_in = jnp.concatenate([moe_in, jnp.zeros((1, width_all), jnp.bfloat16)], axis=0)
    packed = padded_in[source].reshape(experts, 1, capacity, width_all)
    outgoing = jnp.broadcast_to(packed, (experts, 2, capacity, width_all)).reshape(
        2 * experts, capacity, width_all
    )
    arrived = lax.all_to_all(outgoing, ("gx", "gy"), split_axis=0, concat_axis=1, tiled=True)[0]
    gate_in = gate_weight[0]
    up_in = up_weight[0]
    down_in = down_weight[0]
    gate_val = jnp.dot(arrived, gate_in, preferred_element_type=jnp.float32)
    up_val = jnp.dot(arrived, up_in, preferred_element_type=jnp.float32)
    hidden = (jax.nn.silu(gate_val) * up_val).astype(jnp.bfloat16)
    produced = jnp.dot(hidden, down_in, preferred_element_type=jnp.float32).astype(jnp.bfloat16)
    returned = lax.all_to_all(produced[None], ("gx", "gy"), split_axis=1, concat_axis=0, tiled=True)
    summed = (
        returned.reshape(experts, 2, capacity, width_all)
        .astype(jnp.float32)
        .sum(axis=1)
        .reshape(experts * capacity, width_all)
    )
    route_out = summed[target]
    gates_flat = gate_share.reshape(route_count)
    moe_out = jnp.sum((gates_flat[:, None] * route_out).reshape(tok_rows, TOP, width_all), axis=1)
    block_out = residual + moe_out
    output = block_out.astype(jnp.bfloat16)
    grad_out = cotangent.astype(jnp.float32)
    grad_gates = jnp.sum(
        route_out.reshape(tok_rows, TOP, width_all) * grad_out[:, None, :], axis=-1
    )
    slot_gate = jnp.zeros((experts * capacity,), jnp.float32).at[target].set(gates_flat)
    padded_grad = jnp.concatenate([grad_out, jnp.zeros((1, width_all), jnp.float32)], axis=0)
    grad_packed = (
        (slot_gate[:, None] * padded_grad[source])
        .astype(jnp.bfloat16)
        .reshape(experts, 1, capacity, width_all)
    )
    grad_outgoing = jnp.broadcast_to(grad_packed, (experts, 2, capacity, width_all)).reshape(
        2 * experts, capacity, width_all
    )
    grad_arrived = lax.all_to_all(
        grad_outgoing, ("gx", "gy"), split_axis=0, concat_axis=1, tiled=True
    )[0]
    rows_in, grad_use = (arrived, grad_arrived)
    gate_use, up_use, hidden_use = (gate_val, up_val, hidden)
    sigmoid_gate = jax.nn.sigmoid(gate_use)
    silu_gate = gate_use * sigmoid_gate
    grad_hidden = contract_cols(grad_use, down_in)
    down_part = contract_rows(hidden_use, grad_use)
    grad_gate = (
        grad_hidden * up_use * sigmoid_gate * (1.0 + gate_use * (1.0 - sigmoid_gate))
    ).astype(jnp.bfloat16)
    grad_up = (grad_hidden * silu_gate).astype(jnp.bfloat16)
    gate_part = contract_rows(rows_in, grad_gate)
    up_part = contract_rows(rows_in, grad_up)
    grad_in = contract_cols(grad_gate, gate_in) + contract_cols(grad_up, up_in)
    grad_back = lax.all_to_all(
        grad_in.astype(jnp.bfloat16)[None], ("gx", "gy"), split_axis=1, concat_axis=0, tiled=True
    )
    grad_summed = (
        grad_back.reshape(experts, 2, capacity, width_all)
        .astype(jnp.float32)
        .sum(axis=1)
        .reshape(experts * capacity, width_all)
    )
    grad_moe_in = jnp.sum(grad_summed[target].reshape(tok_rows, TOP, width_all), axis=1)
    (grad_logits,) = gate_pull(grad_gates)
    grad_logits_low = grad_logits.astype(jnp.bfloat16)
    router_part = contract_rows(moe_in, grad_logits_low)
    grad_moe_in = grad_moe_in + contract_cols(grad_logits_low, router_weight)
    grad_resid_norm, moe_gain_part = moe_pull(grad_moe_in)
    grad_resid = grad_out + grad_resid_norm
    seq_grad = lax.all_gather(grad_resid.astype(jnp.bfloat16), "gy", axis=0, tiled=True)
    grad_mixed = contract_cols(seq_grad, out_rows).astype(jnp.bfloat16)
    out_part = contract_rows(seq_grad, mixed_seq)

    def backward_block(running, pieces):
        grad_key, grad_value = running
        query_block, grad_block, log_block, doc_block = pieces
        scores = block_scores(query_block, doc_block)
        weights = jnp.exp(scores - log_block[..., None])
        grad_value = grad_value + jnp.einsum(
            "hqk,qhd->khd",
            weights.astype(jnp.bfloat16),
            grad_block,
            preferred_element_type=jnp.float32,
        )
        grad_weights = jnp.einsum(
            "qhd,khd->hqk", grad_block, value_ready, preferred_element_type=jnp.float32
        )
        inner_sum = jnp.sum(weights * grad_weights, axis=-1, keepdims=True)
        grad_scores = (weights * (grad_weights - inner_sum)).astype(jnp.bfloat16)
        grad_query = (
            jnp.einsum("hqk,khd->qhd", grad_scores, key_ready, preferred_element_type=jnp.float32)
            * score_scale
        )
        grad_key = (
            grad_key
            + jnp.einsum(
                "hqk,qhd->khd", grad_scores, query_block, preferred_element_type=jnp.float32
            )
            * score_scale
        )
        return ((grad_key, grad_value), grad_query)

    empty_heads = jnp.zeros((length, local_heads, HD), jnp.float32)
    grad_mixed_blocks = grad_mixed.reshape(block_count, block_rows, local_heads, HD)
    (key_grad_heads, value_grad_heads), query_grad_blocks = lax.scan(
        backward_block,
        (empty_heads, empty_heads),
        (query_blocks, grad_mixed_blocks, log_totals, doc_blocks),
    )
    query_raw_grad, query_gain_part = query_pull(query_grad_blocks.reshape(length, local_heads, HD))
    key_raw_grad, key_gain_part = key_pull(key_grad_heads)
    grad_queries = query_raw_grad.reshape(length, local_width).astype(jnp.bfloat16)
    grad_keys = key_raw_grad.reshape(length, local_width).astype(jnp.bfloat16)
    grad_values = value_grad_heads.reshape(length, local_width).astype(jnp.bfloat16)
    query_part = contract_rows(seq_acts, grad_queries)
    key_part = contract_rows(seq_acts, grad_keys)
    value_part = contract_rows(seq_acts, grad_values)
    query_sum, key_sum, value_sum, out_sum_rows = (
        lax.psum_scatter(
            query_part.astype(jnp.bfloat16), "gx", scatter_dimension=0, tiled=True
        ).astype(jnp.float32),
        lax.psum_scatter(
            key_part.astype(jnp.bfloat16), "gx", scatter_dimension=0, tiled=True
        ).astype(jnp.float32),
        lax.psum_scatter(
            value_part.astype(jnp.bfloat16), "gx", scatter_dimension=0, tiled=True
        ).astype(jnp.float32),
        lax.psum_scatter(
            out_part.astype(jnp.bfloat16), "gx", scatter_dimension=0, tiled=True
        ).astype(jnp.float32),
    )
    partial_sum = contract_cols(grad_queries, full_query)
    partial_sum = partial_sum + contract_cols(grad_keys, full_key)
    grad_acts = lax.psum_scatter(
        (partial_sum + contract_cols(grad_values, full_value)).astype(jnp.bfloat16),
        "gy",
        scatter_dimension=0,
        tiled=True,
    ).astype(jnp.float32)
    norm_input_grad, attn_gain_part = norm_pull(grad_acts)
    input_grad = grad_resid + norm_input_grad
    attn_gain_grad, moe_gain_grad, query_gain_grad, key_gain_grad, router_grad = lax.psum(
        (attn_gain_part, moe_gain_part, query_gain_part, key_gain_part, router_part), ("gx", "gy")
    )
    ranked = -jnp.sort(-peak_global)
    limit = jnp.sum(jnp.where(jnp.arange(NH, dtype=jnp.int32) == clip_rank[0], ranked, 0.0))
    factors = jnp.where(peak_global > limit, limit / peak_global, 1.0)
    own_factors = lax.dynamic_slice_in_dim(factors, start_head, local_heads)
    columns = jnp.repeat(jnp.sqrt(own_factors), HD)
    query_clipped = (query_weight.astype(jnp.float32) * columns[None, :]).astype(jnp.bfloat16)
    key_clipped = (key_weight.astype(jnp.float32) * columns[None, :]).astype(jnp.bfloat16)
    return (
        output,
        input_grad,
        attn_gain_grad,
        moe_gain_grad,
        query_gain_grad,
        key_gain_grad,
        query_sum,
        key_sum,
        value_sum,
        out_sum_rows.T,
        router_grad,
        gate_part[None],
        up_part[None],
        down_part[None],
        query_clipped,
        key_clipped,
        factors,
    )


def solution(mesh):
    placed = (
        P(("gx", "gy"), None),
        P(("gx", "gy"), None),
        P(("gx", "gy"), None),
        P("gx"),
        P(),
        P(),
        P(),
        P(),
        P(),
        P("gx", "gy"),
        P("gx", "gy"),
        P("gx", "gy"),
        P("gy", "gx"),
        P(),
        P(("gx", "gy"), None, None),
        P(("gx", "gy"), None, None),
        P(("gx", "gy"), None, None),
    )
    return jax.shard_map(
        local,
        mesh=mesh,
        in_specs=placed,
        out_specs=(
            P(("gx", "gy"), None),
            P(("gx", "gy"), None),
            P(),
            P(),
            P(),
            P(),
            P("gx", "gy"),
            P("gx", "gy"),
            P("gx", "gy"),
            P("gy", "gx"),
            P(),
            P(("gx", "gy"), None, None),
            P(("gx", "gy"), None, None),
            P(("gx", "gy"), None, None),
            P("gx", "gy"),
            P("gx", "gy"),
            P(),
        ),
        check_vma=False,
    )
```

profile of v0, /device:TPU:0, one launch (start us, length us, event | category | flops | bytes accessed | tf_op | source)
XLA Modules:
  0.0 2032.0 jit_solution(12574165034036365257)
XLA Ops:
  17.9 22.4 %all-gather.13.cloned.1.call-done = bf16[2048,256]{1,0:T(8,128)(2,1)} async-done(((bf16[512,256]{1,0:T(8,128)(2,1)}), bf16[2048,256]{1,0:T(8,128)(2,1)}) %all-gather.13.cloned.1.call-update) | async-done | bytes 1048592 | tf_op jit(solution)/shard_map/all_gather | solution.py:92
  40.3 38.7 %all-gather.7.cloned.1.call-done = bf16[1024,2048]{1,0:T(8,128)(2,1)} async-done(((bf16[128,2048]{1,0:T(8,128)(2,1)}), bf16[1024,2048]{1,0:T(8,128)(2,1)}) %all-gather.7.cloned.1.call-update) | async-done | bytes 4194320 | tf_op jit(solution)/shard_map/all_gather | solution.py:88
  79.0 3.8 convolution_convert_fusion.5
  83.8 24.8 %all-gather.11.cloned.1.call-done = bf16[2048,256]{1,0:T(8,128)(2,1)} async-done(((bf16[512,256]{1,0:T(8,128)(2,1)}), bf16[2048,256]{1,0:T(8,128)(2,1)}) %all-gather.11.cloned.1.call-update) | async-done | bytes 1048592 | tf_op jit(solution)/shard_map/all_gather | solution.py:91
  108.5 4.8 multiply_reduce_fusion.8
  114.9 22.5 %all-gather.9.cloned.1.call-done = bf16[2048,256]{1,0:T(8,128)(2,1)} async-done(((bf16[512,256]{1,0:T(8,128)(2,1)}), bf16[2048,256]{1,0:T(8,128)(2,1)}) %all-gather.9.cloned.1.call-update) | async-done | bytes 1048592 | tf_op jit(solution)/shard_map/all_gather | solution.py:90
  137.4 4.8 multiply_reduce_fusion.9
  148.1 11.6 while.29
  159.7 6.5 all-gather.15.cloned.1.call-done
  166.3 5.9 fusion.64
  173.4 4.5 reduce-window.6
  178.4 4.3 scatter_custom_fusion
  182.7 60.5 %reduce-scatter.7.cloned.1.call-done = f32[128,2048]{1,0:T(8,128)} async-done(((f32[1024,2048]{1,0:T(8,128)}), f32[128,2048]{1,0:T(8,128)}) %reduce-scatter.7.cloned.1.call-update) | async-done | bytes 1048592 | tf_op jit(solution)/shard_map/reduce_scatter | solution.py:147
  246.7 7.1 gather_fusion
  253.8 8.5 broadcast_in_dim.176
  262.4 4.7 all-to-all-start
  268.3 8.0 gather_fusion.2
  279.0 4.3 scatter_custom_fusion.1
  283.4 8.0 multiply_convert_fusion.1
  291.5 254.3 %all-to-all-done = bf16[32,96,2048]{2,1,0:T(8,128)(2,1)} async-done(((bf16[32,96,2048]{2,1,0:T(8,128)(2,1)}), bf16[32,96,2048]{2,1,0:T(8,128)(2,1)}, u32[]{:S(2)}, u32[]{:S(2)}) %all-to-all-start) | async-done | bytes 12582944 | tf_op jit(solution)/shard_map/all_to_all | solution.py:177
  545.8 8.5 broadcast_in_dim.179
  554.3 4.2 all-to-all-start.2
  558.5 12.1 fusion.47
  570.7 11.3 fusion.51
  582.0 255.3 %all-to-all-done.2 = bf16[32,96,2048]{2,1,0:T(8,128)(2,1)} async-done(((bf16[32,96,2048]{2,1,0:T(8,128)(2,1)}), bf16[32,96,2048]{2,1,0:T(8,128)(2,1)}, u32[]{:S(2)}, u32[]{:S(2)}) %all-to-all-start.2) | async-done | bytes 12582944 | tf_op jit(solution)/shard_map/all_to_all | solution.py:211
  837.3 17.7 multiply_convert_fusion.2
  855.0 7.2 convert_bitcast_fusion
  862.2 72.1 %copy.249 = bf16[1,3072,2048]{2,0,1:T(2,128)(2,1)} copy(bf16[1,3072,2048]{2,1,0:T(8,128)(2,1)S(1)} %convert_bitcast_fusion) | data formatting | bytes 25165824 | tf_op jit(solution)/shard_map/broadcast_in_dim | solution.py:185
  934.8 75.4 %reduce.7 = bf16[3072,2048]{1,0:T(8,128)(2,1)} reduce(bf16[3072,1,2048]{2,1,0:T(2,128)(2,1)} %bitcast.234, bf16[]{:T(256)} %broadcast.432), dimensions={1}, to_apply=%bitcast.186.reduce_sub_computation | reduce | bytes 25165826
  1010.2 24.7 %reshape.497 = bf16[32,2,98304]{2,1,0:T(2,128)(2,1)} reshape(bf16[3072,2048]{1,0:T(8,128)(2,1)} %reduce.7) | data formatting | bytes 25165824
  1035.0 4.3 all-to-all-start.1
  1039.3 13.6 fusion.49
  1052.9 15.8 fusion.39
  1068.7 22.3 %copy.248 = bf16[1,3072,2048]{2,0,1:T(2,128)(2,1)} copy(bf16[1,3072,2048]{2,1,0:T(8,128)(2,1)} %fusion.39) | data formatting | bytes 25165824 | tf_op jit(solution)/shard_map/broadcast_in_dim | solution.py:228
  1091.0 75.4 %reduce.6 = bf16[3072,2048]{1,0:T(8,128)(2,1)} reduce(bf16[3072,1,2048]{2,1,0:T(2,128)(2,1)} %bitcast.235, bf16[]{:T(256)} %broadcast.432), dimensions={1}, to_apply=%bitcast.185.reduce_sub_computation | reduce | bytes 25165826
  1166.4 24.8 %reshape.499 = bf16[32,2,98304]{2,1,0:T(2,128)(2,1)} reshape(bf16[3072,2048]{1,0:T(8,128)(2,1)} %reduce.6) | data formatting | bytes 25165824
  1191.2 126.9 %all-to-all-done.1 = bf16[32,2,98304]{2,1,0:T(2,128)(2,1)} async-done(((bf16[32,2,98304]{2,1,0:T(2,128)(2,1)}), bf16[32,2,98304]{2,1,0:T(2,128)(2,1)}, u32[]{:S(2)}, u32[]{:S(2)}) %all-to-all-start.1) | async-done | bytes 12582944 | tf_op jit(solution)/shard_map/all_to_all | solution.py:185
  1318.1 3.8 all-to-all-start.3
  1322.1 27.6 %reshape.498 = bf16[3072,1,2048]{2,1,0:T(2,128)(2,1)} reshape(bf16[32,2,98304]{2,1,0:T(2,128)(2,1)} %all-to-all-done.1) | data formatting | bytes 25165824
  1349.7 22.8 %copy.198 = f32[1,3072,2048]{2,1,0:T(8,128)} copy(bf16[1,3072,2048]{2,0,1:T(2,128)(2,1)} %bitcast.237) | data formatting | bytes 37748736
  1372.5 15.0 reduce_sum.261
  1387.5 13.7 gather_fusion.1
  1401.2 6.3 fusion.41
  1407.7 193.1 %all-to-all-done.3 = bf16[32,2,98304]{2,1,0:T(2,128)(2,1)} async-done(((bf16[32,2,98304]{2,1,0:T(2,128)(2,1)}), bf16[32,2,98304]{2,1,0:T(2,128)(2,1)}, u32[]{:S(2)}, u32[]{:S(2)}) %all-to-all-start.3) | async-done | bytes 12582944 | tf_op jit(solution)/shard_map/all_to_all | solution.py:227
  1600.7 27.5 %reshape.500 = bf16[3072,1,2048]{2,1,0:T(2,128)(2,1)} reshape(bf16[32,2,98304]{2,1,0:T(2,128)(2,1)} %all-to-all-done.3) | data formatting | bytes 25165824
  1628.2 22.8 %copy.197 = f32[1,3072,2048]{2,1,0:T(8,128)} copy(bf16[1,3072,2048]{2,0,1:T(2,128)(2,1)} %bitcast.239) | data formatting | bytes 37748736
  1651.0 15.0 reduce_sum.263
  1666.0 13.6 gather_fusion.3
  1679.6 5.7 bitcast_reduce_fusion
  1687.2 32.7 %all-gather.17.cloned.1.call-done = bf16[1024,2048]{1,0:T(8,128)(2,1)} async-done(((bf16[128,2048]{1,0:T(8,128)(2,1)}), bf16[1024,2048]{1,0:T(8,128)(2,1)}) %all-gather.17.cloned.1.call-update) | async-done | bytes 4194320 | tf_op jit(solution)/shard_map/all_gather | solution.py:243
  1719.9 3.8 convolution_convert_fusion.4
  1723.9 4.7 convolution_convert_fusion
  1728.7 20.0 while.30
  1750.0 4.8 convolution_convert_fusion.1
  1764.3 4.7 convolution_convert_fusion.3
  1773.1 4.6 convolution_convert_fusion.2
  1785.6 40.6 %pmax.7 = f32[16]{0:T(128)S(1)} all-reduce(f32[16]{0:T(128)S(1)} %dynamic_update_slice.19), channel_id=1, replica_groups=mesh['gx'=4,'gy'=8] {'gx','gy'}, use_global_device_ids=true, to_apply=%region_49.50 | all-reduce | flops 16 | bytes 128 | tf_op jit(solution)/shard_map/pmax | solution.py:146
  1829.8 12.1 convolution_bitcast_fusion
  1841.9 11.1 convolution_bitcast_fusion.1
  1853.1 11.7 convolution_bitcast_fusion.2
  1873.2 21.8 %reduce-scatter.9.cloned.1.call-done = bf16[128,2048]{1,0:T(8,128)(2,1)} async-done(((bf16[1024,2048]{1,0:T(8,128)(2,1)}), bf16[128,2048]{1,0:T(8,128)(2,1)}) %reduce-scatter.9.cloned.1.call-update) | async-done | bytes 524304 | tf_op jit(solution)/shard_map/reduce_scatter | solution.py:307
  1896.9 3.7 fusion.60
  1900.5 39.7 %all-reduce.6 = (f32[2048]{0:T(1024)}, f32[2048]{0:T(1024)}, f32[128]{0:T(128)}, f32[128]{0:T(128)}) all-reduce(f32[2048]{0:T(1024)S(1)} %get-tuple-element.402, f32[2048]{0:T(1024)S(1)} %get-tuple-element.400, f32[128]{0:T(128)S(1)} %get-tuple-element.398, f32[128]{0:T(128)S(1)} %get-tuple-element.396), channel_id=1, replica_groups=mesh['gx'=4,'gy'=8] {'gx','gy'}, use_global_device_ids=true, to_apply=%region_36.37 | all-reduce | flops 4352 | bytes 34816 | tf_op jit(solution)/shard_map/psum | solution.py:315
  1940.3 83.4 %all-reduce.9.cloned.1.call-done = f32[2048,16]{0,1:T(8,128)} async-done(((f32[2048,16]{0,1:T(8,128)}), f32[2048,16]{0,1:T(8,128)}) %all-reduce.9.cloned.1.call-update) | async-done | bytes 131088 | tf_op jit(solution)/shard_map/psum | solution.py:315
  (366 shorter events, 98.7 us)
Async XLA Ops:
  7.2 830.1 %copy-start = (bf16[1,512,2048]{2,1,0:T(8,128)(2,1)S(1)}, bf16[1,512,2048]{2,1,0:T(8,128)(2,1)}, u32[]{:S(2)}) copy-start(bf16[1,512,2048]{2,1,0:T(8,128)(2,1)} %param.37) | copy-start | bytes 6291460
  7.2 33.1 %all-gather.13.cloned.1.call-start = ((), (), s32[]{:S(2)}) async-start(), calls=%async_computation.13 | async-start | bytes 1310720 | tf_op jit(solution)/shard_map/all_gather | solution.py:92
  7.9 71.0 %all-gather.7.cloned.1.call-start = ((), (), s32[]{:S(2)}) async-start(), calls=%async_computation.10 | async-start | bytes 4718592 | tf_op jit(solution)/shard_map/all_gather | solution.py:88
  12.4 96.1 %all-gather.11.cloned.1.call-start = ((), (), s32[]{:S(2)}) async-start(), calls=%async_computation.12 | async-start | bytes 1310720 | tf_op jit(solution)/shard_map/all_gather | solution.py:91
  13.1 124.3 %all-gather.9.cloned.1.call-start = ((), (), s32[]{:S(2)}) async-start(), calls=%async_computation.11 | async-start | bytes 1310720 | tf_op jit(solution)/shard_map/all_gather | solution.py:90
  13.7 152.6 %all-gather.15.cloned.1.call-start = ((), (), s32[]{:S(2)}) async-start(), calls=%async_computation.14 | async-start | bytes 1310720 | tf_op jit(solution)/shard_map/all_gather | solution.py:93
  14.3 228.9 %reduce-scatter.7.cloned.1.call-start = ((), (), s32[]{:S(2)}) async-start(), calls=%async_computation.15 | async-start | bytes 9437184 | tf_op jit(solution)/shard_map/reduce_scatter | solution.py:147
  113.3 28.9 %copy-start.58 = (f32[1024,2]{0,1:T(2,128)}, f32[1024,2]{0,1:T(2,128)S(1)}, u32[]{:S(2)}) copy-start(f32[1024,2]{0,1:T(2,128)S(1)} %get-tuple-element.479) | copy-start | bytes 24580
  114.8 29.9 %copy-start.11 = (f32[1024,2,128]{2,0,1:T(8,128)}, f32[1024,2,128]{2,0,1:T(8,128)S(1)}, u32[]{:S(2)}) copy-start(f32[1024,2,128]{2,0,1:T(8,128)S(1)} %copy.163) | copy-start | bytes 3145732
  114.9 29.9 %copy-start.47 = (f32[1024,2]{0,1:T(2,128)}, f32[1024,2]{0,1:T(2,128)S(1)}, u32[]{:S(2)}) copy-start(f32[1024,2]{0,1:T(2,128)S(1)} %fusion.77) | copy-start | bytes 24580
  114.9 29.9 %copy-start.74 = (f32[128]{0:T(128)S(1)}, f32[128]{0:T(128)}, u32[]{:S(2)}) copy-start(f32[128]{0:T(128)} %param.28) | copy-start | bytes 1540
  114.9 29.9 %copy-start.76 = (f32[128]{0:T(128)S(1)}, f32[128]{0:T(128)}, u32[]{:S(2)}) copy-start(f32[128]{0:T(128)} %param.29) | copy-start | bytes 1540
  142.2 5.3 copy-start.60
  159.7 12.5 copy-start.2
  159.7 12.5 copy-start.4
  159.7 12.4 copy-start.43
  159.7 12.4 copy-start.54
  159.7 12.4 copy-start.78
  172.2 71.0 %copy-start.14 = (bf16[128,2048]{1,0:T(8,128)(2,1)S(1)}, bf16[128,2048]{1,0:T(8,128)(2,1)}, u32[]{:S(2)}) copy-start(bf16[128,2048]{1,0:T(8,128)(2,1)} %param.21) | copy-start | bytes 1572868
  172.2 73.5 %copy-start.45 = (f32[2048]{0:T(1024)S(1)}, f32[2048]{0:T(1024)}, u32[]{:S(2)}) copy-start(f32[2048]{0:T(1024)} %param.27) | copy-start | bytes 24580
  178.3 100.7 %copy-start.62 = (s32[1024,1]{0,1:T(1,128)}, s32[1024,1]{0,1:T(1,128)S(1)}, u32[]{:S(2)}) copy-start(s32[1024,1]{0,1:T(1,128)S(1)} %compare_select_fusion) | copy-start | bytes 12292
  244.7 9.2 copy-start.66
  262.4 283.4 %all-to-all-start = ((bf16[32,96,2048]{2,1,0:T(8,128)(2,1)}), bf16[32,96,2048]{2,1,0:T(8,128)(2,1)}, u32[]{:S(2)}, u32[]{:S(2)}) async-start(bf16[32,96,2048]{2,1,0:T(8,128)(2,1)} %bitcast.240), calls=%async_computation.1 | async-start | bytes 25165824 | tf_op jit(solution)/shard_map/all_to_all | solution.py:177
  268.2 8.0 copy-start.39
  278.9 12.5 copy-start.35
  554.3 283.0 %all-to-all-start.2 = ((bf16[32,96,2048]{2,1,0:T(8,128)(2,1)}), bf16[32,96,2048]{2,1,0:T(8,128)(2,1)}, u32[]{:S(2)}, u32[]{:S(2)}) async-start(bf16[32,96,2048]{2,1,0:T(8,128)(2,1)} %bitcast.242), calls=%async_computation.3 | async-start | bytes 25165824 | tf_op jit(solution)/shard_map/all_to_all | solution.py:211
  558.5 12.1 copy-start.84
  855.0 7.2 copy-start.87
  1035.0 283.1 %all-to-all-start.1 = ((bf16[32,2,98304]{2,1,0:T(2,128)(2,1)}), bf16[32,2,98304]{2,1,0:T(2,128)(2,1)}, u32[]{:S(2)}, u32[]{:S(2)}) async-start(bf16[32,2,98304]{2,1,0:T(2,128)(2,1)} %reshape.497), calls=%async_computation.2 | async-start | bytes 25165824 | tf_op jit(solution)/shard_map/all_to_all | solution.py:185
  1191.2 130.7 %copy-start.16 = (bf16[128,2048]{1,0:T(8,128)(2,1)S(1)}, bf16[128,2048]{1,0:T(8,128)(2,1)}, u32[]{:S(2)}) copy-start(bf16[128,2048]{1,0:T(8,128)(2,1)} %param.22) | copy-start | bytes 1572868
  1191.2 130.8 %copy-start.63 = (s32[1024,1]{0,1:T(1,128)S(1)}, s32[1024,1]{0,1:T(1,128)}, u32[]{:S(2)}) copy-start(s32[1024,1]{0,1:T(1,128)} %copy-done.62) | copy-start | bytes 12292
  1191.2 130.8 %copy-start.71 = (f32[128]{0:T(128)S(1)}, f32[128]{0:T(128)}, u32[]{:S(2)}) copy-start(f32[128]{0:T(128)} %copy-done.70) | copy-start | bytes 1540
  1191.2 130.8 %copy-start.73 = (f32[128]{0:T(128)S(1)}, f32[128]{0:T(128)}, u32[]{:S(2)}) copy-start(f32[128]{0:T(128)} %copy-done.72) | copy-start | bytes 1540
  1318.1 282.6 %all-to-all-start.3 = ((bf16[32,2,98304]{2,1,0:T(2,128)(2,1)}), bf16[32,2,98304]{2,1,0:T(2,128)(2,1)}, u32[]{:S(2)}, u32[]{:S(2)}) async-start(bf16[32,2,98304]{2,1,0:T(2,128)(2,1)} %reshape.499), calls=%async_computation.4 | async-start | bytes 25165824 | tf_op jit(solution)/shard_map/all_to_all | solution.py:227
  1321.9 398.0 %all-gather.17.cloned.1.call-start = ((), (), s32[]{:S(2)}) async-start(), calls=%async_computation.16 | async-start | bytes 4718592 | tf_op jit(solution)/shard_map/all_gather | solution.py:243
  1387.5 13.7 copy-start.36
  1401.2 6.3 copy-start.57
  1401.2 6.4 copy-start.53
  1401.2 6.4 copy-start.42
  1401.2 6.4 copy-start.65
  1679.6 5.7 copy-start.7
  1679.6 5.7 copy-start.40
  1679.6 5.7 copy-start.46
  1679.6 5.7 copy-start.67
  1679.6 6.3 copy-start.83
  1685.9 37.8 %copy-start.15 = (f32[128,2048]{1,0:T(8,128)}, f32[128,2048]{1,0:T(8,128)S(1)}, u32[]{:S(2)}) copy-start(f32[128,2048]{1,0:T(8,128)S(1)} %get-tuple-element.483) | copy-start | bytes 3145732
  1687.1 178.5 %reduce-scatter.17.cloned.1.call-start = ((), (), s32[]{:S(2)}) async-start(), calls=%async_computation.21 | async-start | bytes 1310720 | tf_op jit(solution)/shard_map/reduce_scatter | solution.py:301
  1728.6 139.1 %reduce-scatter.15.cloned.1.call-start = ((), (), s32[]{:S(2)}) async-start(), calls=%async_computation.20 | async-start | bytes 1310720 | tf_op jit(solution)/shard_map/reduce_scatter | solution.py:298
  1754.9 114.6 %reduce-scatter.11.cloned.1.call-start = ((), (), s32[]{:S(2)}) async-start(), calls=%async_computation.18 | async-start | bytes 1310720 | tf_op jit(solution)/shard_map/reduce_scatter | solution.py:292
  1764.3 5.7 copy-start.59
  1769.0 102.5 %reduce-scatter.13.cloned.1.call-start = ((), (), s32[]{:S(2)}) async-start(), calls=%async_computation.19 | async-start | bytes 1310720 | tf_op jit(solution)/shard_map/reduce_scatter | solution.py:295
  1777.8 117.2 %reduce-scatter.9.cloned.1.call-start = ((), (), s32[]{:S(2)}) async-start(), calls=%async_computation.17 | async-start | bytes 4718592 | tf_op jit(solution)/shard_map/reduce_scatter | solution.py:307
  1784.0 44.9 %copy-start.31 = (bf16[512,256]{1,0:T(8,128)(2,1)S(1)}, bf16[512,256]{1,0:T(8,128)(2,1)}, u32[]{:S(2)}) copy-start(bf16[512,256]{1,0:T(8,128)(2,1)} %param.31) | copy-start | bytes 786436
  1784.0 44.9 %copy-start.32 = (bf16[512,256]{1,0:T(8,128)(2,1)S(1)}, bf16[512,256]{1,0:T(8,128)(2,1)}, u32[]{:S(2)}) copy-start(bf16[512,256]{1,0:T(8,128)(2,1)} %param.30) | copy-start | bytes 786436
  1784.0 239.7 %all-reduce.9.cloned.1.call-start = ((), (), s32[]{:S(2)}) async-start(), calls=%async_computation.22 | async-start | bytes 262144 | tf_op jit(solution)/shard_map/psum | solution.py:315
  1828.7 13.2 copy-start.86
  1829.8 12.1 copy-start.89
  1841.9 11.2 copy-start.88
  1853.1 11.7 copy-start.18
  1864.7 30.3 %copy-start.51 = (f32[2048]{0:T(1024)S(1)}, f32[2048]{0:T(1024)}, u32[]{:S(2)}) copy-start(f32[2048]{0:T(1024)} %param.26) | copy-start | bytes 24580
  1864.7 30.3 %copy-start.69 = (f32[128]{0:T(128)S(1)}, f32[128]{0:T(128)}, u32[]{:S(2)}) copy-start(f32[128]{0:T(128)} %copy-done.68) | copy-start | bytes 1540
  1864.8 32.1 %copy-start.81 = (f32[128]{0:T(128)S(1)}, f32[128]{0:T(128)}, u32[]{:S(2)}) copy-start(f32[128]{0:T(128)} %copy-done.80) | copy-start | bytes 1540
  1864.8 32.1 %copy-start.8 = (f32[128,2048]{1,0:T(8,128)S(1)}, f32[128,2048]{1,0:T(8,128)}, u32[]{:S(2)}) copy-start(f32[128,2048]{1,0:T(8,128)} %copy-done.6) | copy-start | bytes 3145732
  1869.5 155.7 %copy-start.1 = (bf16[1,512,2048]{2,1,0:T(8,128)(2,1)S(1)}, bf16[1,512,2048]{2,1,0:T(8,128)(2,1)}, u32[]{:S(2)}) copy-start(bf16[1,512,2048]{2,1,0:T(8,128)(2,1)} %param.37) | copy-start | bytes 6291460
  (51 other events, 116.3 us)
Sparse Core Ops, SparseCore 0:
  9.6 30.6 all-gather.12
  42.8 36.1 all-gather.6
  80.6 27.9 all-gather.10
  109.9 27.4 all-gather.8
  138.8 27.3 all-gather.14
  172.3 70.8 reduce-scatter.6
  1687.3 32.5 all-gather.16
  1728.7 27.1 reduce-scatter.16
  1758.2 25.7 reduce-scatter.14
  1786.8 26.5 reduce-scatter.10
  1815.7 25.7 reduce-scatter.12
  1845.1 49.9 reduce-scatter.8
  1901.2 122.4 all-reduce.8
where the time goes:
time: 2040 us; the launch traced here: 2030 us
  waiting for transfers between devices  1150 us (56%)
  local copies, waits for them, and re-layouts  342 us (17%)
  other arithmetic  250 us (12%)
  matrix products  179 us (9%)
  blocking collectives  80.3 us (4%)
    all_to_all x1, waiting for transfers between devices, local(): lax.all_to_all(grad_outgoing, ('gx', 'gy'), split_axis=0, concat_axis=1,...  255 us
    all_to_all x1, waiting for transfers between devices, local(): lax.all_to_all(outgoing, ('gx', 'gy'), split_axis=0, concat_axis=1, tiled...  254 us
    all_to_all x1, waiting for transfers between devices, local(): lax.all_to_all(grad_in.astype(jnp.bfloat16)[None], ('gx', 'gy'), split_ax...  193 us
    unnamed x174, local copies, waits for them, and re-layouts  159 us
    unnamed x4, other arithmetic  151 us
    all_to_all x1, waiting for transfers between devices, local(): lax.all_to_all(produced[None], ('gx', 'gy'), split_axis=1, concat_axis=0,...  127 us
    psum x1, waiting for transfers between devices, local(): lax.psum((attn_gain_part, moe_gain_part, query_gain_part, key_gain_part,...  83.4 us
    broadcast_in_dim x1, local copies, waits for them, and re-layouts, local(): produced[None]  72.1 us
  transfers between devices with their start and end apart: 17, of which 13 were waited for; matrix products, arithmetic and copies ran while one was open for 21% of the time, Pallas kernels for 0%

commit v1 on v0

--- a/solution.py
+++ b/solution.py
@@ -50,6 +50,15 @@
     return chosen / jnp.sum(chosen, axis=-1, keepdims=True)
 
 
+def dense_gates(all_ids, logits, expert):
+    shares = jax.nn.softmax(logits, axis=-1)
+    columns = jnp.arange(logits.shape[-1], dtype=jnp.int32)
+    routed = jnp.any(all_ids[:, :, None] == columns[None, None, :], axis=1)
+    chosen = jnp.where(routed, shares, 0.0)
+    own = jnp.sum(jnp.where(columns[None, :] == expert, chosen, 0.0), axis=-1)
+    return own / jnp.sum(chosen, axis=-1)
+
+
 def contract_rows(left_side, right_side):
     return lax.dot_general(
         left_side, right_side, (((0,), (0,)), ((), ())), preferred_element_type=jnp.float32
@@ -60,6 +69,139 @@
     return lax.dot_general(
         left_side, right_side, (((1,), (1,)), ((), ())), preferred_element_type=jnp.float32
     )
+
+
+def routed_experts(
+    moe_in, cotangent, expert_ids, gate_share, router_weight, gate_weight, up_weight, down_weight
+):
+    tok_rows = moe_in.shape[0]
+    experts = router_weight.shape[1]
+    width_all = moe_in.shape[1]
+    capacity = tok_rows * TOP * 3 // (2 * experts)
+    route_count = tok_rows * TOP
+    flat_ids = expert_ids.reshape(route_count)
+    onehot = (flat_ids[:, None] == jnp.arange(experts, dtype=jnp.int32)[None, :]).astype(jnp.int32)
+    earlier = jnp.cumsum(onehot, axis=0) - onehot
+    slot_index = jnp.sum(earlier * onehot, axis=1)
+    target = flat_ids * capacity + slot_index
+    source = (
+        jnp.full((experts * capacity,), tok_rows, jnp.int32)
+        .at[target]
+        .set(jnp.arange(route_count, dtype=jnp.int32) // TOP)
+    )
+    padded_in = jnp.concatenate([moe_in, jnp.zeros((1, width_all), jnp.bfloat16)], axis=0)
+    packed = padded_in[source].reshape(experts, 1, capacity, width_all)
+    outgoing = jnp.broadcast_to(packed, (experts, 2, capacity, width_all)).reshape(
+        2 * experts, capacity, width_all
+    )
+    arrived = lax.all_to_all(outgoing, ("gx", "gy"), split_axis=0, concat_axis=1, tiled=True)[0]
+    gate_in = gate_weight[0]
+    up_in = up_weight[0]
+    down_in = down_weight[0]
+    gate_val = jnp.dot(arrived, gate_in, preferred_element_type=jnp.float32)
+    up_val = jnp.dot(arrived, up_in, preferred_element_type=jnp.float32)
+    hidden = (jax.nn.silu(gate_val) * up_val).astype(jnp.bfloat16)
+    produced = jnp.dot(hidden, down_in, preferred_element_type=jnp.float32).astype(jnp.bfloat16)
+    returned = lax.all_to_all(produced[None], ("gx", "gy"), split_axis=1, concat_axis=0, tiled=True)
+    summed = (
+        returned.reshape(experts, 2, capacity, width_all)
+        .astype(jnp.float32)
+        .sum(axis=1)
+        .reshape(experts * capacity, width_all)
+    )
+    route_out = summed[target]
+    gates_flat = gate_share.reshape(route_count)
+    moe_out = jnp.sum((gates_flat[:, None] * route_out).reshape(tok_rows, TOP, width_all), axis=1)
+    grad_out = cotangent.astype(jnp.float32)
+    grad_gates = jnp.sum(
+        route_out.reshape(tok_rows, TOP, width_all) * grad_out[:, None, :], axis=-1
+    )
+    slot_gate = jnp.zeros((experts * capacity,), jnp.float32).at[target].set(gates_flat)
+    padded_grad = jnp.concatenate([grad_out, jnp.zeros((1, width_all), jnp.float32)], axis=0)
+    grad_packed = (
+        (slot_gate[:, None] * padded_grad[source])
+        .astype(jnp.bfloat16)
+        .reshape(experts, 1, capacity, width_all)
+    )
+    grad_outgoing = jnp.broadcast_to(grad_packed, (experts, 2, capacity, width_all)).reshape(
+        2 * experts, capacity, width_all
+    )
+    grad_arrived = lax.all_to_all(
+        grad_outgoing, ("gx", "gy"), split_axis=0, concat_axis=1, tiled=True
+    )[0]
+    rows_in, grad_use = (arrived, grad_arrived)
+    gate_use, up_use, hidden_use = (gate_val, up_val, hidden)
+    sigmoid_gate = jax.nn.sigmoid(gate_use)
+    silu_gate = gate_use * sigmoid_gate
+    grad_hidden = contract_cols(grad_use, down_in)
+    down_part = contract_rows(hidden_use, grad_use)
+    grad_gate = (
+        grad_hidden * up_use * sigmoid_gate * (1.0 + gate_use * (1.0 - sigmoid_gate))
+    ).astype(jnp.bfloat16)
+    grad_up = (grad_hidden * silu_gate).astype(jnp.bfloat16)
+    gate_part = contract_rows(rows_in, grad_gate)
+    up_part = contract_rows(rows_in, grad_up)
+    grad_in = contract_cols(grad_gate, gate_in) + contract_cols(grad_up, up_in)
+    grad_back = lax.all_to_all(
+        grad_in.astype(jnp.bfloat16)[None], ("gx", "gy"), split_axis=1, concat_axis=0, tiled=True
+    )
+    grad_summed = (
+        grad_back.reshape(experts, 2, capacity, width_all)
+        .astype(jnp.float32)
+        .sum(axis=1)
+        .reshape(experts * capacity, width_all)
+    )
+    grad_moe_in = jnp.sum(grad_summed[target].reshape(tok_rows, TOP, width_all), axis=1)
+    return moe_out, grad_gates, grad_moe_in, gate_part, up_part, down_part
+
+
+def dense_experts(
+    moe_in, cotangent, expert_ids, gate_share, router_weight, gate_weight, up_weight, down_weight
+):
+    experts = router_weight.shape[1]
+    everyone = ("gx", "gy")
+    all_ids = lax.all_gather(expert_ids, everyone, axis=0, tiled=True)
+    all_cot = lax.all_gather(cotangent, everyone, axis=0, tiled=True)
+    all_moe = lax.all_gather(moe_in, everyone, axis=0, tiled=True)
+    rank = lax.axis_index("gx") * lax.axis_size("gy") + lax.axis_index("gy")
+    own_gate = dense_gates(
+        all_ids, jnp.dot(all_moe, router_weight, preferred_element_type=jnp.float32), rank // 2
+    )
+    gate_in = gate_weight[0]
+    up_in = up_weight[0]
+    down_in = down_weight[0]
+    gate_val = jnp.dot(all_moe, gate_in, preferred_element_type=jnp.float32)
+    up_val = jnp.dot(all_moe, up_in, preferred_element_type=jnp.float32)
+    sigmoid_gate = jax.nn.sigmoid(gate_val)
+    silu_gate = gate_val * sigmoid_gate
+    hidden = (silu_gate * up_val).astype(jnp.bfloat16)
+    piece = jnp.dot(hidden, down_in, preferred_element_type=jnp.float32)
+    cot_float = all_cot.astype(jnp.float32)
+    gate_dots = jnp.sum(piece * cot_float, axis=-1)
+    devices = lax.axis_size("gx") * lax.axis_size("gy")
+    dots_back = lax.all_to_all(
+        gate_dots.reshape(devices, -1), everyone, split_axis=0, concat_axis=0, tiled=True
+    )
+    dots_experts = dots_back.reshape(experts, 2, -1).sum(axis=1).T
+    matches = expert_ids[:, :, None] == jnp.arange(experts, dtype=jnp.int32)[None, None, :]
+    grad_gates = jnp.sum(jnp.where(matches, dots_experts[:, None, :], 0.0), axis=-1)
+    moe_out = lax.psum_scatter(
+        (piece * own_gate[:, None]).astype(jnp.bfloat16), everyone, scatter_dimension=0, tiled=True
+    ).astype(jnp.float32)
+    grad_use = (cot_float * own_gate[:, None]).astype(jnp.bfloat16)
+    grad_hidden = contract_cols(grad_use, down_in)
+    down_part = contract_rows(hidden, grad_use)
+    grad_gate = (
+        grad_hidden * up_val * sigmoid_gate * (1.0 + gate_val * (1.0 - sigmoid_gate))
+    ).astype(jnp.bfloat16)
+    grad_up = (grad_hidden * silu_gate).astype(jnp.bfloat16)
+    gate_part = contract_rows(all_moe, grad_gate)
+    up_part = contract_rows(all_moe, grad_up)
+    grad_in = contract_cols(grad_gate, gate_in) + contract_cols(grad_up, up_in)
+    grad_moe_in = lax.psum_scatter(
+        grad_in.astype(jnp.bfloat16), everyone, scatter_dimension=0, tiled=True
+    ).astype(jnp.float32)
+    return moe_out, grad_gates, grad_moe_in, gate_part, up_part, down_part
 
 
 def local(
@@ -81,26 +223,21 @@
     up_weight,
     down_weight,
 ):
-    tok_rows = tokens.shape[0]
     inputs = tokens.astype(jnp.float32)
     acts_float, norm_pull = jax.vjp(norm_rows, inputs, attn_gain)
     acts_low = acts_float.astype(jnp.bfloat16)
     seq_acts = lax.all_gather(acts_low, "gy", axis=0, tiled=True)
-    full_query, full_key, full_value, out_rows = (
-        lax.all_gather(query_weight, "gx", axis=0, tiled=True),
-        lax.all_gather(key_weight, "gx", axis=0, tiled=True),
-        lax.all_gather(value_weight, "gx", axis=0, tiled=True),
-        lax.all_gather(out_weight, "gx", axis=1, tiled=True),
-    )
+    in_weights = jnp.concatenate([query_weight, key_weight, value_weight], axis=1)
+    full_in = lax.all_gather(in_weights, "gx", axis=0, tiled=True)
+    out_rows = lax.all_gather(out_weight, "gx", axis=1, tiled=True)
     length = seq_acts.shape[0]
-    local_width = full_query.shape[1]
+    local_width = query_weight.shape[1]
     local_heads = local_width // HD
-    queries = jnp.dot(seq_acts, full_query, preferred_element_type=jnp.float32)
-    key_raw = jnp.dot(seq_acts, full_key, preferred_element_type=jnp.float32)
+    projected = jnp.dot(seq_acts, full_in, preferred_element_type=jnp.float32)
+    queries = projected[:, :local_width]
+    key_raw = projected[:, local_width : 2 * local_width]
     value_ready = (
-        jnp.dot(seq_acts, full_value, preferred_element_type=jnp.float32)
-        .astype(jnp.bfloat16)
-        .reshape(length, local_heads, HD)
+        projected[:, 2 * local_width :].astype(jnp.bfloat16).reshape(length, local_heads, HD)
     )
     query_float, query_pull = jax.vjp(
         prepare_heads, queries.reshape(length, local_heads, HD), query_gain
@@ -145,95 +282,29 @@
     )
     peak_global = lax.pmax(peak_local, ("gx", "gy"))
     attended = lax.psum_scatter(
-        jnp.dot(mixed_seq, out_rows, preferred_element_type=jnp.float32),
+        jnp.dot(mixed_seq, out_rows, preferred_element_type=jnp.float32).astype(jnp.bfloat16),
         "gy",
         scatter_dimension=0,
         tiled=True,
-    )
+    ).astype(jnp.float32)
     residual = inputs + attended
     moe_float, moe_pull = jax.vjp(norm_rows, residual, moe_gain)
     moe_in = moe_float.astype(jnp.bfloat16)
     logits = jnp.dot(moe_in, router_weight, preferred_element_type=jnp.float32)
     gate_share, gate_pull = jax.vjp(partial(route_gates, expert_ids), logits)
-    experts = router_weight.shape[1]
-    width_all = moe_in.shape[1]
-    capacity = tok_rows * TOP * 3 // (2 * experts)
-    route_count = tok_rows * TOP
-    flat_ids = expert_ids.reshape(route_count)
-    onehot = (flat_ids[:, None] == jnp.arange(experts, dtype=jnp.int32)[None, :]).astype(jnp.int32)
-    earlier = jnp.cumsum(onehot, axis=0) - onehot
-    slot_index = jnp.sum(earlier * onehot, axis=1)
-    target = flat_ids * capacity + slot_index
-    source = (
-        jnp.full((experts * capacity,), tok_rows, jnp.int32)
-        .at[target]
-        .set(jnp.arange(route_count, dtype=jnp.int32) // TOP)
-    )
-    padded_in = jnp.concatenate([moe_in, jnp.zeros((1, width_all), jnp.bfloat16)], axis=0)
-    packed = padded_in[source].reshape(experts, 1, capacity, width_all)
-    outgoing = jnp.broadcast_to(packed, (experts, 2, capacity, width_all)).reshape(
-        2 * experts, capacity, width_all
-    )
-    arrived = lax.all_to_all(outgoing, ("gx", "gy"), split_axis=0, concat_axis=1, tiled=True)[0]
-    gate_in = gate_weight[0]
-    up_in = up_weight[0]
-    down_in = down_weight[0]
-    gate_val = jnp.dot(arrived, gate_in, preferred_element_type=jnp.float32)
-    up_val = jnp.dot(arrived, up_in, preferred_element_type=jnp.float32)
-    hidden = (jax.nn.silu(gate_val) * up_val).astype(jnp.bfloat16)
-    produced = jnp.dot(hidden, down_in, preferred_element_type=jnp.float32).astype(jnp.bfloat16)
-    returned = lax.all_to_all(produced[None], ("gx", "gy"), split_axis=1, concat_axis=0, tiled=True)
-    summed = (
-        returned.reshape(experts, 2, capacity, width_all)
-        .astype(jnp.float32)
-        .sum(axis=1)
-        .reshape(experts * capacity, width_all)
-    )
-    route_out = summed[target]
-    gates_flat = gate_share.reshape(route_count)
-    moe_out = jnp.sum((gates_flat[:, None] * route_out).reshape(tok_rows, TOP, width_all), axis=1)
-    block_out = residual + moe_out
-    output = block_out.astype(jnp.bfloat16)
+    experts_pass = dense_experts if router_weight.shape[1] <= 2 * TOP else routed_experts
+    moe_out, grad_gates, grad_moe_in, gate_part, up_part, down_part = experts_pass(
+        moe_in,
+        cotangent,
+        expert_ids,
+        gate_share,
+        router_weight,
+        gate_weight,
+        up_weight,
+        down_weight,
+    )
+    output = (residual + moe_out).astype(jnp.bfloat16)
     grad_out = cotangent.astype(jnp.float32)
-    grad_gates = jnp.sum(
-        route_out.reshape(tok_rows, TOP, width_all) * grad_out[:, None, :], axis=-1
-    )
-    slot_gate = jnp.zeros((experts * capacity,), jnp.float32).at[target].set(gates_flat)
-    padded_grad = jnp.concatenate([grad_out, jnp.zeros((1, width_all), jnp.float32)], axis=0)
-    grad_packed = (
-        (slot_gate[:, None] * padded_grad[source])
-        .astype(jnp.bfloat16)
-        .reshape(experts, 1, capacity, width_all)
-    )
-    grad_outgoing = jnp.broadcast_to(grad_packed, (experts, 2, capacity, width_all)).reshape(
-        2 * experts, capacity, width_all
-    )
-    grad_arrived = lax.all_to_all(
-        grad_outgoing, ("gx", "gy"), split_axis=0, concat_axis=1, tiled=True
-    )[0]
-    rows_in, grad_use = (arrived, grad_arrived)
-    gate_use, up_use, hidden_use = (gate_val, up_val, hidden)
-    sigmoid_gate = jax.nn.sigmoid(gate_use)
-    silu_gate = gate_use * sigmoid_gate
-    grad_hidden = contract_cols(grad_use, down_in)
-    down_part = contract_rows(hidden_use, grad_use)
-    grad_gate = (
-        grad_hidden * up_use * sigmoid_gate * (1.0 + gate_use * (1.0 - sigmoid_gate))
-    ).astype(jnp.bfloat16)
-    grad_up = (grad_hidden * silu_gate).astype(jnp.bfloat16)
-    gate_part = contract_rows(rows_in, grad_gate)
-    up_part = contract_rows(rows_in, grad_up)
-    grad_in = contract_cols(grad_gate, gate_in) + contract_cols(grad_up, up_in)
-    grad_back = lax.all_to_all(
-        grad_in.astype(jnp.bfloat16)[None], ("gx", "gy"), split_axis=1, concat_axis=0, tiled=True
-    )
-    grad_summed = (
-        grad_back.reshape(experts, 2, capacity, width_all)
-        .astype(jnp.float32)
-        .sum(axis=1)
-        .reshape(experts * capacity, width_all)
-    )
-    grad_moe_in = jnp.sum(grad_summed[target].reshape(tok_rows, TOP, width_all), axis=1)
     (grad_logits,) = gate_pull(grad_gates)
     grad_logits_low = grad_logits.astype(jnp.bfloat16)
     router_part = contract_rows(moe_in, grad_logits_low)
@@ -285,27 +356,21 @@
     grad_queries = query_raw_grad.reshape(length, local_width).astype(jnp.bfloat16)
     grad_keys = key_raw_grad.reshape(length, local_width).astype(jnp.bfloat16)
     grad_values = value_grad_heads.reshape(length, local_width).astype(jnp.bfloat16)
-    query_part = contract_rows(seq_acts, grad_queries)
-    key_part = contract_rows(seq_acts, grad_keys)
-    value_part = contract_rows(seq_acts, grad_values)
-    query_sum, key_sum, value_sum, out_sum_rows = (
-        lax.psum_scatter(
-            query_part.astype(jnp.bfloat16), "gx", scatter_dimension=0, tiled=True
-        ).astype(jnp.float32),
-        lax.psum_scatter(
-            key_part.astype(jnp.bfloat16), "gx", scatter_dimension=0, tiled=True
-        ).astype(jnp.float32),
-        lax.psum_scatter(
-            value_part.astype(jnp.bfloat16), "gx", scatter_dimension=0, tiled=True
-        ).astype(jnp.float32),
-        lax.psum_scatter(
-            out_part.astype(jnp.bfloat16), "gx", scatter_dimension=0, tiled=True
-        ).astype(jnp.float32),
-    )
-    partial_sum = contract_cols(grad_queries, full_query)
-    partial_sum = partial_sum + contract_cols(grad_keys, full_key)
+    grad_heads = jnp.concatenate([grad_queries, grad_keys, grad_values], axis=1)
+    in_sum = lax.psum_scatter(
+        contract_rows(seq_acts, grad_heads).astype(jnp.bfloat16),
+        "gx",
+        scatter_dimension=0,
+        tiled=True,
+    ).astype(jnp.float32)
+    query_sum = in_sum[:, :local_width]
+    key_sum = in_sum[:, local_width : 2 * local_width]
+    value_sum = in_sum[:, 2 * local_width :]
+    out_sum_rows = lax.psum_scatter(
+        out_part.astype(jnp.bfloat16), "gx", scatter_dimension=0, tiled=True
+    ).astype(jnp.float32)
     grad_acts = lax.psum_scatter(
-        (partial_sum + contract_cols(grad_values, full_value)).astype(jnp.bfloat16),
+        contract_cols(grad_heads, full_in).astype(jnp.bfloat16),
         "gy",
         scatter_dimension=0,
         tiled=True,

time: 2040 us -> 1230 us (0.60)
  waiting for transfers between devices: 1150 us -> 794 us
  local copies, waits for them, and re-layouts: 342 us -> 26.8 us
  other arithmetic: 250 us -> 46.2 us
  blocking collectives: 80.3 us -> 122 us
  matrix products: 179 us -> 207 us
    all_to_all x4 -> x1, waiting for transfers between devices: 830 us -> 7.07 us  [dense_experts(): lax.all_to_all(gate_dots.reshape(devices, -1), everyone, split_axis=0, co...]
    reduce_scatter x4, waiting for transfers between devices: 21.9 us -> 357 us  [the longest x1 150 us: dense_experts(): lax.psum_scatter(grad_in.astype(jnp.bfloat16), everyone, scatter_dimensio...]
    unnamed x174 -> x106, local copies, waits for them, and re-layouts: 159 us -> 5.06 us
    unnamed x4 -> x3, other arithmetic: 151 us -> 0.01 us
    all_gather x4, waiting for transfers between devices: 76.2 us -> 214 us  [the longest x1 81.7 us: dense_experts(): all_cot = lax.all_gather(cotangent, everyone, axis=0, tiled=True)]
    broadcast_in_dim x4 -> x0, local copies, waits for them, and re-layouts: 111 us -> none  [the longest x1 72.1 us: local(): produced[None]]
    gather x4 -> x0, local copies, waits for them, and re-layouts: 42.5 us -> none  [the longest x1 13.7 us: local(): route_out = summed[target]]
    reduce_sum x5 -> x3, other arithmetic: 41.9 us -> 0.25 us  [the longest x1 0.16 us: dense_gates(): return own / jnp.sum(chosen, axis=-1)]
  transfers between devices with their start and end apart: 17 -> 14, of which waited for: 13 -> 12; matrix products, arithmetic and copies ran while one was open for 21% -> 14% of each run, Pallas kernels for 0% -> 0%
where the time goes in v1:
time: 1230 us; the launch traced here: 1220 us
  waiting for transfers between devices  794 us (65%)
  matrix products  207 us (17%)
  blocking collectives  122 us (10%)
  other arithmetic  46.2 us (4%)
  local copies, waits for them, and re-layouts  26.8 us (2%)
  between operations  15.6 us (1%)
    reduce_scatter x1, waiting for transfers between devices, dense_experts(): lax.psum_scatter(grad_in.astype(jnp.bfloat16), everyone, scatter_dimensio...  150 us
    reduce_scatter x1, waiting for transfers between devices, dense_experts(): lax.psum_scatter((piece * own_gate[:, None]).astype(jnp.bfloat16), everyo...  146 us
    psum x1, waiting for transfers between devices, local(): lax.psum((attn_gain_part, moe_gain_part, query_gain_part, key_gain_part,...  86.6 us
    all_gather x1, waiting for transfers between devices, dense_experts(): all_cot = lax.all_gather(cotangent, everyone, axis=0, tiled=True)  81.7 us
    all_gather x1, waiting for transfers between devices, dense_experts(): all_moe = lax.all_gather(moe_in, everyone, axis=0, tiled=True)  72.7 us
    dot_general x6, matrix products, contract_cols(): lax.dot_general(left_side, right_side, (((1,), (1,)), ((), ())), preferre...  71.7 us
    reduce_scatter x1, waiting for transfers between devices, local(): lax.psum_scatter(contract_rows(seq_acts, grad_heads).astype(jnp.bfloat16)...  60.6 us
    all_gather x1, waiting for transfers between devices, local(): full_in = lax.all_gather(in_weights, 'gx', axis=0, tiled=True)  58.9 us
  transfers between devices with their start and end apart: 14, of which 12 were waited for; matrix products, arithmetic and copies ran while one was open for 14% of the time, Pallas kernels for 0%

profile of v1, /device:TPU:0, one launch (start us, length us, event | category | flops | bytes accessed | tf_op | source)
XLA Modules:
  0.0 1216.1 jit_solution(5947473423096933716)
XLA Ops:
  7.3 2.2 pad_maximum_fusion.1
  11.8 2.0 fusion.62
  14.7 2.8 fusion.73
  17.5 58.9 %all-gather.9.cloned.1.call-done = bf16[2048,768]{1,0:T(8,128)(2,1)} async-done(((bf16[512,768]{1,0:T(8,128)(2,1)}), bf16[2048,768]{1,0:T(8,128)(2,1)}) %all-gather.9.cloned.1.call-update) | async-done | bytes 3145744 | tf_op jit(solution)/shard_map/all_gather | solution.py:231
  76.4 37.9 %all-gather.7.cloned.1.call-done = bf16[1024,2048]{1,0:T(8,128)(2,1)} async-done(((bf16[128,2048]{1,0:T(8,128)(2,1)}), bf16[1024,2048]{1,0:T(8,128)(2,1)}) %all-gather.7.cloned.1.call-update) | async-done | bytes 4194320 | tf_op jit(solution)/shard_map/all_gather | solution.py:229
  114.3 6.2 fusion.92
  122.8 1.3 copy.147
  124.2 1.5 copy.144
  125.7 2.4 copy.148
  128.5 1.6 multiply_multiply_fusion
  131.5 11.4 while.29
  133.0 1.5 fusion.147
  134.5 1.7 fusion.148
  138.7 1.5 fusion.147
  140.2 1.7 fusion.148
  143.8 4.7 convolution_convert_fusion
  148.8 50.7 %reduce-scatter.7.cloned.1.call-done = bf16[128,2048]{1,0:T(8,128)(2,1)} async-done(((bf16[1024,2048]{1,0:T(8,128)(2,1)}), bf16[128,2048]{1,0:T(8,128)(2,1)}) %reduce-scatter.7.cloned.1.call-update) | async-done | bytes 524304 | tf_op jit(solution)/shard_map/reduce_scatter | solution.py:284
  199.5 1.5 multiply_reduce_fusion.7
  201.0 2.2 multiply_convert_fusion.5
  203.8 41.6 %all_gather.25 = s32[4096,8]{0,1:T(8,128)S(1)} all-gather(s32[128,8]{0,1:T(8,128)S(1)} %copy-done.39), channel_id=1, replica_groups=mesh['gx'=4,'gy'=8] {'gx','gy'}, dimensions={0}, use_global_device_ids=true | all-gather | bytes 135168 | tf_op jit(solution)/shard_map/all_gather | solution.py:163
  245.8 72.7 %all-gather.13.cloned.1.call-done = bf16[4096,2048]{1,0:T(8,128)(2,1)} async-done(((bf16[128,2048]{1,0:T(8,128)(2,1)}), bf16[4096,2048]{1,0:T(8,128)(2,1)}) %all-gather.13.cloned.1.call-update) | async-done | bytes 16777232 | tf_op jit(solution)/shard_map/all_gather | solution.py:165
  318.5 10.4 fusion.91
  329.4 12.5 %fusion.53 = f32[4096,512]{1,0:T(8,128)} fusion(bf16[4096,2048]{1,0:T(8,128)(2,1)S(1)} %copy-done.5, bf16[1,2048,512]{2,1,0:T(8,128)(2,1)} %param.36), kind=kOutput, calls=%fused_computation.76 | convolution fusion | flops 8589934592 | bytes 27262976 | tf_op jit(solution)/shard_map/dot_general | solution.py:174
  341.9 11.0 fusion.57
  352.9 81.7 %all-gather.15.cloned.1.call-done = bf16[4096,2048]{1,0:T(8,128)(2,1)} async-done(((bf16[128,2048]{1,0:T(8,128)(2,1)}), bf16[4096,2048]{1,0:T(8,128)(2,1)}) %all-gather.15.cloned.1.call-update) | async-done | bytes 16777232 | tf_op jit(solution)/shard_map/all_gather | solution.py:164
  434.7 20.8 %multiply_convert_fusion.2 = (bf16[4096,512]{1,0:T(8,128)(2,1)}, bf16[4096,512]{1,0:T(8,128)(2,1)S(1)}, bf16[4096,512]{1,0:T(8,128)(2,1)}) fusion(f32[4096,512]{1,0:T(8,128)} %fusion.57, f32[4096,512]{1,0:T(8,128)} %fusion.53, bf16[1,512,2048]{2,1,0:T(8,128)(2,1)S(1)} %copy-done, bf16[4096,2048]{1,0:T(8,128)(2,1)} %all-gather.15.cloned.1.call-done, ...), kind=kOutput, calls=%fused_computation.57 | convolution fusion | flops 8646557696 | bytes 48250880 | tf_op jit(solution)/shard_map/dot_general | solution.py:69
  455.5 14.6 %fusion.55 = f32[4096,2048]{1,0:T(8,128)} fusion(bf16[4096,512]{1,0:T(8,128)(2,1)S(1)} %get-tuple-element.460, bf16[1,2048,512]{2,1,0:T(8,128)(2,1)S(1)} %copy-done.51), kind=kOutput, calls=%fused_computation.78 | convolution fusion | flops 8589934592 | bytes 39845888 | tf_op jit(solution)/shard_map/dot_general | solution.py:69
  470.0 22.6 %add_convert_fusion = bf16[4096,2048]{1,0:T(8,128)(2,1)} fusion(f32[4096,2048]{1,0:T(8,128)} %fusion.55, bf16[4096,512]{1,0:T(8,128)(2,1)} %get-tuple-element.459, bf16[1,2048,512]{2,1,0:T(8,128)(2,1)} %param.36), kind=kOutput, calls=%fused_computation.55 | convolution fusion | flops 8606711808 | bytes 56623104 | tf_op jit(solution)/shard_map/dot_general | solution.py:69
  492.7 1.3 fusion.90
  494.0 19.6 %fusion.40 = (f32[4096]{0:T(1024)}, bf16[4096,2048]{1,0:T(8,128)(2,1)}) fusion(bf16[4096,2048]{1,0:T(8,128)(2,1)} %all-gather.15.cloned.1.call-done, f32[4096]{0:T(1024)S(1)} %div.134, bf16[4096,512]{1,0:T(8,128)(2,1)} %get-tuple-element.461, bf16[1,512,2048]{2,1,0:T(8,128)(2,1)S(1)} %copy-done), kind=kOutput, calls=%fused_computation.54 | convolution fusion | flops 8631873536 | bytes 39878656 | tf_op jit(solution)/shard_map/dot_general | solution.py:178
  513.6 2.7 all-to-all-start
  516.4 7.1 all-to-all-done
  523.6 150.4 %reduce-scatter.11.cloned.1.call-done = bf16[128,2048]{1,0:T(8,128)(2,1)} async-done(((bf16[4096,2048]{1,0:T(8,128)(2,1)}), bf16[128,2048]{1,0:T(8,128)(2,1)}) %reduce-scatter.11.cloned.1.call-update) | async-done | bytes 524304 | tf_op jit(solution)/shard_map/reduce_scatter | solution.py:201
  674.0 2.0 multiply_reduce_fusion.3
  676.0 3.0 fusion.87
  679.1 38.4 %all-gather.17.cloned.1.call-done = bf16[1024,2048]{1,0:T(8,128)(2,1)} async-done(((bf16[128,2048]{1,0:T(8,128)(2,1)}), bf16[1024,2048]{1,0:T(8,128)(2,1)}) %all-gather.17.cloned.1.call-update) | async-done | bytes 4194320 | tf_op jit(solution)/shard_map/all_gather | solution.py:314
  717.6 4.3 convolution_convert_fusion.4
  723.0 19.8 %while.30 = (s32[]{:T(128)}, f32[1024,2,128]{0,2,1:T(8,128)S(1)}, f32[1024,2,128]{0,2,1:T(8,128)}, f32[2,512,2,128]{3,1,0,2:T(8,128)}, bf16[2,512,2,128]{3,1,2,0...) while((s32[]{:T(128)}, f32[1024,2,128]{0,2,1:T(8,128)S(1)}, ...), condition=%wide.region_30.31_spmd.clone, body=%wide.region_28.30_spmd.clone.sunk | while | flops 1359870976 | bytes 64526696 | solution.py:349
  725.3 1.5 fusion.159
  726.9 1.8 multiply_reduce_fusion.13
  728.7 1.4 multiply_convert_fusion.10
  735.1 1.5 fusion.159
  736.7 1.9 multiply_reduce_fusion.13
  738.5 1.4 multiply_convert_fusion.10
  742.8 4.8 convolution_convert_fusion.3
  748.6 1.3 copy.159
  749.9 3.2 multiply_add_fusion.3
  756.1 2.1 fusion.66
  758.2 2.1 copy.163
  760.3 2.0 fusion.65
  762.6 7.5 convolution_convert_fusion.1
  771.8 39.6 %pmax.7 = f32[16]{0:T(128)S(1)} all-reduce(f32[16]{0:T(128)S(1)} %dynamic_update_slice.19), channel_id=1, replica_groups=mesh['gx'=4,'gy'=8] {'gx','gy'}, use_global_device_ids=true, to_apply=%region_47.48 | all-reduce | flops 16 | bytes 128 | tf_op jit(solution)/shard_map/pmax | solution.py:283
  815.1 7.5 convolution_convert_fusion.2
  822.7 15.7 %fusion.46 = f32[1,512,2048]{2,1,0:T(8,128)} fusion(bf16[4096,512]{1,0:T(8,128)(2,1)} %get-tuple-element.461, bf16[4096,2048]{1,0:T(8,128)(2,1)} %all-gather.15.cloned.1.call-done, f32[4096]{0:T(1024)S(1)} %div.134), kind=kOutput, calls=%fused_computation.67 | convolution fusion | flops 8615100416 | bytes 25182208 | tf_op jit(solution)/shard_map/dot_general | solution.py:63
  838.3 13.9 %convolution_bitcast_fusion = f32[1,2048,512]{2,1,0:T(8,128)} fusion(bf16[4096,2048]{1,0:T(8,128)(2,1)} %all-gather.13.cloned.1.call-done, bf16[4096,512]{1,0:T(8,128)(2,1)S(1)} %copy-done.55), kind=kOutput, calls=%fused_computation.68 | convolution fusion | flops 8589934592 | bytes 25165824 | tf_op jit(solution)/shard_map/dot_general | solution.py:63
  852.3 10.6 convolution_bitcast_fusion.1
  865.9 1.6 fusion.63
  867.5 146.5 %reduce-scatter.9.cloned.1.call-done = bf16[128,2048]{1,0:T(8,128)(2,1)} async-done(((bf16[4096,2048]{1,0:T(8,128)(2,1)}), bf16[128,2048]{1,0:T(8,128)(2,1)}) %reduce-scatter.9.cloned.1.call-update) | async-done | bytes 524304 | tf_op jit(solution)/shard_map/reduce_scatter | solution.py:188
  1014.0 3.6 fusion.67
  1017.7 60.6 %reduce-scatter.15.cloned.1.call-done = bf16[512,768]{1,0:T(8,128)(2,1)} async-done(((bf16[2048,768]{1,0:T(8,128)(2,1)}), bf16[512,768]{1,0:T(8,128)(2,1)}) %reduce-scatter.15.cloned.1.call-update) | async-done | bytes 786448 | tf_op jit(solution)/shard_map/reduce_scatter | solution.py:360
  1078.3 2.3 fusion.89
  1080.5 40.6 %all-reduce.4 = (f32[2048]{0:T(1024)}, f32[2048]{0:T(1024)}, f32[128]{0:T(128)}, f32[128]{0:T(128)}) all-reduce(f32[2048]{0:T(1024)S(1)} %get-tuple-element.402, f32[2048]{0:T(1024)S(1)} %get-tuple-element.400, f32[128]{0:T(128)S(1)} %get-tuple-element.396, f32[128]{0:T(128)S(1)} %get-tuple-element.394), channel_id=1, replica_groups=mesh['gx'=4,'gy'=8] {'gx','gy'}, use_global_device_ids=true, to_apply=%region_36.37 | all-reduce | flops 4352 | bytes 34816 | tf_op jit(solution)/shard_map/psum | solution.py:380
  1121.2 86.6 %all-reduce.7.cloned.1.call-done = f32[2048,16]{0,1:T(8,128)} async-done(((f32[2048,16]{0,1:T(8,128)}), f32[2048,16]{0,1:T(8,128)}) %all-reduce.7.cloned.1.call-update) | async-done | bytes 131088 | tf_op jit(solution)/shard_map/psum | solution.py:380
  1207.8 1.6 copy.256
  (253 shorter events, 37.8 us)
Async XLA Ops:
  7.2 427.5 %copy-start = (bf16[1,512,2048]{2,1,0:T(8,128)(2,1)S(1)}, bf16[1,512,2048]{2,1,0:T(8,128)(2,1)}, u32[]{:S(2)}) copy-start(bf16[1,512,2048]{2,1,0:T(8,128)(2,1)} %param.37) | copy-start | bytes 6291460
  7.2 7.4 copy-start.28
  7.2 69.2 %all-gather.9.cloned.1.call-start = ((), (), s32[]{:S(2)}) async-start(), calls=%async_computation.8 | async-start | bytes 3932160 | tf_op jit(solution)/shard_map/all_gather | solution.py:231
  9.5 104.8 %all-gather.7.cloned.1.call-start = ((), (), s32[]{:S(2)}) async-start(), calls=%async_computation.7 | async-start | bytes 4718592 | tf_op jit(solution)/shard_map/all_gather | solution.py:229
  13.8 130.0 %all-gather.11.cloned.1.call-start = ((), (), s32[]{:S(2)}) async-start(), calls=%async_computation.9 | async-start | bytes 1310720 | tf_op jit(solution)/shard_map/all_gather | solution.py:232
  14.6 184.9 %reduce-scatter.7.cloned.1.call-start = ((), (), s32[]{:S(2)}) async-start(), calls=%async_computation.10 | async-start | bytes 4718592 | tf_op jit(solution)/shard_map/reduce_scatter | solution.py:284
  120.8 5.0 copy-start.37
  121.6 6.5 copy-start.44
  122.8 5.8 copy-start.42
  122.8 7.3 copy-start.32
  122.8 7.3 copy-start.30
  125.7 5.1 copy-start.6
  131.9 2.6 copy-start.3
  137.6 2.6 copy-start.3
  142.9 5.6 copy-start.46
  148.5 52.5 %copy-start.29 = (f32[2048]{0:T(1024)S(1)}, f32[2048]{0:T(1024)}, u32[]{:S(2)}) copy-start(f32[2048]{0:T(1024)} %param.27) | copy-start | bytes 24580
  148.5 55.3 %copy-start.39 = (s32[128,8]{0,1:T(8,128)S(1)}, s32[128,8]{0,1:T(8,128)}, u32[]{:S(2)}) copy-start(s32[128,8]{0,1:T(8,128)} %param.23) | copy-start | bytes 12292
  148.5 170.0 %copy-start.25 = (bf16[2048,16]{0,1:T(8,128)(2,1)S(1)}, bf16[2048,16]{0,1:T(8,128)(2,1)}, u32[]{:S(2)}) copy-start(bf16[2048,16]{0,1:T(8,128)(2,1)} %param.34) | copy-start | bytes 196612
  148.5 169.9 %all-gather.13.cloned.1.call-start = ((), (), s32[]{:S(2)}) async-start(), calls=%async_computation.11 | async-start | bytes 17301504 | tf_op jit(solution)/shard_map/all_gather | solution.py:165
  203.2 231.5 %all-gather.15.cloned.1.call-start = ((), (), s32[]{:S(2)}) async-start(), calls=%async_computation.13 | async-start | bytes 17301504 | tf_op jit(solution)/shard_map/all_gather | solution.py:164
  203.8 470.3 %reduce-scatter.11.cloned.1.call-start = ((), (), s32[]{:S(2)}) async-start(), calls=%async_computation.14 | async-start | bytes 17301504 | tf_op jit(solution)/shard_map/reduce_scatter | solution.py:201
  318.5 10.9 copy-start.5
  329.4 12.5 %copy-start.50 = (bf16[1,2048,512]{2,1,0:T(8,128)(2,1)S(1)}, bf16[1,2048,512]{2,1,0:T(8,128)(2,1)}, u32[]{:S(2)}) copy-start(bf16[1,2048,512]{2,1,0:T(8,128)(2,1)} %param.35) | copy-start | bytes 6291460
  434.6 20.8 %copy-start.51 = (bf16[1,2048,512]{2,1,0:T(8,128)(2,1)S(1)}, bf16[1,2048,512]{2,1,0:T(8,128)(2,1)}, u32[]{:S(2)}) copy-start(bf16[1,2048,512]{2,1,0:T(8,128)(2,1)} %param.35) | copy-start | bytes 6291460
  455.4 14.6 %copy-start.53 = (bf16[4096,512]{1,0:T(8,128)(2,1)}, bf16[4096,512]{1,0:T(8,128)(2,1)S(1)}, u32[]{:S(2)}) copy-start(bf16[4096,512]{1,0:T(8,128)(2,1)S(1)} %get-tuple-element.460) | copy-start | bytes 12582916
  513.6 204.0 %copy-start.24 = (bf16[256,2048]{1,0:T(8,128)(2,1)S(1)}, bf16[256,2048]{1,0:T(8,128)(2,1)}, u32[]{:S(2)}) copy-start(bf16[256,2048]{1,0:T(8,128)(2,1)} %all-gather.11.cloned.1.call-done) | copy-start | bytes 3145732
  513.6 9.8 all-to-all-start
  516.3 201.2 %all-gather.17.cloned.1.call-start = ((), (), s32[]{:S(2)}) async-start(), calls=%async_computation.15 | async-start | bytes 4718592 | tf_op jit(solution)/shard_map/all_gather | solution.py:314
  676.0 3.1 copy-start.10
  679.0 184.9 %reduce-scatter.17.cloned.1.call-start = ((), (), s32[]{:S(2)}) async-start(), calls=%async_computation.18 | async-start | bytes 1310720 | tf_op jit(solution)/shard_map/reduce_scatter | solution.py:369
  730.1 2.9 copy-start.14
  733.0 2.1 copy-start.19
  739.9 2.9 copy-start.14
  742.8 4.9 copy-start.21
  747.6 118.2 %reduce-scatter.13.cloned.1.call-start = ((), (), s32[]{:S(2)}) async-start(), calls=%async_computation.16 | async-start | bytes 4718592 | tf_op jit(solution)/shard_map/reduce_scatter | solution.py:372
  749.9 4.3 copy-start.7
  749.9 4.3 copy-start.31
  749.9 4.3 copy-start.45
  749.9 5.2 copy-start.8
  749.9 5.2 copy-start.33
  749.9 5.2 copy-start.43
  753.2 2.9 copy-start.36
  753.2 2.9 copy-start.38
  758.2 4.4 copy-start.26
  770.1 243.9 %reduce-scatter.9.cloned.1.call-start = ((), (), s32[]{:S(2)}) async-start(), calls=%async_computation.12 | async-start | bytes 17301504 | tf_op jit(solution)/shard_map/reduce_scatter | solution.py:188
  770.1 44.0 %copy-start.22 = (bf16[512,256]{1,0:T(8,128)(2,1)S(1)}, bf16[512,256]{1,0:T(8,128)(2,1)}, u32[]{:S(2)}) copy-start(bf16[512,256]{1,0:T(8,128)(2,1)} %param.31) | copy-start | bytes 786436
  770.2 44.0 %copy-start.23 = (bf16[512,256]{1,0:T(8,128)(2,1)S(1)}, bf16[512,256]{1,0:T(8,128)(2,1)}, u32[]{:S(2)}) copy-start(bf16[512,256]{1,0:T(8,128)(2,1)} %param.30) | copy-start | bytes 786436
  770.2 44.9 %copy-start.27 = (bf16[1024,2,128]{0,2,1:T(8,128)(2,1)S(1)}, bf16[1024,2,128]{0,2,1:T(8,128)(2,1)}, u32[]{:S(2)}) copy-start(bf16[1024,2,128]{0,2,1:T(8,128)(2,1)} %copy.163) | copy-start | bytes 1572868
  770.8 307.4 %reduce-scatter.15.cloned.1.call-start = ((), (), s32[]{:S(2)}) async-start(), calls=%async_computation.17 | async-start | bytes 3932160 | tf_op jit(solution)/shard_map/reduce_scatter | solution.py:360
  814.0 8.6 copy-start.52
  822.6 385.2 %all-reduce.7.cloned.1.call-start = ((), (), s32[]{:S(2)}) async-start(), calls=%async_computation.19 | async-start | bytes 262144 | tf_op jit(solution)/shard_map/psum | solution.py:380
  822.6 15.7 %copy-start.55 = (bf16[4096,512]{1,0:T(8,128)(2,1)S(1)}, bf16[4096,512]{1,0:T(8,128)(2,1)}, u32[]{:S(2)}) copy-start(bf16[4096,512]{1,0:T(8,128)(2,1)} %get-tuple-element.459) | copy-start | bytes 12582916
  822.6 29.6 %slice-start = ((s8[16777216]{0:T(1024)(128)(4,1)}), s8[4194304]{0:T(1024)(128)(4,1)S(1)}, s32[]{:S(2)}) async-start(s8[16777216]{0:T(1024)(128)(4,1)} %bitcast.170), calls=%async_computation.20 | async-start | bytes 8388608
  822.6 29.6 %slice-start.1 = ((s8[16777216]{0:T(1024)(128)(4,1)}), s8[4194304]{0:T(1024)(128)(4,1)S(1)}, s32[]{:S(2)}) async-start(s8[16777216]{0:T(1024)(128)(4,1)} %bitcast.170), calls=%async_computation.21 | async-start | bytes 8388608
  822.6 29.6 %slice-start.2 = ((s8[16777216]{0:T(1024)(128)(4,1)}), s8[4194304]{0:T(1024)(128)(4,1)S(1)}, s32[]{:S(2)}) async-start(s8[16777216]{0:T(1024)(128)(4,1)} %bitcast.170), calls=%async_computation.22 | async-start | bytes 8388608
  838.3 13.9 %slice-start.3 = ((s8[16777216]{0:T(1024)(128)(4,1)}), s8[4194304]{0:T(1024)(128)(4,1)S(1)}, s32[]{:S(2)}) async-start(s8[16777216]{0:T(1024)(128)(4,1)} %bitcast.170), calls=%async_computation.23 | async-start | bytes 8388608
  838.3 13.9 %copy-start.54 = (bf16[4096,512]{1,0:T(8,128)(2,1)S(1)}, bf16[4096,512]{1,0:T(8,128)(2,1)}, u32[]{:S(2)}) copy-start(bf16[4096,512]{1,0:T(8,128)(2,1)} %copy-done.53) | copy-start | bytes 12582916
  852.3 10.7 copy-start.12
  852.3 13.6 %copy-start.2 = (bf16[128,2048]{1,0:T(8,128)(2,1)S(1)}, bf16[128,2048]{1,0:T(8,128)(2,1)}, u32[]{:S(2)}) copy-start(bf16[128,2048]{1,0:T(8,128)(2,1)} %param.21) | copy-start | bytes 1572868
  852.3 13.6 %copy-start.34 = (f32[2048]{0:T(1024)S(1)}, f32[2048]{0:T(1024)}, u32[]{:S(2)}) copy-start(f32[2048]{0:T(1024)} %param.26) | copy-start | bytes 24580
  852.3 13.6 %copy-start.41 = (f32[128]{0:T(128)S(1)}, f32[128]{0:T(128)}, u32[]{:S(2)}) copy-start(f32[128]{0:T(128)} %copy-done.40) | copy-start | bytes 1540
  852.3 15.2 %copy-start.49 = (f32[128]{0:T(128)S(1)}, f32[128]{0:T(128)}, u32[]{:S(2)}) copy-start(f32[128]{0:T(128)} %copy-done.48) | copy-start | bytes 1540
  852.3 161.7 %copy-start.9 = (bf16[128,2048]{1,0:T(8,128)(2,1)S(1)}, bf16[128,2048]{1,0:T(8,128)(2,1)}, u32[]{:S(2)}) copy-start(bf16[128,2048]{1,0:T(8,128)(2,1)} %reduce-scatter.7.cloned.1.call-done) | copy-start | bytes 1572868
  867.5 341.8 %copy-start.1 = (bf16[1,512,2048]{2,1,0:T(8,128)(2,1)S(1)}, bf16[1,512,2048]{2,1,0:T(8,128)(2,1)}, u32[]{:S(2)}) copy-start(bf16[1,512,2048]{2,1,0:T(8,128)(2,1)} %param.37) | copy-start | bytes 6291460
  (18 other events, 23.5 us)
Sparse Core Ops, SparseCore 0:
  10.2 66.1 all-gather.8
  78.9 35.3 all-gather.6
  115.9 27.9 all-gather.10
  148.6 50.8 reduce-scatter.6
  203.3 115.1 all-gather.12
  321.6 113.0 all-gather.14
  492.8 181.1 reduce-scatter.10
  679.2 38.3 all-gather.16
  747.8 27.1 reduce-scatter.16
  778.1 50.6 reduce-scatter.12
  831.2 182.7 reduce-scatter.8
  1016.3 61.9 reduce-scatter.14
  1085.3 122.4 all-reduce.6

commit v2 on v1

--- a/solution.py
+++ b/solution.py
@@ -3,6 +3,8 @@
 import jax
 import jax.numpy as jnp
 from jax import lax
+from jax.experimental import pallas as pl
+from jax.experimental.pallas import tpu as pltpu
 from jax.sharding import PartitionSpec as P
 
 NH = 16
@@ -12,6 +14,303 @@
 
 EPSILON = 1e-06
 NEGATIVE = -1e30
+
+
+def barrier_with(partners):
+    barrier = pltpu.get_barrier_semaphore()
+    for ok, device in partners:
+        @pl.when(ok)
+        def _():
+            pl.semaphore_signal(barrier, inc=1, device_id=device, device_id_type=pl.DeviceIdType.MESH)
+    pl.semaphore_wait(barrier, sum(ok.astype(jnp.int32) for ok, _ in partners))
+
+def gather_kernel(n_z, span, own_ref, out_ref, send_sem, recv_sem, local_sem):
+    z = lax.axis_index("gx"); g = lax.axis_index("gy")
+    core = {"gx": z, "gy": g + 1 - 2 * (g % 2)}
+    xn = {"gx": z, "gy": g + 2 - 4 * ((g // 2) % 2)}
+    yn = {"gx": z, "gy": g + 4 - 8 * ((g // 4) % 2)}
+    gx_ = g + 2 - 4 * ((g // 2) % 2)
+    gy_ = g + 4 - 8 * ((g // 4) % 2)
+    gd_ = gx_ + gy_ - g
+    gc = lambda v: v + 1 - 2 * (v % 2)
+    zup = {"gx": z + 1, "gy": g}; zdn = {"gx": z - 1, "gy": g}
+    zb = z if n_z > 1 else 0
+    partners = [(z >= 0, core), (z >= 0, xn), (z >= 0, yn)]
+    if n_z > 1:
+        partners += [(z < n_z - 1, zup), (z > 0, zdn)]
+    barrier_with(partners)
+    sends = []
+    def send(ok, src, b, h, dev):
+        k = len(sends)
+        def make():
+            return pltpu.make_async_remote_copy(
+                src_ref=src, dst_ref=out_ref.at[b, h], send_sem=send_sem.at[k], recv_sem=recv_sem.at[b, h],
+                device_id=dev, device_id_type=pl.DeviceIdType.MESH)
+        sends.append((ok, make))
+        if ok is True:
+            make().start()
+        else:
+            @pl.when(ok)
+            def _(): make().start()
+    def arrive(ok, b, h):
+        def go():
+            pltpu.make_async_remote_copy(
+                src_ref=out_ref.at[b, h], dst_ref=out_ref.at[b, h], send_sem=send_sem.at[0], recv_sem=recv_sem.at[b, h],
+                device_id=core, device_id_type=pl.DeviceIdType.MESH).wait_recv()
+        if ok is True:
+            go()
+        else:
+            @pl.when(ok)
+            def _(): go()
+    own_b = zb * span + g
+    local = pltpu.make_async_copy(own_ref, out_ref.at[own_b], local_sem)
+    local.start()
+    items = [(True, zb, 0)]
+    for d in range(1, n_z):
+        items += [(z >= d, z - d, -d), (z < n_z - d, z + d, d)]
+    def and_(a, b):
+        if a is True: return b
+        if b is True: return a
+        return jnp.logical_and(a, b)
+    def first(it):
+        ok, zs, d = it
+        b = zs * span + g
+        src = (lambda h: own_ref.at[h]) if d == 0 else (lambda h: out_ref.at[b, h])
+        if d != 0:
+            arrive(ok, b, 0); arrive(ok, b, 1)
+        if n_z > 1:
+            if d <= 0:
+                for h in range(2): send(and_(ok, z < n_z - 1), src(h), b, h, zup)
+            if d >= 0:
+                for h in range(2): send(and_(ok, z > 0), src(h), b, h, zdn)
+        send(ok, src(0), b, 0, xn)
+        send(ok, src(1), b, 1, yn)
+        send(ok, src(1), b, 1, xn)
+        send(ok, src(0), b, 0, yn)
+        send(ok, src(0), b, 0, core)
+        send(ok, src(1), b, 1, core)
+    def second(it):
+        ok, zs, d = it
+        b = zs * span + gx_
+        arrive(ok, b, 0)
+        send(ok, out_ref.at[b, 0], b, 0, yn)
+        send(ok, out_ref.at[b, 0], b, 0, core)
+        b = zs * span + gy_
+        arrive(ok, b, 1)
+        send(ok, out_ref.at[b, 1], b, 1, xn)
+        send(ok, out_ref.at[b, 1], b, 1, core)
+    def third(it):
+        ok, zs, d = it
+        for b, h in ((zs * span + gd_, 0), (zs * span + gd_, 1), (zs * span + gy_, 0), (zs * span + gx_, 1)):
+            arrive(ok, b, h)
+            send(ok, out_ref.at[b, h], b, h, core)
+    n = len(items)
+    for i in range(n + 2):
+        if i < n: first(items[i])
+        if 1 <= i <= n: second(items[i - 1])
+        if i >= 2: third(items[i - 2])
+    for ok, zs, d in items:
+        for gg in (g, gx_, gy_, gd_):
+            for h in range(2): arrive(ok, zs * span + gc(gg), h)
+    local.wait()
+    for ok, make in sends:
+        if ok is True: make().wait_send()
+        else:
+            @pl.when(ok)
+            def _(): make().wait_send()
+
+def all_gather(block, both, collective_id):
+    n_z = lax.axis_size("gx") if both else 1
+    span = lax.axis_size("gy")
+    rows, cols = block.shape
+    own = block.reshape(2, rows // 2, cols)
+    n_sends = (2 * n_z - 1) * 24
+    out = pl.pallas_call(
+        partial(gather_kernel, n_z, span),
+        out_shape=jax.ShapeDtypeStruct((n_z * span, 2, rows // 2, cols), block.dtype),
+        in_specs=[pl.BlockSpec(memory_space=pltpu.VMEM)],
+        out_specs=pl.BlockSpec(memory_space=pl.ANY),
+        scratch_shapes=[pltpu.SemaphoreType.DMA((n_sends,)), pltpu.SemaphoreType.DMA((n_z * span, 2)), pltpu.SemaphoreType.DMA],
+        compiler_params=pltpu.CompilerParams(collective_id=collective_id, has_side_effects=True),
+        name="gather_all" if both else "gather_plane",
+    )(own)
+    return out.reshape(n_z * span * rows, cols)
+
+
+def add_into(dst, parts, rows):
+    step = min(rows, 32)
+
+    @pl.loop(0, rows // step)
+    def _(r):
+        at = pl.ds(pl.multiple_of(r * step, step), step)
+        if len(parts) == 2 and dst.dtype == jnp.bfloat16:
+            dst[at, :] = parts[0][at, :] + parts[1][at, :]
+        else:
+            total = parts[0][at, :].astype(jnp.float32)
+            for term in parts[1:]:
+                total = total + term[at, :].astype(jnp.float32)
+            dst[at, :] = total.astype(dst.dtype)
+
+
+def scatter_kernel(chain, n_i, rows, part_ref, out_ref, held, from_core, from_a, from_b, from_z,
+                   load_sem, core_send, a_send, b_send, z_send, core_recv, a_recv, b_recv, z_recv):
+    z = lax.axis_index("gx"); g = lax.axis_index("gy")
+    flip_x = g + 2 - 4 * ((g // 2) % 2)
+    flip_y = g + 4 - 8 * ((g // 4) % 2)
+    flip_c = lambda v: v + 1 - 2 * (v % 2)
+    quads = (flip_x + flip_y - g, flip_x, flip_y, g)
+    core = {"gx": z, "gy": flip_c(g)}
+    xn = {"gx": z, "gy": flip_x}
+    yn = {"gx": z, "gy": flip_y}
+    every = z >= 0
+    partners = [(every, core), (every, xn), (every, yn)]
+    if chain:
+        partners += [(every, {"gx": lax.rem(z + j, n_i), "gy": g}) for j in range(1, n_i)]
+    barrier_with(partners)
+    mesh_id = pl.DeviceIdType.MESH
+
+    def item(i):
+        return lax.rem(z + n_i - 1 - i + n_i, n_i) if chain else i
+
+    def block(it, gg):
+        return part_ref.at[it, gg]
+
+    def remote(src, dst, ssem, rsem, dev):
+        return pltpu.make_async_remote_copy(src_ref=src, dst_ref=dst, send_sem=ssem, recv_sem=rsem, device_id=dev, device_id_type=mesh_id)
+
+    def core_copy(i, q):
+        it = item(i)
+        return remote(block(it, flip_c(quads[q])), from_core.at[it, q], core_send.at[i, q], core_recv.at[it, q], core)
+
+    def load(i, q):
+        it = item(i)
+        return pltpu.make_async_copy(block(it, quads[q]), held.at[it, q], load_sem.at[i, q])
+
+    a_plan = ((0, 0, 0, xn), (0, 1, 0, yn), (1, 0, 1, xn), (2, 1, 1, yn))
+    def a_copy(i, k):
+        it = item(i)
+        q, h, slot, dev = a_plan[k]
+        return remote(held.at[it, q, h], from_a.at[it, h, slot], a_send.at[i, k], a_recv.at[it, h, slot], dev)
+
+    b_plan = ((2, 0, yn), (1, 1, xn))
+    def b_copy(i, h):
+        it = item(i)
+        q, _, dev = b_plan[h]
+        return remote(held.at[it, q, h], from_b.at[it, h], b_send.at[i, h], b_recv.at[it, h], dev)
+
+    def z_copy(i):
+        it = item(i)
+        return remote(held.at[it, 3], from_z.at[z], z_send.at[i], z_recv.at[z], {"gx": it, "gy": g})
+
+    def z_arrival(i):
+        it = item(i)
+        return remote(held.at[it, 3], from_z.at[it], z_send.at[i], z_recv.at[it], core)
+
+    for i in range(n_i):
+        for q in range(4):
+            core_copy(i, q).start()
+            load(i, q).start()
+
+    def stage_a(i):
+        it = item(i)
+        for q in range(4):
+            load(i, q).wait()
+            core_copy(i, q).wait_recv()
+            for h in range(2):
+                add_into(held.at[it, q, h], (held.at[it, q, h], from_core.at[it, q, h]), rows)
+            for k in range(4):
+                if a_plan[k][0] == q:
+                    a_copy(i, k).start()
+
+    def stage_b(i):
+        it = item(i)
+        for q, h, slot in ((2, 0, 0), (1, 1, 0), (3, 0, 1), (3, 1, 1)):
+            remote(held.at[it, q, h], from_a.at[it, h, slot], a_send.at[i, 0], a_recv.at[it, h, slot], core).wait_recv()
+            add_into(held.at[it, q, h], (held.at[it, q, h], from_a.at[it, h, slot]), rows)
+            if slot == 0:
+                b_copy(i, h).start()
+
+    def stage_c(i):
+        it = item(i)
+        for h in range(2):
+            b_copy(i, h).wait_recv()
+            if chain:
+                add_into(held.at[it, 3, h], (held.at[it, 3, h], from_b.at[it, h]), rows)
+            else:
+                add_into(out_ref.at[it, h], (held.at[it, 3, h], from_b.at[it, h]), rows)
+
+    def stage_d(i):
+        if i < n_i - 1:
+            z_copy(i).start()
+        else:
+            for j in range(n_i - 1):
+                z_arrival(j).wait_recv()
+            for h in range(2):
+                add_into(
+                    out_ref.at[h],
+                    [held.at[item(i), 3, h]] + [from_z.at[item(j), h] for j in range(n_i - 1)],
+                    rows,
+                )
+
+    for i in range(n_i + 2):
+        if i < n_i: stage_a(i)
+        if 0 <= i - 1 < n_i: stage_b(i - 1)
+        if 0 <= i - 2 < n_i: stage_c(i - 2)
+        if chain and 0 <= i - 2 < n_i: stage_d(i - 2)
+    for i in range(n_i):
+        for q in range(4): core_copy(i, q).wait_send()
+        for k in range(4): a_copy(i, k).wait_send()
+        for h in range(2): b_copy(i, h).wait_send()
+        if chain and i < n_i - 1: z_copy(i).wait_send()
+
+
+def reduce_scatter(part, both, collective_id, pieces=4, out_dtype=jnp.float32):
+    n_z = lax.axis_size("gx") if both else 1
+    span = lax.axis_size("gy")
+    total, cols = part.shape
+    n_i = n_z if both else pieces
+    if both:
+        rows = total // (n_z * span) // 2
+        shaped = part.reshape(n_z, span, 2, rows, cols)
+        out_shape = (2, rows, cols)
+    else:
+        rows = total // span // (2 * pieces)
+        shaped = part.reshape(span, pieces, 2, rows, cols).swapaxes(0, 1)
+        out_shape = (pieces, 2, rows, cols)
+    dma = pltpu.SemaphoreType.DMA
+    half = (rows, cols)
+    z_items = n_i if both else 1
+    z_half = half if both else (16, 128)
+    out = pl.pallas_call(
+        partial(scatter_kernel, both, n_i, rows),
+        out_shape=jax.ShapeDtypeStruct(out_shape, out_dtype),
+        in_specs=[pl.BlockSpec(memory_space=pl.ANY)],
+        out_specs=pl.BlockSpec(memory_space=pltpu.VMEM),
+        scratch_shapes=[
+            pltpu.VMEM((n_i, 4, 2) + half, jnp.bfloat16),
+            pltpu.VMEM((n_i, 4, 2) + half, jnp.bfloat16),
+            pltpu.VMEM((n_i, 2, 2) + half, jnp.bfloat16),
+            pltpu.VMEM((n_i, 2) + half, jnp.bfloat16),
+            pltpu.VMEM((z_items, 2) + z_half, jnp.bfloat16),
+            dma((n_i, 4)), dma((n_i, 4)), dma((n_i, 4)), dma((n_i, 2)), dma((n_i,)),
+            dma((n_i, 4)), dma((n_i, 2, 2)), dma((n_i, 2)), dma((n_i,)),
+        ],
+        compiler_params=pltpu.CompilerParams(collective_id=collective_id, has_side_effects=True, vmem_limit_bytes=60 << 20),
+        name="scatter_all" if both else "scatter_plane",
+    )(shaped)
+    return out.reshape(total // (n_z * span), cols)
+
+
+def gather_plane(block, collective_id):
+    if lax.axis_size("gy") == 8:
+        return all_gather(block, False, collective_id)
+    return lax.all_gather(block, "gy", axis=0, tiled=True)
+
+
+def scatter_plane(part, collective_id):
+    if lax.axis_size("gy") == 8:
+        return reduce_scatter(part, False, collective_id)
+    return lax.psum_scatter(part, "gy", scatter_dimension=0, tiled=True).astype(jnp.float32)
 
 
 def norm_rows(values, gain_row):
@@ -162,7 +461,7 @@
     everyone = ("gx", "gy")
     all_ids = lax.all_gather(expert_ids, everyone, axis=0, tiled=True)
     all_cot = lax.all_gather(cotangent, everyone, axis=0, tiled=True)
-    all_moe = lax.all_gather(moe_in, everyone, axis=0, tiled=True)
+    all_moe = all_gather(moe_in, True, 2)
     rank = lax.axis_index("gx") * lax.axis_size("gy") + lax.axis_index("gy")
     own_gate = dense_gates(
         all_ids, jnp.dot(all_moe, router_weight, preferred_element_type=jnp.float32), rank // 2
@@ -185,9 +484,7 @@
     dots_experts = dots_back.reshape(experts, 2, -1).sum(axis=1).T
     matches = expert_ids[:, :, None] == jnp.arange(experts, dtype=jnp.int32)[None, None, :]
     grad_gates = jnp.sum(jnp.where(matches, dots_experts[:, None, :], 0.0), axis=-1)
-    moe_out = lax.psum_scatter(
-        (piece * own_gate[:, None]).astype(jnp.bfloat16), everyone, scatter_dimension=0, tiled=True
-    ).astype(jnp.float32)
+    moe_out = reduce_scatter((piece * own_gate[:, None]).astype(jnp.bfloat16), True, 4)
     grad_use = (cot_float * own_gate[:, None]).astype(jnp.bfloat16)
     grad_hidden = contract_cols(grad_use, down_in)
     down_part = contract_rows(hidden, grad_use)
@@ -198,9 +495,7 @@
     gate_part = contract_rows(all_moe, grad_gate)
     up_part = contract_rows(all_moe, grad_up)
     grad_in = contract_cols(grad_gate, gate_in) + contract_cols(grad_up, up_in)
-    grad_moe_in = lax.psum_scatter(
-        grad_in.astype(jnp.bfloat16), everyone, scatter_dimension=0, tiled=True
-    ).astype(jnp.float32)
+    grad_moe_in = reduce_scatter(grad_in.astype(jnp.bfloat16), True, 4)
     return moe_out, grad_gates, grad_moe_in, gate_part, up_part, down_part
 
 
@@ -226,7 +521,7 @@
     inputs = tokens.astype(jnp.float32)
     acts_float, norm_pull = jax.vjp(norm_rows, inputs, attn_gain)
     acts_low = acts_float.astype(jnp.bfloat16)
-    seq_acts = lax.all_gather(acts_low, "gy", axis=0, tiled=True)
+    seq_acts = gather_plane(acts_low, 1)
     in_weights = jnp.concatenate([query_weight, key_weight, value_weight], axis=1)
     full_in = lax.all_gather(in_weights, "gx", axis=0, tiled=True)
     out_rows = lax.all_gather(out_weight, "gx", axis=1, tiled=True)
@@ -281,18 +576,15 @@
         jnp.full((NH,), NEGATIVE, jnp.float32), jnp.max(peak_blocks, axis=0), (start_head,)
     )
     peak_global = lax.pmax(peak_local, ("gx", "gy"))
-    attended = lax.psum_scatter(
-        jnp.dot(mixed_seq, out_rows, preferred_element_type=jnp.float32).astype(jnp.bfloat16),
-        "gy",
-        scatter_dimension=0,
-        tiled=True,
-    ).astype(jnp.float32)
+    attended = scatter_plane(
+        jnp.dot(mixed_seq, out_rows, preferred_element_type=jnp.float32).astype(jnp.bfloat16), 3
+    )
     residual = inputs + attended
     moe_float, moe_pull = jax.vjp(norm_rows, residual, moe_gain)
     moe_in = moe_float.astype(jnp.bfloat16)
     logits = jnp.dot(moe_in, router_weight, preferred_element_type=jnp.float32)
     gate_share, gate_pull = jax.vjp(partial(route_gates, expert_ids), logits)
-    experts_pass = dense_experts if router_weight.shape[1] <= 2 * TOP else routed_experts
+    experts_pass = dense_experts if lax.axis_size("gy") == 8 and router_weight.shape[1] <= 2 * TOP else routed_experts
     moe_out, grad_gates, grad_moe_in, gate_part, up_part, down_part = experts_pass(
         moe_in,
         cotangent,
@@ -311,7 +603,7 @@
     grad_moe_in = grad_moe_in + contract_cols(grad_logits_low, router_weight)
     grad_resid_norm, moe_gain_part = moe_pull(grad_moe_in)
     grad_resid = grad_out + grad_resid_norm
-    seq_grad = lax.all_gather(grad_resid.astype(jnp.bfloat16), "gy", axis=0, tiled=True)
+    seq_grad = gather_plane(grad_resid.astype(jnp.bfloat16), 1)
     grad_mixed = contract_cols(seq_grad, out_rows).astype(jnp.bfloat16)
     out_part = contract_rows(seq_grad, mixed_seq)
 
@@ -369,12 +661,7 @@
     out_sum_rows = lax.psum_scatter(
         out_part.astype(jnp.bfloat16), "gx", scatter_dimension=0, tiled=True
     ).astype(jnp.float32)
-    grad_acts = lax.psum_scatter(
-        contract_cols(grad_heads, full_in).astype(jnp.bfloat16),
-        "gy",
-        scatter_dimension=0,
-        tiled=True,
-    ).astype(jnp.float32)
+    grad_acts = scatter_plane(contract_cols(grad_heads, full_in).astype(jnp.bfloat16), 3)
     norm_input_grad, attn_gain_part = norm_pull(grad_acts)
     input_grad = grad_resid + norm_input_grad
     attn_gain_grad, moe_gain_grad, query_gain_grad, key_gain_grad, router_grad = lax.psum(

time: 1230 us -> 897 us (0.73)
  waiting for transfers between devices: 794 us -> 75.2 us
  Pallas kernels: 0 us -> 395 us
    pallas_call x0 -> x7, Pallas kernels: none -> 395 us  [the longest x4 250 us: reduce_scatter(): pl.pallas_call(partial(scatter_kernel, both, n_i, rows), out_shape=jax.Sh...]
    reduce_scatter x4 -> x0, waiting for transfers between devices: 348 us -> none  [the longest x1 150 us: dense_experts(): lax.psum_scatter(grad_in.astype(jnp.bfloat16), everyone, scatter_dimensio...]
    all_gather x3 -> x0, waiting for transfers between devices: 149 us -> none  [the longest x1 72.7 us: dense_experts(): all_moe = lax.all_gather(moe_in, everyone, axis=0, tiled=True)]
    all_gather x1, waiting for transfers between devices: 81.7 us -> 0.01 us  [dense_experts(): all_cot = lax.all_gather(cotangent, everyone, axis=0, tiled=True)]
    reduce_scatter x1, waiting for transfers between devices: 60.6 us -> 0.01 us  [local(): lax.psum_scatter(contract_rows(seq_acts, grad_heads).astype(jnp.bfloat16)...]
    all_gather x1, waiting for transfers between devices: 58.9 us -> 0.01 us  [local(): full_in = lax.all_gather(in_weights, 'gx', axis=0, tiled=True)]
    psum x1, waiting for transfers between devices: 86.6 us -> 73.7 us  [local(): lax.psum((attn_gain_part, moe_gain_part, query_gain_part, key_gain_part,...]
  transfers between devices with their start and end apart: 14 -> 7, of which waited for: 12 -> 1; matrix products, arithmetic and copies ran while one was open for 14% -> 23% of each run, Pallas kernels for 0% -> 42%
where the time goes in v2:
time: 897 us; the launch traced here: 889 us
  Pallas kernels  395 us (44%)
  matrix products  207 us (23%)
  blocking collectives  118 us (13%)
  waiting for transfers between devices  75.2 us (8%)
  other arithmetic  43 us (5%)
  local copies, waits for them, and re-layouts  30.8 us (3%)
  between operations  16.1 us (2%)
    pallas_call x4, Pallas kernels, reduce_scatter(): pl.pallas_call(partial(scatter_kernel, both, n_i, rows), out_shape=jax.Sh...  250 us
    pallas_call x3, Pallas kernels, all_gather(): pl.pallas_call(partial(gather_kernel, n_z, span), out_shape=jax.ShapeDtyp...  145 us
    psum x1, waiting for transfers between devices, local(): lax.psum((attn_gain_part, moe_gain_part, query_gain_part, key_gain_part,...  73.7 us
    dot_general x6, matrix products, contract_cols(): lax.dot_general(left_side, right_side, (((1,), (1,)), ((), ())), preferre...  72.1 us
    dot_general x6, matrix products, contract_rows(): lax.dot_general(left_side, right_side, (((0,), (0,)), ((), ())), preferre...  57.3 us
    all_gather x1, blocking collectives, dense_experts(): all_ids = lax.all_gather(expert_ids, everyone, axis=0, tiled=True)  42 us
    pmax x1, blocking collectives, local(): peak_global = lax.pmax(peak_local, ('gx', 'gy'))  38.4 us
    psum x1, blocking collectives, local(): lax.psum((attn_gain_part, moe_gain_part, query_gain_part, key_gain_part,...  37.9 us
  transfers between devices with their start and end apart: 7, of which 1 were waited for; matrix products, arithmetic and copies ran while one was open for 23% of the time, Pallas kernels for 42%

profile of v2, /device:TPU:0, one launch (start us, length us, event | category | flops | bytes accessed | tf_op | source)
XLA Modules:
  0.0 888.9 jit_solution(7380919499691401333)
XLA Ops:
  7.3 2.2 pad_maximum_fusion.1
  11.7 1.2 fusion.68
  14.0 2.0 fusion.62
  16.1 25.9 %gather_plane.2 = bf16[8,2,64,2048]{3,2,1,0:T(8,128)(2,1)} custom-call(bf16[2,64,2048]{2,1,0:T(8,128)(2,1)} %bitcast.223), custom_call_target="tpu_custom_call" | custom-call | tf_op jit(solution)/shard_map/gather_plane/pallas_call | solution.py:128
  41.9 42.0 %all_gather.14 = s32[4096,8]{0,1:T(8,128)S(1)} all-gather(s32[128,8]{0,1:T(8,128)S(1)} %copy-done.53), channel_id=1, replica_groups=mesh['gx'=4,'gy'=8] {'gx','gy'}, dimensions={0}, use_global_device_ids=true | all-gather | bytes 135168 | tf_op jit(solution)/shard_map/all_gather | solution.py:462
  84.2 2.8 fusion.74
  87.0 6.2 fusion.93
  96.2 1.3 copy.145
  97.5 1.6 copy.142
  99.1 2.4 copy.146
  101.6 1.9 multiply_reduce_fusion.8
  106.3 11.4 %while.29 = (s32[]{:T(128)}, bf16[2,512,2,128]{3,2,1,0:T(2,128)(2,1)}, f32[2,2,512]{2,1,0:T(2,128)S(1)}, f32[2,2]{1,0:T(2,128)S(1)}, s32[2,512]{1,0:T(2,128)S(1)...) while((s32[]{:T(128)}, ...), condition=%wide.region_7.8_spmd, body=%wide.region_3.7_spmd.sunk | while | flops 551156736 | bytes 18917564 | solution.py:572
  107.8 1.5 fusion.148
  109.3 1.7 fusion.149
  113.4 1.5 fusion.148
  115.0 1.7 fusion.149
  118.7 38.4 %pmax.7 = f32[16]{0:T(128)S(1)} all-reduce(f32[16]{0:T(128)S(1)} %dynamic_update_slice.19), channel_id=1, replica_groups=mesh['gx'=4,'gy'=8] {'gx','gy'}, use_global_device_ids=true, to_apply=%region_43.44 | all-reduce | flops 16 | bytes 128 | tf_op jit(solution)/shard_map/pmax | solution.py:578
  157.1 2.6 convolution_convert_fusion
  159.8 2.3 copy.219
  162.1 36.7 %scatter_plane.2 = f32[4,2,16,2048]{3,2,1,0:T(8,128)} custom-call(bf16[4,8,2,16,2048]{4,3,2,1,0:T(8,128)(2,1)} %bitcast.207), custom_call_target="tpu_custom_call" | custom-call | tf_op jit(solution)/shard_map/scatter_plane/pallas_call | solution.py:284
  198.8 1.4 multiply_reduce_fusion.7
  200.3 1.1 multiply_convert_fusion.5
  201.5 95.5 %gather_all.1 = bf16[32,2,64,2048]{3,2,1,0:T(8,128)(2,1)} custom-call(bf16[2,64,2048]{2,1,0:T(8,128)(2,1)} %bitcast.211), custom_call_target="tpu_custom_call" | custom-call | tf_op jit(solution)/shard_map/gather_all/pallas_call | solution.py:128
  297.0 1.3 sort.15
  298.3 10.4 %fusion.91 = (f32[4096]{0:T(1024)S(1)}, f32[4096,16]{0,1:T(8,128)S(1)}) fusion(bf16[4096,2048]{1,0:T(8,128)(2,1)} %bitcast.201, bf16[2048,16]{0,1:T(8,128)(2,1)S(1)} %copy-done.34), kind=kOutput, calls=%fused_computation.189 | convolution fusion | flops 268496896 | bytes 17121280 | tf_op jit(solution)/shard_map/dot_general | solution.py:467
  312.1 11.4 %fusion.53 = f32[4096,512]{1,0:T(8,128)} fusion(bf16[4096,2048]{1,0:T(8,128)(2,1)S(1)} %bitcast.204, bf16[1,2048,512]{2,1,0:T(8,128)(2,1)S(1)} %copy-done.65), kind=kOutput, calls=%fused_computation.78 | convolution fusion | flops 8589934592 | bytes 27262976 | tf_op jit(solution)/shard_map/dot_general | solution.py:473
  323.5 11.0 %fusion.57 = f32[4096,512]{1,0:T(8,128)} fusion(bf16[4096,2048]{1,0:T(8,128)(2,1)S(1)} %bitcast.205, bf16[1,2048,512]{2,1,0:T(8,128)(2,1)S(1)} %copy-done.64), kind=kOutput, calls=%fused_computation.82 | convolution fusion | flops 8589934592 | bytes 27262976 | tf_op jit(solution)/shard_map/dot_general | solution.py:472
  334.5 21.5 %multiply_convert_fusion.2 = (bf16[4096,512]{1,0:T(8,128)(2,1)}, bf16[4096,512]{1,0:T(8,128)(2,1)}, bf16[4096,512]{1,0:T(8,128)(2,1)}) fusion(f32[4096,512]{1,0:T(8,128)} %fusion.57, f32[4096,512]{1,0:T(8,128)} %fusion.53, bf16[1,512,2048]{2,1,0:T(8,128)(2,1)S(1)} %copy-done, bf16[4096,2048]{1,0:T(8,128)(2,1)} %all-gather.8.cloned.1.call-done, ...), kind=kOutput, calls=%fused_computation.57 | convolution fusion | flops 8646557696 | bytes 48250880 | tf_op jit(solution)/shard_map/dot_general | solution.py:368
  356.0 19.2 %fusion.40 = (f32[4096]{0:T(1024)}, bf16[4096,2048]{1,0:T(8,128)(2,1)}) fusion(bf16[4096,2048]{1,0:T(8,128)(2,1)} %all-gather.8.cloned.1.call-done, f32[4096]{0:T(1024)S(1)} %div.134, bf16[4096,512]{1,0:T(8,128)(2,1)} %get-tuple-element.463, bf16[1,512,2048]{2,1,0:T(8,128)(2,1)S(1)} %copy-done), kind=kOutput, calls=%fused_computation.54 | convolution fusion | flops 8631873536 | bytes 39878656 | tf_op jit(solution)/shard_map/dot_general | solution.py:477
  375.2 2.5 all-to-all-start
  377.8 17.8 %fusion.55 = f32[4096,2048]{1,0:T(8,128)} fusion(bf16[4096,512]{1,0:T(8,128)(2,1)} %get-tuple-element.462, bf16[1,2048,512]{2,1,0:T(8,128)(2,1)} %param.35), kind=kOutput, calls=%fused_computation.80 | convolution fusion | flops 8589934592 | bytes 39845888 | tf_op jit(solution)/shard_map/dot_general | solution.py:368
  395.6 22.6 %add_convert_fusion = bf16[4096,2048]{1,0:T(8,128)(2,1)} fusion(f32[4096,2048]{1,0:T(8,128)} %fusion.55, bf16[4096,512]{1,0:T(8,128)(2,1)} %get-tuple-element.461, bf16[1,2048,512]{2,1,0:T(8,128)(2,1)} %param.36), kind=kOutput, calls=%fused_computation.55 | convolution fusion | flops 8606711808 | bytes 56623104 | tf_op jit(solution)/shard_map/dot_general | solution.py:368
  418.2 90.6 %scatter_all.3 = f32[2,64,2048]{2,1,0:T(8,128)} custom-call(bf16[4,8,2,64,2048]{4,3,2,1,0:T(8,128)(2,1)} %bitcast.210), custom_call_target="tpu_custom_call" | custom-call | tf_op jit(solution)/shard_map/scatter_all/pallas_call | solution.py:284
  509.1 1.7 multiply_reduce_fusion.3
  510.9 1.2 fusion.88
  512.1 23.8 %gather_plane.3 = bf16[8,2,64,2048]{3,2,1,0:T(8,128)(2,1)} custom-call(bf16[2,64,2048]{2,1,0:T(8,128)(2,1)} %bitcast.225), custom_call_target="tpu_custom_call" | custom-call | tf_op jit(solution)/shard_map/gather_plane/pallas_call | solution.py:128
  535.9 4.5 convolution_convert_fusion.3
  540.4 4.7 convolution_convert_fusion.4
  545.2 1.2 reshape.378
  546.4 17.9 %while.30 = (s32[]{:T(128)}, f32[1024,2,128]{0,2,1:T(8,128)S(1)}, f32[1024,2,128]{0,2,1:T(8,128)}, f32[2,512,2,128]{3,1,0,2:T(8,128)}, bf16[2,512,2,128]{3,1,2,0...) while((s32[]{:T(128)}, f32[1024,2,128]{0,2,1:T(8,128)S(1)}, ...), condition=%wide.region_27.28_spmd.clone, body=%wide.region_25.27_spmd.clone.sunk | while | flops 1359870976 | bytes 58235156 | solution.py:641
  547.8 1.5 fusion.160
  549.3 1.8 multiply_reduce_fusion.13
  551.1 1.3 multiply_convert_fusion.10
  556.7 1.5 fusion.160
  558.2 1.8 multiply_reduce_fusion.13
  560.1 1.3 multiply_convert_fusion.10
  565.2 2.6 multiply_add_fusion.3
  570.9 1.7 fusion.66
  572.6 2.1 copy.160
  574.7 2.0 fusion.65
  577.0 7.6 convolution_convert_fusion.2
  584.6 15.3 %fusion.46 = f32[1,512,2048]{2,1,0:T(8,128)} fusion(bf16[4096,512]{1,0:T(8,128)(2,1)} %get-tuple-element.463, bf16[4096,2048]{1,0:T(8,128)(2,1)} %all-gather.8.cloned.1.call-done, f32[4096]{0:T(1024)S(1)} %div.134), kind=kOutput, calls=%fused_computation.69 | convolution fusion | flops 8615100416 | bytes 25182208 | tf_op jit(solution)/shard_map/dot_general | solution.py:362
  599.9 98.4 %scatter_all.2 = f32[2,64,2048]{2,1,0:T(8,128)} custom-call(bf16[4,8,2,64,2048]{4,3,2,1,0:T(8,128)(2,1)} %bitcast.209), custom_call_target="tpu_custom_call" | custom-call | tf_op jit(solution)/shard_map/scatter_all/pallas_call | solution.py:284
  698.4 15.1 %convolution_bitcast_fusion = f32[1,2048,512]{2,1,0:T(8,128)} fusion(bf16[4096,2048]{1,0:T(8,128)(2,1)} %bitcast.202, bf16[4096,512]{1,0:T(8,128)(2,1)} %get-tuple-element.461), kind=kOutput, calls=%fused_computation.70 | convolution fusion | flops 8589934592 | bytes 25165824 | tf_op jit(solution)/shard_map/dot_general | solution.py:362
  713.5 14.0 %convolution_bitcast_fusion.1 = f32[1,2048,512]{2,1,0:T(8,128)} fusion(bf16[4096,2048]{1,0:T(8,128)(2,1)} %bitcast.203, bf16[4096,512]{1,0:T(8,128)(2,1)S(1)} %copy-done.67), kind=kOutput, calls=%fused_computation.71 | convolution fusion | flops 8589934592 | bytes 25165824 | tf_op jit(solution)/shard_map/dot_general | solution.py:362
  727.5 3.7 convolution_convert_fusion.1
  731.2 2.4 copy.218
  733.6 24.3 %scatter_plane.3 = f32[4,2,16,2048]{3,2,1,0:T(8,128)} custom-call(bf16[4,8,2,16,2048]{4,3,2,1,0:T(8,128)(2,1)} %bitcast.208), custom_call_target="tpu_custom_call" | custom-call | tf_op jit(solution)/shard_map/scatter_plane/pallas_call | solution.py:284
  757.9 1.6 fusion.63
  760.5 3.9 fusion.67
  764.4 37.9 %all-reduce.4 = (f32[2048]{0:T(1024)}, f32[2048]{0:T(1024)}, f32[128]{0:T(128)}, f32[128]{0:T(128)}) all-reduce(f32[2048]{0:T(1024)S(1)} %get-tuple-element.402, f32[2048]{0:T(1024)S(1)} %get-tuple-element.400, f32[128]{0:T(128)S(1)} %get-tuple-element.396, f32[128]{0:T(128)S(1)} %get-tuple-element.394), channel_id=1, replica_groups=mesh['gx'=4,'gy'=8] {'gx','gy'}, use_global_device_ids=true, to_apply=%region_32.33 | all-reduce | flops 4352 | bytes 34816 | tf_op jit(solution)/shard_map/psum | solution.py:667
  804.3 2.3 fusion.90
  806.5 73.7 %all-reduce.7.cloned.1.call-done = f32[2048,16]{0,1:T(8,128)} async-done(((f32[2048,16]{0,1:T(8,128)}), f32[2048,16]{0,1:T(8,128)}) %all-reduce.7.cloned.1.call-update) | async-done | bytes 131088 | tf_op jit(solution)/shard_map/psum | solution.py:667
  880.2 1.6 copy.257
  (250 shorter events, 33.4 us)
Async XLA Ops:
  7.2 327.3 %copy-start = (bf16[1,512,2048]{2,1,0:T(8,128)(2,1)S(1)}, bf16[1,512,2048]{2,1,0:T(8,128)(2,1)}, u32[]{:S(2)}) copy-start(bf16[1,512,2048]{2,1,0:T(8,128)(2,1)} %param.37) | copy-start | bytes 6291460
  7.2 79.8 %all-gather.4.cloned.1.call-start = ((), (), s32[]{:S(2)}) async-start(), calls=%async_computation.3 | async-start | bytes 3932160 | tf_op jit(solution)/shard_map/all_gather | solution.py:526
  9.4 32.5 %copy-start.53 = (s32[128,8]{0,1:T(8,128)S(1)}, s32[128,8]{0,1:T(8,128)}, u32[]{:S(2)}) copy-start(s32[128,8]{0,1:T(8,128)} %param.23) | copy-start | bytes 12292
  9.5 147.6 %all-gather.6.cloned.1.call-start = ((), (), s32[]{:S(2)}) async-start(), calls=%async_computation.4 | async-start | bytes 1310720 | tf_op jit(solution)/shard_map/all_gather | solution.py:527
  10.2 324.3 %all-gather.8.cloned.1.call-start = ((), (), s32[]{:S(2)}) async-start(), calls=%async_computation.5 | async-start | bytes 17301504 | tf_op jit(solution)/shard_map/all_gather | solution.py:463
  96.2 7.9 copy-start.59
  97.5 6.9 copy-start.57
  99.1 6.5 copy-start.12
  101.6 2.9 copy-start.14
  101.6 3.3 copy-start.23
  101.6 3.3 copy-start.24
  103.5 2.1 copy-start.49
  106.7 2.6 copy-start.10
  112.4 2.6 copy-start.10
  117.7 44.4 %copy-start.3 = (bf16[1024,2,128]{2,0,1:T(8,128)(2,1)}, bf16[1024,2,128]{2,0,1:T(8,128)(2,1)S(1)}, u32[]{:S(2)}) copy-start(bf16[1024,2,128]{2,0,1:T(8,128)(2,1)S(1)} %get-tuple-element.723) | copy-start | bytes 1572868
  117.7 44.4 %copy-start.5 = (bf16[2,512,2,128]{3,1,2,0:T(8,128)(2,1)}, bf16[2,512,2,128]{3,1,2,0:T(8,128)(2,1)S(1)}, u32[]{:S(2)}) copy-start(bf16[2,512,2,128]{3,1,2,0:T(8,128)(2,1)S(1)} %get-tuple-element.724) | copy-start | bytes 1572868
  117.7 44.4 %copy-start.39 = (s32[2,512]{1,0:T(2,128)}, s32[2,512]{1,0:T(2,128)S(1)}, u32[]{:S(2)}) copy-start(s32[2,512]{1,0:T(2,128)S(1)} %get-tuple-element.742) | copy-start | bytes 12292
  117.7 44.4 %copy-start.51 = (f32[2,2,512]{2,1,0:T(2,128)}, f32[2,2,512]{2,1,0:T(2,128)S(1)}, u32[]{:S(2)}) copy-start(f32[2,2,512]{2,1,0:T(2,128)S(1)} %get-tuple-element.669) | copy-start | bytes 24580
  162.1 36.8 %copy-start.16 = (bf16[128,2048]{1,0:T(8,128)(2,1)S(1)}, bf16[128,2048]{1,0:T(8,128)(2,1)}, u32[]{:S(2)}) copy-start(bf16[128,2048]{1,0:T(8,128)(2,1)} %param.21) | copy-start | bytes 1572868
  162.1 38.2 %copy-start.41 = (f32[2048]{0:T(1024)S(1)}, f32[2048]{0:T(1024)}, u32[]{:S(2)}) copy-start(f32[2048]{0:T(1024)} %param.27) | copy-start | bytes 24580
  200.3 310.6 %copy-start.8 = (f32[128,2048]{1,0:T(8,128)}, f32[128,2048]{1,0:T(8,128)S(1)}, u32[]{:S(2)}) copy-start(f32[128,2048]{1,0:T(8,128)S(1)} %get-tuple-element.454) | copy-start | bytes 3145732
  201.5 96.8 %copy-start.34 = (bf16[2048,16]{0,1:T(8,128)(2,1)S(1)}, bf16[2048,16]{0,1:T(8,128)(2,1)}, u32[]{:S(2)}) copy-start(bf16[2048,16]{0,1:T(8,128)(2,1)} %param.34) | copy-start | bytes 196612
  298.3 12.5 %copy-start.20 = (bf16[128,2048]{1,0:T(8,128)(2,1)S(1)}, bf16[128,2048]{1,0:T(8,128)(2,1)}, u32[]{:S(2)}) copy-start(bf16[128,2048]{1,0:T(8,128)(2,1)} %multiply_convert_fusion.5) | copy-start | bytes 1572868
  298.3 12.9 %copy-start.32 = (bf16[512,256]{1,0:T(8,128)(2,1)S(1)}, bf16[512,256]{1,0:T(8,128)(2,1)}, u32[]{:S(2)}) copy-start(bf16[512,256]{1,0:T(8,128)(2,1)} %param.31) | copy-start | bytes 786436
  298.3 12.9 %copy-start.33 = (bf16[512,256]{1,0:T(8,128)(2,1)S(1)}, bf16[512,256]{1,0:T(8,128)(2,1)}, u32[]{:S(2)}) copy-start(bf16[512,256]{1,0:T(8,128)(2,1)} %param.30) | copy-start | bytes 786436
  298.3 13.8 %copy-start.2 = (bf16[32,2,64,2048]{3,2,1,0:T(8,128)(2,1)S(1)}, bf16[32,2,64,2048]{3,2,1,0:T(8,128)(2,1)}, u32[]{:S(2)}) copy-start(bf16[32,2,64,2048]{3,2,1,0:T(8,128)(2,1)} %gather_all.1) | copy-start | bytes 50331652
  298.3 13.8 %copy-start.65 = (bf16[1,2048,512]{2,1,0:T(8,128)(2,1)S(1)}, bf16[1,2048,512]{2,1,0:T(8,128)(2,1)}, u32[]{:S(2)}) copy-start(bf16[1,2048,512]{2,1,0:T(8,128)(2,1)} %param.36) | copy-start | bytes 6291460
  312.1 11.4 %copy-start.64 = (bf16[1,2048,512]{2,1,0:T(8,128)(2,1)S(1)}, bf16[1,2048,512]{2,1,0:T(8,128)(2,1)}, u32[]{:S(2)}) copy-start(bf16[1,2048,512]{2,1,0:T(8,128)(2,1)} %param.35) | copy-start | bytes 6291460
  375.2 133.7 %all-to-all-start = ((f32[32,1,128]{2,1,0:T(1,128)}), f32[32,1,128]{2,1,0:T(1,128)S(1)}, u32[]{:S(2)}, u32[]{:S(2)}) async-start(f32[32,1,128]{2,1,0:T(1,128)} %bitcast.25), calls=%async_computation | async-start | bytes 32768 | tf_op jit(solution)/shard_map/all_to_all | solution.py:481
  377.7 424.5 %reduce-scatter.5.cloned.1.call-start = ((), (), s32[]{:S(2)}) async-start(), calls=%async_computation.7 | async-start | bytes 1310720 | tf_op jit(solution)/shard_map/reduce_scatter | solution.py:661
  418.2 90.7 %copy-start.54 = (s32[128,8]{0,1:T(8,128)S(1)}, s32[128,8]{0,1:T(8,128)}, u32[]{:S(2)}) copy-start(s32[128,8]{0,1:T(8,128)} %param.23) | copy-start | bytes 12292
  418.2 92.7 %copy-start.25 = (bf16[128,2048]{1,0:T(8,128)(2,1)S(1)}, bf16[128,2048]{1,0:T(8,128)(2,1)}, u32[]{:S(2)}) copy-start(bf16[128,2048]{1,0:T(8,128)(2,1)} %param.22) | copy-start | bytes 1572868
  510.8 29.5 %copy-start.18 = (f32[128,2048]{1,0:T(8,128)}, f32[128,2048]{1,0:T(8,128)S(1)}, u32[]{:S(2)}) copy-start(f32[128,2048]{1,0:T(8,128)S(1)} %get-tuple-element.491) | copy-start | bytes 3145732
  510.9 25.0 %copy-start.28 = (bf16[2,512,2,128]{3,2,1,0:T(2,128)(2,1)S(1)}, bf16[2,512,2,128]{3,2,1,0:T(2,128)(2,1)}, u32[]{:S(2)}) copy-start(bf16[2,512,2,128]{3,2,1,0:T(2,128)(2,1)} %get-tuple-element.127) | copy-start | bytes 1572868
  540.4 6.0 copy-start.4
  540.4 6.0 copy-start.6
  540.4 6.0 copy-start.7
  540.4 6.0 copy-start.11
  540.4 6.0 copy-start.38
  540.4 6.0 copy-start.40
  540.4 6.0 copy-start.52
  549.3 1.9 copy-start.30
  564.4 239.9 %reduce-scatter.3.cloned.1.call-start = ((), (), s32[]{:S(2)}) async-start(), calls=%async_computation.6 | async-start | bytes 3932160 | tf_op jit(solution)/shard_map/reduce_scatter | solution.py:652
  565.1 2.7 copy-start.31
  565.2 3.8 copy-start.13
  565.2 3.8 copy-start.43
  565.2 3.8 copy-start.60
  567.8 2.1 copy-start.15
  567.8 2.1 copy-start.45
  567.8 2.1 copy-start.58
  567.8 3.0 copy-start.48
  567.8 3.0 copy-start.50
  572.6 4.4 copy-start.35
  584.6 295.7 %all-reduce.7.cloned.1.call-start = ((), (), s32[]{:S(2)}) async-start(), calls=%async_computation.8 | async-start | bytes 262144 | tf_op jit(solution)/shard_map/psum | solution.py:667
  698.3 15.1 %copy-start.67 = (bf16[4096,512]{1,0:T(8,128)(2,1)S(1)}, bf16[4096,512]{1,0:T(8,128)(2,1)}, u32[]{:S(2)}) copy-start(bf16[4096,512]{1,0:T(8,128)(2,1)} %get-tuple-element.462) | copy-start | bytes 12582916
  713.5 14.0 %copy-start.36 = (bf16[1024,2,128]{0,2,1:T(8,128)(2,1)S(1)}, bf16[1024,2,128]{0,2,1:T(8,128)(2,1)}, u32[]{:S(2)}) copy-start(bf16[1024,2,128]{0,2,1:T(8,128)(2,1)} %copy.160) | copy-start | bytes 1572868
  713.5 14.0 %copy-start.63 = (bf16[2048,768]{1,0:T(8,128)(2,1)S(1)}, bf16[2048,768]{1,0:T(8,128)(2,1)}, u32[]{:S(2)}) copy-start(bf16[2048,768]{1,0:T(8,128)(2,1)} %all-gather.4.cloned.1.call-done) | copy-start | bytes 9437188
  733.6 24.3 %copy-start.17 = (bf16[128,2048]{1,0:T(8,128)(2,1)S(1)}, bf16[128,2048]{1,0:T(8,128)(2,1)}, u32[]{:S(2)}) copy-start(bf16[128,2048]{1,0:T(8,128)(2,1)} %param.21) | copy-start | bytes 1572868
  733.6 24.3 %copy-start.46 = (f32[2048]{0:T(1024)S(1)}, f32[2048]{0:T(1024)}, u32[]{:S(2)}) copy-start(f32[2048]{0:T(1024)} %param.26) | copy-start | bytes 24580
  733.6 24.3 %copy-start.56 = (f32[128]{0:T(128)S(1)}, f32[128]{0:T(128)}, u32[]{:S(2)}) copy-start(f32[128]{0:T(128)} %copy-done.55) | copy-start | bytes 1540
  733.6 26.0 %copy-start.62 = (f32[128]{0:T(128)S(1)}, f32[128]{0:T(128)}, u32[]{:S(2)}) copy-start(f32[128]{0:T(128)} %copy-done.61) | copy-start | bytes 1540
  733.6 26.0 %copy-start.21 = (bf16[128,2048]{1,0:T(8,128)(2,1)S(1)}, bf16[128,2048]{1,0:T(8,128)(2,1)}, u32[]{:S(2)}) copy-start(bf16[128,2048]{1,0:T(8,128)(2,1)} %multiply_convert_fusion.5) | copy-start | bytes 1572868
  733.6 26.8 %copy-start.9 = (f32[128,2048]{1,0:T(8,128)S(1)}, f32[128,2048]{1,0:T(8,128)}, u32[]{:S(2)}) copy-start(f32[128,2048]{1,0:T(8,128)} %copy-done.8) | copy-start | bytes 3145732
  760.5 121.3 %copy-start.1 = (bf16[1,512,2048]{2,1,0:T(8,128)(2,1)S(1)}, bf16[1,512,2048]{2,1,0:T(8,128)(2,1)}, u32[]{:S(2)}) copy-start(bf16[1,512,2048]{2,1,0:T(8,128)(2,1)} %param.37) | copy-start | bytes 6291460
  (16 other events, 18.5 us)
Sparse Core Ops, SparseCore 0:
  10.2 66.7 all-gather.3
  78.5 26.5 all-gather.5
  108.0 141.0 all-gather.7
  564.5 26.2 reduce-scatter.4
  593.0 71.9 reduce-scatter.2
  760.6 119.6 all-reduce.6

commit v3 on v2

--- a/solution.py
+++ b/solution.py
@@ -1,4 +1,5 @@
 from functools import partial
+from itertools import accumulate
 
 import jax
 import jax.numpy as jnp
@@ -24,7 +25,72 @@
             pl.semaphore_signal(barrier, inc=1, device_id=device, device_id_type=pl.DeviceIdType.MESH)
     pl.semaphore_wait(barrier, sum(ok.astype(jnp.int32) for ok, _ in partners))
 
-def gather_kernel(n_z, span, own_ref, out_ref, send_sem, recv_sem, local_sem):
+def always(ok, other):
+    if ok is True:
+        return other
+    return ok if other is True else jnp.logical_and(ok, other)
+
+
+def run_if(ok, action):
+    if ok is True:
+        action()
+    else:
+        pl.when(ok)(action)
+
+
+def chain_gather(n_z, own_ref, out_ref, send_sem, recv_sem, local_sem):
+    z = lax.axis_index("gx")
+    g = lax.axis_index("gy")
+
+    def hop(source, owner, k, peer):
+        return pltpu.make_async_remote_copy(
+            src_ref=source,
+            dst_ref=out_ref.at[owner],
+            send_sem=send_sem.at[k],
+            recv_sem=recv_sem.at[owner],
+            device_id={"gx": peer, "gy": g},
+            device_id_type=pl.DeviceIdType.MESH,
+        )
+
+    local = pltpu.make_async_copy(own_ref, out_ref.at[z], local_sem)
+    upward = [(z < n_z - 1, lambda: hop(own_ref, z, 0, z + 1))]
+    downward = [(z > 0, lambda: hop(own_ref, z, n_z, z - 1))]
+    for d in range(1, n_z - 1):
+        upward.append(
+            (
+                jnp.logical_and(z >= d, z < n_z - 1),
+                lambda d=d: hop(out_ref.at[z - d], z - d, d, z + 1),
+            )
+        )
+        downward.append(
+            (
+                jnp.logical_and(z < n_z - d, z > 0),
+                lambda d=d: hop(out_ref.at[z + d], z + d, n_z + d, z - 1),
+            )
+        )
+
+    def start():
+        local.start()
+        for ok, copy in (upward[0], downward[0]):
+            run_if(ok, lambda copy=copy: copy().start())
+
+    def relay(d):
+        run_if(z >= d, lambda: hop(own_ref, z - d, 0, z).wait_recv())
+        if d < n_z - 1:
+            run_if(upward[d][0], lambda: upward[d][1]().start())
+        run_if(z < n_z - d, lambda: hop(own_ref, z + d, 0, z).wait_recv())
+        if d < n_z - 1:
+            run_if(downward[d][0], lambda: downward[d][1]().start())
+
+    def finish():
+        local.wait()
+        for ok, copy in upward + downward:
+            run_if(ok, lambda copy=copy: copy().wait_send())
+
+    return start, [partial(relay, d) for d in range(1, n_z)], finish
+
+
+def gather_kernel(n_z, span, own_ref, out_ref, send_sem, recv_sem, local_sem, chain=None):
     z = lax.axis_index("gx"); g = lax.axis_index("gy")
     core = {"gx": z, "gy": g + 1 - 2 * (g % 2)}
     xn = {"gx": z, "gy": g + 2 - 4 * ((g // 2) % 2)}
@@ -36,9 +102,12 @@
     zup = {"gx": z + 1, "gy": g}; zdn = {"gx": z - 1, "gy": g}
     zb = z if n_z > 1 else 0
     partners = [(z >= 0, core), (z >= 0, xn), (z >= 0, yn)]
-    if n_z > 1:
-        partners += [(z < n_z - 1, zup), (z > 0, zdn)]
+    n_chain = lax.axis_size("gx") if chain else n_z
+    if n_chain > 1:
+        partners += [(z < n_chain - 1, zup), (z > 0, zdn)]
     barrier_with(partners)
+    if chain:
+        chain[0]()
     sends = []
     def send(ok, src, b, h, dev):
         k = len(sends)
@@ -109,9 +178,15 @@
         if i < n: first(items[i])
         if 1 <= i <= n: second(items[i - 1])
         if i >= 2: third(items[i - 2])
+    if chain:
+        chain[1][0]()
     for ok, zs, d in items:
         for gg in (g, gx_, gy_, gd_):
             for h in range(2): arrive(ok, zs * span + gc(gg), h)
+    if chain:
+        for relay in chain[1][1:]:
+            relay()
+        chain[2]()
     local.wait()
     for ok, make in sends:
         if ok is True: make().wait_send()
@@ -153,7 +228,7 @@
 
 
 def scatter_kernel(chain, n_i, rows, part_ref, out_ref, held, from_core, from_a, from_b, from_z,
-                   load_sem, core_send, a_send, b_send, z_send, core_recv, a_recv, b_recv, z_recv):
+                   load_sem, core_send, a_send, b_send, z_send, core_recv, a_recv, b_recv, z_recv, beside=None):
     z = lax.axis_index("gx"); g = lax.axis_index("gy")
     flip_x = g + 2 - 4 * ((g // 2) % 2)
     flip_y = g + 4 - 8 * ((g // 4) % 2)
@@ -166,7 +241,12 @@
     partners = [(every, core), (every, xn), (every, yn)]
     if chain:
         partners += [(every, {"gx": lax.rem(z + j, n_i), "gy": g}) for j in range(1, n_i)]
+    if beside:
+        n_z = lax.axis_size("gx")
+        partners += [(z < n_z - 1, {"gx": z + 1, "gy": g}), (z > 0, {"gx": z - 1, "gy": g})]
     barrier_with(partners)
+    if beside:
+        beside[0]()
     mesh_id = pl.DeviceIdType.MESH
 
     def item(i):
@@ -257,6 +337,12 @@
         if 0 <= i - 1 < n_i: stage_b(i - 1)
         if 0 <= i - 2 < n_i: stage_c(i - 2)
         if chain and 0 <= i - 2 < n_i: stage_d(i - 2)
+        if beside and i == n_i:
+            beside[1][0]()
+    if beside:
+        for relay in beside[1][1:]:
+            relay()
+        beside[2]()
     for i in range(n_i):
         for q in range(4): core_copy(i, q).wait_send()
         for k in range(4): a_copy(i, k).wait_send()
@@ -301,10 +387,336 @@
     return out.reshape(total // (n_z * span), cols)
 
 
+def sum_kernel(n_z, bits, vec_ref, out_ref, held, arrived, from_z, send_sem, z_send, recv_sem, z_recv):
+    z = lax.axis_index("gx")
+    g = lax.axis_index("gy")
+    half = vec_ref.shape[1]
+    side = lax.rem(g, 2)
+    core = {"gx": z, "gy": g + 1 - 2 * (g % 2)}
+    peers = [
+        {"gx": z, "gy": g + bit - 2 * bit * ((g // bit) % 2)}
+        for bit in (2**power for power in range(1, bits))
+    ]
+    others = [{"gx": lax.rem(z + j, n_z), "gy": g} for j in range(1, n_z)]
+    barrier_with([(z >= 0, peer) for peer in (core, *peers, *others)])
+
+    def remote(src, dst, ssem, rsem, peer):
+        return pltpu.make_async_remote_copy(
+            src_ref=src,
+            dst_ref=dst,
+            send_sem=ssem,
+            recv_sem=rsem,
+            device_id=peer,
+            device_id_type=pl.DeviceIdType.MESH,
+        )
+
+    first = remote(vec_ref.at[1 - side], arrived.at[0], send_sem.at[0], recv_sem.at[0], core)
+    first.start()
+    first.wait()
+    held[0] = vec_ref[side] + arrived[0]
+    for k, peer in enumerate(peers, 1):
+        step = remote(held.at[k - 1], arrived.at[k], send_sem.at[k], recv_sem.at[k], peer)
+        step.start()
+        step.wait()
+        held[k] = held[k - 1] + arrived[k]
+    copies = [
+        remote(held.at[bits - 1], from_z.at[j], z_send.at[j], z_recv.at[j], peer)
+        for j, peer in enumerate(others)
+    ]
+    for copy in copies:
+        copy.start()
+    for copy in copies:
+        copy.wait()
+    total = jnp.zeros_like(held[0])
+    for owner in range(n_z):
+        term = held[bits - 1]
+        for j in range(1, n_z):
+            term = jnp.where(lax.rem(z - j + n_z, n_z) == owner, from_z[j - 1], term)
+        total = total + term
+    held[bits] = total
+    last = remote(held.at[bits], arrived.at[bits], send_sem.at[bits], recv_sem.at[bits], core)
+    last.start()
+    out_ref[side] = total
+    last.wait()
+    out_ref[1 - side] = arrived[bits]
+
+
+def sum_everywhere(vector, collective_id):
+    n_z = lax.axis_size("gx")
+    bits = lax.axis_size("gy").bit_length() - 1
+    lanes = 128
+    length = vector.shape[0]
+    rows = -(-length // (lanes * 16)) * 8
+    padded = jnp.pad(vector, (0, 2 * rows * lanes - length)).reshape(2, rows, lanes)
+    dma = pltpu.SemaphoreType.DMA
+    out = pl.pallas_call(
+        partial(sum_kernel, n_z, bits),
+        out_shape=jax.ShapeDtypeStruct((2, rows, lanes), jnp.float32),
+        in_specs=[pl.BlockSpec(memory_space=pltpu.VMEM)],
+        out_specs=pl.BlockSpec(memory_space=pltpu.VMEM),
+        scratch_shapes=[
+            pltpu.VMEM((bits + 1, rows, lanes), jnp.float32),
+            pltpu.VMEM((bits + 1, rows, lanes), jnp.float32),
+            pltpu.VMEM((n_z - 1, rows, lanes), jnp.float32),
+            dma((bits + 1,)),
+            dma((n_z - 1,)),
+            dma((bits + 1,)),
+            dma((n_z - 1,)),
+        ],
+        compiler_params=pltpu.CompilerParams(collective_id=collective_id, has_side_effects=True),
+        name="sum_everywhere",
+    )(padded)
+    return out.reshape(-1)[:length]
+
+
+def enter_kernel(
+    n_z,
+    span,
+    acts_ref,
+    weight_ref,
+    seq_ref,
+    full_ref,
+    send_sem,
+    recv_sem,
+    local_sem,
+    chain_send,
+    chain_recv,
+    chain_local,
+):
+    chain = chain_gather(n_z, weight_ref, full_ref, chain_send, chain_recv, chain_local)
+    gather_kernel(1, span, acts_ref, seq_ref, send_sem, recv_sem, local_sem, chain)
+
+
+def enter(acts, weights, collective_id):
+    n_z = lax.axis_size("gx")
+    span = lax.axis_size("gy")
+    rows, cols = acts.shape
+    dma = pltpu.SemaphoreType.DMA
+    seq, full = pl.pallas_call(
+        partial(enter_kernel, n_z, span),
+        out_shape=(
+            jax.ShapeDtypeStruct((span, 2, rows // 2, cols), acts.dtype),
+            jax.ShapeDtypeStruct((n_z,) + weights.shape, weights.dtype),
+        ),
+        in_specs=[pl.BlockSpec(memory_space=pltpu.VMEM)] * 2,
+        out_specs=(pl.BlockSpec(memory_space=pl.ANY),) * 2,
+        scratch_shapes=[
+            dma((24,)),
+            dma((span, 2)),
+            dma,
+            dma((2 * n_z,)),
+            dma((n_z,)),
+            dma,
+        ],
+        compiler_params=pltpu.CompilerParams(collective_id=collective_id, has_side_effects=True),
+        name="enter",
+    )(acts.reshape(2, rows // 2, cols), weights)
+    return seq.reshape(span * rows, cols), full.reshape(n_z * weights.shape[0], weights.shape[1])
+
+
+def chain_scatter(n_z, part_ref, out_ref, from_low, from_high, send_sem, low_recv, high_recv):
+    z = lax.axis_index("gx")
+    g = lax.axis_index("gy")
+    rows = part_ref.shape[1]
+
+    def up(dest):
+        return pltpu.make_async_remote_copy(
+            src_ref=part_ref.at[dest],
+            dst_ref=from_low.at[dest],
+            send_sem=send_sem.at[dest],
+            recv_sem=low_recv.at[dest],
+            device_id={"gx": z + 1, "gy": g},
+            device_id_type=pl.DeviceIdType.MESH,
+        )
+
+    def down(dest):
+        return pltpu.make_async_remote_copy(
+            src_ref=part_ref.at[dest],
+            dst_ref=from_high.at[dest],
+            send_sem=send_sem.at[dest],
+            recv_sem=high_recv.at[dest],
+            device_id={"gx": z - 1, "gy": g},
+            device_id_type=pl.DeviceIdType.MESH,
+        )
+
+    def start():
+        for k in range(n_z - 1):
+            run_if(z == 0, lambda k=k: up(n_z - 1 - k).start())
+            run_if(z == n_z - 1, lambda k=k: down(k).start())
+
+    def pass_up(dest):
+        up(dest).wait_recv()
+        add_into(part_ref.at[dest], (part_ref.at[dest], from_low.at[dest]), rows)
+        up(dest).start()
+
+    def pass_down(dest):
+        down(dest).wait_recv()
+        add_into(part_ref.at[dest], (part_ref.at[dest], from_high.at[dest]), rows)
+        down(dest).start()
+
+    def relay(time):
+        for k in range(time):
+            low, dest = time - k, n_z - 1 - k
+            if 0 < low < dest:
+                run_if(z == low, partial(pass_up, dest))
+            high, dest = n_z - 1 - (time - k), k
+            if dest < high < n_z - 1:
+                run_if(z == high, partial(pass_down, dest))
+
+    def finish():
+        for dest in range(n_z):
+            terms = [part_ref.at[dest]]
+            terms += [from_low.at[dest]] if dest > 0 else []
+            terms += [from_high.at[dest]] if dest < n_z - 1 else []
+
+            def last(dest=dest, terms=terms):
+                if dest > 0:
+                    up(dest).wait_recv()
+                if dest < n_z - 1:
+                    down(dest).wait_recv()
+                add_into(out_ref, terms, rows)
+
+            run_if(z == dest, last)
+        for dest in range(n_z):
+            run_if(z != dest, lambda dest=dest: up(dest).wait_send())
+
+    return start, [partial(relay, time) for time in range(1, n_z)], finish
+
+
+def leave_kernel(
+    n_i,
+    rows,
+    part_ref,
+    weight_ref,
+    out_ref,
+    weight_out,
+    held,
+    from_core,
+    from_a,
+    from_b,
+    from_z,
+    sums,
+    from_low,
+    from_high,
+    load_sem,
+    core_send,
+    a_send,
+    b_send,
+    z_send,
+    core_recv,
+    a_recv,
+    b_recv,
+    z_recv,
+    copy_sem,
+    chain_send,
+    low_recv,
+    high_recv,
+):
+    n_z = lax.axis_size("gx")
+    copy = pltpu.make_async_copy(weight_ref, sums, copy_sem)
+    copy.start()
+    chain = chain_scatter(
+        n_z, sums, weight_out, from_low, from_high, chain_send, low_recv, high_recv
+    )
+
+    def start():
+        copy.wait()
+        chain[0]()
+
+    scatter_kernel(
+        False,
+        n_i,
+        rows,
+        part_ref,
+        out_ref,
+        held,
+        from_core,
+        from_a,
+        from_b,
+        from_z,
+        load_sem,
+        core_send,
+        a_send,
+        b_send,
+        z_send,
+        core_recv,
+        a_recv,
+        b_recv,
+        z_recv,
+        (start, chain[1], chain[2]),
+    )
+
+
+def leave(part, weight_part, collective_id, pieces=4):
+    n_z = lax.axis_size("gx")
+    span = lax.axis_size("gy")
+    total, cols = part.shape
+    rows = total // span // (2 * pieces)
+    shaped = part.reshape(span, pieces, 2, rows, cols).swapaxes(0, 1)
+    half = (rows, cols)
+    dma = pltpu.SemaphoreType.DMA
+    block = (weight_part.shape[0] // n_z, weight_part.shape[1])
+    out, sums = pl.pallas_call(
+        partial(leave_kernel, pieces, rows),
+        out_shape=(
+            jax.ShapeDtypeStruct((pieces, 2, rows, cols), jnp.float32),
+            jax.ShapeDtypeStruct(block, jnp.float32),
+        ),
+        in_specs=[pl.BlockSpec(memory_space=pl.ANY)] * 2,
+        out_specs=(pl.BlockSpec(memory_space=pltpu.VMEM),) * 2,
+        scratch_shapes=[
+            pltpu.VMEM((pieces, 4, 2) + half, jnp.bfloat16),
+            pltpu.VMEM((pieces, 4, 2) + half, jnp.bfloat16),
+            pltpu.VMEM((pieces, 2, 2) + half, jnp.bfloat16),
+            pltpu.VMEM((pieces, 2) + half, jnp.bfloat16),
+            pltpu.VMEM((1, 2, 16, 128), jnp.bfloat16),
+            pltpu.VMEM((n_z,) + block, jnp.bfloat16),
+            pltpu.VMEM((n_z,) + block, jnp.bfloat16),
+            pltpu.VMEM((n_z,) + block, jnp.bfloat16),
+            dma((pieces, 4)),
+            dma((pieces, 4)),
+            dma((pieces, 4)),
+            dma((pieces, 2)),
+            dma((pieces,)),
+            dma((pieces, 4)),
+            dma((pieces, 2, 2)),
+            dma((pieces, 2)),
+            dma((pieces,)),
+            dma,
+            dma((n_z,)),
+            dma((n_z,)),
+            dma((n_z,)),
+        ],
+        compiler_params=pltpu.CompilerParams(
+            collective_id=collective_id, has_side_effects=True, vmem_limit_bytes=60 << 20
+        ),
+        name="leave",
+    )(shaped, weight_part.reshape((n_z,) + block))
+    return out.reshape(total // span, cols), sums
+
+
 def gather_plane(block, collective_id):
     if lax.axis_size("gy") == 8:
         return all_gather(block, False, collective_id)
     return lax.all_gather(block, "gy", axis=0, tiled=True)
+
+
+def gather_inputs(acts, weights):
+    if lax.axis_size("gy") == 8:
+        return enter(acts, weights, 6)
+    return (
+        lax.all_gather(acts, "gy", axis=0, tiled=True),
+        lax.all_gather(weights, "gx", axis=0, tiled=True),
+    )
+
+
+def scatter_grads(acts_part, weight_part):
+    if lax.axis_size("gy") == 8:
+        return leave(acts_part, weight_part, 7)
+    return (
+        lax.psum_scatter(acts_part, "gy", scatter_dimension=0, tiled=True).astype(jnp.float32),
+        lax.psum_scatter(weight_part, "gx", scatter_dimension=0, tiled=True).astype(jnp.float32),
+    )
 
 
 def scatter_plane(part, collective_id):
@@ -521,9 +933,8 @@
     inputs = tokens.astype(jnp.float32)
     acts_float, norm_pull = jax.vjp(norm_rows, inputs, attn_gain)
     acts_low = acts_float.astype(jnp.bfloat16)
-    seq_acts = gather_plane(acts_low, 1)
     in_weights = jnp.concatenate([query_weight, key_weight, value_weight], axis=1)
-    full_in = lax.all_gather(in_weights, "gx", axis=0, tiled=True)
+    seq_acts, full_in = gather_inputs(acts_low, in_weights)
     out_rows = lax.all_gather(out_weight, "gx", axis=1, tiled=True)
     length = seq_acts.shape[0]
     local_width = query_weight.shape[1]
@@ -572,10 +983,11 @@
     mixed_blocks, log_totals, peak_blocks = lax.map(forward_block, (query_blocks, doc_blocks))
     mixed_seq = mixed_blocks.reshape(length, local_width)
     start_head = lax.axis_index("gy") * local_heads
-    peak_local = lax.dynamic_update_slice(
-        jnp.full((NH,), NEGATIVE, jnp.float32), jnp.max(peak_blocks, axis=0), (start_head,)
-    )
-    peak_global = lax.pmax(peak_local, ("gx", "gy"))
+    peak_slots = lax.dynamic_update_slice(
+        jnp.zeros((lax.axis_size("gx"), NH), jnp.float32),
+        jnp.max(peak_blocks, axis=0)[None],
+        (lax.axis_index("gx"), start_head),
+    )
     attended = scatter_plane(
         jnp.dot(mixed_seq, out_rows, preferred_element_type=jnp.float32).astype(jnp.bfloat16), 3
     )
@@ -649,24 +1061,33 @@
     grad_keys = key_raw_grad.reshape(length, local_width).astype(jnp.bfloat16)
     grad_values = value_grad_heads.reshape(length, local_width).astype(jnp.bfloat16)
     grad_heads = jnp.concatenate([grad_queries, grad_keys, grad_values], axis=1)
-    in_sum = lax.psum_scatter(
+    grad_acts, in_sum = scatter_grads(
+        contract_cols(grad_heads, full_in).astype(jnp.bfloat16),
         contract_rows(seq_acts, grad_heads).astype(jnp.bfloat16),
-        "gx",
-        scatter_dimension=0,
-        tiled=True,
-    ).astype(jnp.float32)
+    )
     query_sum = in_sum[:, :local_width]
     key_sum = in_sum[:, local_width : 2 * local_width]
     value_sum = in_sum[:, 2 * local_width :]
     out_sum_rows = lax.psum_scatter(
         out_part.astype(jnp.bfloat16), "gx", scatter_dimension=0, tiled=True
     ).astype(jnp.float32)
-    grad_acts = scatter_plane(contract_cols(grad_heads, full_in).astype(jnp.bfloat16), 3)
     norm_input_grad, attn_gain_part = norm_pull(grad_acts)
     input_grad = grad_resid + norm_input_grad
-    attn_gain_grad, moe_gain_grad, query_gain_grad, key_gain_grad, router_grad = lax.psum(
-        (attn_gain_part, moe_gain_part, query_gain_part, key_gain_part, router_part), ("gx", "gy")
-    )
+    small = (
+        attn_gain_part,
+        moe_gain_part,
+        query_gain_part,
+        key_gain_part,
+        router_part.T,
+        peak_slots,
+    )
+    summed = sum_everywhere(jnp.concatenate([part.reshape(-1) for part in small]), 5)
+    ends = list(accumulate(part.size for part in small))
+    attn_gain_grad, moe_gain_grad, query_gain_grad, key_gain_grad, router_flat, peaks = (
+        summed[end - part.size : end].reshape(part.shape) for end, part in zip(ends, small)
+    )
+    router_grad = router_flat.T
+    peak_global = jnp.max(peaks, axis=0)
     ranked = -jnp.sort(-peak_global)
     limit = jnp.sum(jnp.where(jnp.arange(NH, dtype=jnp.int32) == clip_rank[0], ranked, 0.0))
     factors = jnp.where(peak_global > limit, limit / peak_global, 1.0)

time: 897 us -> 880 us (0.981)
  Pallas kernels: 395 us -> 516 us
  blocking collectives: 118 us -> 40.3 us
  waiting for transfers between devices: 75.2 us -> 1.42 us
    pallas_call x0 -> x3, Pallas kernels: none -> 205 us  [the longest x1 107 us: enter(): pl.pallas_call(partial(enter_kernel, n_z, span), out_shape=(jax.ShapeDtyp...]
    psum x1 -> x0, waiting for transfers between devices: 73.7 us -> none  [local(): lax.psum((attn_gain_part, moe_gain_part, query_gain_part, key_gain_part,...]
    pallas_call x4 -> x3, Pallas kernels: 250 us -> 203 us  [reduce_scatter(): pl.pallas_call(partial(scatter_kernel, both, n_i, rows), out_shape=jax.Sh...]
    pmax x1 -> x0, blocking collectives: 38.4 us -> none  [local(): peak_global = lax.pmax(peak_local, ('gx', 'gy'))]
    psum x1 -> x0, blocking collectives: 37.9 us -> none  [local(): lax.psum((attn_gain_part, moe_gain_part, query_gain_part, key_gain_part,...]
    pallas_call x3 -> x2, Pallas kernels: 145 us -> 107 us  [all_gather(): pl.pallas_call(partial(gather_kernel, n_z, span), out_shape=jax.ShapeDtyp...]
  transfers between devices with their start and end apart: 7 -> 4, of which waited for: 1 -> 0; matrix products, arithmetic and copies ran while one was open for 23% -> 17% of each run, Pallas kernels for 42% -> 57%
where the time goes in v3:
time: 880 us; the launch traced here: 870 us
  Pallas kernels  516 us (59%)
  matrix products  209 us (24%)
  other arithmetic  46.3 us (5%)
  blocking collectives  40.3 us (5%)
  local copies, waits for them, and re-layouts  38.2 us (4%)
  between operations  16.2 us (2%)
    pallas_call x3, Pallas kernels, reduce_scatter(): pl.pallas_call(partial(scatter_kernel, both, n_i, rows), out_shape=jax.Sh...  203 us
    pallas_call x2, Pallas kernels, all_gather(): pl.pallas_call(partial(gather_kernel, n_z, span), out_shape=jax.ShapeDtyp...  107 us
    pallas_call x1, Pallas kernels, enter(): pl.pallas_call(partial(enter_kernel, n_z, span), out_shape=(jax.ShapeDtyp...  107 us
    pallas_call x1, Pallas kernels, leave(): pl.pallas_call(partial(leave_kernel, pieces, rows), out_shape=(jax.ShapeD...  77.4 us
    dot_general x6, matrix products, contract_cols(): lax.dot_general(left_side, right_side, (((1,), (1,)), ((), ())), preferre...  72.2 us
    dot_general x6, matrix products, contract_rows(): lax.dot_general(left_side, right_side, (((0,), (0,)), ((), ())), preferre...  57.8 us
    all_gather x1, blocking collectives, dense_experts(): all_ids = lax.all_gather(expert_ids, everyone, axis=0, tiled=True)  40.3 us
    pallas_call x1, Pallas kernels, sum_everywhere(): pl.pallas_call(partial(sum_kernel, n_z, bits), out_shape=jax.ShapeDtypeSt...  20.8 us
  transfers between devices with their start and end apart: 4, of which 0 were waited for; matrix products, arithmetic and copies ran while one was open for 17% of the time, Pallas kernels for 57%

profile of v3, /device:TPU:0, one launch (start us, length us, event | category | flops | bytes accessed | tf_op | source)
XLA Modules:
  0.0 870.4 jit_solution(14547949596437954156)
XLA Ops:
  10.1 2.0 pad_maximum_fusion.1.weight_ref
  12.1 1.2 fusion.68
  13.4 2.0 fusion.62
  15.4 107.0 %enter.1 = (bf16[8,2,64,2048]{3,2,1,0:T(8,128)(2,1)}, bf16[4,512,768]{2,1,0:T(8,128)(2,1)}) custom-call(bf16[2,64,2048]{2,1,0:T(8,128)(2,1)} %bitcast.232, bf16[512,768]{1,0:T(8,128)(2,1)} %pad_maximum_fusion.1.weight_ref), custom_call_target="tpu_custom_call" | custom-call | tf_op jit(solution)/shard_map/enter/pallas_call | solution.py:495
  122.5 6.3 fusion.95
  129.7 1.6 fusion.89
  132.3 1.9 copy.145
  134.2 2.9 copy.142
  137.1 2.0 copy.146
  139.2 1.8 multiply_reduce_fusion.8
  141.6 1.9 fusion.74
  143.6 1.9 multiply_multiply_fusion.1
  145.9 1.7 subtract_convert_fusion
  147.9 1.5 pad_maximum_fusion.5
  149.5 11.4 %while.29 = (s32[]{:T(128)}, bf16[2,512,2,128]{3,2,1,0:T(2,128)(2,1)}, f32[2,2,512]{2,1,0:T(2,128)S(1)}, f32[2,2]{1,0:T(2,128)S(1)}, s32[2,512]{1,0:T(2,128)S(1)...) while((s32[]{:T(128)}, ...), condition=%wide.region_7.8_spmd, body=%wide.region_3.7_spmd.sunk | while | flops 551156736 | bytes 18917564 | solution.py:983
  151.0 1.5 fusion.149
  152.5 1.7 fusion.150
  156.6 1.5 fusion.149
  158.2 1.7 fusion.150
  161.7 40.3 %all_gather.10 = s32[4096,8]{0,1:T(8,128)S(1)} all-gather(s32[128,8]{0,1:T(8,128)S(1)} %copy-done.54), channel_id=1, replica_groups=mesh['gx'=4,'gy'=8] {'gx','gy'}, dimensions={0}, use_global_device_ids=true | all-gather | bytes 135168 | tf_op jit(solution)/shard_map/all_gather | solution.py:874
  202.3 2.6 convolution_convert_fusion
  205.0 2.3 copy.221
  207.3 23.3 %scatter_plane.1 = f32[4,2,16,2048]{3,2,1,0:T(8,128)} custom-call(bf16[4,8,2,16,2048]{4,3,2,1,0:T(8,128)(2,1)} %bitcast.217), custom_call_target="tpu_custom_call" | custom-call | tf_op jit(solution)/shard_map/scatter_plane/pallas_call | solution.py:370
  230.6 1.4 multiply_reduce_fusion.7
  234.0 84.0 %gather_all.1 = bf16[32,2,64,2048]{3,2,1,0:T(8,128)(2,1)} custom-call(bf16[2,64,2048]{2,1,0:T(8,128)(2,1)} %bitcast.220), custom_call_target="tpu_custom_call" | custom-call | tf_op jit(solution)/shard_map/gather_all/pallas_call | solution.py:203
  318.1 10.4 %fusion.93 = (f32[4096]{0:T(1024)S(1)}, f32[4096,16]{0,1:T(8,128)S(1)}) fusion(bf16[4096,2048]{1,0:T(8,128)(2,1)} %bitcast.210, bf16[2048,16]{0,1:T(8,128)(2,1)S(1)} %copy-done.32), kind=kOutput, calls=%fused_computation.199 | convolution fusion | flops 268496896 | bytes 17121280 | tf_op jit(solution)/shard_map/dot_general | solution.py:879
  330.1 12.6 %fusion.53 = f32[4096,512]{1,0:T(8,128)} fusion(bf16[4096,2048]{1,0:T(8,128)(2,1)S(1)} %bitcast.213, bf16[1,2048,512]{2,1,0:T(8,128)(2,1)} %param.36), kind=kOutput, calls=%fused_computation.78 | convolution fusion | flops 8589934592 | bytes 27262976 | tf_op jit(solution)/shard_map/dot_general | solution.py:885
  342.8 11.0 %fusion.57 = f32[4096,512]{1,0:T(8,128)} fusion(bf16[4096,2048]{1,0:T(8,128)(2,1)S(1)} %bitcast.214, bf16[1,2048,512]{2,1,0:T(8,128)(2,1)S(1)} %copy-done.76), kind=kOutput, calls=%fused_computation.82 | convolution fusion | flops 8589934592 | bytes 27262976 | tf_op jit(solution)/shard_map/dot_general | solution.py:884
  353.8 20.4 %multiply_convert_fusion.2 = (bf16[4096,512]{1,0:T(8,128)(2,1)S(1)}, bf16[4096,512]{1,0:T(8,128)(2,1)}, bf16[4096,512]{1,0:T(8,128)(2,1)}) fusion(f32[4096,512]{1,0:T(8,128)} %fusion.57, f32[4096,512]{1,0:T(8,128)} %fusion.53, bf16[1,512,2048]{2,1,0:T(8,128)(2,1)S(1)} %copy-done, bf16[4096,2048]{1,0:T(8,128)(2,1)} %all-gather.5.cloned.1.call-done, ...), kind=kOutput, calls=%fused_computation.57 | convolution fusion | flops 8646557696 | bytes 48250880 | tf_op jit(solution)/shard_map/dot_general | solution.py:780
  374.2 16.5 %convolution_bitcast_fusion.1 = f32[1,2048,512]{2,1,0:T(8,128)} fusion(bf16[4096,2048]{1,0:T(8,128)(2,1)} %bitcast.211, bf16[4096,512]{1,0:T(8,128)(2,1)} %get-tuple-element.466), kind=kOutput, calls=%fused_computation.71 | convolution fusion | flops 8589934592 | bytes 25165824 | tf_op jit(solution)/shard_map/dot_general | solution.py:774
  390.7 17.7 %fusion.55 = f32[4096,2048]{1,0:T(8,128)} fusion(bf16[4096,512]{1,0:T(8,128)(2,1)} %get-tuple-element.466, bf16[1,2048,512]{2,1,0:T(8,128)(2,1)S(1)} %copy-done.77), kind=kOutput, calls=%fused_computation.80 | convolution fusion | flops 8589934592 | bytes 39845888 | tf_op jit(solution)/shard_map/dot_general | solution.py:780
  408.4 13.8 %convolution_bitcast_fusion = f32[1,2048,512]{2,1,0:T(8,128)} fusion(bf16[4096,2048]{1,0:T(8,128)(2,1)} %bitcast.212, bf16[4096,512]{1,0:T(8,128)(2,1)S(1)} %get-tuple-element.465), kind=kOutput, calls=%fused_computation.70 | convolution fusion | flops 8589934592 | bytes 25165824 | tf_op jit(solution)/shard_map/dot_general | solution.py:774
  422.2 19.4 %fusion.40 = (f32[4096]{0:T(1024)}, bf16[4096,2048]{1,0:T(8,128)(2,1)}) fusion(bf16[4096,2048]{1,0:T(8,128)(2,1)} %all-gather.5.cloned.1.call-done, f32[4096]{0:T(1024)S(1)} %div.134, bf16[4096,512]{1,0:T(8,128)(2,1)} %get-tuple-element.467, bf16[1,512,2048]{2,1,0:T(8,128)(2,1)S(1)} %copy-done), kind=kOutput, calls=%fused_computation.54 | convolution fusion | flops 8631873536 | bytes 39878656 | tf_op jit(solution)/shard_map/dot_general | solution.py:889
  441.6 2.5 all-to-all-start
  444.2 22.6 %add_convert_fusion = bf16[4096,2048]{1,0:T(8,128)(2,1)} fusion(f32[4096,2048]{1,0:T(8,128)} %fusion.55, bf16[4096,512]{1,0:T(8,128)(2,1)} %copy-done.79, bf16[1,2048,512]{2,1,0:T(8,128)(2,1)} %param.36), kind=kOutput, calls=%fused_computation.55 | convolution fusion | flops 8606711808 | bytes 56623104 | tf_op jit(solution)/shard_map/dot_general | solution.py:780
  466.8 15.2 %fusion.46 = f32[1,512,2048]{2,1,0:T(8,128)} fusion(bf16[4096,512]{1,0:T(8,128)(2,1)} %get-tuple-element.467, bf16[4096,2048]{1,0:T(8,128)(2,1)} %all-gather.5.cloned.1.call-done, f32[4096]{0:T(1024)S(1)} %div.134), kind=kOutput, calls=%fused_computation.69 | convolution fusion | flops 8615100416 | bytes 25182208 | tf_op jit(solution)/shard_map/dot_general | solution.py:774
  482.0 90.7 %scatter_all.2 = f32[2,64,2048]{2,1,0:T(8,128)} custom-call(bf16[4,8,2,64,2048]{4,3,2,1,0:T(8,128)(2,1)} %bitcast.218), custom_call_target="tpu_custom_call" | custom-call | tf_op jit(solution)/shard_map/scatter_all/pallas_call | solution.py:370
  572.9 89.4 %scatter_all.3 = f32[2,64,2048]{2,1,0:T(8,128)} custom-call(bf16[4,8,2,64,2048]{4,3,2,1,0:T(8,128)(2,1)} %bitcast.219), custom_call_target="tpu_custom_call" | custom-call | tf_op jit(solution)/shard_map/scatter_all/pallas_call | solution.py:370
  662.8 1.7 multiply_reduce_fusion.3
  665.7 23.3 %gather_plane.1 = bf16[8,2,64,2048]{3,2,1,0:T(8,128)(2,1)} custom-call(bf16[2,64,2048]{2,1,0:T(8,128)(2,1)} %bitcast.233), custom_call_target="tpu_custom_call" | custom-call | tf_op jit(solution)/shard_map/gather_plane/pallas_call | solution.py:203
  689.1 4.5 convolution_convert_fusion.3
  693.7 4.7 convolution_convert_fusion.4
  699.6 18.1 %while.30 = (s32[]{:T(128)}, f32[1024,2,128]{0,2,1:T(8,128)S(1)}, f32[1024,2,128]{0,2,1:T(8,128)}, f32[2,512,2,128]{3,1,0,2:T(8,128)}, bf16[2,512,2,128]{3,1,2,0...) while((s32[]{:T(128)}, f32[1024,2,128]{0,2,1:T(8,128)S(1)}, ...), condition=%wide.region_27.28_spmd.clone, body=%wide.region_25.27_spmd.clone.sunk | while | flops 1359870976 | bytes 58235156 | solution.py:1053
  701.2 1.5 fusion.161
  702.7 1.8 multiply_reduce_fusion.13
  704.5 1.3 multiply_convert_fusion.10
  710.1 1.5 fusion.161
  711.7 1.8 multiply_reduce_fusion.13
  713.5 1.3 multiply_convert_fusion.10
  717.8 2.1 convert_element_type.129
  720.3 2.6 multiply_add_fusion.3
  725.9 1.3 fusion.66
  727.6 7.6 convolution_convert_fusion.2
  735.2 5.1 convolution_convert_fusion.1
  740.4 4.7 copy.220
  745.1 77.4 %leave.1 = (f32[4,2,16,2048]{3,2,1,0:T(8,128)}, f32[512,768]{1,0:T(8,128)}) custom-call(bf16[4,8,2,16,2048]{4,3,2,1,0:T(8,128)(2,1)} %bitcast.216, bf16[4,512,768]{2,1,0:T(8,128)(2,1)} %bitcast.228), custom_call_target="tpu_custom_call" | custom-call | tf_op jit(solution)/shard_map/leave/pallas_call | solution.py:659
  822.6 1.7 fusion.63
  825.1 20.8 %sum_everywhere.1 = f32[2,152,128]{2,1,0:T(8,128)} custom-call(f32[2,152,128]{2,1,0:T(8,128)} %bitcast.239), custom_call_target="tpu_custom_call" | custom-call | tf_op jit(solution)/shard_map/sum_everywhere/pallas_call | solution.py:452
  845.9 1.3 slice.74
  847.2 1.3 sort.15
  851.5 1.3 fusion.91
  852.8 1.3 fusion.92
  855.0 2.7 fusion.90
  857.7 3.8 fusion.67
  (278 shorter events, 36.8 us)
Async XLA Ops:
  7.2 346.6 %copy-start = (bf16[1,512,2048]{2,1,0:T(8,128)(2,1)S(1)}, bf16[1,512,2048]{2,1,0:T(8,128)(2,1)}, u32[]{:S(2)}) copy-start(bf16[1,512,2048]{2,1,0:T(8,128)(2,1)} %param.37) | copy-start | bytes 6291460
  7.2 195.1 %all-gather.3.cloned.1.call-start = ((), (), s32[]{:S(2)}) async-start(), calls=%async_computation.2 | async-start | bytes 1310720 | tf_op jit(solution)/shard_map/all_gather | solution.py:938
  7.9 345.9 %all-gather.5.cloned.1.call-start = ((), (), s32[]{:S(2)}) async-start(), calls=%async_computation.3 | async-start | bytes 17301504 | tf_op jit(solution)/shard_map/all_gather | solution.py:875
  13.4 115.4 %copy-start.69 = (f32[128]{0:T(128)}, f32[128]{0:T(128)S(1)}, u32[]{:S(2)}) copy-start(f32[128]{0:T(128)S(1)} %fusion.68) | copy-start | bytes 1540
  13.4 115.4 %copy-start.61 = (f32[128]{0:T(128)}, f32[128]{0:T(128)S(1)}, u32[]{:S(2)}) copy-start(f32[128]{0:T(128)S(1)} %fusion.84) | copy-start | bytes 1540
  132.3 11.2 %copy-start.65 = (f32[128]{0:T(128)S(1)}, f32[128]{0:T(128)}, u32[]{:S(2)}) copy-start(f32[128]{0:T(128)} %param.28) | copy-start | bytes 1540
  134.2 11.3 %copy-start.13 = (f32[1024,2,128]{2,0,1:T(8,128)}, f32[1024,2,128]{2,0,1:T(8,128)S(1)}, u32[]{:S(2)}) copy-start(f32[1024,2,128]{2,0,1:T(8,128)S(1)} %copy.145) | copy-start | bytes 3145732
  134.2 11.3 %copy-start.67 = (f32[128]{0:T(128)S(1)}, f32[128]{0:T(128)}, u32[]{:S(2)}) copy-start(f32[128]{0:T(128)} %param.29) | copy-start | bytes 1540
  141.0 6.6 copy-start.50
  141.6 6.0 copy-start.43
  141.6 6.0 copy-start.45
  143.5 4.0 copy-start.22
  143.5 4.0 copy-start.23
  149.5 12.2 %copy-start.54 = (s32[128,8]{0,1:T(8,128)S(1)}, s32[128,8]{0,1:T(8,128)}, u32[]{:S(2)}) copy-start(s32[128,8]{0,1:T(8,128)} %param.23) | copy-start | bytes 12292
  160.9 44.1 %copy-start.3 = (bf16[1024,2,128]{2,0,1:T(8,128)(2,1)}, bf16[1024,2,128]{2,0,1:T(8,128)(2,1)S(1)}, u32[]{:S(2)}) copy-start(bf16[1024,2,128]{2,0,1:T(8,128)(2,1)S(1)} %get-tuple-element.711) | copy-start | bytes 1572868
  160.9 44.1 %copy-start.5 = (bf16[2,512,2,128]{3,1,2,0:T(8,128)(2,1)}, bf16[2,512,2,128]{3,1,2,0:T(8,128)(2,1)S(1)}, u32[]{:S(2)}) copy-start(bf16[2,512,2,128]{3,1,2,0:T(8,128)(2,1)S(1)} %get-tuple-element.712) | copy-start | bytes 1572868
  160.9 44.1 %copy-start.39 = (s32[2,512]{1,0:T(2,128)}, s32[2,512]{1,0:T(2,128)S(1)}, u32[]{:S(2)}) copy-start(s32[2,512]{1,0:T(2,128)S(1)} %get-tuple-element.723) | copy-start | bytes 12292
  160.9 44.1 %copy-start.52 = (f32[2,2,512]{2,1,0:T(2,128)}, f32[2,2,512]{2,1,0:T(2,128)S(1)}, u32[]{:S(2)}) copy-start(f32[2,2,512]{2,1,0:T(2,128)S(1)} %get-tuple-element.677) | copy-start | bytes 24580
  207.3 23.3 %copy-start.16 = (bf16[128,2048]{1,0:T(8,128)(2,1)S(1)}, bf16[128,2048]{1,0:T(8,128)(2,1)}, u32[]{:S(2)}) copy-start(bf16[128,2048]{1,0:T(8,128)(2,1)} %param.21) | copy-start | bytes 1572868
  207.3 25.7 %copy-start.41 = (f32[2048]{0:T(1024)S(1)}, f32[2048]{0:T(1024)}, u32[]{:S(2)}) copy-start(f32[2048]{0:T(1024)} %param.27) | copy-start | bytes 24580
  232.1 86.0 %copy-start.73 = (f32[128]{0:T(128)}, f32[128]{0:T(128)S(1)}, u32[]{:S(2)}) copy-start(f32[128]{0:T(128)S(1)} %get-tuple-element.457) | copy-start | bytes 1540
  234.0 84.0 %copy-start.32 = (bf16[2048,16]{0,1:T(8,128)(2,1)S(1)}, bf16[2048,16]{0,1:T(8,128)(2,1)}, u32[]{:S(2)}) copy-start(bf16[2048,16]{0,1:T(8,128)(2,1)} %param.34) | copy-start | bytes 196612
  318.0 10.7 %copy-start.19 = (bf16[128,2048]{1,0:T(8,128)(2,1)S(1)}, bf16[128,2048]{1,0:T(8,128)(2,1)}, u32[]{:S(2)}) copy-start(bf16[128,2048]{1,0:T(8,128)(2,1)} %multiply_convert_fusion.5) | copy-start | bytes 1572868
  318.1 12.1 %copy-start.2 = (bf16[32,2,64,2048]{3,2,1,0:T(8,128)(2,1)S(1)}, bf16[32,2,64,2048]{3,2,1,0:T(8,128)(2,1)}, u32[]{:S(2)}) copy-start(bf16[32,2,64,2048]{3,2,1,0:T(8,128)(2,1)} %gather_all.1) | copy-start | bytes 50331652
  329.0 13.8 %copy-start.37 = (f32[128,16]{0,1:T(8,128)}, f32[128,16]{0,1:T(8,128)S(1)}, u32[]{:S(2)}) copy-start(f32[128,16]{0,1:T(8,128)S(1)} %get-tuple-element.498) | copy-start | bytes 24580
  329.0 13.8 %copy-start.57 = (f32[128]{0:T(128)}, f32[128]{0:T(128)S(1)}, u32[]{:S(2)}) copy-start(f32[128]{0:T(128)S(1)} %get-tuple-element.497) | copy-start | bytes 1540
  329.0 13.7 %copy-start.63 = (f32[128]{0:T(128)}, f32[128]{0:T(128)S(1)}, u32[]{:S(2)}) copy-start(f32[128]{0:T(128)S(1)} %fusion.80) | copy-start | bytes 1540
  330.1 12.6 %copy-start.76 = (bf16[1,2048,512]{2,1,0:T(8,128)(2,1)S(1)}, bf16[1,2048,512]{2,1,0:T(8,128)(2,1)}, u32[]{:S(2)}) copy-start(bf16[1,2048,512]{2,1,0:T(8,128)(2,1)} %param.35) | copy-start | bytes 6291460
  374.2 34.2 %copy-start.79 = (bf16[4096,512]{1,0:T(8,128)(2,1)}, bf16[4096,512]{1,0:T(8,128)(2,1)S(1)}, u32[]{:S(2)}) copy-start(bf16[4096,512]{1,0:T(8,128)(2,1)S(1)} %get-tuple-element.465) | copy-start | bytes 12582916
  374.2 16.5 %copy-start.77 = (bf16[1,2048,512]{2,1,0:T(8,128)(2,1)S(1)}, bf16[1,2048,512]{2,1,0:T(8,128)(2,1)}, u32[]{:S(2)}) copy-start(bf16[1,2048,512]{2,1,0:T(8,128)(2,1)} %param.35) | copy-start | bytes 6291460
  441.6 220.6 %all-to-all-start = ((f32[32,1,128]{2,1,0:T(1,128)}), f32[32,1,128]{2,1,0:T(1,128)S(1)}, u32[]{:S(2)}, u32[]{:S(2)}) async-start(f32[32,1,128]{2,1,0:T(1,128)} %bitcast.26), calls=%async_computation | async-start | bytes 32768 | tf_op jit(solution)/shard_map/all_to_all | solution.py:893
  444.2 417.3 %reduce-scatter.2.cloned.1.call-start = ((), (), s32[]{:S(2)}) async-start(), calls=%async_computation.4 | async-start | bytes 1310720 | tf_op jit(solution)/shard_map/reduce_scatter | solution.py:1071
  572.7 89.6 %copy-start.55 = (s32[128,8]{0,1:T(8,128)S(1)}, s32[128,8]{0,1:T(8,128)}, u32[]{:S(2)}) copy-start(s32[128,8]{0,1:T(8,128)} %param.23) | copy-start | bytes 12292
  572.8 89.6 %copy-start.56 = (f32[128,16]{0,1:T(8,128)S(1)}, f32[128,16]{0,1:T(8,128)}, u32[]{:S(2)}) copy-start(f32[128,16]{0,1:T(8,128)} %fusion.79) | copy-start | bytes 24580
  572.8 89.7 %copy-start.38 = (f32[128,16]{0,1:T(8,128)S(1)}, f32[128,16]{0,1:T(8,128)}, u32[]{:S(2)}) copy-start(f32[128,16]{0,1:T(8,128)} %copy-done.37) | copy-start | bytes 24580
  572.8 89.7 %copy-start.58 = (f32[128]{0:T(128)S(1)}, f32[128]{0:T(128)}, u32[]{:S(2)}) copy-start(f32[128]{0:T(128)} %copy-done.57) | copy-start | bytes 1540
  572.8 89.7 %copy-start.72 = (f32[128]{0:T(128)S(1)}, f32[128]{0:T(128)}, u32[]{:S(2)}) copy-start(f32[128]{0:T(128)} %multiply_divide_fusion) | copy-start | bytes 1540
  572.8 89.7 %copy-start.64 = (f32[128]{0:T(128)S(1)}, f32[128]{0:T(128)}, u32[]{:S(2)}) copy-start(f32[128]{0:T(128)} %copy-done.63) | copy-start | bytes 1540
  572.8 89.7 %copy-start.20 = (bf16[128,2048]{1,0:T(8,128)(2,1)S(1)}, bf16[128,2048]{1,0:T(8,128)(2,1)}, u32[]{:S(2)}) copy-start(bf16[128,2048]{1,0:T(8,128)(2,1)} %multiply_convert_fusion.5) | copy-start | bytes 1572868
  572.8 89.9 %copy-start.9 = (f32[128,2048]{1,0:T(8,128)S(1)}, f32[128,2048]{1,0:T(8,128)}, u32[]{:S(2)}) copy-start(f32[128,2048]{1,0:T(8,128)} %copy-done.8) | copy-start | bytes 3145732
  572.8 89.9 %copy-start.33 = (bf16[2048,16]{0,1:T(8,128)(2,1)S(1)}, bf16[2048,16]{0,1:T(8,128)(2,1)}, u32[]{:S(2)}) copy-start(bf16[2048,16]{0,1:T(8,128)(2,1)} %param.34) | copy-start | bytes 196612
  572.8 89.9 %copy-start.42 = (f32[2048]{0:T(1024)S(1)}, f32[2048]{0:T(1024)}, u32[]{:S(2)}) copy-start(f32[2048]{0:T(1024)} %param.27) | copy-start | bytes 24580
  572.9 89.9 %copy-start.60 = (f32[128]{0:T(128)S(1)}, f32[128]{0:T(128)}, u32[]{:S(2)}) copy-start(f32[128]{0:T(128)} %copy-done.59) | copy-start | bytes 1540
  572.9 91.7 %copy-start.74 = (f32[128]{0:T(128)S(1)}, f32[128]{0:T(128)}, u32[]{:S(2)}) copy-start(f32[128]{0:T(128)} %copy-done.73) | copy-start | bytes 1540
  664.5 29.1 %copy-start.18 = (f32[128,2048]{1,0:T(8,128)}, f32[128,2048]{1,0:T(8,128)S(1)}, u32[]{:S(2)}) copy-start(f32[128,2048]{1,0:T(8,128)S(1)} %get-tuple-element.499) | copy-start | bytes 3145732
  664.5 24.6 %copy-start.27 = (bf16[2,512,2,128]{3,2,1,0:T(2,128)(2,1)S(1)}, bf16[2,512,2,128]{3,2,1,0:T(2,128)(2,1)}, u32[]{:S(2)}) copy-start(bf16[2,512,2,128]{3,2,1,0:T(2,128)(2,1)} %get-tuple-element.133) | copy-start | bytes 1572868
  693.6 6.0 copy-start.4
  693.6 6.0 copy-start.6
  693.6 6.0 copy-start.7
  693.6 6.0 copy-start.12
  693.6 6.0 copy-start.36
  693.6 6.0 copy-start.40
  693.6 6.0 copy-start.53
  727.6 7.6 copy-start.75
  745.1 77.5 %copy-start.17 = (bf16[128,2048]{1,0:T(8,128)(2,1)S(1)}, bf16[128,2048]{1,0:T(8,128)(2,1)}, u32[]{:S(2)}) copy-start(bf16[128,2048]{1,0:T(8,128)(2,1)} %param.21) | copy-start | bytes 1572868
  745.1 77.5 %copy-start.47 = (f32[2048]{0:T(1024)S(1)}, f32[2048]{0:T(1024)}, u32[]{:S(2)}) copy-start(f32[2048]{0:T(1024)} %param.26) | copy-start | bytes 24580
  745.1 77.5 %copy-start.62 = (f32[128]{0:T(128)S(1)}, f32[128]{0:T(128)}, u32[]{:S(2)}) copy-start(f32[128]{0:T(128)} %copy-done.61) | copy-start | bytes 1540
  745.1 79.3 %copy-start.71 = (f32[64]{0:T(128)S(1)}, f32[64]{0:T(128)}, u32[]{:S(2)}) copy-start(f32[64]{0:T(128)} %reshape.409) | copy-start | bytes 772
  745.1 106.3 %copy-start.70 = (f32[128]{0:T(128)S(1)}, f32[128]{0:T(128)}, u32[]{:S(2)}) copy-start(f32[128]{0:T(128)} %copy-done.69) | copy-start | bytes 1540
  745.1 109.0 %copy-start.30 = (bf16[512,256]{1,0:T(8,128)(2,1)S(1)}, bf16[512,256]{1,0:T(8,128)(2,1)}, u32[]{:S(2)}) copy-start(bf16[512,256]{1,0:T(8,128)(2,1)} %param.31) | copy-start | bytes 786436
  745.1 109.0 %copy-start.31 = (bf16[512,256]{1,0:T(8,128)(2,1)S(1)}, bf16[512,256]{1,0:T(8,128)(2,1)}, u32[]{:S(2)}) copy-start(bf16[512,256]{1,0:T(8,128)(2,1)} %param.30) | copy-start | bytes 786436
  822.6 35.1 %copy-start.10 = (f32[128,2048]{1,0:T(8,128)S(1)}, f32[128,2048]{1,0:T(8,128)}, u32[]{:S(2)}) copy-start(f32[128,2048]{1,0:T(8,128)} %copy-done.8) | copy-start | bytes 3145732
  849.7 11.7 %copy-start.78 = (f32[16]{0:T(128)}, f32[16]{0:T(128)S(1)}, u32[]{:S(2)}) copy-start(f32[16]{0:T(128)S(1)} %compare_select_fusion) | copy-start | bytes 196
  855.0 8.5 copy-start.1
  (25 other events, 54.5 us)
Sparse Core Ops, SparseCore 0:
  9.6 43.8 all-gather.2
  56.4 127.2 all-gather.4
  740.5 41.5 reduce-scatter.1

commit v4 on v3

--- a/solution.py
+++ b/solution.py
@@ -761,15 +761,6 @@
     return chosen / jnp.sum(chosen, axis=-1, keepdims=True)
 
 
-def dense_gates(all_ids, logits, expert):
-    shares = jax.nn.softmax(logits, axis=-1)
-    columns = jnp.arange(logits.shape[-1], dtype=jnp.int32)
-    routed = jnp.any(all_ids[:, :, None] == columns[None, None, :], axis=1)
-    chosen = jnp.where(routed, shares, 0.0)
-    own = jnp.sum(jnp.where(columns[None, :] == expert, chosen, 0.0), axis=-1)
-    return own / jnp.sum(chosen, axis=-1)
-
-
 def contract_rows(left_side, right_side):
     return lax.dot_general(
         left_side, right_side, (((0,), (0,)), ((), ())), preferred_element_type=jnp.float32
@@ -871,13 +862,13 @@
 ):
     experts = router_weight.shape[1]
     everyone = ("gx", "gy")
-    all_ids = lax.all_gather(expert_ids, everyone, axis=0, tiled=True)
     all_cot = lax.all_gather(cotangent, everyone, axis=0, tiled=True)
+    matches = expert_ids[:, :, None] == jnp.arange(experts, dtype=jnp.int32)[None, None, :]
+    dense_gates = jnp.sum(jnp.where(matches, gate_share[:, :, None], 0.0), axis=1)
+    own_gate = lax.all_to_all(
+        jnp.repeat(dense_gates.T, 2, axis=0), everyone, split_axis=0, concat_axis=0, tiled=True
+    ).reshape(-1)
     all_moe = all_gather(moe_in, True, 2)
-    rank = lax.axis_index("gx") * lax.axis_size("gy") + lax.axis_index("gy")
-    own_gate = dense_gates(
-        all_ids, jnp.dot(all_moe, router_weight, preferred_element_type=jnp.float32), rank // 2
-    )
     gate_in = gate_weight[0]
     up_in = up_weight[0]
     down_in = down_weight[0]
@@ -894,9 +885,10 @@
         gate_dots.reshape(devices, -1), everyone, split_axis=0, concat_axis=0, tiled=True
     )
     dots_experts = dots_back.reshape(experts, 2, -1).sum(axis=1).T
-    matches = expert_ids[:, :, None] == jnp.arange(experts, dtype=jnp.int32)[None, None, :]
     grad_gates = jnp.sum(jnp.where(matches, dots_experts[:, None, :], 0.0), axis=-1)
-    moe_out = reduce_scatter((piece * own_gate[:, None]).astype(jnp.bfloat16), True, 4)
+    moe_out = lax.psum_scatter(
+        (piece * own_gate[:, None]).astype(jnp.bfloat16), everyone, scatter_dimension=0, tiled=True
+    ).astype(jnp.float32)
     grad_use = (cot_float * own_gate[:, None]).astype(jnp.bfloat16)
     grad_hidden = contract_cols(grad_use, down_in)
     down_part = contract_rows(hidden, grad_use)
@@ -935,7 +927,9 @@
     acts_low = acts_float.astype(jnp.bfloat16)
     in_weights = jnp.concatenate([query_weight, key_weight, value_weight], axis=1)
     seq_acts, full_in = gather_inputs(acts_low, in_weights)
+    seq_acts, full_in, out_weight = lax.optimization_barrier((seq_acts, full_in, out_weight))
     out_rows = lax.all_gather(out_weight, "gx", axis=1, tiled=True)
+    out_rows, later_cot = lax.optimization_barrier((out_rows, cotangent))
     length = seq_acts.shape[0]
     local_width = query_weight.shape[1]
     local_heads = local_width // HD
@@ -999,7 +993,7 @@
     experts_pass = dense_experts if lax.axis_size("gy") == 8 and router_weight.shape[1] <= 2 * TOP else routed_experts
     moe_out, grad_gates, grad_moe_in, gate_part, up_part, down_part = experts_pass(
         moe_in,
-        cotangent,
+        later_cot,
         expert_ids,
         gate_share,
         router_weight,

time: 880 us -> 883 us (level)
  Pallas kernels: 516 us -> 466 us
  blocking collectives: 40.3 us -> 0 us
  waiting for transfers between devices: 1.42 us -> 40.8 us
  local copies, waits for them, and re-layouts: 38.2 us -> 60.7 us
  other arithmetic: 46.3 us -> 64.7 us
  starting transfers between devices: 2.66 us -> 17.3 us
    pallas_call x3 -> x2, Pallas kernels: 203 us -> 113 us  [reduce_scatter(): pl.pallas_call(partial(scatter_kernel, both, n_i, rows), out_shape=jax.Sh...]
    pallas_call x2, Pallas kernels: 107 us -> 168 us  [all_gather(): pl.pallas_call(partial(gather_kernel, n_z, span), out_shape=jax.ShapeDtyp...]
    pallas_call x1, Pallas kernels: 107 us -> 60.2 us  [enter(): pl.pallas_call(partial(enter_kernel, n_z, span), out_shape=(jax.ShapeDtyp...]
    all_gather x1 -> x0, blocking collectives: 40.3 us -> none  [dense_experts(): all_ids = lax.all_gather(expert_ids, everyone, axis=0, tiled=True)]
    all_gather x1, waiting for transfers between devices: 0.02 us -> 26.7 us  [local(): out_rows = lax.all_gather(out_weight, 'gx', axis=1, tiled=True)]
    unnamed x157 -> x142, local copies, waits for them, and re-layouts: 3.92 us -> 28.6 us
    convert_element_type x0 -> x1, other arithmetic: none -> 19 us  [dense_experts(): (piece * own_gate[:, None]).astype(jnp.bfloat16)]
    all_to_all x0 -> x1, starting transfers between devices: none -> 14.6 us  [dense_experts(): lax.all_to_all(jnp.repeat(dense_gates.T, 2, axis=0), everyone, split_axis...]
  transfers between devices with their start and end apart: 4 -> 6, of which waited for: 0 -> 3; matrix products, arithmetic and copies ran while one was open for 17% -> 26% of each run, Pallas kernels for 57% -> 34%
where the time goes in v4:
time: 883 us; the launch traced here: 873 us
  Pallas kernels  466 us (53%)
  matrix products  207 us (23%)
  other arithmetic  64.7 us (7%)
  local copies, waits for them, and re-layouts  60.7 us (7%)
  waiting for transfers between devices  40.8 us (5%)
  starting transfers between devices  17.3 us (2%)
  between operations  15.8 us (2%)
    pallas_call x2, Pallas kernels, all_gather(): pl.pallas_call(partial(gather_kernel, n_z, span), out_shape=jax.ShapeDtyp...  168 us
    pallas_call x2, Pallas kernels, reduce_scatter(): pl.pallas_call(partial(scatter_kernel, both, n_i, rows), out_shape=jax.Sh...  113 us
    pallas_call x1, Pallas kernels, leave(): pl.pallas_call(partial(leave_kernel, pieces, rows), out_shape=(jax.ShapeD...  91.3 us
    dot_general x6, matrix products, contract_cols(): lax.dot_general(left_side, right_side, (((1,), (1,)), ((), ())), preferre...  70.7 us
    pallas_call x1, Pallas kernels, enter(): pl.pallas_call(partial(enter_kernel, n_z, span), out_shape=(jax.ShapeDtyp...  60.2 us
    dot_general x6, matrix products, contract_rows(): lax.dot_general(left_side, right_side, (((0,), (0,)), ((), ())), preferre...  51.7 us
    pallas_call x1, Pallas kernels, sum_everywhere(): pl.pallas_call(partial(sum_kernel, n_z, bits), out_shape=jax.ShapeDtypeSt...  34.3 us
    unnamed x142, local copies, waits for them, and re-layouts  28.6 us
  transfers between devices with their start and end apart: 6, of which 3 were waited for; matrix products, arithmetic and copies ran while one was open for 26% of the time, Pallas kernels for 34%

profile of v4, /device:TPU:0, one launch (start us, length us, event | category | flops | bytes accessed | tf_op | source)
XLA Modules:
  0.0 872.8 jit_solution(3438923231172148866)
XLA Ops:
  7.3 1.4 fusion.67
  8.7 2.0 fusion.61
  10.7 2.0 pad_maximum_fusion.1.weight_ref
  12.7 60.2 %enter.1 = (bf16[8,2,64,2048]{3,2,1,0:T(8,128)(2,1)}, bf16[4,512,768]{2,1,0:T(8,128)(2,1)}) custom-call(bf16[2,64,2048]{2,1,0:T(8,128)(2,1)} %bitcast.229, bf16[512,768]{1,0:T(8,128)(2,1)} %pad_maximum_fusion.1.weight_ref), custom_call_target="tpu_custom_call" | custom-call | tf_op jit(solution)/shard_map/enter/pallas_call | solution.py:495
  73.0 26.7 %all-gather.3.cloned.1.call-done = bf16[256,2048]{1,0:T(8,128)(2,1)} async-done(((bf16[256,512]{1,0:T(8,128)(2,1)}), bf16[256,2048]{1,0:T(8,128)(2,1)}) %all-gather.3.cloned.1.call-update) | async-done | bytes 1048592 | tf_op jit(solution)/shard_map/all_gather | solution.py:931
  100.8 6.2 fusion.90
  110.0 1.3 copy.214
  111.3 1.6 copy.211
  112.9 2.4 copy.215
  115.3 1.9 multiply_reduce_fusion.8
  117.8 1.9 fusion.72
  122.0 11.6 %while.29 = (s32[]{:T(128)}, bf16[2,512,2,128]{3,2,1,0:T(2,128)(2,1)}, f32[2,2,512]{2,1,0:T(2,128)S(1)}, f32[2,2]{1,0:T(2,128)S(1)}, s32[2,512]{1,0:T(2,128)S(1)...) while((s32[]{:T(128)}, ...), condition=%wide.region_7.8_spmd, body=%wide.region_3.7_spmd.sunk | while | flops 551156736 | bytes 18917564 | solution.py:977
  123.4 1.5 fusion.142
  125.0 1.7 fusion.143
  129.1 1.5 fusion.142
  130.6 1.7 fusion.143
  133.6 3.0 convolution_convert_fusion
  136.6 2.3 copy.292
  139.0 24.3 %scatter_plane.1 = f32[4,2,16,2048]{3,2,1,0:T(8,128)} custom-call(bf16[4,8,2,16,2048]{4,3,2,1,0:T(8,128)(2,1)} %bitcast.211), custom_call_target="tpu_custom_call" | custom-call | tf_op jit(solution)/shard_map/scatter_plane/pallas_call | solution.py:370
  163.3 1.4 multiply_reduce_fusion.7
  166.0 144.1 %gather_all.1 = bf16[32,2,64,2048]{3,2,1,0:T(8,128)(2,1)} custom-call(bf16[2,64,2048]{2,1,0:T(8,128)(2,1)} %bitcast.217), custom_call_target="tpu_custom_call" | custom-call | tf_op jit(solution)/shard_map/gather_all/pallas_call | solution.py:203
  311.4 15.1 %fusion.57 = f32[4096,512]{1,0:T(8,128)} fusion(bf16[4096,2048]{1,0:T(8,128)(2,1)} %bitcast.212, bf16[1,2048,512]{2,1,0:T(8,128)(2,1)} %param.35), kind=kOutput, calls=%fused_computation.82 | convolution fusion | flops 8589934592 | bytes 27262976 | tf_op jit(solution)/shard_map/dot_general | solution.py:875
  326.5 20.2 %multiply_convert_fusion.4 = (bf16[4096,512]{1,0:T(8,128)(2,1)}, f32[4096,512]{1,0:T(8,128)}) fusion(f32[4096,512]{1,0:T(8,128)} %fusion.57, bf16[4096,2048]{1,0:T(8,128)(2,1)} %bitcast.213, bf16[1,2048,512]{2,1,0:T(8,128)(2,1)S(1)} %copy-done.67), kind=kOutput, calls=%fused_computation.61 | convolution fusion | flops 8602517504 | bytes 39845888 | tf_op jit(solution)/shard_map/dot_general | solution.py:876
  346.8 22.0 %fusion.40 = (f32[4096]{0:T(1024)}, f32[4096,2048]{0,1:T(8,128)}) fusion(bf16[4096,2048]{0,1:T(8,128)(2,1)} %all-gather.5.cloned.1.call-done, bf16[4096,512]{1,0:T(8,128)(2,1)} %get-tuple-element.543, bf16[1,512,2048]{2,1,0:T(8,128)(2,1)S(1)} %copy-done), kind=kOutput, calls=%fused_computation.54 | convolution fusion | flops 8615096320 | bytes 56639488 | tf_op jit(solution)/shard_map/dot_general | solution.py:880
  368.7 2.5 all-to-all-start.1
  371.3 7.1 all-to-all-done.1
  379.2 14.6 %all-to-all-start = ((f32[32,1,128]{2,1,0:T(1,128)}), f32[32,1,128]{2,1,0:T(1,128)S(1)}, u32[]{:S(2)}, u32[]{:S(2)}) async-start(f32[32,1,128]{2,1,0:T(1,128)} %bitcast.23), calls=%async_computation | async-start | bytes 32768 | tf_op jit(solution)/shard_map/all_to_all | solution.py:868
  393.9 7.0 all-to-all-done
  400.9 20.5 %multiply_convert_fusion.2 = (bf16[4096,512]{1,0:T(8,128)(2,1)}, bf16[4096,512]{1,0:T(8,128)(2,1)}) fusion(f32[4096,512]{1,0:T(8,128)} %fusion.57, f32[4096,512]{1,0:T(8,128)} %get-tuple-element.544, bf16[1,512,2048]{2,1,0:T(8,128)(2,1)S(1)} %copy-done, bf16[4096,2048]{0,1:T(8,128)(2,1)} %all-gather.5.cloned.1.call-done, f32[4096]{0:T(1024)S(1)} %bitcast.247), kind=kOutput, calls=%fused_computation.59 | convolution fusion | flops 8642363392 | bytes 44056576 | tf_op jit(solution)/shard_map/dot_general | solution.py:771
  421.4 17.9 %fusion.55 = f32[4096,2048]{1,0:T(8,128)} fusion(bf16[4096,512]{1,0:T(8,128)(2,1)} %get-tuple-element.511, bf16[1,2048,512]{2,1,0:T(8,128)(2,1)} %param.35), kind=kOutput, calls=%fused_computation.80 | convolution fusion | flops 8589934592 | bytes 39845888 | tf_op jit(solution)/shard_map/dot_general | solution.py:771
  439.3 20.2 %add_convert_fusion = bf16[4096,2048]{1,0:T(8,128)(2,1)} fusion(f32[4096,2048]{1,0:T(8,128)} %fusion.55, bf16[4096,512]{1,0:T(8,128)(2,1)} %get-tuple-element.510, bf16[1,2048,512]{2,1,0:T(8,128)(2,1)S(1)} %copy-done.68), kind=kOutput, calls=%fused_computation.55 | convolution fusion | flops 8606711808 | bytes 56623104 | tf_op jit(solution)/shard_map/dot_general | solution.py:771
  459.6 88.4 %scatter_all.1 = f32[2,64,2048]{2,1,0:T(8,128)} custom-call(bf16[4,8,2,64,2048]{4,3,2,1,0:T(8,128)(2,1)} %bitcast.216), custom_call_target="tpu_custom_call" | custom-call | tf_op jit(solution)/shard_map/scatter_all/pallas_call | solution.py:370
  548.0 1.7 multiply_reduce_fusion.3
  551.0 23.8 %gather_plane.1 = bf16[8,2,64,2048]{3,2,1,0:T(8,128)(2,1)} custom-call(bf16[2,64,2048]{2,1,0:T(8,128)(2,1)} %bitcast.230), custom_call_target="tpu_custom_call" | custom-call | tf_op jit(solution)/shard_map/gather_plane/pallas_call | solution.py:203
  574.8 4.5 convolution_convert_fusion.3
  579.4 19.0 %multiply_convert_fusion.1 = bf16[4096,2048]{0,1:T(8,128)(2,1)} fusion(f32[4096,2048]{0,1:T(8,128)} %get-tuple-element.546, f32[4096]{0:T(1024)S(1)} %bitcast.248), kind=kLoop, calls=%fused_computation.56 | loop fusion | flops 16777216 | bytes 50348032 | tf_op jit(solution)/shard_map/convert_element_type | solution.py:890
  598.4 22.6 %copy.237 = bf16[4096,2048]{1,0:T(8,128)(2,1)} copy(bf16[4096,2048]{0,1:T(8,128)(2,1)} %multiply_convert_fusion.1) | data formatting | bytes 33554432
  622.3 4.7 convolution_convert_fusion.4
  628.2 18.1 %while.30 = (s32[]{:T(128)}, f32[1024,2,128]{0,2,1:T(8,128)S(1)}, f32[1024,2,128]{0,2,1:T(8,128)}, f32[2,512,2,128]{3,1,0,2:T(8,128)}, bf16[2,512,2,128]{3,1,2,0...) while((s32[]{:T(128)}, f32[1024,2,128]{0,2,1:T(8,128)S(1)}, ...), condition=%wide.region_24.25_spmd.clone, body=%wide.region_22.24_spmd.clone.sunk | while | flops 1359870976 | bytes 58235156 | solution.py:1047
  629.6 1.5 fusion.154
  631.1 1.8 multiply_reduce_fusion.13
  633.0 1.3 multiply_convert_fusion.10
  638.6 1.5 fusion.154
  640.1 1.8 multiply_reduce_fusion.13
  642.0 1.3 multiply_convert_fusion.10
  646.3 2.1 convert_element_type.133
  649.8 3.3 multiply_add_fusion.3
  656.0 1.7 fusion.65
  657.7 2.1 copy.231
  659.8 2.2 fusion.64
  662.3 5.6 convolution_convert_fusion.1
  667.9 2.6 copy.291
  671.8 4.9 convolution_convert_fusion.2
  676.7 91.3 %leave.1 = (f32[4,2,16,2048]{3,2,1,0:T(8,128)}, f32[512,768]{1,0:T(8,128)}) custom-call(bf16[4,8,2,16,2048]{4,3,2,1,0:T(8,128)(2,1)} %bitcast.210, bf16[4,512,768]{2,1,0:T(8,128)(2,1)} %bitcast.225), custom_call_target="tpu_custom_call" | custom-call | tf_op jit(solution)/shard_map/leave/pallas_call | solution.py:659
  768.0 1.7 fusion.62
  770.5 34.3 %sum_everywhere.1 = f32[2,152,128]{2,1,0:T(8,128)} custom-call(f32[2,152,128]{2,1,0:T(8,128)} %bitcast.236), custom_call_target="tpu_custom_call" | custom-call | tf_op jit(solution)/shard_map/sum_everywhere/pallas_call | solution.py:452
  812.0 1.3 fusion.88
  813.3 1.9 multiply_convert_fusion.6
  816.4 14.3 %convolution_bitcast_fusion = f32[1,2048,512]{2,1,0:T(8,128)} fusion(bf16[4096,2048]{1,0:T(8,128)(2,1)} %bitcast.214, bf16[4096,512]{1,0:T(8,128)(2,1)S(1)} %copy-done.71), kind=kOutput, calls=%fused_computation.70 | convolution fusion | flops 8589934592 | bytes 25165824 | tf_op jit(solution)/shard_map/dot_general | solution.py:765
  830.7 13.9 %convolution_bitcast_fusion.1 = f32[1,2048,512]{2,1,0:T(8,128)} fusion(bf16[4096,2048]{1,0:T(8,128)(2,1)} %bitcast.215, bf16[4096,512]{1,0:T(8,128)(2,1)S(1)} %copy-done.70), kind=kOutput, calls=%fused_computation.71 | convolution fusion | flops 8589934592 | bytes 25165824 | tf_op jit(solution)/shard_map/dot_general | solution.py:765
  844.7 14.0 %fusion.46 = f32[1,512,2048]{2,1,0:T(8,128)} fusion(bf16[4096,512]{1,0:T(8,128)(2,1)S(1)} %copy-done.20, bf16[4096,2048]{0,1:T(8,128)(2,1)} %all-gather.5.cloned.1.call-done, f32[4096]{0:T(1024)S(1)} %bitcast.249), kind=kOutput, calls=%fused_computation.69 | convolution fusion | flops 8615100416 | bytes 25182208 | tf_op jit(solution)/shard_map/dot_general | solution.py:765
  858.6 1.8 convert_bitcast_fusion
  860.4 2.0 copy.233
  862.5 3.6 fusion.66
  (263 shorter events, 41.3 us)
Async XLA Ops:
  7.2 339.6 %copy-start = (bf16[1,512,2048]{2,1,0:T(8,128)(2,1)S(1)}, bf16[1,512,2048]{2,1,0:T(8,128)(2,1)}, u32[]{:S(2)}) copy-start(bf16[1,512,2048]{2,1,0:T(8,128)(2,1)} %param.37) | copy-start | bytes 6291460
  7.2 92.5 %copy-start.23 = (bf16[128,2048]{1,0:T(8,128)(2,1)S(1)}, bf16[128,2048]{1,0:T(8,128)(2,1)}, u32[]{:S(2)}) copy-start(bf16[128,2048]{1,0:T(8,128)(2,1)} %param.22) | copy-start | bytes 1572868
  7.2 93.5 %copy-start.33 = (s32[1024]{0:T(1024)S(1)}, s32[1024]{0:T(1024)}, u32[]{:S(2)}) copy-start(s32[1024]{0:T(1024)} %param.24) | copy-start | bytes 12292
  7.2 92.5 %all-gather.3.cloned.1.call-start = ((), (), s32[]{:S(2)}) async-start(), calls=%async_computation.4 | async-start | bytes 1310720 | tf_op jit(solution)/shard_map/all_gather | solution.py:931
  8.7 98.3 %copy-start.64 = (f32[128]{0:T(128)}, f32[128]{0:T(128)S(1)}, u32[]{:S(2)}) copy-start(f32[128]{0:T(128)S(1)} %fusion.67) | copy-start | bytes 1540
  8.7 98.3 %copy-start.54 = (f32[128]{0:T(128)}, f32[128]{0:T(128)S(1)}, u32[]{:S(2)}) copy-start(f32[128]{0:T(128)S(1)} %fusion.80) | copy-start | bytes 1540
  73.0 273.8 %all-gather.5.cloned.1.call-start = ((), (), s32[]{:S(2)}) async-start(), calls=%async_computation.5 | async-start | bytes 17301504 | tf_op jit(solution)/shard_map/all_gather | solution.py:865
  110.0 9.8 %copy-start.58 = (f32[128]{0:T(128)S(1)}, f32[128]{0:T(128)}, u32[]{:S(2)}) copy-start(f32[128]{0:T(128)} %param.28) | copy-start | bytes 1540
  111.3 8.9 %copy-start.56 = (f32[128]{0:T(128)S(1)}, f32[128]{0:T(128)}, u32[]{:S(2)}) copy-start(f32[128]{0:T(128)} %param.29) | copy-start | bytes 1540
  112.9 7.6 copy-start.10
  115.3 4.8 copy-start.12
  117.2 4.1 copy-start.47
  117.8 3.5 copy-start.42
  117.8 3.5 copy-start.40
  133.6 5.4 copy-start.2
  133.6 5.4 copy-start.4
  133.6 5.4 copy-start.36
  133.6 5.3 copy-start.49
  133.6 5.3 copy-start.62
  139.0 24.3 %copy-start.14 = (bf16[128,2048]{1,0:T(8,128)(2,1)S(1)}, bf16[128,2048]{1,0:T(8,128)(2,1)}, u32[]{:S(2)}) copy-start(bf16[128,2048]{1,0:T(8,128)(2,1)} %param.21) | copy-start | bytes 1572868
  139.0 25.8 %copy-start.38 = (f32[2048]{0:T(1024)S(1)}, f32[2048]{0:T(1024)}, u32[]{:S(2)}) copy-start(f32[2048]{0:T(1024)} %param.27) | copy-start | bytes 24580
  164.8 385.0 %copy-start.6 = (f32[128,2048]{1,0:T(8,128)}, f32[128,2048]{1,0:T(8,128)S(1)}, u32[]{:S(2)}) copy-start(f32[128,2048]{1,0:T(8,128)S(1)} %get-tuple-element.505) | copy-start | bytes 3145732
  164.8 385.0 %copy-start.52 = (f32[128]{0:T(128)}, f32[128]{0:T(128)S(1)}, u32[]{:S(2)}) copy-start(f32[128]{0:T(128)S(1)} %fusion.81) | copy-start | bytes 1540
  166.0 144.1 %copy-start.35 = (bf16[2048,16]{0,1:T(8,128)(2,1)S(1)}, bf16[2048,16]{0,1:T(8,128)(2,1)}, u32[]{:S(2)}) copy-start(bf16[2048,16]{0,1:T(8,128)(2,1)} %param.34) | copy-start | bytes 196612
  311.4 15.1 %copy-start.67 = (bf16[1,2048,512]{2,1,0:T(8,128)(2,1)S(1)}, bf16[1,2048,512]{2,1,0:T(8,128)(2,1)}, u32[]{:S(2)}) copy-start(bf16[1,2048,512]{2,1,0:T(8,128)(2,1)} %param.36) | copy-start | bytes 6291460
  346.8 31.6 %copy-start.51 = (s32[128,8]{0,1:T(8,128)S(1)}, s32[128,8]{0,1:T(8,128)}, u32[]{:S(2)}) copy-start(s32[128,8]{0,1:T(8,128)} %param.23) | copy-start | bytes 12292
  368.7 9.6 %all-to-all-start.1 = ((f32[32,1,128]{2,1,0:T(1,128)}), f32[32,1,128]{2,1,0:T(1,128)S(1)}, u32[]{:S(2)}, u32[]{:S(2)}) async-start(f32[32,1,128]{2,1,0:T(1,128)} %bitcast.27), calls=%async_computation.1 | async-start | bytes 32768 | tf_op jit(solution)/shard_map/all_to_all | solution.py:884
  379.2 21.7 %all-to-all-start = ((f32[32,1,128]{2,1,0:T(1,128)}), f32[32,1,128]{2,1,0:T(1,128)S(1)}, u32[]{:S(2)}, u32[]{:S(2)}) async-start(f32[32,1,128]{2,1,0:T(1,128)} %bitcast.23), calls=%async_computation | async-start | bytes 32768 | tf_op jit(solution)/shard_map/all_to_all | solution.py:868
  393.8 464.8 %reduce-scatter.5.cloned.1.call-start = ((), (), s32[]{:S(2)}) async-start(), calls=%async_computation.6 | async-start | bytes 1310720 | tf_op jit(solution)/shard_map/reduce_scatter | solution.py:1065
  421.4 17.9 %copy-start.68 = (bf16[1,2048,512]{2,1,0:T(8,128)(2,1)S(1)}, bf16[1,2048,512]{2,1,0:T(8,128)(2,1)}, u32[]{:S(2)}) copy-start(bf16[1,2048,512]{2,1,0:T(8,128)(2,1)} %param.36) | copy-start | bytes 6291460
  459.6 90.2 %copy-start.24 = (bf16[128,2048]{1,0:T(8,128)(2,1)S(1)}, bf16[128,2048]{1,0:T(8,128)(2,1)}, u32[]{:S(2)}) copy-start(bf16[128,2048]{1,0:T(8,128)(2,1)} %param.22) | copy-start | bytes 1572868
  549.7 29.6 %copy-start.16 = (f32[128,2048]{1,0:T(8,128)}, f32[128,2048]{1,0:T(8,128)S(1)}, u32[]{:S(2)}) copy-start(f32[128,2048]{1,0:T(8,128)S(1)} %get-tuple-element.547) | copy-start | bytes 3145732
  549.7 25.1 %copy-start.28 = (bf16[2,512,2,128]{3,2,1,0:T(2,128)(2,1)S(1)}, bf16[2,512,2,128]{3,2,1,0:T(2,128)(2,1)}, u32[]{:S(2)}) copy-start(bf16[2,512,2,128]{3,2,1,0:T(2,128)(2,1)} %get-tuple-element.140) | copy-start | bytes 1572868
  549.8 29.5 %copy-start.60 = (f32[128]{0:T(128)}, f32[128]{0:T(128)S(1)}, u32[]{:S(2)}) copy-start(f32[128]{0:T(128)S(1)} %multiply_multiply_fusion.5) | copy-start | bytes 1540
  579.3 283.1 %reduce-scatter.7.cloned.1.call-start = ((), (), s32[]{:S(2)}) async-start(), calls=%async_computation.7 | async-start | bytes 17301504 | tf_op jit(solution)/shard_map/reduce_scatter | solution.py:889
  622.3 5.9 copy-start.3
  622.3 5.9 copy-start.5
  622.3 5.9 copy-start.9
  622.3 5.9 copy-start.34
  622.3 5.9 copy-start.37
  622.3 5.9 copy-start.50
  649.7 4.4 copy-start.11
  649.7 4.4 copy-start.41
  649.7 4.4 copy-start.59
  649.7 5.3 copy-start.13
  649.7 5.3 copy-start.43
  649.7 5.3 copy-start.57
  653.1 2.9 copy-start.46
  657.7 4.5 copy-start.31
  667.9 3.9 copy-start.66
  676.7 91.3 %copy-start.15 = (bf16[128,2048]{1,0:T(8,128)(2,1)S(1)}, bf16[128,2048]{1,0:T(8,128)(2,1)}, u32[]{:S(2)}) copy-start(bf16[128,2048]{1,0:T(8,128)(2,1)} %param.21) | copy-start | bytes 1572868
  676.7 91.3 %copy-start.44 = (f32[2048]{0:T(1024)S(1)}, f32[2048]{0:T(1024)}, u32[]{:S(2)}) copy-start(f32[2048]{0:T(1024)} %param.26) | copy-start | bytes 24580
  676.7 91.3 %copy-start.55 = (f32[128]{0:T(128)S(1)}, f32[128]{0:T(128)}, u32[]{:S(2)}) copy-start(f32[128]{0:T(128)} %copy-done.54) | copy-start | bytes 1540
  676.7 134.0 %copy-start.65 = (f32[128]{0:T(128)S(1)}, f32[128]{0:T(128)}, u32[]{:S(2)}) copy-start(f32[128]{0:T(128)} %copy-done.64) | copy-start | bytes 1540
  767.9 47.3 %copy-start.27 = (f32[512,768]{1,0:T(8,128)S(1)}, f32[512,768]{1,0:T(8,128)}, u32[]{:S(2)}) copy-start(f32[512,768]{1,0:T(8,128)} %get-tuple-element.150) | copy-start | bytes 4718596
  809.0 7.5 copy-start.71
  810.6 20.1 %copy-start.69 = (f32[16]{0:T(128)}, f32[16]{0:T(128)S(1)}, u32[]{:S(2)}) copy-start(f32[16]{0:T(128)S(1)} %compare_select_fusion) | copy-start | bytes 196
  816.4 14.3 %copy-start.70 = (bf16[4096,512]{1,0:T(8,128)(2,1)S(1)}, bf16[4096,512]{1,0:T(8,128)(2,1)}, u32[]{:S(2)}) copy-start(bf16[4096,512]{1,0:T(8,128)(2,1)} %get-tuple-element.511) | copy-start | bytes 12582916
  830.7 13.9 %copy-start.20 = (bf16[4096,512]{1,0:T(8,128)(2,1)S(1)}, bf16[4096,512]{1,0:T(8,128)(2,1)}, u32[]{:S(2)}) copy-start(bf16[4096,512]{1,0:T(8,128)(2,1)} %get-tuple-element.543) | copy-start | bytes 12582916
  844.6 17.8 %copy-start.7 = (f32[128,2048]{1,0:T(8,128)S(1)}, f32[128,2048]{1,0:T(8,128)}, u32[]{:S(2)}) copy-start(f32[128,2048]{1,0:T(8,128)} %copy-done.6) | copy-start | bytes 3145732
  844.6 17.8 %copy-start.39 = (f32[2048]{0:T(1024)S(1)}, f32[2048]{0:T(1024)}, u32[]{:S(2)}) copy-start(f32[2048]{0:T(1024)} %param.27) | copy-start | bytes 24580
  844.6 17.8 %copy-start.53 = (f32[128]{0:T(128)S(1)}, f32[128]{0:T(128)}, u32[]{:S(2)}) copy-start(f32[128]{0:T(128)} %copy-done.52) | copy-start | bytes 1540
  844.6 17.8 %copy-start.61 = (f32[128]{0:T(128)S(1)}, f32[128]{0:T(128)}, u32[]{:S(2)}) copy-start(f32[128]{0:T(128)} %copy-done.60) | copy-start | bytes 1540
  844.6 21.4 %copy-start.1 = (bf16[1,512,2048]{2,1,0:T(8,128)(2,1)S(1)}, bf16[1,512,2048]{2,1,0:T(8,128)(2,1)}, u32[]{:S(2)}) copy-start(bf16[1,512,2048]{2,1,0:T(8,128)(2,1)} %param.37) | copy-start | bytes 6291460
  (19 other events, 29.9 us)
Sparse Core Ops, SparseCore 0:
  73.1 26.5 all-gather.2
  103.1 190.4 all-gather.4
  579.4 25.2 reduce-scatter.4
  621.1 209.2 reduce-scatter.6

commit v5 on v4

--- a/solution.py
+++ b/solution.py
@@ -15,6 +15,10 @@
 
 EPSILON = 1e-06
 NEGATIVE = -1e30
+
+
+def flip(index):
+    return index + 1 - 2 * (index % 2)
 
 
 def barrier_with(partners):
@@ -90,109 +94,131 @@
     return start, [partial(relay, d) for d in range(1, n_z)], finish
 
 
-def gather_kernel(n_z, span, own_ref, out_ref, send_sem, recv_sem, local_sem, chain=None):
-    z = lax.axis_index("gx"); g = lax.axis_index("gy")
-    core = {"gx": z, "gy": g + 1 - 2 * (g % 2)}
-    xn = {"gx": z, "gy": g + 2 - 4 * ((g // 2) % 2)}
-    yn = {"gx": z, "gy": g + 4 - 8 * ((g // 4) % 2)}
-    gx_ = g + 2 - 4 * ((g // 2) % 2)
-    gy_ = g + 4 - 8 * ((g // 4) % 2)
-    gd_ = gx_ + gy_ - g
-    gc = lambda v: v + 1 - 2 * (v % 2)
-    zup = {"gx": z + 1, "gy": g}; zdn = {"gx": z - 1, "gy": g}
-    zb = z if n_z > 1 else 0
-    partners = [(z >= 0, core), (z >= 0, xn), (z >= 0, yn)]
-    n_chain = lax.axis_size("gx") if chain else n_z
-    if n_chain > 1:
-        partners += [(z < n_chain - 1, zup), (z > 0, zdn)]
-    barrier_with(partners)
-    if chain:
-        chain[0]()
+def gather_steps(n_z, span, own_ref, out_ref, send_sem, recv_sem, local_sem):
+    z = lax.axis_index("gx")
+    g = lax.axis_index("gy")
+    flip_x = g + 2 - 4 * ((g // 2) % 2)
+    flip_y = g + 4 - 8 * ((g // 4) % 2)
+    flip_both = flip_x + flip_y - g
+    core = {"gx": z, "gy": flip(g)}
+    x_peer = {"gx": z, "gy": flip_x}
+    y_peer = {"gx": z, "gy": flip_y}
+    above = {"gx": z + 1, "gy": g}
+    below = {"gx": z - 1, "gy": g}
+    first_z = z if n_z > 1 else 0
     sends = []
-    def send(ok, src, b, h, dev):
+
+    def send(ok, source, b, h, peer):
         k = len(sends)
+
         def make():
             return pltpu.make_async_remote_copy(
-                src_ref=src, dst_ref=out_ref.at[b, h], send_sem=send_sem.at[k], recv_sem=recv_sem.at[b, h],
-                device_id=dev, device_id_type=pl.DeviceIdType.MESH)
+                src_ref=source,
+                dst_ref=out_ref.at[b, h],
+                send_sem=send_sem.at[k],
+                recv_sem=recv_sem.at[b, h],
+                device_id=peer,
+                device_id_type=pl.DeviceIdType.MESH,
+            )
+
         sends.append((ok, make))
-        if ok is True:
-            make().start()
-        else:
-            @pl.when(ok)
-            def _(): make().start()
+        run_if(ok, lambda: make().start())
+
     def arrive(ok, b, h):
-        def go():
+        def wait():
             pltpu.make_async_remote_copy(
-                src_ref=out_ref.at[b, h], dst_ref=out_ref.at[b, h], send_sem=send_sem.at[0], recv_sem=recv_sem.at[b, h],
-                device_id=core, device_id_type=pl.DeviceIdType.MESH).wait_recv()
-        if ok is True:
-            go()
-        else:
-            @pl.when(ok)
-            def _(): go()
-    own_b = zb * span + g
-    local = pltpu.make_async_copy(own_ref, out_ref.at[own_b], local_sem)
-    local.start()
-    items = [(True, zb, 0)]
+                src_ref=out_ref.at[b, h],
+                dst_ref=out_ref.at[b, h],
+                send_sem=send_sem.at[0],
+                recv_sem=recv_sem.at[b, h],
+                device_id=core,
+                device_id_type=pl.DeviceIdType.MESH,
+            ).wait_recv()
+
+        run_if(ok, wait)
+
+    local = pltpu.make_async_copy(own_ref, out_ref.at[first_z * span + g], local_sem)
+    items = [(True, first_z, 0)]
     for d in range(1, n_z):
         items += [(z >= d, z - d, -d), (z < n_z - d, z + d, d)]
-    def and_(a, b):
-        if a is True: return b
-        if b is True: return a
-        return jnp.logical_and(a, b)
-    def first(it):
-        ok, zs, d = it
-        b = zs * span + g
-        src = (lambda h: own_ref.at[h]) if d == 0 else (lambda h: out_ref.at[b, h])
-        if d != 0:
-            arrive(ok, b, 0); arrive(ok, b, 1)
-        if n_z > 1:
-            if d <= 0:
-                for h in range(2): send(and_(ok, z < n_z - 1), src(h), b, h, zup)
-            if d >= 0:
-                for h in range(2): send(and_(ok, z > 0), src(h), b, h, zdn)
-        send(ok, src(0), b, 0, xn)
-        send(ok, src(1), b, 1, yn)
-        send(ok, src(1), b, 1, xn)
-        send(ok, src(0), b, 0, yn)
-        send(ok, src(0), b, 0, core)
-        send(ok, src(1), b, 1, core)
-    def second(it):
-        ok, zs, d = it
-        b = zs * span + gx_
-        arrive(ok, b, 0)
-        send(ok, out_ref.at[b, 0], b, 0, yn)
-        send(ok, out_ref.at[b, 0], b, 0, core)
-        b = zs * span + gy_
-        arrive(ok, b, 1)
-        send(ok, out_ref.at[b, 1], b, 1, xn)
-        send(ok, out_ref.at[b, 1], b, 1, core)
-    def third(it):
-        ok, zs, d = it
-        for b, h in ((zs * span + gd_, 0), (zs * span + gd_, 1), (zs * span + gy_, 0), (zs * span + gx_, 1)):
+
+    def first(item):
+        ok, owner, d = item
+        b = owner * span + g
+        if d == 0:
+            local.start()
+            source = own_ref
+        else:
+            arrive(ok, b, 0)
+            arrive(ok, b, 1)
+            source = out_ref.at[b]
+        for h in range(2):
+            if n_z > 1 and d <= 0:
+                send(always(ok, z < n_z - 1), source.at[h], b, h, above)
+            if n_z > 1 and d >= 0:
+                send(always(ok, z > 0), source.at[h], b, h, below)
+        send(ok, source.at[0], b, 0, x_peer)
+        send(ok, source.at[1], b, 1, y_peer)
+        send(ok, source.at[1], b, 1, x_peer)
+        send(ok, source.at[0], b, 0, y_peer)
+        send(ok, source.at[0], b, 0, core)
+        send(ok, source.at[1], b, 1, core)
+
+    def second(item):
+        ok, owner, _ = item
+        for side, h, peer in ((flip_x, 0, y_peer), (flip_y, 1, x_peer)):
+            b = owner * span + side
+            arrive(ok, b, h)
+            send(ok, out_ref.at[b, h], b, h, peer)
+            send(ok, out_ref.at[b, h], b, h, core)
+
+    def third(item):
+        ok, owner, _ = item
+        for side, h in ((flip_both, 0), (flip_both, 1), (flip_y, 0), (flip_x, 1)):
+            b = owner * span + side
             arrive(ok, b, h)
             send(ok, out_ref.at[b, h], b, h, core)
+
     n = len(items)
-    for i in range(n + 2):
-        if i < n: first(items[i])
-        if 1 <= i <= n: second(items[i - 1])
-        if i >= 2: third(items[i - 2])
-    if chain:
-        chain[1][0]()
-    for ok, zs, d in items:
-        for gg in (g, gx_, gy_, gd_):
-            for h in range(2): arrive(ok, zs * span + gc(gg), h)
-    if chain:
-        for relay in chain[1][1:]:
-            relay()
-        chain[2]()
-    local.wait()
-    for ok, make in sends:
-        if ok is True: make().wait_send()
-        else:
-            @pl.when(ok)
-            def _(): make().wait_send()
+
+    def step(i):
+        if i < n:
+            first(items[i])
+        if 1 <= i <= n:
+            second(items[i - 1])
+        if i >= 2:
+            third(items[i - 2])
+
+    def finish():
+        for ok, owner, _ in items:
+            for side in (g, flip_x, flip_y, flip_both):
+                for h in range(2):
+                    arrive(ok, owner * span + flip(side), h)
+        local.wait()
+        for ok, make in sends:
+            run_if(ok, lambda make=make: make().wait_send())
+
+    return [partial(step, i) for i in range(n + 2)], finish
+
+
+def greet(n_z):
+    z = lax.axis_index("gx")
+    g = lax.axis_index("gy")
+    peers = [
+        (z >= 0, {"gx": z, "gy": g + bit - 2 * bit * ((g // bit) % 2)}) for bit in (1, 2, 4)
+    ]
+    if n_z > 1:
+        peers += [(z < n_z - 1, {"gx": z + 1, "gy": g}), (z > 0, {"gx": z - 1, "gy": g})]
+    barrier_with(peers)
+
+
+def gather_kernel(n_z, span, own_ref, out_ref, send_sem, recv_sem, local_sem):
+    greet(n_z)
+    steps, finish = gather_steps(n_z, span, own_ref, out_ref, send_sem, recv_sem, local_sem)
+    for step in steps:
+        step()
+    finish()
+
 
 def all_gather(block, both, collective_id):
     n_z = lax.axis_size("gx") if both else 1
@@ -232,9 +258,8 @@
     z = lax.axis_index("gx"); g = lax.axis_index("gy")
     flip_x = g + 2 - 4 * ((g // 2) % 2)
     flip_y = g + 4 - 8 * ((g // 4) % 2)
-    flip_c = lambda v: v + 1 - 2 * (v % 2)
     quads = (flip_x + flip_y - g, flip_x, flip_y, g)
-    core = {"gx": z, "gy": flip_c(g)}
+    core = {"gx": z, "gy": flip(g)}
     xn = {"gx": z, "gy": flip_x}
     yn = {"gx": z, "gy": flip_y}
     every = z >= 0
@@ -260,7 +285,7 @@
 
     def core_copy(i, q):
         it = item(i)
-        return remote(block(it, flip_c(quads[q])), from_core.at[it, q], core_send.at[i, q], core_recv.at[it, q], core)
+        return remote(block(it, flip(quads[q])), from_core.at[it, q], core_send.at[i, q], core_recv.at[it, q], core)
 
     def load(i, q):
         it = item(i)
@@ -474,32 +499,57 @@
     span,
     acts_ref,
     weight_ref,
+    cot_ref,
     seq_ref,
     full_ref,
+    all_cot_ref,
     send_sem,
     recv_sem,
     local_sem,
     chain_send,
     chain_recv,
     chain_local,
+    cot_send,
+    cot_recv,
+    cot_local,
 ):
-    chain = chain_gather(n_z, weight_ref, full_ref, chain_send, chain_recv, chain_local)
-    gather_kernel(1, span, acts_ref, seq_ref, send_sem, recv_sem, local_sem, chain)
-
-
-def enter(acts, weights, collective_id):
+    greet(n_z)
+    start, relays, end_chain = chain_gather(
+        n_z, weight_ref, full_ref, chain_send, chain_recv, chain_local
+    )
+    near, end_near = gather_steps(1, span, acts_ref, seq_ref, send_sem, recv_sem, local_sem)
+    far, end_far = gather_steps(n_z, span, cot_ref, all_cot_ref, cot_send, cot_recv, cot_local)
+    start()
+    near[0]()
+    far[0]()
+    near[1]()
+    near[2]()
+    for k, step in enumerate(far[1:]):
+        if k % 2 == 0 and k // 2 < len(relays):
+            relays[k // 2]()
+        step()
+    for relay in relays[len(far) // 2 :]:
+        relay()
+    end_chain()
+    end_near()
+    end_far()
+
+
+def enter(acts, weights, cotangent, collective_id):
     n_z = lax.axis_size("gx")
     span = lax.axis_size("gy")
     rows, cols = acts.shape
     dma = pltpu.SemaphoreType.DMA
-    seq, full = pl.pallas_call(
+    half = (2, rows // 2, cols)
+    seq, full, all_cot = pl.pallas_call(
         partial(enter_kernel, n_z, span),
         out_shape=(
-            jax.ShapeDtypeStruct((span, 2, rows // 2, cols), acts.dtype),
+            jax.ShapeDtypeStruct((span,) + half, acts.dtype),
             jax.ShapeDtypeStruct((n_z,) + weights.shape, weights.dtype),
+            jax.ShapeDtypeStruct((n_z * span,) + half, cotangent.dtype),
         ),
-        in_specs=[pl.BlockSpec(memory_space=pltpu.VMEM)] * 2,
-        out_specs=(pl.BlockSpec(memory_space=pl.ANY),) * 2,
+        in_specs=[pl.BlockSpec(memory_space=pltpu.VMEM)] * 3,
+        out_specs=(pl.BlockSpec(memory_space=pl.ANY),) * 3,
         scratch_shapes=[
             dma((24,)),
             dma((span, 2)),
@@ -507,11 +557,18 @@
             dma((2 * n_z,)),
             dma((n_z,)),
             dma,
+            dma((24 * (2 * n_z - 1),)),
+            dma((n_z * span, 2)),
+            dma,
         ],
         compiler_params=pltpu.CompilerParams(collective_id=collective_id, has_side_effects=True),
         name="enter",
-    )(acts.reshape(2, rows // 2, cols), weights)
-    return seq.reshape(span * rows, cols), full.reshape(n_z * weights.shape[0], weights.shape[1])
+    )(acts.reshape(half), weights, cotangent.reshape(half))
+    return (
+        seq.reshape(span * rows, cols),
+        full.reshape(n_z * weights.shape[0], weights.shape[1]),
+        all_cot.reshape(n_z * span * rows, cols),
+    )
 
 
 def chain_scatter(n_z, part_ref, out_ref, from_low, from_high, send_sem, low_recv, high_recv):
@@ -695,18 +752,539 @@
     return out.reshape(total // span, cols), sums
 
 
+def expert_kernel(n_z, span, own_ref, cot_ref, share_ref, gate_ref, up_ref, down_ref,
+                  all_ref, moe_part_ref, pair_ref, dots_ref, down_out,
+                  moe_buf, cot_buf, share_buf, moe_stage, pair_stage, dots_buf,
+                  gate_val, up_val, scaled, scaled_t, down_t,
+                  send_sem, recv_sem, local_sem, fetch_sem, store_sem):
+    z = lax.axis_index("gx")
+    g = lax.axis_index("gy")
+    rows = own_ref.shape[1]
+    block = 2 * rows
+    step_rows = moe_buf.shape[1]
+    steps = 2 * n_z
+    flip_x = g + 2 - 4 * ((g // 2) % 2)
+    flip_y = g + 4 - 8 * ((g // 4) % 2)
+    flip_both = flip_x + flip_y - g
+    core = {"gx": z, "gy": flip(g)}
+    x_peer = {"gx": z, "gy": flip_x}
+    y_peer = {"gx": z, "gy": flip_y}
+    above = {"gx": z + 1, "gy": g}
+    below = {"gx": z - 1, "gy": g}
+
+    order = [z]
+    candidates = []
+    for d in range(1, n_z):
+        candidates += [(z >= d, z - d), (z < n_z - d, z + d)]
+    for k in range(1, n_z):
+        rank, chosen = 0, 0
+        for ok, owner in candidates:
+            ok = ok.astype(jnp.int32)
+            rank = rank + ok
+            chosen = chosen + ok * (rank == k).astype(jnp.int32) * owner
+        order.append(chosen)
+
+    onward = [(z < n_z - 1, z > 0)]
+    for owner in order[1:]:
+        onward.append(
+            (
+                jnp.logical_and(owner < z, z < n_z - 1),
+                jnp.logical_and(owner > z, z > 0),
+            )
+        )
+    barrier_with(
+        [(z >= 0, core), (z >= 0, x_peer), (z >= 0, y_peer), (z < n_z - 1, above), (z > 0, below)]
+    )
+
+    def at(owner, gg, h):
+        return pl.ds(pl.multiple_of((owner * span + gg) * block + h * rows, rows), rows)
+
+    def copy(k, slot, owner, gg, h, peer, own=False):
+        return pltpu.make_async_remote_copy(
+            src_ref=own_ref.at[h] if own else all_ref.at[at(owner, gg, h)],
+            dst_ref=all_ref.at[at(owner, gg, h)],
+            send_sem=send_sem.at[k, slot],
+            recv_sem=recv_sem.at[owner * span + gg, h],
+            device_id=peer,
+            device_id_type=pl.DeviceIdType.MESH,
+        )
+
+    sends = []
+
+    def send(ok, *where, **options):
+        k = where[0]
+        slot = sum(1 for entry in sends if entry[2] == k)
+        make = partial(copy, k, slot, *where[1:], **options)
+        sends.append((ok, make, k))
+        run_if(ok, lambda: make().start())
+
+    def arrive(owner, gg, h):
+        copy(0, 0, owner, gg, h, core).wait_recv()
+
+    locals_ = [
+        pltpu.make_async_copy(own_ref.at[h], all_ref.at[at(z, g, h)], local_sem.at[h])
+        for h in range(2)
+    ]
+
+    def first(k):
+        owner = order[k]
+        own = k == 0
+        if own:
+            for item in locals_:
+                item.start()
+        else:
+            arrive(owner, g, 0)
+            arrive(owner, g, 1)
+        go_up, go_down = onward[k]
+        for h in range(2):
+            send(go_up, k, owner, g, h, above, own=own)
+            send(go_down, k, owner, g, h, below, own=own)
+        send(True, k, owner, g, 0, x_peer, own=own)
+        send(True, k, owner, g, 1, y_peer, own=own)
+        send(True, k, owner, g, 1, x_peer, own=own)
+        send(True, k, owner, g, 0, y_peer, own=own)
+        send(True, k, owner, g, 0, core, own=own)
+        send(True, k, owner, g, 1, core, own=own)
+
+    def second(k):
+        owner = order[k]
+        arrive(owner, flip_x, 0)
+        send(True, k, owner, flip_x, 0, y_peer)
+        send(True, k, owner, flip_x, 0, core)
+        arrive(owner, flip_y, 1)
+        send(True, k, owner, flip_y, 1, x_peer)
+        send(True, k, owner, flip_y, 1, core)
+
+    def third(k):
+        owner = order[k]
+        for gg, h in ((flip_y, 0), (flip_x, 1), (flip_both, 0), (flip_both, 1)):
+            arrive(owner, gg, h)
+            send(True, k, owner, gg, h, core)
+
+    def complete(k):
+        for gg in (g, flip_x, flip_y, flip_both):
+            for h in range(2):
+                arrive(order[k], flip(gg), h)
+        if k == 0:
+            for item in locals_:
+                item.wait()
+
+    def place(s):
+        k, side = (s // 2, s % 2) if isinstance(s, int) else (lax.div(s, 2), lax.rem(s, 2))
+        if isinstance(s, int):
+            owner = order[k]
+        else:
+            owner = sum((k == j).astype(jnp.int32) * order[j] for j in range(n_z))
+        return pl.ds(pl.multiple_of(owner * (span * block) + side * step_rows, step_rows), step_rows)
+
+    def parity(s):
+        return s % 2 if isinstance(s, int) else lax.rem(s, 2)
+
+    def fetches(s):
+        slot = parity(s)
+        return [
+            pltpu.make_async_copy(source.at[place(s)], target.at[slot], fetch_sem.at[j, slot])
+            for j, (source, target) in enumerate(
+                ((all_ref, moe_buf), (cot_ref, cot_buf), (share_ref, share_buf))
+            )
+        ]
+
+    def stores(s, chosen=(0, 1, 2)):
+        slot = parity(s)
+        pairs = ((moe_stage, moe_part_ref), (dots_buf, dots_ref), (pair_stage, pair_ref))
+        return [
+            pltpu.make_async_copy(
+                pairs[j][0].at[slot], pairs[j][1].at[place(s)], store_sem.at[j, slot]
+            )
+            for j in chosen
+        ]
+
+    f32 = jnp.float32
+    dot = partial(lax.dot_general, preferred_element_type=f32)
+    plain = (((1,), (0,)), ((), ()))
+    last_dims = (((1,), (1,)), ((), ()))
+    first_dims = (((0,), (0,)), ((), ()))
+    half_width = scaled.shape[1]
+    width = moe_buf.shape[2]
+    tile = 256
+
+    def events(s, phase):
+        for k in range(1, n_z):
+            if k >= 2 and phase == 1:
+                pl.when(s == k - 2)(partial(first, k))
+            if phase == 2:
+                pl.when(s == 2 * (k - 1))(partial(second, k))
+            if phase == 2:
+                pl.when(s == 2 * (k - 1) + 1)(partial(third, k))
+            if phase == 4:
+                pl.when(s == 2 * k - 1)(partial(complete, k))
+
+    first(0)
+
+    @pl.loop(0, width // tile)
+    def _(t):
+        cols = pl.ds(pl.multiple_of(t * tile, tile), tile)
+        down_t[cols, :] = down_ref[:, cols].T
+
+    second(0)
+    if n_z > 1:
+        first(1)
+    third(0)
+    complete(0)
+    for item in fetches(0):
+        item.start()
+
+    @pl.loop(0, steps)
+    def _(s):
+        slot = lax.rem(s, 2)
+        moe, cot, share = moe_buf.at[slot], cot_buf.at[slot], share_buf.at[slot]
+        for item in fetches(s):
+            item.wait()
+
+        @pl.when(s >= 2)
+        def _():
+            for item in stores(s - 2):
+                item.wait()
+
+        wide = jnp.concatenate([share[...]] * (tile // share.shape[1]), axis=1)
+
+        @pl.loop(0, half_width // tile)
+        def _(t):
+            cols = pl.ds(pl.multiple_of(t * tile, tile), tile)
+            gated = dot(moe[...], gate_ref[:, cols], plain)
+            lifted = dot(moe[...], up_ref[:, cols], plain)
+            gate_val[:, cols] = gated
+            up_val[:, cols] = lifted
+            scaled[:, cols] = (gated * jax.nn.sigmoid(gated) * lifted * wide).astype(jnp.bfloat16)
+
+        events(s, 1)
+        scaled_t[...] = scaled[...].T
+
+        @pl.loop(0, width // (2 * tile))
+        def _(t):
+            cols = pl.ds(pl.multiple_of(t * 2 * tile, 2 * tile), 2 * tile)
+            moe_stage[slot, :, cols] = dot(scaled[...], down_ref[:, cols], plain).astype(jnp.bfloat16)
+
+        stores(s, (0,))[0].start()
+        events(s, 2)
+        dots_buf[slot] = jnp.zeros(dots_buf.shape[1:], f32)
+
+        @pl.loop(0, half_width // tile)
+        def _(t):
+            cols = pl.ds(pl.multiple_of(t * tile, tile), tile)
+            pulled = dot(cot[...], down_t[:, cols], plain)
+            gated = gate_val[:, cols]
+            lifted = up_val[:, cols]
+            sig = jax.nn.sigmoid(gated)
+            silu = gated * sig
+            product = pulled * (silu * lifted)
+            lanes = share.shape[1]
+            dots_buf[slot] = dots_buf[slot] + sum(
+                product[:, j * lanes : (j + 1) * lanes] for j in range(tile // lanes)
+            )
+            pulled = pulled * wide
+            pair_stage[slot, :, cols] = (pulled * lifted * sig * (1.0 + gated * (1.0 - sig))).astype(
+                jnp.bfloat16
+            )
+            more = pl.ds(pl.multiple_of(half_width + t * tile, tile), tile)
+            pair_stage[slot, :, more] = (pulled * silu).astype(jnp.bfloat16)
+
+        for item in stores(s, (1, 2)):
+            item.start()
+        events(s, 3)
+        events(s, 4)
+
+        @pl.when(s < steps - 1)
+        def _():
+            for item in fetches(s + 1):
+                item.start()
+
+        @pl.loop(0, width // (2 * tile))
+        def _(t):
+            cols = pl.ds(pl.multiple_of(t * 2 * tile, 2 * tile), 2 * tile)
+            grown = dot(scaled_t[...], cot[:, cols], plain)
+            down_out[:, cols] = jnp.where(s == 0, 0.0, down_out[:, cols]) + grown
+
+    for s in (steps - 2, steps - 1):
+        for item in stores(s):
+            item.wait()
+    for ok, make, k in sends:
+        run_if(ok, lambda make=make: make().wait_send())
+
+
+def run_experts(moe_in, all_cot, shares, gate_w, up_w, down_w, collective_id):
+    n_z = lax.axis_size("gx")
+    span = lax.axis_size("gy")
+    rows, width = moe_in.shape
+    half = down_w.shape[0]
+    total = n_z * span * rows
+    step = span * rows // 2
+    lanes = shares.shape[1]
+    bf16, f32 = jnp.bfloat16, jnp.float32
+    dma = pltpu.SemaphoreType.DMA
+    vmem = pl.BlockSpec(memory_space=pltpu.VMEM)
+    hbm = pl.BlockSpec(memory_space=pl.ANY)
+    return pl.pallas_call(
+        partial(expert_kernel, n_z, span),
+        out_shape=(
+            jax.ShapeDtypeStruct((total, width), bf16),
+            jax.ShapeDtypeStruct((total, width), bf16),
+            jax.ShapeDtypeStruct((total, 2 * half), bf16),
+            jax.ShapeDtypeStruct((total, lanes), f32),
+            jax.ShapeDtypeStruct((half, width), f32),
+        ),
+        in_specs=[vmem, hbm, hbm, vmem, vmem, vmem],
+        out_specs=(hbm, hbm, hbm, hbm, vmem),
+        scratch_shapes=[
+            pltpu.VMEM((2, step, width), bf16),
+            pltpu.VMEM((2, step, width), bf16),
+            pltpu.VMEM((2, step, lanes), f32),
+            pltpu.VMEM((2, step, width), bf16),
+            pltpu.VMEM((2, step, 2 * half), bf16),
+            pltpu.VMEM((2, step, lanes), f32),
+            pltpu.VMEM((step, half), f32),
+            pltpu.VMEM((step, half), f32),
+            pltpu.VMEM((step, half), bf16),
+            pltpu.VMEM((half, step), bf16),
+            pltpu.VMEM((width, half), bf16),
+            dma((n_z, 18)),
+            dma((n_z * span, 2)),
+            dma((2,)),
+            dma((3, 2)),
+            dma((3, 2)),
+        ],
+        compiler_params=pltpu.CompilerParams(
+            collective_id=collective_id, has_side_effects=True, vmem_limit_bytes=60 << 20
+        ),
+        name="experts",
+    )(moe_in.reshape(2, rows // 2, width), all_cot, shares, gate_w, up_w, down_w)
+
+
+def pull_kernel(n_i, rows, all_ref, pair_ref, gate_ref, up_ref, out_ref, gate_out, up_out,
+                held, from_core, from_a, from_b, from_z, moe_buf, pair_buf,
+                fetch_sem, core_send, a_send, b_send, z_send, core_recv, a_recv, b_recv, z_recv):
+    z = lax.axis_index("gx")
+    g = lax.axis_index("gy")
+    flip_x = g + 2 - 4 * ((g // 2) % 2)
+    flip_y = g + 4 - 8 * ((g // 4) % 2)
+    quads = (flip_x + flip_y - g, flip_x, flip_y, g)
+    core = {"gx": z, "gy": flip(g)}
+    x_peer = {"gx": z, "gy": flip_x}
+    y_peer = {"gx": z, "gy": flip_y}
+    along = [{"gx": lax.rem(z + j, n_i), "gy": g} for j in range(1, n_i)]
+    barrier_with([(z >= 0, peer) for peer in (core, x_peer, y_peer, *along)])
+    item_rows = moe_buf.shape[1]
+    width = moe_buf.shape[2]
+    half_width = gate_out.shape[1]
+    owners = [lax.rem(z + n_i - 1 - i + n_i, n_i) for i in range(n_i)]
+
+    def remote(src, dst, ssem, rsem, peer):
+        return pltpu.make_async_remote_copy(
+            src_ref=src,
+            dst_ref=dst,
+            send_sem=ssem,
+            recv_sem=rsem,
+            device_id=peer,
+            device_id_type=pl.DeviceIdType.MESH,
+        )
+
+    def fetches(i):
+        place = pl.ds(pl.multiple_of(owners[i] * item_rows, item_rows), item_rows)
+        return [
+            pltpu.make_async_copy(all_ref.at[place], moe_buf.at[i % 2], fetch_sem.at[0, i % 2]),
+            pltpu.make_async_copy(pair_ref.at[place], pair_buf.at[i % 2], fetch_sem.at[1, i % 2]),
+        ]
+
+    def core_copy(i, q):
+        return remote(
+            held.at[i, flip(quads[q])],
+            from_core.at[i, q],
+            core_send.at[i, q],
+            core_recv.at[i, q],
+            core,
+        )
+
+    a_plan = ((0, 0, 0, x_peer), (0, 1, 0, y_peer), (1, 0, 1, x_peer), (2, 1, 1, y_peer))
+
+    def a_copy(i, k):
+        q, h, slot, peer = a_plan[k]
+        return remote(
+            held.at[i, quads[q], h],
+            from_a.at[i, h, slot],
+            a_send.at[i, k],
+            a_recv.at[i, h, slot],
+            peer,
+        )
+
+    b_plan = ((2, y_peer), (1, x_peer))
+
+    def b_copy(i, h):
+        q, peer = b_plan[h]
+        return remote(
+            held.at[i, quads[q], h], from_b.at[i, h], b_send.at[i, h], b_recv.at[i, h], peer
+        )
+
+    def z_copy(i):
+        return remote(
+            held.at[i, g], from_z.at[z], z_send.at[i], z_recv.at[z], {"gx": owners[i], "gy": g}
+        )
+
+    dot = partial(lax.dot_general, preferred_element_type=jnp.float32)
+    last_dims = (((1,), (1,)), ((), ()))
+    first_dims = (((0,), (0,)), ((), ()))
+
+    def multiply(i):
+        for copy in fetches(i):
+            copy.wait()
+        pair = pair_buf.at[i % 2]
+        tile = 256
+
+        @pl.loop(0, width // tile)
+        def _(t):
+            cols = pl.ds(pl.multiple_of(t * tile, tile), tile)
+            total = dot(pair[:, :half_width], gate_ref[cols, :], last_dims)
+            total = total + dot(pair[:, half_width:], up_ref[cols, :], last_dims)
+            held[i, :, :, :, cols] = total.astype(jnp.bfloat16).reshape(held.shape[1:4] + (tile,))
+
+        for q in range(4):
+            core_copy(i, q).start()
+
+    def accumulate(i):
+        moe, pair = moe_buf.at[i % 2], pair_buf.at[i % 2]
+        tile = 256
+
+        @pl.loop(0, width // tile)
+        def _(t):
+            cols = pl.ds(pl.multiple_of(t * tile, tile), tile)
+            grown = dot(moe[:, cols], pair[...], first_dims)
+            if i == 0:
+                gate_out[cols, :] = grown[:, :half_width]
+                up_out[cols, :] = grown[:, half_width:]
+            else:
+                gate_out[cols, :] = gate_out[cols, :] + grown[:, :half_width]
+                up_out[cols, :] = up_out[cols, :] + grown[:, half_width:]
+
+        if i + 2 < n_i:
+            for copy in fetches(i + 2):
+                copy.start()
+
+    def stage_a(i):
+        for q in range(4):
+            core_copy(i, q).wait_recv()
+            for h in range(2):
+                mine = held.at[i, quads[q], h]
+                add_into(mine, (mine, from_core.at[i, q, h]), rows)
+            for k in range(4):
+                if a_plan[k][0] == q:
+                    a_copy(i, k).start()
+
+    def stage_b(i):
+        for q, h, slot in ((2, 0, 0), (1, 1, 0), (3, 0, 1), (3, 1, 1)):
+            mine, arrived = held.at[i, quads[q], h], from_a.at[i, h, slot]
+            remote(mine, arrived, a_send.at[i, 0], a_recv.at[i, h, slot], core).wait_recv()
+            add_into(mine, (mine, arrived), rows)
+            if slot == 0:
+                b_copy(i, h).start()
+
+    def stage_c(i):
+        for h in range(2):
+            b_copy(i, h).wait_recv()
+            mine = held.at[i, g, h]
+            add_into(mine, (mine, from_b.at[i, h]), rows)
+        if i < n_i - 1:
+            z_copy(i).start()
+        else:
+            for j in range(n_i - 1):
+                arrived = from_z.at[owners[j]]
+                remote(held.at[j, g], arrived, z_send.at[j], z_recv.at[owners[j]], core).wait_recv()
+            for h in range(2):
+                terms = [held.at[i, g, h]] + [from_z.at[owners[j], h] for j in range(n_i - 1)]
+                add_into(out_ref.at[h], terms, rows)
+
+    for i in range(min(2, n_i)):
+        for copy in fetches(i):
+            copy.start()
+    for t in range(n_i + 3):
+        if t < n_i:
+            multiply(t)
+        if 0 <= t - 1 < n_i:
+            stage_a(t - 1)
+        if 0 <= t - 2 < n_i:
+            stage_b(t - 2)
+        if 0 <= t - 1 < n_i:
+            accumulate(t - 1)
+        if 0 <= t - 3 < n_i:
+            stage_c(t - 3)
+    for i in range(n_i):
+        for q in range(4):
+            core_copy(i, q).wait_send()
+        for k in range(4):
+            a_copy(i, k).wait_send()
+        for h in range(2):
+            b_copy(i, h).wait_send()
+        if i < n_i - 1:
+            z_copy(i).wait_send()
+
+
+def pull_experts(all_moe, pair, gate_w, up_w, collective_id):
+    n_i = lax.axis_size("gx")
+    span = lax.axis_size("gy")
+    total, width = all_moe.shape
+    half_width = gate_w.shape[1]
+    rows = total // (n_i * span) // 2
+    half = (rows, width)
+    bf16 = jnp.bfloat16
+    dma = pltpu.SemaphoreType.DMA
+    vmem = pl.BlockSpec(memory_space=pltpu.VMEM)
+    hbm = pl.BlockSpec(memory_space=pl.ANY)
+    out, gate_part, up_part = pl.pallas_call(
+        partial(pull_kernel, n_i, rows),
+        out_shape=(
+            jax.ShapeDtypeStruct((2,) + half, jnp.float32),
+            jax.ShapeDtypeStruct((width, half_width), jnp.float32),
+            jax.ShapeDtypeStruct((width, half_width), jnp.float32),
+        ),
+        in_specs=[hbm, hbm, vmem, vmem],
+        out_specs=(vmem, vmem, vmem),
+        scratch_shapes=[
+            pltpu.VMEM((n_i, span, 2) + half, bf16),
+            pltpu.VMEM((n_i, 4, 2) + half, bf16),
+            pltpu.VMEM((n_i, 2, 2) + half, bf16),
+            pltpu.VMEM((n_i, 2) + half, bf16),
+            pltpu.VMEM((n_i, 2) + half, bf16),
+            pltpu.VMEM((2, span * 2 * rows, width), bf16),
+            pltpu.VMEM((2, span * 2 * rows, 2 * half_width), bf16),
+            dma((2, 2)),
+            dma((n_i, 4)),
+            dma((n_i, 4)),
+            dma((n_i, 2)),
+            dma((n_i,)),
+            dma((n_i, 4)),
+            dma((n_i, 2, 2)),
+            dma((n_i, 2)),
+            dma((n_i,)),
+        ],
+        compiler_params=pltpu.CompilerParams(
+            collective_id=collective_id, has_side_effects=True, vmem_limit_bytes=67043328
+        ),
+        name="pull_experts",
+    )(all_moe, pair, gate_w, up_w)
+    return out.reshape(2 * rows, width), gate_part, up_part
+
+
 def gather_plane(block, collective_id):
     if lax.axis_size("gy") == 8:
         return all_gather(block, False, collective_id)
     return lax.all_gather(block, "gy", axis=0, tiled=True)
 
 
-def gather_inputs(acts, weights):
+def gather_inputs(acts, weights, cotangent):
     if lax.axis_size("gy") == 8:
-        return enter(acts, weights, 6)
+        return enter(acts, weights, cotangent, 6)
     return (
         lax.all_gather(acts, "gy", axis=0, tiled=True),
         lax.all_gather(weights, "gx", axis=0, tiled=True),
+        None,
     )
 
 
@@ -858,48 +1436,31 @@
 
 
 def dense_experts(
-    moe_in, cotangent, expert_ids, gate_share, router_weight, gate_weight, up_weight, down_weight
+    moe_in, all_cot, expert_ids, gate_share, gate_weight, up_weight, down_weight
 ):
-    experts = router_weight.shape[1]
     everyone = ("gx", "gy")
-    all_cot = lax.all_gather(cotangent, everyone, axis=0, tiled=True)
+    devices = lax.axis_size("gx") * lax.axis_size("gy")
+    experts = devices // 2
     matches = expert_ids[:, :, None] == jnp.arange(experts, dtype=jnp.int32)[None, None, :]
     dense_gates = jnp.sum(jnp.where(matches, gate_share[:, :, None], 0.0), axis=1)
     own_gate = lax.all_to_all(
         jnp.repeat(dense_gates.T, 2, axis=0), everyone, split_axis=0, concat_axis=0, tiled=True
     ).reshape(-1)
-    all_moe = all_gather(moe_in, True, 2)
-    gate_in = gate_weight[0]
-    up_in = up_weight[0]
-    down_in = down_weight[0]
-    gate_val = jnp.dot(all_moe, gate_in, preferred_element_type=jnp.float32)
-    up_val = jnp.dot(all_moe, up_in, preferred_element_type=jnp.float32)
-    sigmoid_gate = jax.nn.sigmoid(gate_val)
-    silu_gate = gate_val * sigmoid_gate
-    hidden = (silu_gate * up_val).astype(jnp.bfloat16)
-    piece = jnp.dot(hidden, down_in, preferred_element_type=jnp.float32)
-    cot_float = all_cot.astype(jnp.float32)
-    gate_dots = jnp.sum(piece * cot_float, axis=-1)
-    devices = lax.axis_size("gx") * lax.axis_size("gy")
+    shares = jnp.broadcast_to(own_gate[:, None], (own_gate.shape[0], 128))
+    all_moe, moe_share, pair, gate_dots, down_part = run_experts(
+        moe_in, all_cot, shares, gate_weight[0], up_weight[0], down_weight[0], 8
+    )
+    moe_out = reduce_scatter(moe_share, True, 4)
     dots_back = lax.all_to_all(
-        gate_dots.reshape(devices, -1), everyone, split_axis=0, concat_axis=0, tiled=True
+        jnp.sum(gate_dots, axis=-1).reshape(devices, -1),
+        everyone,
+        split_axis=0,
+        concat_axis=0,
+        tiled=True,
     )
     dots_experts = dots_back.reshape(experts, 2, -1).sum(axis=1).T
     grad_gates = jnp.sum(jnp.where(matches, dots_experts[:, None, :], 0.0), axis=-1)
-    moe_out = lax.psum_scatter(
-        (piece * own_gate[:, None]).astype(jnp.bfloat16), everyone, scatter_dimension=0, tiled=True
-    ).astype(jnp.float32)
-    grad_use = (cot_float * own_gate[:, None]).astype(jnp.bfloat16)
-    grad_hidden = contract_cols(grad_use, down_in)
-    down_part = contract_rows(hidden, grad_use)
-    grad_gate = (
-        grad_hidden * up_val * sigmoid_gate * (1.0 + gate_val * (1.0 - sigmoid_gate))
-    ).astype(jnp.bfloat16)
-    grad_up = (grad_hidden * silu_gate).astype(jnp.bfloat16)
-    gate_part = contract_rows(all_moe, grad_gate)
-    up_part = contract_rows(all_moe, grad_up)
-    grad_in = contract_cols(grad_gate, gate_in) + contract_cols(grad_up, up_in)
-    grad_moe_in = reduce_scatter(grad_in.astype(jnp.bfloat16), True, 4)
+    grad_moe_in, gate_part, up_part = pull_experts(all_moe, pair, gate_weight[0], up_weight[0], 9)
     return moe_out, grad_gates, grad_moe_in, gate_part, up_part, down_part
 
 
@@ -926,10 +1487,9 @@
     acts_float, norm_pull = jax.vjp(norm_rows, inputs, attn_gain)
     acts_low = acts_float.astype(jnp.bfloat16)
     in_weights = jnp.concatenate([query_weight, key_weight, value_weight], axis=1)
-    seq_acts, full_in = gather_inputs(acts_low, in_weights)
+    seq_acts, full_in, all_cot = gather_inputs(acts_low, in_weights, cotangent)
     seq_acts, full_in, out_weight = lax.optimization_barrier((seq_acts, full_in, out_weight))
     out_rows = lax.all_gather(out_weight, "gx", axis=1, tiled=True)
-    out_rows, later_cot = lax.optimization_barrier((out_rows, cotangent))
     length = seq_acts.shape[0]
     local_width = query_weight.shape[1]
     local_heads = local_width // HD
@@ -990,17 +1550,21 @@
     moe_in = moe_float.astype(jnp.bfloat16)
     logits = jnp.dot(moe_in, router_weight, preferred_element_type=jnp.float32)
     gate_share, gate_pull = jax.vjp(partial(route_gates, expert_ids), logits)
-    experts_pass = dense_experts if lax.axis_size("gy") == 8 and router_weight.shape[1] <= 2 * TOP else routed_experts
-    moe_out, grad_gates, grad_moe_in, gate_part, up_part, down_part = experts_pass(
-        moe_in,
-        later_cot,
-        expert_ids,
-        gate_share,
-        router_weight,
-        gate_weight,
-        up_weight,
-        down_weight,
-    )
+    if all_cot is not None and router_weight.shape[1] <= 2 * TOP:
+        moe_out, grad_gates, grad_moe_in, gate_part, up_part, down_part = dense_experts(
+            moe_in, all_cot, expert_ids, gate_share, gate_weight, up_weight, down_weight
+        )
+    else:
+        moe_out, grad_gates, grad_moe_in, gate_part, up_part, down_part = routed_experts(
+            moe_in,
+            cotangent,
+            expert_ids,
+            gate_share,
+            router_weight,
+            gate_weight,
+            up_weight,
+            down_weight,
+        )
     output = (residual + moe_out).astype(jnp.bfloat16)
     grad_out = cotangent.astype(jnp.float32)
     (grad_logits,) = gate_pull(grad_gates)

time: 883 us -> 784 us (0.89)
  matrix products: 207 us -> 61 us
  Pallas kernels: 466 us -> 567 us
  waiting for transfers between devices: 40.8 us -> 20.7 us
  other arithmetic: 64.7 us -> 52.2 us
  local copies, waits for them, and re-layouts: 60.7 us -> 49.4 us
  starting transfers between devices: 17.3 us -> 6.97 us
    pallas_call x0 -> x2, Pallas kernels: none -> 233 us  [the longest x1 123 us: run_experts(): pl.pallas_call(partial(expert_kernel, n_z, span), out_shape=(jax.ShapeDty...]
    pallas_call x2 -> x1, Pallas kernels: 168 us -> 22.8 us  [all_gather(): pl.pallas_call(partial(gather_kernel, n_z, span), out_shape=jax.ShapeDtyp...]
    dot_general x6 -> x3, matrix products: 70.7 us -> 11.3 us  [contract_cols(): lax.dot_general(left_side, right_side, (((1,), (1,)), ((), ())), preferre...]
    dot_general x3 -> x0, matrix products: 57.3 us -> none  [the longest x1 22 us: dense_experts(): piece = jnp.dot(hidden, down_in, preferred_element_type=jnp.float32)]
    pallas_call x1, Pallas kernels: 60.2 us -> 115 us  [enter(): pl.pallas_call(partial(enter_kernel, n_z, span), out_shape=(jax.ShapeDtyp...]
    dot_general x6 -> x3, matrix products: 51.7 us -> 11.3 us  [contract_rows(): lax.dot_general(left_side, right_side, (((0,), (0,)), ((), ())), preferre...]
    pallas_call x1, Pallas kernels: 91.3 us -> 61.8 us  [leave(): pl.pallas_call(partial(leave_kernel, pieces, rows), out_shape=(jax.ShapeD...]
    all_gather x1, waiting for transfers between devices: 26.7 us -> 0.02 us  [local(): out_rows = lax.all_gather(out_weight, 'gx', axis=1, tiled=True)]
  transfers between devices with their start and end apart: 6 -> 4, of which waited for: 3 -> 2; matrix products, arithmetic and copies ran while one was open for 26% -> 5% of each run, Pallas kernels for 34% -> 26%
where the time goes in v5:
time: 784 us; the launch traced here: 774 us
  Pallas kernels  567 us (72%)
  matrix products  61 us (8%)
  other arithmetic  52.2 us (7%)
  local copies, waits for them, and re-layouts  49.4 us (6%)
  waiting for transfers between devices  20.7 us (3%)
  between operations  16.3 us (2%)
    pallas_call x1, Pallas kernels, run_experts(): pl.pallas_call(partial(expert_kernel, n_z, span), out_shape=(jax.ShapeDty...  123 us
    pallas_call x1, Pallas kernels, enter(): pl.pallas_call(partial(enter_kernel, n_z, span), out_shape=(jax.ShapeDtyp...  115 us
    pallas_call x2, Pallas kernels, reduce_scatter(): pl.pallas_call(partial(scatter_kernel, both, n_i, rows), out_shape=jax.Sh...  114 us
    pallas_call x1, Pallas kernels, pull_experts(): pl.pallas_call(partial(pull_kernel, n_i, rows), out_shape=(jax.ShapeDtype...  110 us
    pallas_call x1, Pallas kernels, leave(): pl.pallas_call(partial(leave_kernel, pieces, rows), out_shape=(jax.ShapeD...  61.8 us
    pallas_call x1, Pallas kernels, all_gather(): pl.pallas_call(partial(gather_kernel, n_z, span), out_shape=jax.ShapeDtyp...  22.8 us
    pallas_call x1, Pallas kernels, sum_everywhere(): pl.pallas_call(partial(sum_kernel, n_z, bits), out_shape=jax.ShapeDtypeSt...  19.4 us
  transfers between devices with their start and end apart: 4, of which 2 were waited for; matrix products, arithmetic and copies ran while one was open for 5% of the time, Pallas kernels for 26%

profile of v5, /device:TPU:0, one launch (start us, length us, event | category | flops | bytes accessed | tf_op | source)
XLA Modules:
  0.0 773.7 jit_solution(5970300459526117118)
XLA Ops:
  9.5 2.0 fusion.41
  11.5 2.0 pad_maximum_fusion.1.weight_ref
  13.5 115.5 %enter.1 = (bf16[8,2,64,2048]{3,2,1,0:T(8,128)(2,1)}, bf16[4,512,768]{2,1,0:T(8,128)(2,1)}, bf16[32,2,64,2048]{3,2,1,0:T(8,128)(2,1)}) custom-call(bf16[2,64,2048]{2,1,0:T(8,128)(2,1)} %bitcast.206, bf16[512,768]{1,0:T(8,128)(2,1)} %pad_maximum_fusion.1.weight_ref, bf16[2,64,2048]{2,1,0:T(8,128)(2,1)} %bitcast.192), custom_call_target="tpu_custom_call" | custom-call | tf_op jit(solution)/shard_map/enter/pallas_call | solution.py:544
  129.1 6.2 fusion.71
  137.4 1.9 fusion.53
  142.0 1.3 copy.170
  143.7 13.1 %while.29 = (s32[]{:T(128)}, bf16[2,512,2,128]{3,2,1,0:T(2,128)(2,1)S(1)}, f32[2,2,512]{2,1,0:T(2,128)}, f32[2,2]{1,0:T(2,128)S(1)}, s32[2,512]{1,0:T(2,128)S(1)...) while((s32[]{:T(128)}, ...), condition=%wide.region_7.8_spmd, body=%wide.region_3.7_spmd.sunk | while | flops 551156736 | bytes 16821392 | solution.py:1537
  144.0 2.0 fusion.112
  146.1 1.5 fusion.113
  148.2 1.6 fusion.114
  150.6 2.0 fusion.112
  152.6 1.5 fusion.113
  154.7 1.6 fusion.114
  158.7 2.5 convolution_convert_fusion
  161.2 2.3 copy.243
  163.6 23.5 %scatter_plane.1 = f32[4,2,16,2048]{3,2,1,0:T(8,128)} custom-call(bf16[4,8,2,16,2048]{4,3,2,1,0:T(8,128)(2,1)} %bitcast.184), custom_call_target="tpu_custom_call" | custom-call | tf_op jit(solution)/shard_map/scatter_plane/pallas_call | solution.py:395
  187.1 1.4 multiply_reduce_fusion.7
  191.9 3.7 all-to-all-start
  196.2 6.6 all-to-all-done
  202.7 1.9 broadcast_in_dim.179.share_ref
  204.6 123.4 %experts.1 = (bf16[4096,2048]{1,0:T(8,128)(2,1)}, bf16[4096,2048]{1,0:T(8,128)(2,1)}, bf16[4096,1024]{1,0:T(8,128)(2,1)}, f32[4096,128]{1,0:T(8,128)}, f32[512,2048]{1,0:T(8,128)}) custom-call(bf16[2,64,2048]{2,1,0:T(8,128)(2,1)} %bitcast.191, bf16[4096,2048]{1,0:T(8,128)(2,1)} %bitcast.185, f32[4096,128]{1,0:T(8,128)} %broadcast_in_dim.179.share_ref, ...), custom_call_target="tpu_custom_call" | custom-call | tf_op jit(solution)/shard_map/experts/pallas_call | solution.py:1027
  328.0 2.8 reduce_sum.236
  330.9 3.2 all-to-all-start.1
  334.6 90.5 %scatter_all.1 = f32[2,64,2048]{2,1,0:T(8,128)} custom-call(bf16[4,8,2,64,2048]{4,3,2,1,0:T(8,128)(2,1)} %bitcast.186), custom_call_target="tpu_custom_call" | custom-call | tf_op jit(solution)/shard_map/scatter_all/pallas_call | solution.py:395
  425.1 109.7 %pull_experts.1 = (f32[2,64,2048]{2,1,0:T(8,128)}, f32[2048,512]{1,0:T(8,128)}, f32[2048,512]{1,0:T(8,128)}) custom-call(bf16[4096,2048]{1,0:T(8,128)(2,1)} %get-tuple-element.151.all_ref, bf16[4096,1024]{1,0:T(8,128)(2,1)} %get-tuple-element.152.pair_ref, bf16[2048,512]{1,0:T(8,128)(2,1)} %bitcast.188, bf16[2048,512]{1,0:T(8,128)(2,1)} %bitcast.190), custom_call_target="tpu_custom_call" | custom-call | tf_op jit(solution)/shard_map/pull_experts/pallas_call | solution.py:1240
  541.2 2.7 multiply_reduce_fusion.3
  544.6 1.9 fusion.65
  546.5 22.8 %gather_plane.1 = bf16[8,2,64,2048]{3,2,1,0:T(8,128)(2,1)} custom-call(bf16[2,64,2048]{2,1,0:T(8,128)(2,1)} %bitcast.208), custom_call_target="tpu_custom_call" | custom-call | tf_op jit(solution)/shard_map/gather_plane/pallas_call | solution.py:229
  569.4 3.6 convolution_convert_fusion.4
  573.1 27.8 %while.30 = (s32[]{:T(128)}, f32[1024,2,128]{0,2,1:T(8,128)}, f32[1024,2,128]{0,2,1:T(8,128)}, f32[2,512,2,128]{3,1,0,2:T(8,128)}, bf16[2,512,2,128]{3,1,2,0:T(8...) while((s32[]{:T(128)}, f32[1024,2,128]{0,2,1:T(8,128)}, ...), condition=%wide.region_23.24_spmd.clone, body=%wide.region_21.23_spmd.clone.sunk | while | flops 1359870976 | bytes 81305392 | solution.py:1611
  573.4 1.8 fusion.123
  576.5 1.9 multiply_reduce_fusion.13
  578.4 1.4 multiply_convert_fusion.6
  579.8 2.6 fusion.124
  582.4 1.5 fusion.126
  583.9 2.4 fusion.125
  586.3 1.8 fusion.123
  589.5 1.9 multiply_reduce_fusion.13
  591.3 1.4 multiply_convert_fusion.6
  592.7 3.0 fusion.124
  595.7 1.5 fusion.126
  597.2 3.7 fusion.125
  600.9 2.5 copy.180
  603.5 3.2 multiply_add_fusion.3
  609.1 1.7 fusion.44
  610.8 2.0 copy.179
  612.8 1.9 fusion.45
  617.3 7.7 convolution_convert_fusion.2
  625.1 5.0 convolution_convert_fusion.1
  630.1 2.4 convolution_convert_fusion.3
  632.5 4.8 copy.242
  637.4 61.8 %leave.1 = (f32[4,2,16,2048]{3,2,1,0:T(8,128)}, f32[512,768]{1,0:T(8,128)}) custom-call(bf16[4,8,2,16,2048]{4,3,2,1,0:T(8,128)(2,1)} %bitcast.183, bf16[4,512,768]{2,1,0:T(8,128)(2,1)} %bitcast.202), custom_call_target="tpu_custom_call" | custom-call | tf_op jit(solution)/shard_map/leave/pallas_call | solution.py:716
  699.2 2.2 fusion.42
  702.2 19.4 %sum_everywhere.1 = f32[2,152,128]{2,1,0:T(8,128)} custom-call(f32[2,152,128]{2,1,0:T(8,128)} %bitcast.215), custom_call_target="tpu_custom_call" | custom-call | tf_op jit(solution)/shard_map/sum_everywhere/pallas_call | solution.py:477
  721.7 2.3 slice.74
  732.3 1.3 fusion.69
  733.6 1.8 multiply_convert_fusion.2
  735.5 2.5 fusion.67
  738.1 1.7 fusion.46
  739.7 14.1 %reduce-scatter.2.cloned.1.call-done = bf16[512,256]{1,0:T(8,128)(2,1)} async-done(((bf16[2048,256]{1,0:T(8,128)(2,1)}), bf16[512,256]{1,0:T(8,128)(2,1)}) %reduce-scatter.2.cloned.1.call-update) | async-done | bytes 262160 | tf_op jit(solution)/shard_map/reduce_scatter | solution.py:1629
  755.8 4.8 copy.288
  760.7 2.1 copy.289
  762.8 1.6 copy-done.28
  764.4 2.0 copy.290
  (264 shorter events, 41.2 us)
Async XLA Ops:
  7.2 151.6 %all-gather.2.cloned.1.call-start = ((), (), s32[]{:S(2)}) async-start(), calls=%async_computation.3 | async-start | bytes 1310720 | tf_op jit(solution)/shard_map/all_gather | solution.py:1492
  135.7 3.6 copy-start.64
  135.7 4.0 copy-start.66
  136.6 3.4 copy-start.46
  137.0 3.8 copy-start.12
  137.4 3.5 copy-start.10
  140.1 3.3 copy-start.36
  156.7 6.8 copy-start.2
  156.7 6.8 copy-start.7
  156.7 6.8 copy-start.31
  156.7 6.8 copy-start.40
  163.6 23.5 %copy-start.14 = (bf16[128,2048]{1,0:T(8,128)(2,1)S(1)}, bf16[128,2048]{1,0:T(8,128)(2,1)}, u32[]{:S(2)}) copy-start(bf16[128,2048]{1,0:T(8,128)(2,1)} %param.21) | copy-start | bytes 1572868
  163.6 26.0 %copy-start.42 = (f32[2048]{0:T(1024)S(1)}, f32[2048]{0:T(1024)}, u32[]{:S(2)}) copy-start(f32[2048]{0:T(1024)} %param.27) | copy-start | bytes 24580
  163.6 26.1 %copy-start.38 = (bf16[2048,16]{0,1:T(8,128)(2,1)S(1)}, bf16[2048,16]{0,1:T(8,128)(2,1)}, u32[]{:S(2)}) copy-start(bf16[2048,16]{0,1:T(8,128)(2,1)} %param.34) | copy-start | bytes 196612
  163.6 27.0 %copy-start.53 = (s32[128,8]{0,1:T(8,128)S(1)}, s32[128,8]{0,1:T(8,128)}, u32[]{:S(2)}) copy-start(s32[128,8]{0,1:T(8,128)} %param.23) | copy-start | bytes 12292
  189.8 14.9 %copy-start.18 = (bf16[128,2048]{1,0:T(8,128)(2,1)}, bf16[128,2048]{1,0:T(8,128)(2,1)S(1)}, u32[]{:S(2)}) copy-start(bf16[128,2048]{1,0:T(8,128)(2,1)S(1)} %multiply_convert_fusion.1) | copy-start | bytes 1572868
  190.6 143.4 %copy-start.62 = (f32[128]{0:T(128)}, f32[128]{0:T(128)S(1)}, u32[]{:S(2)}) copy-start(f32[128]{0:T(128)S(1)} %fusion.57) | copy-start | bytes 1540
  190.7 137.3 %copy-start.63 = (f32[128]{0:T(128)}, f32[128]{0:T(128)S(1)}, u32[]{:S(2)}) copy-start(f32[128]{0:T(128)S(1)} %get-tuple-element.473) | copy-start | bytes 1540
  191.9 10.8 %all-to-all-start = ((f32[32,1,128]{2,1,0:T(1,128)}), f32[32,1,128]{2,1,0:T(1,128)S(1)}, u32[]{:S(2)}, u32[]{:S(2)}) async-start(f32[32,1,128]{2,1,0:T(1,128)} %bitcast.21), calls=%async_computation | async-start | bytes 32768 | tf_op jit(solution)/shard_map/all_to_all | solution.py:1446
  330.9 204.0 %all-to-all-start.1 = ((f32[32,1,128]{2,1,0:T(1,128)}), f32[32,1,128]{2,1,0:T(1,128)}, u32[]{:S(2)}, u32[]{:S(2)}) async-start(f32[32,1,128]{2,1,0:T(1,128)} %bitcast.29), calls=%async_computation.1 | async-start | bytes 32768 | tf_op jit(solution)/shard_map/all_to_all | solution.py:1454
  334.0 419.8 %reduce-scatter.2.cloned.1.call-start = ((), (), s32[]{:S(2)}) async-start(), calls=%async_computation.4 | async-start | bytes 1310720 | tf_op jit(solution)/shard_map/reduce_scatter | solution.py:1629
  534.8 9.8 %copy-start.5 = (f32[128,2048]{1,0:T(8,128)S(1)}, f32[128,2048]{1,0:T(8,128)}, u32[]{:S(2)}) copy-start(f32[128,2048]{1,0:T(8,128)} %copy-done.4) | copy-start | bytes 3145732
  534.8 9.8 %copy-start.23 = (bf16[128,2048]{1,0:T(8,128)(2,1)S(1)}, bf16[128,2048]{1,0:T(8,128)(2,1)}, u32[]{:S(2)}) copy-start(bf16[128,2048]{1,0:T(8,128)(2,1)} %param.22) | copy-start | bytes 1572868
  543.9 25.4 %copy-start.34 = (bf16[256,2048]{1,0:T(8,128)(2,1)S(1)}, bf16[256,2048]{1,0:T(8,128)(2,1)}, u32[]{:S(2)}) copy-start(bf16[256,2048]{1,0:T(8,128)(2,1)} %all-gather.2.cloned.1.call-done) | copy-start | bytes 3145732
  544.6 24.7 %copy-start.68 = (f32[128]{0:T(128)}, f32[128]{0:T(128)S(1)}, u32[]{:S(2)}) copy-start(f32[128]{0:T(128)S(1)} %multiply_multiply_fusion.5) | copy-start | bytes 1540
  569.4 3.7 copy-start.3
  569.4 3.7 copy-start.8
  569.4 3.7 copy-start.37
  569.4 3.7 copy-start.41
  573.4 5.0 copy-start.19
  579.8 4.2 copy-start.1
  586.3 5.0 copy-start.19
  592.7 4.5 copy-start.1
  597.2 3.7 copy-start.9
  597.2 3.7 copy-start.20
  603.5 3.3 copy-start.13
  603.5 3.3 copy-start.47
  603.5 3.3 copy-start.65
  603.5 4.5 copy-start.11
  603.5 4.5 copy-start.45
  603.5 4.5 copy-start.67
  617.3 7.8 %copy-start.35 = (bf16[1024,2,128]{0,2,1:T(8,128)(2,1)S(1)}, bf16[1024,2,128]{0,2,1:T(8,128)(2,1)}, u32[]{:S(2)}) copy-start(bf16[1024,2,128]{0,2,1:T(8,128)(2,1)} %copy.179) | copy-start | bytes 1572868
  617.3 7.7 %copy-start.75 = (bf16[4,512,768]{2,1,0:T(8,128)(2,1)S(1)}, bf16[4,512,768]{2,1,0:T(8,128)(2,1)}, u32[]{:S(2)}) copy-start(bf16[4,512,768]{2,1,0:T(8,128)(2,1)} %get-tuple-element.144) | copy-start | bytes 9437188
  625.1 5.1 copy-start.27
  625.1 5.1 copy-start.32
  637.3 61.9 %copy-start.15 = (bf16[128,2048]{1,0:T(8,128)(2,1)S(1)}, bf16[128,2048]{1,0:T(8,128)(2,1)}, u32[]{:S(2)}) copy-start(bf16[128,2048]{1,0:T(8,128)(2,1)} %param.21) | copy-start | bytes 1572868
  637.3 61.9 %copy-start.48 = (f32[2048]{0:T(1024)S(1)}, f32[2048]{0:T(1024)}, u32[]{:S(2)}) copy-start(f32[2048]{0:T(1024)} %param.26) | copy-start | bytes 24580
  637.3 61.9 %copy-start.60 = (f32[128]{0:T(128)S(1)}, f32[128]{0:T(128)}, u32[]{:S(2)}) copy-start(f32[128]{0:T(128)} %copy-done.59) | copy-start | bytes 1540
  637.3 64.1 %copy-start.55 = (f32[2048]{0:T(1024)S(1)}, f32[2048]{0:T(1024)}, u32[]{:S(2)}) copy-start(f32[2048]{0:T(1024)} %get-tuple-element.469) | copy-start | bytes 24580
  637.3 64.1 %copy-start.71 = (f32[128]{0:T(128)S(1)}, f32[128]{0:T(128)}, u32[]{:S(2)}) copy-start(f32[128]{0:T(128)} %get-tuple-element.465) | copy-start | bytes 1540
  637.3 64.1 %copy-start.72 = (f32[128]{0:T(128)S(1)}, f32[128]{0:T(128)}, u32[]{:S(2)}) copy-start(f32[128]{0:T(128)} %get-tuple-element.463) | copy-start | bytes 1540
  637.4 64.2 %copy-start.73 = (f32[64]{0:T(128)S(1)}, f32[64]{0:T(128)}, u32[]{:S(2)}) copy-start(f32[64]{0:T(128)} %reshape.419) | copy-start | bytes 772
  699.2 34.4 %copy-start.33 = (bf16[512,256]{1,0:T(8,128)(2,1)S(1)}, bf16[512,256]{1,0:T(8,128)(2,1)}, u32[]{:S(2)}) copy-start(bf16[512,256]{1,0:T(8,128)(2,1)} %param.31) | copy-start | bytes 786436
  701.4 36.6 %copy-start.6 = (f32[128,2048]{1,0:T(8,128)S(1)}, f32[128,2048]{1,0:T(8,128)}, u32[]{:S(2)}) copy-start(f32[128,2048]{1,0:T(8,128)} %copy-done.4) | copy-start | bytes 3145732
  701.4 36.6 %copy-start.17 = (f32[128,2048]{1,0:T(8,128)S(1)}, f32[128,2048]{1,0:T(8,128)}, u32[]{:S(2)}) copy-start(f32[128,2048]{1,0:T(8,128)} %copy-done.16) | copy-start | bytes 3145732
  701.4 36.6 %copy-start.24 = (bf16[128,2048]{1,0:T(8,128)(2,1)S(1)}, bf16[128,2048]{1,0:T(8,128)(2,1)}, u32[]{:S(2)}) copy-start(bf16[128,2048]{1,0:T(8,128)(2,1)} %param.22) | copy-start | bytes 1572868
  701.4 36.6 %copy-start.43 = (f32[2048]{0:T(1024)S(1)}, f32[2048]{0:T(1024)}, u32[]{:S(2)}) copy-start(f32[2048]{0:T(1024)} %param.27) | copy-start | bytes 24580
  729.5 8.6 %copy-start.25 = (f32[2,64,2048]{2,1,0:T(8,128)S(1)}, f32[2,64,2048]{2,1,0:T(8,128)}, u32[]{:S(2)}) copy-start(f32[2,64,2048]{2,1,0:T(8,128)} %scatter_all.1) | copy-start | bytes 3145732
  729.5 8.6 %copy-start.26 = (f32[4,2,16,2048]{3,2,1,0:T(8,128)S(1)}, f32[4,2,16,2048]{3,2,1,0:T(8,128)}, u32[]{:S(2)}) copy-start(f32[4,2,16,2048]{3,2,1,0:T(8,128)} %get-tuple-element.159) | copy-start | bytes 3145732
  729.5 8.6 %copy-start.58 = (f32[128]{0:T(128)S(1)}, f32[128]{0:T(128)}, u32[]{:S(2)}) copy-start(f32[128]{0:T(128)} %copy-done.57) | copy-start | bytes 1540
  729.5 8.6 %copy-start.61 = (f32[128]{0:T(128)S(1)}, f32[128]{0:T(128)}, u32[]{:S(2)}) copy-start(f32[128]{0:T(128)} %copy-done.59) | copy-start | bytes 1540
  729.5 8.6 %copy-start.69 = (f32[128]{0:T(128)S(1)}, f32[128]{0:T(128)}, u32[]{:S(2)}) copy-start(f32[128]{0:T(128)} %copy-done.68) | copy-start | bytes 1540
  755.8 4.8 copy-start.29
  760.7 3.7 copy-start.28
  (22 other events, 37.6 us)
Sparse Core Ops, SparseCore 0:
  129.2 27.2 all-gather.1
  727.4 26.4 reduce-scatter.1

commit v6 on v5

--- a/solution.py
+++ b/solution.py
@@ -375,41 +375,38 @@
         if chain and i < n_i - 1: z_copy(i).wait_send()
 
 
-def reduce_scatter(part, both, collective_id, pieces=4, out_dtype=jnp.float32):
-    n_z = lax.axis_size("gx") if both else 1
+def scatter_plane(part, collective_id):
     span = lax.axis_size("gy")
-    total, cols = part.shape
-    n_i = n_z if both else pieces
-    if both:
-        rows = total // (n_z * span) // 2
-        shaped = part.reshape(n_z, span, 2, rows, cols)
-        out_shape = (2, rows, cols)
-    else:
-        rows = total // span // (2 * pieces)
-        shaped = part.reshape(span, pieces, 2, rows, cols).swapaxes(0, 1)
-        out_shape = (pieces, 2, rows, cols)
+    pieces, _, _, rows, cols = part.shape
     dma = pltpu.SemaphoreType.DMA
     half = (rows, cols)
-    z_items = n_i if both else 1
-    z_half = half if both else (16, 128)
     out = pl.pallas_call(
-        partial(scatter_kernel, both, n_i, rows),
-        out_shape=jax.ShapeDtypeStruct(out_shape, out_dtype),
+        partial(scatter_kernel, False, pieces, rows),
+        out_shape=jax.ShapeDtypeStruct((pieces, 2, rows, cols), jnp.float32),
         in_specs=[pl.BlockSpec(memory_space=pl.ANY)],
         out_specs=pl.BlockSpec(memory_space=pltpu.VMEM),
         scratch_shapes=[
-            pltpu.VMEM((n_i, 4, 2) + half, jnp.bfloat16),
-            pltpu.VMEM((n_i, 4, 2) + half, jnp.bfloat16),
-            pltpu.VMEM((n_i, 2, 2) + half, jnp.bfloat16),
-            pltpu.VMEM((n_i, 2) + half, jnp.bfloat16),
-            pltpu.VMEM((z_items, 2) + z_half, jnp.bfloat16),
-            dma((n_i, 4)), dma((n_i, 4)), dma((n_i, 4)), dma((n_i, 2)), dma((n_i,)),
-            dma((n_i, 4)), dma((n_i, 2, 2)), dma((n_i, 2)), dma((n_i,)),
+            pltpu.VMEM((pieces, 4, 2) + half, jnp.bfloat16),
+            pltpu.VMEM((pieces, 4, 2) + half, jnp.bfloat16),
+            pltpu.VMEM((pieces, 2, 2) + half, jnp.bfloat16),
+            pltpu.VMEM((pieces, 2) + half, jnp.bfloat16),
+            pltpu.VMEM((1, 2, 16, 128), jnp.bfloat16),
+            dma((pieces, 4)),
+            dma((pieces, 4)),
+            dma((pieces, 4)),
+            dma((pieces, 2)),
+            dma((pieces,)),
+            dma((pieces, 4)),
+            dma((pieces, 2, 2)),
+            dma((pieces, 2)),
+            dma((pieces,)),
         ],
-        compiler_params=pltpu.CompilerParams(collective_id=collective_id, has_side_effects=True, vmem_limit_bytes=60 << 20),
-        name="scatter_all" if both else "scatter_plane",
-    )(shaped)
-    return out.reshape(total // (n_z * span), cols)
+        compiler_params=pltpu.CompilerParams(
+            collective_id=collective_id, has_side_effects=True, vmem_limit_bytes=60 << 20
+        ),
+        name="scatter_plane",
+    )(part)
+    return out.reshape(pieces * 2 * rows, cols)
 
 
 def sum_kernel(n_z, bits, vec_ref, out_ref, held, arrived, from_z, send_sem, z_send, recv_sem, z_recv):
@@ -704,12 +701,11 @@
     )
 
 
-def leave(part, weight_part, collective_id, pieces=4):
+def leave(part, weight_part, collective_id):
     n_z = lax.axis_size("gx")
     span = lax.axis_size("gy")
-    total, cols = part.shape
-    rows = total // span // (2 * pieces)
-    shaped = part.reshape(span, pieces, 2, rows, cols).swapaxes(0, 1)
+    pieces, _, _, rows, cols = part.shape
+    total = span * pieces * 2 * rows
     half = (rows, cols)
     dma = pltpu.SemaphoreType.DMA
     block = (weight_part.shape[0] // n_z, weight_part.shape[1])
@@ -748,15 +744,17 @@
             collective_id=collective_id, has_side_effects=True, vmem_limit_bytes=60 << 20
         ),
         name="leave",
-    )(shaped, weight_part.reshape((n_z,) + block))
+    )(part, weight_part.reshape((n_z,) + block))
     return out.reshape(total // span, cols), sums
 
 
 def expert_kernel(n_z, span, own_ref, cot_ref, share_ref, gate_ref, up_ref, down_ref,
-                  all_ref, moe_part_ref, pair_ref, dots_ref, down_out,
-                  moe_buf, cot_buf, share_buf, moe_stage, pair_stage, dots_buf,
+                  all_ref, pair_ref, dots_ref, down_out, out_ref,
+                  moe_buf, cot_buf, share_buf, pair_stage, dots_buf,
                   gate_val, up_val, scaled, scaled_t, down_t,
-                  send_sem, recv_sem, local_sem, fetch_sem, store_sem):
+                  held, from_core, from_a, from_b, from_z,
+                  send_sem, recv_sem, local_sem, fetch_sem, store_sem,
+                  core_send, a_send, b_send, z_send, core_recv, a_recv, b_recv, z_recv):
     z = lax.axis_index("gx")
     g = lax.axis_index("gy")
     rows = own_ref.shape[1]
@@ -792,9 +790,8 @@
                 jnp.logical_and(owner > z, z > 0),
             )
         )
-    barrier_with(
-        [(z >= 0, core), (z >= 0, x_peer), (z >= 0, y_peer), (z < n_z - 1, above), (z > 0, below)]
-    )
+    along = [{"gx": lax.rem(z + j, n_z), "gy": g} for j in range(1, n_z)]
+    barrier_with([(z >= 0, peer) for peer in (core, x_peer, y_peer, *along)])
 
     def at(owner, gg, h):
         return pl.ds(pl.multiple_of((owner * span + gg) * block + h * rows, rows), rows)
@@ -889,14 +886,14 @@
             )
         ]
 
-    def stores(s, chosen=(0, 1, 2)):
+    def stores(s):
         slot = parity(s)
-        pairs = ((moe_stage, moe_part_ref), (dots_buf, dots_ref), (pair_stage, pair_ref))
+        pairs = ((dots_buf, dots_ref), (pair_stage, pair_ref))
         return [
             pltpu.make_async_copy(
                 pairs[j][0].at[slot], pairs[j][1].at[place(s)], store_sem.at[j, slot]
             )
-            for j in chosen
+            for j in range(2)
         ]
 
     f32 = jnp.float32
@@ -908,7 +905,94 @@
     width = moe_buf.shape[2]
     tile = 256
 
+    quads = (flip_both, flip_x, flip_y, g)
+
+    def remote(src, dst, ssem, rsem, peer):
+        return pltpu.make_async_remote_copy(
+            src_ref=src,
+            dst_ref=dst,
+            send_sem=ssem,
+            recv_sem=rsem,
+            device_id=peer,
+            device_id_type=pl.DeviceIdType.MESH,
+        )
+
+    def core_copy(k, q):
+        return remote(
+            held.at[k, flip(quads[q])],
+            from_core.at[k, q],
+            core_send.at[k, q],
+            core_recv.at[k, q],
+            core,
+        )
+
+    a_plan = ((0, 0, 0, x_peer), (0, 1, 0, y_peer), (1, 0, 1, x_peer), (2, 1, 1, y_peer))
+
+    def a_copy(k, j):
+        q, h, slot, peer = a_plan[j]
+        return remote(
+            held.at[k, quads[q], h],
+            from_a.at[k, h, slot],
+            a_send.at[k, j],
+            a_recv.at[k, h, slot],
+            peer,
+        )
+
+    b_plan = ((2, y_peer), (1, x_peer))
+
+    def b_copy(k, h):
+        q, peer = b_plan[h]
+        return remote(
+            held.at[k, quads[q], h], from_b.at[k, h], b_send.at[k, h], b_recv.at[k, h], peer
+        )
+
+    def z_copy(k):
+        return remote(
+            held.at[k, g], from_z.at[z], z_send.at[k], z_recv.at[z], {"gx": order[k], "gy": g}
+        )
+
+    def stage_core(k):
+        for q in range(4):
+            core_copy(k, q).start()
+
+    def stage_a(k):
+        for q in range(4):
+            core_copy(k, q).wait_recv()
+            for h in range(2):
+                mine = held.at[k, quads[q], h]
+                add_into(mine, (mine, from_core.at[k, q, h]), rows)
+            for j in range(4):
+                if a_plan[j][0] == q:
+                    a_copy(k, j).start()
+
+    def stage_b(k):
+        for q, h, slot in ((2, 0, 0), (1, 1, 0), (3, 0, 1), (3, 1, 1)):
+            mine, arrived = held.at[k, quads[q], h], from_a.at[k, h, slot]
+            remote(mine, arrived, a_send.at[k, 0], a_recv.at[k, h, slot], core).wait_recv()
+            add_into(mine, (mine, arrived), rows)
+            if slot == 0:
+                b_copy(k, h).start()
+
+    def stage_c(k):
+        for h in range(2):
+            b_copy(k, h).wait_recv()
+            mine = held.at[k, g, h]
+            add_into(mine, (mine, from_b.at[k, h]), rows)
+        if k > 0:
+            z_copy(k).start()
+
+    backs = (
+        (stage_core, lambda k: 2 * k + 1, 2),
+        (stage_a, lambda k: 2 * k + 2, 2),
+        (stage_b, lambda k: 2 * k + 3, 2),
+        (stage_c, lambda k: 2 * k + 4, 1),
+    )
+
     def events(s, phase):
+        for action, start, when in backs:
+            for k in range(n_z):
+                if when == phase and start(k) < steps:
+                    pl.when(s == start(k))(partial(action, k))
         for k in range(1, n_z):
             if k >= 2 and phase == 1:
                 pl.when(s == k - 2)(partial(first, k))
@@ -963,9 +1047,11 @@
         @pl.loop(0, width // (2 * tile))
         def _(t):
             cols = pl.ds(pl.multiple_of(t * 2 * tile, 2 * tile), 2 * tile)
-            moe_stage[slot, :, cols] = dot(scaled[...], down_ref[:, cols], plain).astype(jnp.bfloat16)
-
-        stores(s, (0,))[0].start()
+            sent = dot(scaled[...], down_ref[:, cols], plain).astype(jnp.bfloat16)
+            held[lax.div(s, 2), pl.ds(slot * (span // 2), span // 2), :, :, cols] = sent.reshape(
+                (span // 2, 2, rows, 2 * tile)
+            )
+
         events(s, 2)
         dots_buf[slot] = jnp.zeros(dots_buf.shape[1:], f32)
 
@@ -989,7 +1075,7 @@
             more = pl.ds(pl.multiple_of(half_width + t * tile, tile), tile)
             pair_stage[slot, :, more] = (pulled * silu).astype(jnp.bfloat16)
 
-        for item in stores(s, (1, 2)):
+        for item in stores(s):
             item.start()
         events(s, 3)
         events(s, 4)
@@ -1005,9 +1091,29 @@
             grown = dot(scaled_t[...], cot[:, cols], plain)
             down_out[:, cols] = jnp.where(s == 0, 0.0, down_out[:, cols]) + grown
 
+    for t in range(steps, 2 * steps):
+        for action, start, _ in backs[::-1]:
+            for k in range(n_z):
+                if start(k) == t:
+                    action(k)
     for s in (steps - 2, steps - 1):
         for item in stores(s):
             item.wait()
+    for k in range(1, n_z):
+        arrived = from_z.at[order[k]]
+        remote(held.at[k, g], arrived, z_send.at[k], z_recv.at[order[k]], core).wait_recv()
+    for h in range(2):
+        terms = [held.at[0, g, h]] + [from_z.at[order[k], h] for k in range(1, n_z)]
+        add_into(out_ref.at[h], terms, rows)
+    for k in range(n_z):
+        for q in range(4):
+            core_copy(k, q).wait_send()
+        for j in range(4):
+            a_copy(k, j).wait_send()
+        for h in range(2):
+            b_copy(k, h).wait_send()
+        if k > 0:
+            z_copy(k).wait_send()
     for ok, make, k in sends:
         run_if(ok, lambda make=make: make().wait_send())
 
@@ -1028,18 +1134,17 @@
         partial(expert_kernel, n_z, span),
         out_shape=(
             jax.ShapeDtypeStruct((total, width), bf16),
-            jax.ShapeDtypeStruct((total, width), bf16),
             jax.ShapeDtypeStruct((total, 2 * half), bf16),
             jax.ShapeDtypeStruct((total, lanes), f32),
             jax.ShapeDtypeStruct((half, width), f32),
+            jax.ShapeDtypeStruct((2, rows // 2, width), f32),
         ),
         in_specs=[vmem, hbm, hbm, vmem, vmem, vmem],
-        out_specs=(hbm, hbm, hbm, hbm, vmem),
+        out_specs=(hbm, hbm, hbm, vmem, vmem),
         scratch_shapes=[
             pltpu.VMEM((2, step, width), bf16),
             pltpu.VMEM((2, step, width), bf16),
             pltpu.VMEM((2, step, lanes), f32),
-            pltpu.VMEM((2, step, width), bf16),
             pltpu.VMEM((2, step, 2 * half), bf16),
             pltpu.VMEM((2, step, lanes), f32),
             pltpu.VMEM((step, half), f32),
@@ -1047,14 +1152,27 @@
             pltpu.VMEM((step, half), bf16),
             pltpu.VMEM((half, step), bf16),
             pltpu.VMEM((width, half), bf16),
+            pltpu.VMEM((n_z, span, 2, rows // 2, width), bf16),
+            pltpu.VMEM((n_z, 4, 2, rows // 2, width), bf16),
+            pltpu.VMEM((n_z, 2, 2, rows // 2, width), bf16),
+            pltpu.VMEM((n_z, 2, rows // 2, width), bf16),
+            pltpu.VMEM((n_z, 2, rows // 2, width), bf16),
             dma((n_z, 18)),
             dma((n_z * span, 2)),
             dma((2,)),
             dma((3, 2)),
-            dma((3, 2)),
+            dma((2, 2)),
+            dma((n_z, 4)),
+            dma((n_z, 4)),
+            dma((n_z, 2)),
+            dma((n_z,)),
+            dma((n_z, 4)),
+            dma((n_z, 2, 2)),
+            dma((n_z, 2)),
+            dma((n_z,)),
         ],
         compiler_params=pltpu.CompilerParams(
-            collective_id=collective_id, has_side_effects=True, vmem_limit_bytes=60 << 20
+            collective_id=collective_id, has_side_effects=True, vmem_limit_bytes=67043328
         ),
         name="experts",
     )(moe_in.reshape(2, rows // 2, width), all_cot, shares, gate_w, up_w, down_w)
@@ -1272,35 +1390,286 @@
     return out.reshape(2 * rows, width), gate_part, up_part
 
 
-def gather_plane(block, collective_id):
-    if lax.axis_size("gy") == 8:
-        return all_gather(block, False, collective_id)
-    return lax.all_gather(block, "gy", axis=0, tiled=True)
-
-
-def gather_inputs(acts, weights, cotangent):
-    if lax.axis_size("gy") == 8:
-        return enter(acts, weights, cotangent, 6)
-    return (
-        lax.all_gather(acts, "gy", axis=0, tiled=True),
-        lax.all_gather(weights, "gx", axis=0, tiled=True),
-        None,
-    )
-
-
-def scatter_grads(acts_part, weight_part):
-    if lax.axis_size("gy") == 8:
-        return leave(acts_part, weight_part, 7)
-    return (
-        lax.psum_scatter(acts_part, "gy", scatter_dimension=0, tiled=True).astype(jnp.float32),
-        lax.psum_scatter(weight_part, "gx", scatter_dimension=0, tiled=True).astype(jnp.float32),
-    )
-
-
-def scatter_plane(part, collective_id):
-    if lax.axis_size("gy") == 8:
-        return reduce_scatter(part, False, collective_id)
-    return lax.psum_scatter(part, "gy", scatter_dimension=0, tiled=True).astype(jnp.float32)
+def turn(values, cosine, sine):
+    return values * cosine + pltpu.roll(values, values.shape[-1] // 2, 1) * sine
+
+
+def attend_kernel(
+    heads,
+    pieces,
+    acts_ref,
+    weight_ref,
+    out_weight_ref,
+    query_gain,
+    key_gain,
+    cosine_ref,
+    sine_ref,
+    row_docs,
+    col_docs,
+    part_ref,
+    query_raw,
+    key_raw,
+    ready_ref,
+    mixed_ref,
+    totals_ref,
+    peaks_ref,
+):
+    f32, bf16 = jnp.float32, jnp.bfloat16
+    dot = partial(lax.dot_general, preferred_element_type=f32)
+    plain = (((1,), (0,)), ((), ()))
+    last_dims = (((1,), (1,)), ((), ()))
+    length = acts_ref.shape[0]
+    span = part_ref.shape[1]
+    local = heads * HD
+    block = 256
+    scale = HD ** (-0.5)
+
+    for source, raw, gain in ((0, query_raw, query_gain), (1, key_raw, key_gain)):
+        raw[...] = dot(acts_ref[...], weight_ref[:, source * local : (source + 1) * local], plain)
+        for h in range(heads):
+            cols = slice(h * HD, (h + 1) * HD)
+
+            @pl.loop(0, length // block)
+            def _(t):
+                at = pl.ds(pl.multiple_of(t * block, block), block)
+                value = raw[at, cols]
+                normed = value * lax.rsqrt(jnp.mean(value * value, axis=-1, keepdims=True) + EPSILON)
+                turned = turn(normed * gain[...], cosine_ref[at, :], sine_ref[at, :])
+                where = source * local + h * HD
+                ready_ref[at, where : where + HD] = turned.astype(bf16)
+
+    ready_ref[:, 2 * local :] = dot(acts_ref[...], weight_ref[:, 2 * local :], plain).astype(bf16)
+    lanes = lax.broadcasted_iota(jnp.int32, (block, HD), 1)
+    peaks_ref[...] = jnp.full(peaks_ref.shape, NEGATIVE, f32)
+
+    @pl.loop(0, length // block)
+    def _(t):
+        at = pl.ds(pl.multiple_of(t * block, block), block)
+        same = row_docs[at, :1] == col_docs[:1, :]
+        kept = jnp.zeros((block, HD), f32)
+        for h in range(heads):
+            query = ready_ref[at, h * HD : (h + 1) * HD]
+            key = ready_ref[:, local + h * HD : local + (h + 1) * HD]
+            value = ready_ref[:, 2 * local + h * HD : 2 * local + (h + 1) * HD]
+            scores = jnp.where(same, dot(query, key, last_dims) * scale, NEGATIVE)
+            highest = jnp.max(scores, axis=-1, keepdims=True)
+            weights = jnp.exp(scores - highest)
+            total = jnp.sum(weights, axis=-1, keepdims=True)
+            shares = (weights * (1.0 / total)).astype(bf16)
+            mixed_ref[at, h * HD : (h + 1) * HD] = dot(shares, value, plain).astype(bf16)
+            kept = jnp.where(lanes == h, highest + jnp.log(total), kept)
+            top = jnp.max(highest, axis=0, keepdims=True)
+            peaks_ref[h : h + 1, :] = jnp.maximum(peaks_ref[h : h + 1, :], top)
+        totals_ref[at, :] = kept
+
+    rows = part_ref.shape[3]
+
+    @pl.loop(0, out_weight_ref.shape[1] // block)
+    def _(t):
+        cols = pl.ds(pl.multiple_of(t * block, block), block)
+        sent = dot(mixed_ref[...], out_weight_ref[:, cols], plain).astype(bf16)
+        sent = sent.reshape(span, pieces, 2, rows, block)
+        for p in range(pieces):
+            part_ref[p, :, :, :, cols] = sent[:, p]
+
+
+def attend(acts, weights, out_weight, query_gain, key_gain, tables, docs, pieces=4):
+    length, width = acts.shape
+    local = weights.shape[1] // 3
+    heads = local // HD
+    span = lax.axis_size("gy")
+    rows = length // (span * pieces * 2)
+    f32, bf16 = jnp.float32, jnp.bfloat16
+    vmem = pl.BlockSpec(memory_space=pltpu.VMEM)
+    return pl.pallas_call(
+        partial(attend_kernel, heads, pieces),
+        out_shape=(
+            jax.ShapeDtypeStruct((pieces, span, 2, rows, width), bf16),
+            jax.ShapeDtypeStruct((length, local), f32),
+            jax.ShapeDtypeStruct((length, local), f32),
+            jax.ShapeDtypeStruct((length, 3 * local), bf16),
+            jax.ShapeDtypeStruct((length, local), bf16),
+            jax.ShapeDtypeStruct((length, HD), f32),
+            jax.ShapeDtypeStruct((8, HD), f32),
+        ),
+        in_specs=[vmem] * 9,
+        out_specs=(vmem,) * 7,
+        compiler_params=pltpu.CompilerParams(vmem_limit_bytes=60 << 20),
+        name="attend",
+    )(
+        acts,
+        weights,
+        out_weight,
+        query_gain.reshape(1, HD),
+        key_gain.reshape(1, HD),
+        *tables,
+        *docs,
+    )
+
+
+def attend_back_kernel(
+    heads,
+    pieces,
+    grad_ref,
+    out_weight_ref,
+    mixed_ref,
+    ready_ref,
+    query_raw,
+    key_raw,
+    totals_ref,
+    query_gain,
+    key_gain,
+    cosine_ref,
+    sine_ref,
+    row_docs,
+    col_docs,
+    acts_hbm,
+    weight_hbm,
+    part_ref,
+    weight_part,
+    out_part,
+    gain_ref,
+    acts_ref,
+    weight_ref,
+    grad_mixed,
+    grad_heads,
+    turned,
+    key_sum,
+    value_sum,
+    copy_sem,
+):
+    f32, bf16 = jnp.float32, jnp.bfloat16
+    dot = partial(lax.dot_general, preferred_element_type=f32)
+    plain = (((1,), (0,)), ((), ()))
+    last_dims = (((1,), (1,)), ((), ()))
+    first_dims = (((0,), (0,)), ((), ()))
+    length, width = grad_ref.shape
+    span = part_ref.shape[1]
+    rows = part_ref.shape[3]
+    local = heads * HD
+    block = 256
+    scale = HD ** (-0.5)
+    copies = [
+        pltpu.make_async_copy(acts_hbm, acts_ref, copy_sem.at[0]),
+        pltpu.make_async_copy(weight_hbm, weight_ref, copy_sem.at[1]),
+    ]
+    for copy in copies:
+        copy.start()
+    grad_mixed[...] = dot(grad_ref[...], out_weight_ref[...], last_dims).astype(bf16)
+
+    @pl.loop(0, width // block)
+    def _(t):
+        cols = pl.ds(pl.multiple_of(t * block, block), block)
+        out_part[cols, :] = dot(grad_ref[:, cols], mixed_ref[...], first_dims).astype(bf16)
+
+    gain_ref[...] = jnp.zeros_like(gain_ref)
+    for h in range(heads):
+        cols = slice(h * HD, (h + 1) * HD)
+        key = ready_ref[:, local + h * HD : local + (h + 1) * HD]
+        value = ready_ref[:, 2 * local + h * HD : 2 * local + (h + 1) * HD]
+        key_sum[...] = jnp.zeros_like(key_sum)
+        value_sum[...] = jnp.zeros_like(value_sum)
+
+        @pl.loop(0, length // block)
+        def _(t):
+            at = pl.ds(pl.multiple_of(t * block, block), block)
+            same = row_docs[at, :1] == col_docs[:1, :]
+            query = ready_ref[at, cols]
+            grad = grad_mixed[at, cols]
+            scores = jnp.where(same, dot(query, key, last_dims) * scale, NEGATIVE)
+            weights = jnp.exp(scores - totals_ref[at, h : h + 1])
+            value_sum[...] += dot(weights.astype(bf16), grad, first_dims)
+            pulled = dot(grad, value, last_dims)
+            inner = jnp.sum(weights * pulled, axis=-1, keepdims=True)
+            grad_scores = (weights * (pulled - inner)).astype(bf16)
+            turned[at, :] = dot(grad_scores, key, plain) * scale
+            key_sum[...] += dot(grad_scores, query, first_dims)
+
+        for source, raw, gain, incoming, factor in (
+            (0, query_raw, query_gain, turned, 1.0),
+            (1, key_raw, key_gain, key_sum, scale),
+        ):
+
+            @pl.loop(0, length // block)
+            def _(t):
+                at = pl.ds(pl.multiple_of(t * block, block), block)
+                back = turn(incoming[at, :] * factor, cosine_ref[at, :], -sine_ref[at, :])
+                item = raw[at, cols]
+                inverse = lax.rsqrt(jnp.mean(item * item, axis=-1, keepdims=True) + EPSILON)
+                normed = item * inverse
+                gain_ref[source : source + 1, :] += jnp.sum(back * normed, axis=0, keepdims=True)
+                inner = back * gain[...]
+                pulled = inverse * (
+                    inner - normed * jnp.mean(inner * normed, axis=-1, keepdims=True)
+                )
+                where = source * local + h * HD
+                grad_heads[at, where : where + HD] = pulled.astype(bf16)
+
+        where = 2 * local + h * HD
+        grad_heads[:, where : where + HD] = value_sum[...].astype(bf16)
+
+    for copy in copies:
+        copy.wait()
+
+    @pl.loop(0, width // block)
+    def _(t):
+        cols = pl.ds(pl.multiple_of(t * block, block), block)
+        weight_part[cols, :] = dot(acts_ref[:, cols], grad_heads[...], first_dims).astype(bf16)
+        sent = dot(grad_heads[...], weight_ref[cols, :], last_dims).astype(bf16)
+        sent = sent.reshape(span, pieces, 2, rows, block)
+        for p in range(pieces):
+            part_ref[p, :, :, :, cols] = sent[:, p]
+
+
+def attend_back(
+    seq_grad, out_weight, saved, query_gain, key_gain, tables, docs, acts, weights, pieces=4
+):
+    query_raw, key_raw, ready, mixed, totals = saved
+    length, width = seq_grad.shape
+    local = query_raw.shape[1]
+    heads = local // HD
+    span = lax.axis_size("gy")
+    rows = length // (span * pieces * 2)
+    f32, bf16 = jnp.float32, jnp.bfloat16
+    vmem = pl.BlockSpec(memory_space=pltpu.VMEM)
+    hbm = pl.BlockSpec(memory_space=pl.ANY)
+    return pl.pallas_call(
+        partial(attend_back_kernel, heads, pieces),
+        out_shape=(
+            jax.ShapeDtypeStruct((pieces, span, 2, rows, width), bf16),
+            jax.ShapeDtypeStruct((width, 3 * local), bf16),
+            jax.ShapeDtypeStruct((width, local), bf16),
+            jax.ShapeDtypeStruct((8, HD), f32),
+        ),
+        in_specs=[vmem] * 13 + [hbm] * 2,
+        out_specs=(vmem,) * 4,
+        scratch_shapes=[
+            pltpu.VMEM((length, width), bf16),
+            pltpu.VMEM((width, 3 * local), bf16),
+            pltpu.VMEM((length, local), bf16),
+            pltpu.VMEM((length, 3 * local), bf16),
+            pltpu.VMEM((length, HD), f32),
+            pltpu.VMEM((length, HD), f32),
+            pltpu.VMEM((length, HD), f32),
+            pltpu.SemaphoreType.DMA((2,)),
+        ],
+        compiler_params=pltpu.CompilerParams(vmem_limit_bytes=60 << 20),
+        name="attend_back",
+    )(
+        seq_grad,
+        out_weight,
+        mixed,
+        ready,
+        query_raw,
+        key_raw,
+        totals,
+        query_gain.reshape(1, HD),
+        key_gain.reshape(1, HD),
+        *tables,
+        *docs,
+        acts,
+        weights,
+    )
 
 
 def norm_rows(values, gain_row):
@@ -1447,10 +1816,10 @@
         jnp.repeat(dense_gates.T, 2, axis=0), everyone, split_axis=0, concat_axis=0, tiled=True
     ).reshape(-1)
     shares = jnp.broadcast_to(own_gate[:, None], (own_gate.shape[0], 128))
-    all_moe, moe_share, pair, gate_dots, down_part = run_experts(
+    all_moe, pair, gate_dots, down_part, moe_out = run_experts(
         moe_in, all_cot, shares, gate_weight[0], up_weight[0], down_weight[0], 8
     )
-    moe_out = reduce_scatter(moe_share, True, 4)
+    moe_out = moe_out.reshape(moe_in.shape)
     dots_back = lax.all_to_all(
         jnp.sum(gate_dots, axis=-1).reshape(devices, -1),
         everyone,
@@ -1462,6 +1831,157 @@
     grad_gates = jnp.sum(jnp.where(matches, dots_experts[:, None, :], 0.0), axis=-1)
     grad_moe_in, gate_part, up_part = pull_experts(all_moe, pair, gate_weight[0], up_weight[0], 9)
     return moe_out, grad_gates, grad_moe_in, gate_part, up_part, down_part
+
+
+def plain_attention(
+    seq_acts, full_in, out_rows, query_gain, key_gain, doc_ids
+):
+    local_width = full_in.shape[1] // 3
+    length = seq_acts.shape[0]
+    local_heads = local_width // HD
+    projected = jnp.dot(seq_acts, full_in, preferred_element_type=jnp.float32)
+    queries = projected[:, :local_width]
+    key_raw = projected[:, local_width : 2 * local_width]
+    value_ready = (
+        projected[:, 2 * local_width :].astype(jnp.bfloat16).reshape(length, local_heads, HD)
+    )
+    query_float, query_pull = jax.vjp(
+        prepare_heads, queries.reshape(length, local_heads, HD), query_gain
+    )
+    key_float, key_pull = jax.vjp(prepare_heads, key_raw.reshape(length, local_heads, HD), key_gain)
+    query_ready = query_float.astype(jnp.bfloat16)
+    key_ready = key_float.astype(jnp.bfloat16)
+    block_rows = min(512, length)
+    block_count = length // block_rows
+    score_scale = HD ** (-0.5)
+    query_blocks = query_ready.reshape(block_count, block_rows, local_heads, HD)
+    doc_blocks = doc_ids.reshape(block_count, block_rows)
+
+    def block_scores(query_block, doc_block):
+        scores = (
+            jnp.einsum("qhd,khd->hqk", query_block, key_ready, preferred_element_type=jnp.float32)
+            * score_scale
+        )
+        same_doc = doc_block[:, None] == doc_ids[None, :]
+        return jnp.where(same_doc[None], scores, NEGATIVE)
+
+    def forward_block(pieces):
+        scores = block_scores(pieces[0], pieces[1])
+        highest = jnp.max(scores, axis=-1, keepdims=True)
+        weights = jnp.exp(scores - highest)
+        totals = jnp.sum(weights, axis=-1, keepdims=True)
+        shares = (weights / totals).astype(jnp.bfloat16)
+        mixed_heads = jnp.einsum(
+            "hqk,khd->qhd", shares, value_ready, preferred_element_type=jnp.float32
+        )
+        return (
+            mixed_heads.astype(jnp.bfloat16),
+            highest[..., 0] + jnp.log(totals[..., 0]),
+            jnp.max(highest[..., 0], axis=-1),
+        )
+
+    mixed_blocks, log_totals, peak_blocks = lax.map(forward_block, (query_blocks, doc_blocks))
+    mixed_seq = mixed_blocks.reshape(length, local_width)
+    attended = lax.psum_scatter(
+        jnp.dot(mixed_seq, out_rows, preferred_element_type=jnp.float32),
+        "gy",
+        scatter_dimension=0,
+        tiled=True,
+    )
+
+    def back(grad_resid):
+        seq_grad = lax.all_gather(grad_resid.astype(jnp.bfloat16), "gy", axis=0, tiled=True)
+        grad_mixed = contract_cols(seq_grad, out_rows).astype(jnp.bfloat16)
+        out_part = contract_rows(seq_grad, mixed_seq)
+
+        def backward_block(running, pieces):
+            grad_key, grad_value = running
+            query_block, grad_block, log_block, doc_block = pieces
+            scores = block_scores(query_block, doc_block)
+            weights = jnp.exp(scores - log_block[..., None])
+            grad_value = grad_value + jnp.einsum(
+                "hqk,qhd->khd",
+                weights.astype(jnp.bfloat16),
+                grad_block,
+                preferred_element_type=jnp.float32,
+            )
+            grad_weights = jnp.einsum(
+                "qhd,khd->hqk", grad_block, value_ready, preferred_element_type=jnp.float32
+            )
+            inner_sum = jnp.sum(weights * grad_weights, axis=-1, keepdims=True)
+            grad_scores = (weights * (grad_weights - inner_sum)).astype(jnp.bfloat16)
+            grad_query = (
+                jnp.einsum("hqk,khd->qhd", grad_scores, key_ready, preferred_element_type=jnp.float32)
+                * score_scale
+            )
+            grad_key = (
+                grad_key
+                + jnp.einsum(
+                    "hqk,qhd->khd", grad_scores, query_block, preferred_element_type=jnp.float32
+                )
+                * score_scale
+            )
+            return ((grad_key, grad_value), grad_query)
+
+        empty_heads = jnp.zeros((length, local_heads, HD), jnp.float32)
+        grad_mixed_blocks = grad_mixed.reshape(block_count, block_rows, local_heads, HD)
+        (key_grad_heads, value_grad_heads), query_grad_blocks = lax.scan(
+            backward_block,
+            (empty_heads, empty_heads),
+            (query_blocks, grad_mixed_blocks, log_totals, doc_blocks),
+        )
+        query_raw_grad, query_gain_part = query_pull(query_grad_blocks.reshape(length, local_heads, HD))
+        key_raw_grad, key_gain_part = key_pull(key_grad_heads)
+        grad_queries = query_raw_grad.reshape(length, local_width).astype(jnp.bfloat16)
+        grad_keys = key_raw_grad.reshape(length, local_width).astype(jnp.bfloat16)
+        grad_values = value_grad_heads.reshape(length, local_width).astype(jnp.bfloat16)
+        grad_heads = jnp.concatenate([grad_queries, grad_keys, grad_values], axis=1)
+        acts_part = contract_cols(grad_heads, full_in).astype(jnp.bfloat16)
+        in_sum = lax.psum_scatter(
+            contract_rows(seq_acts, grad_heads).astype(jnp.bfloat16),
+            "gx",
+            scatter_dimension=0,
+            tiled=True,
+        ).astype(jnp.float32)
+        grad_acts = lax.psum_scatter(acts_part, "gy", scatter_dimension=0, tiled=True)
+        return grad_acts.astype(jnp.float32), in_sum, out_part, query_gain_part, key_gain_part
+
+    return attended, jnp.max(peak_blocks, axis=0), back
+
+
+def kernel_attention(
+    seq_acts, full_in, out_rows, query_gain, key_gain, doc_ids
+):
+    length = seq_acts.shape[0]
+    halfway = HD // 2
+    frequency = jnp.exp(
+        jnp.arange(halfway, dtype=jnp.float32) * (-2.0 * jnp.log(10000.0) / HD)
+    )
+    angles = jnp.arange(length, dtype=jnp.float32)[:, None] * frequency[None, :]
+    cosine, sine = jnp.cos(angles), jnp.sin(angles)
+    tables = (
+        jnp.concatenate([cosine, cosine], axis=1),
+        jnp.concatenate([-sine, sine], axis=1),
+    )
+    docs = (
+        jnp.broadcast_to(doc_ids[:, None], (length, HD)),
+        jnp.broadcast_to(doc_ids[None, :], (8, length)),
+    )
+    part, *saved, peaks = attend(
+        seq_acts, full_in, out_rows, query_gain, key_gain, tables, docs
+    )
+    attended = scatter_plane(part, 3)
+    heads = full_in.shape[1] // (3 * HD)
+
+    def back(grad_resid):
+        seq_grad = all_gather(grad_resid.astype(jnp.bfloat16), False, 1)
+        part, weight_part, out_part, gains = attend_back(
+            seq_grad, out_rows, saved, query_gain, key_gain, tables, docs, seq_acts, full_in
+        )
+        grad_acts, in_sum = leave(part, weight_part, 7)
+        return grad_acts, in_sum, out_part, gains[0], gains[1]
+
+    return attended, peaks[:heads, 0], back
 
 
 def local(
@@ -1487,70 +2007,32 @@
     acts_float, norm_pull = jax.vjp(norm_rows, inputs, attn_gain)
     acts_low = acts_float.astype(jnp.bfloat16)
     in_weights = jnp.concatenate([query_weight, key_weight, value_weight], axis=1)
-    seq_acts, full_in, all_cot = gather_inputs(acts_low, in_weights, cotangent)
+    by_kernels = lax.axis_size("gy") == 8
+    if by_kernels:
+        seq_acts, full_in, all_cot = enter(acts_low, in_weights, cotangent, 6)
+    else:
+        seq_acts = lax.all_gather(acts_low, "gy", axis=0, tiled=True)
+        full_in = lax.all_gather(in_weights, "gx", axis=0, tiled=True)
     seq_acts, full_in, out_weight = lax.optimization_barrier((seq_acts, full_in, out_weight))
     out_rows = lax.all_gather(out_weight, "gx", axis=1, tiled=True)
-    length = seq_acts.shape[0]
     local_width = query_weight.shape[1]
     local_heads = local_width // HD
-    projected = jnp.dot(seq_acts, full_in, preferred_element_type=jnp.float32)
-    queries = projected[:, :local_width]
-    key_raw = projected[:, local_width : 2 * local_width]
-    value_ready = (
-        projected[:, 2 * local_width :].astype(jnp.bfloat16).reshape(length, local_heads, HD)
-    )
-    query_float, query_pull = jax.vjp(
-        prepare_heads, queries.reshape(length, local_heads, HD), query_gain
-    )
-    key_float, key_pull = jax.vjp(prepare_heads, key_raw.reshape(length, local_heads, HD), key_gain)
-    query_ready = query_float.astype(jnp.bfloat16)
-    key_ready = key_float.astype(jnp.bfloat16)
-    block_rows = min(512, length)
-    block_count = length // block_rows
-    score_scale = HD ** (-0.5)
-    query_blocks = query_ready.reshape(block_count, block_rows, local_heads, HD)
-    doc_blocks = doc_ids.reshape(block_count, block_rows)
-
-    def block_scores(query_block, doc_block):
-        scores = (
-            jnp.einsum("qhd,khd->hqk", query_block, key_ready, preferred_element_type=jnp.float32)
-            * score_scale
-        )
-        same_doc = doc_block[:, None] == doc_ids[None, :]
-        return jnp.where(same_doc[None], scores, NEGATIVE)
-
-    def forward_block(pieces):
-        scores = block_scores(pieces[0], pieces[1])
-        highest = jnp.max(scores, axis=-1, keepdims=True)
-        weights = jnp.exp(scores - highest)
-        totals = jnp.sum(weights, axis=-1, keepdims=True)
-        shares = (weights / totals).astype(jnp.bfloat16)
-        mixed_heads = jnp.einsum(
-            "hqk,khd->qhd", shares, value_ready, preferred_element_type=jnp.float32
-        )
-        return (
-            mixed_heads.astype(jnp.bfloat16),
-            highest[..., 0] + jnp.log(totals[..., 0]),
-            jnp.max(highest[..., 0], axis=-1),
-        )
-
-    mixed_blocks, log_totals, peak_blocks = lax.map(forward_block, (query_blocks, doc_blocks))
-    mixed_seq = mixed_blocks.reshape(length, local_width)
+    attention = kernel_attention if by_kernels else plain_attention
+    attended, own_peaks, attention_back = attention(
+        seq_acts, full_in, out_rows, query_gain, key_gain, doc_ids
+    )
     start_head = lax.axis_index("gy") * local_heads
     peak_slots = lax.dynamic_update_slice(
         jnp.zeros((lax.axis_size("gx"), NH), jnp.float32),
-        jnp.max(peak_blocks, axis=0)[None],
+        own_peaks[None],
         (lax.axis_index("gx"), start_head),
-    )
-    attended = scatter_plane(
-        jnp.dot(mixed_seq, out_rows, preferred_element_type=jnp.float32).astype(jnp.bfloat16), 3
     )
     residual = inputs + attended
     moe_float, moe_pull = jax.vjp(norm_rows, residual, moe_gain)
     moe_in = moe_float.astype(jnp.bfloat16)
     logits = jnp.dot(moe_in, router_weight, preferred_element_type=jnp.float32)
     gate_share, gate_pull = jax.vjp(partial(route_gates, expert_ids), logits)
-    if all_cot is not None and router_weight.shape[1] <= 2 * TOP:
+    if by_kernels and router_weight.shape[1] <= 2 * TOP:
         moe_out, grad_gates, grad_moe_in, gate_part, up_part, down_part = dense_experts(
             moe_in, all_cot, expert_ids, gate_share, gate_weight, up_weight, down_weight
         )
@@ -1573,56 +2055,7 @@
     grad_moe_in = grad_moe_in + contract_cols(grad_logits_low, router_weight)
     grad_resid_norm, moe_gain_part = moe_pull(grad_moe_in)
     grad_resid = grad_out + grad_resid_norm
-    seq_grad = gather_plane(grad_resid.astype(jnp.bfloat16), 1)
-    grad_mixed = contract_cols(seq_grad, out_rows).astype(jnp.bfloat16)
-    out_part = contract_rows(seq_grad, mixed_seq)
-
-    def backward_block(running, pieces):
-        grad_key, grad_value = running
-        query_block, grad_block, log_block, doc_block = pieces
-        scores = block_scores(query_block, doc_block)
-        weights = jnp.exp(scores - log_block[..., None])
-        grad_value = grad_value + jnp.einsum(
-            "hqk,qhd->khd",
-            weights.astype(jnp.bfloat16),
-            grad_block,
-            preferred_element_type=jnp.float32,
-        )
-        grad_weights = jnp.einsum(
-            "qhd,khd->hqk", grad_block, value_ready, preferred_element_type=jnp.float32
-        )
-        inner_sum = jnp.sum(weights * grad_weights, axis=-1, keepdims=True)
-        grad_scores = (weights * (grad_weights - inner_sum)).astype(jnp.bfloat16)
-        grad_query = (
-            jnp.einsum("hqk,khd->qhd", grad_scores, key_ready, preferred_element_type=jnp.float32)
-            * score_scale
-        )
-        grad_key = (
-            grad_key
-            + jnp.einsum(
-                "hqk,qhd->khd", grad_scores, query_block, preferred_element_type=jnp.float32
-            )
-            * score_scale
-        )
-        return ((grad_key, grad_value), grad_query)
-
-    empty_heads = jnp.zeros((length, local_heads, HD), jnp.float32)
-    grad_mixed_blocks = grad_mixed.reshape(block_count, block_rows, local_heads, HD)
-    (key_grad_heads, value_grad_heads), query_grad_blocks = lax.scan(
-        backward_block,
-        (empty_heads, empty_heads),
-        (query_blocks, grad_mixed_blocks, log_totals, doc_blocks),
-    )
-    query_raw_grad, query_gain_part = query_pull(query_grad_blocks.reshape(length, local_heads, HD))
-    key_raw_grad, key_gain_part = key_pull(key_grad_heads)
-    grad_queries = query_raw_grad.reshape(length, local_width).astype(jnp.bfloat16)
-    grad_keys = key_raw_grad.reshape(length, local_width).astype(jnp.bfloat16)
-    grad_values = value_grad_heads.reshape(length, local_width).astype(jnp.bfloat16)
-    grad_heads = jnp.concatenate([grad_queries, grad_keys, grad_values], axis=1)
-    grad_acts, in_sum = scatter_grads(
-        contract_cols(grad_heads, full_in).astype(jnp.bfloat16),
-        contract_rows(seq_acts, grad_heads).astype(jnp.bfloat16),
-    )
+    grad_acts, in_sum, out_part, query_gain_part, key_gain_part = attention_back(grad_resid)
     query_sum = in_sum[:, :local_width]
     key_sum = in_sum[:, local_width : 2 * local_width]
     value_sum = in_sum[:, 2 * local_width :]

time: 784 us -> 742 us (0.946); the launches traced: 774 us -> 741 us
  matrix products: 61 us -> 4.18 us
  Pallas kernels: 567 us -> 615 us
  other arithmetic: 52.2 us -> 31.1 us
  local copies, waits for them, and re-layouts: 49.4 us -> 33.3 us
  waiting for transfers between devices: 20.7 us -> 30 us
    pallas_call x1, Pallas kernels: 123 us -> 183 us  [run_experts(): pl.pallas_call(partial(expert_kernel, n_z, span), out_shape=(jax.ShapeDty...]
    dot_general x16 -> x0, matrix products: 38.1 us -> none  [the longest x4 7.67 us: block_scores(): jnp.einsum('qhd,khd->hqk', query_block, key_ready, preferred_element_type...]
    pallas_call x2 -> x3, Pallas kernels: 114 us -> 85.2 us  [the longest x1 36.6 us: attend_back(): pl.pallas_call(partial(attend_back_kernel, heads, pieces), out_shape=(jax...]
    all_gather x1, waiting for transfers between devices: 0.02 us -> 23.4 us  [local(): out_rows = lax.all_gather(out_weight, 'gx', axis=1, tiled=True)]
    reduce_scatter x1, waiting for transfers between devices: 14.1 us -> 0.01 us  [local(): lax.psum_scatter(out_part.astype(jnp.bfloat16), 'gx', scatter_dimension=0...]
    pallas_call x1, Pallas kernels: 61.8 us -> 75.5 us  [leave(): pl.pallas_call(partial(leave_kernel, pieces, rows), out_shape=(jax.ShapeD...]
    dot_general x3 -> x1, matrix products: 11.3 us -> 1.22 us  [contract_rows(): lax.dot_general(left_side, right_side, (((0,), (0,)), ((), ())), preferre...]
    dot_general x3 -> x1, matrix products: 11.3 us -> 2.7 us  [contract_cols(): lax.dot_general(left_side, right_side, (((1,), (1,)), ((), ())), preferre...]
  transfers between devices with their start and end apart: 4 -> 4, of which waited for: 2 -> 2; matrix products, arithmetic and copies ran while one was open for 5% -> 4% of each run, Pallas kernels for 26% -> 28%
where the time goes in v6:
time: 742 us; the launch traced here: 741 us
  Pallas kernels  615 us (83%)
  local copies, waits for them, and re-layouts  33.3 us (4%)
  other arithmetic  31.1 us (4%)
  waiting for transfers between devices  30 us (4%)
  between operations  15.2 us (2%)
  starting transfers between devices  12 us (2%)
    pallas_call x1, Pallas kernels, run_experts(): pl.pallas_call(partial(expert_kernel, n_z, span), out_shape=(jax.ShapeDty...  183 us
    pallas_call x1, Pallas kernels, enter(): pl.pallas_call(partial(enter_kernel, n_z, span), out_shape=(jax.ShapeDtyp...  116 us
    pallas_call x1, Pallas kernels, pull_experts(): pl.pallas_call(partial(pull_kernel, n_i, rows), out_shape=(jax.ShapeDtype...  111 us
    pallas_call x1, Pallas kernels, leave(): pl.pallas_call(partial(leave_kernel, pieces, rows), out_shape=(jax.ShapeD...  75.5 us
    pallas_call x1, Pallas kernels, attend_back(): pl.pallas_call(partial(attend_back_kernel, heads, pieces), out_shape=(jax...  36.6 us
    pallas_call x1, Pallas kernels, attend(): pl.pallas_call(partial(attend_kernel, heads, pieces), out_shape=(jax.Shap...  24.3 us
    pallas_call x1, Pallas kernels, scatter_plane(): pl.pallas_call(partial(scatter_kernel, False, pieces, rows), out_shape=ja...  24.3 us
    pallas_call x1, Pallas kernels, all_gather(): pl.pallas_call(partial(gather_kernel, n_z, span), out_shape=jax.ShapeDtyp...  23.8 us
  transfers between devices with their start and end apart: 4, of which 2 were waited for; matrix products, arithmetic and copies ran while one was open for 4% of the time, Pallas kernels for 28%

profile of v6, /device:TPU:0, one launch (start us, length us, event | category | flops | bytes accessed | tf_op | source)
XLA Modules:
  0.0 740.5 jit_solution(360878085720779630)
XLA Ops:
  7.2 1.2 fusion.6
  9.0 0.6 copy-done.24
  9.6 2.0 fusion.2
  11.6 2.0 pad_maximum_fusion.weight_ref
  13.7 115.5 %enter.1 = (bf16[8,2,64,2048]{3,2,1,0:T(8,128)(2,1)}, bf16[4,512,768]{2,1,0:T(8,128)(2,1)}, bf16[32,2,64,2048]{3,2,1,0:T(8,128)(2,1)}) custom-call(bf16[2,64,2048]{2,1,0:T(8,128)(2,1)} %bitcast.78, bf16[512,768]{1,0:T(8,128)(2,1)} %pad_maximum_fusion.weight_ref, bf16[2,64,2048]{2,1,0:T(8,128)(2,1)} %bitcast.72), custom_call_target="tpu_custom_call" | custom-call | tf_op jit(solution)/shard_map/enter/pallas_call | solution.py:541
  129.9 2.0 fusion.11
  131.8 1.3 pad_maximum_fusion.1
  133.1 23.4 %all-gather.2.cloned.1.call-done.out_weight_ref = bf16[256,2048]{1,0:T(8,128)(2,1)} async-done(((bf16[256,512]{1,0:T(8,128)(2,1)}), bf16[256,2048]{1,0:T(8,128)(2,1)}) %all-gather.2.cloned.1.call-update) | async-done | bytes 1048592 | tf_op jit(solution)/shard_map/all_gather | solution.py:2017
  156.6 0.6 broadcast_in_dim.112.col_docs
  157.2 1.0 broadcast_in_dim.111.row_docs
  158.2 24.3 %attend.1 = (bf16[4,8,2,16,2048]{4,3,2,1,0:T(8,128)(2,1)}, f32[1024,256]{1,0:T(8,128)}, f32[1024,256]{1,0:T(8,128)}, bf16[1024,768]{1,0:T(8,128)(2,1)}, bf16[102...) custom-call(bf16[1024,2048]{1,0:T(8,128)(2,1)} %bitcast.61, bf16[2048,768]{1,0:T(8,128)(2,1)} %bitcast.65, ...), custom_call_target="tpu_custom_call" | custom-call | tf_op jit(solution)/shard_map/attend/pallas_call | solution.py:1484
  182.5 24.3 %scatter_plane.1 = f32[4,2,16,2048]{3,2,1,0:T(8,128)} custom-call(bf16[4,8,2,16,2048]{4,3,2,1,0:T(8,128)(2,1)} %get-tuple-element.51.part_ref), custom_call_target="tpu_custom_call" | custom-call | tf_op jit(solution)/shard_map/scatter_plane/pallas_call | solution.py:383
  206.8 1.5 multiply_reduce_fusion.2
  208.4 0.9 copy-done
  209.5 0.8 copy-done.4
  211.8 0.6 broadcast_in_dim.116
  212.4 3.2 all-to-all-start
  216.1 6.6 all-to-all-done
  222.7 1.9 broadcast_in_dim.118.share_ref
  224.6 183.1 %experts.1 = (bf16[4096,2048]{1,0:T(8,128)(2,1)}, bf16[4096,1024]{1,0:T(8,128)(2,1)}, f32[4096,128]{1,0:T(8,128)}, f32[512,2048]{1,0:T(8,128)}, f32[2,64,2048]{2,1,0:T(8,128)}) custom-call(bf16[2,64,2048]{2,1,0:T(8,128)(2,1)} %bitcast.71, bf16[4096,2048]{1,0:T(8,128)(2,1)} %bitcast.64, f32[4096,128]{1,0:T(8,128)} %broadcast_in_dim.118.share_ref, ...), custom_call_target="tpu_custom_call" | custom-call | tf_op jit(solution)/shard_map/experts/pallas_call | solution.py:1133
  407.7 2.8 reduce_sum.162
  410.5 8.7 %all-to-all-start.1 = ((f32[32,1,128]{2,1,0:T(1,128)}), f32[32,1,128]{2,1,0:T(1,128)}, u32[]{:S(2)}, u32[]{:S(2)}) async-start(f32[32,1,128]{2,1,0:T(1,128)} %bitcast.17), calls=%async_computation.1 | async-start | bytes 32768 | tf_op jit(solution)/shard_map/all_to_all | solution.py:1823
  419.3 0.8 slice_reduce_fusion.1
  420.3 0.6 reshape.223
  420.9 111.1 %pull_experts.1 = (f32[2,64,2048]{2,1,0:T(8,128)}, f32[2048,512]{1,0:T(8,128)}, f32[2048,512]{1,0:T(8,128)}) custom-call(bf16[4096,2048]{1,0:T(8,128)(2,1)} %get-tuple-element.54.all_ref, bf16[4096,1024]{1,0:T(8,128)(2,1)} %get-tuple-element.55.pair_ref, bf16[2048,512]{1,0:T(8,128)(2,1)} %bitcast.68, bf16[2048,512]{1,0:T(8,128)(2,1)} %bitcast.70), custom_call_target="tpu_custom_call" | custom-call | tf_op jit(solution)/shard_map/pull_experts/pallas_call | solution.py:1358
  532.1 0.9 reduce_sum.163
  532.9 0.7 select_reduce_fusion.3
  533.6 0.7 multiply_reduce_fusion.4
  534.4 0.7 divide_add_fusion
  535.0 0.7 select_reduce_fusion.2
  535.7 0.7 multiply_reduce_fusion.3
  536.5 0.7 multiply_convert_fusion.3
  537.2 1.2 convolution_bitcast_fusion
  538.4 2.7 multiply_reduce_fusion
  541.2 1.2 fusion.17
  542.4 23.8 %gather_plane.1 = bf16[8,2,64,2048]{3,2,1,0:T(8,128)(2,1)} custom-call(bf16[2,64,2048]{2,1,0:T(8,128)(2,1)} %bitcast.79), custom_call_target="tpu_custom_call" | custom-call | tf_op jit(solution)/shard_map/gather_plane/pallas_call | solution.py:229
  566.2 36.6 %attend_back.1 = (bf16[4,8,2,16,2048]{4,3,2,1,0:T(8,128)(2,1)}, bf16[2048,768]{1,0:T(8,128)(2,1)}, bf16[2048,256]{1,0:T(8,128)(2,1)}, f32[8,128]{1,0:T(8,128)}) custom-call(bf16[1024,2048]{1,0:T(8,128)(2,1)} %bitcast.63, bf16[256,2048]{1,0:T(8,128)(2,1)} %all-gather.2.cloned.1.call-done.out_weight_ref, bf16[1024,256]{1,0:T(8,128)(2,1)} %get-tuple-element.58.mixed_ref, ...), custom_call_target="tpu_custom_call" | custom-call | tf_op jit(solution)/shard_map/attend_back/pallas_call | solution.py:1636
  602.9 75.5 %leave.1 = (f32[4,2,16,2048]{3,2,1,0:T(8,128)}, f32[512,768]{1,0:T(8,128)}) custom-call(bf16[4,8,2,16,2048]{4,3,2,1,0:T(8,128)(2,1)} %get-tuple-element.63.part_ref, bf16[4,512,768]{2,1,0:T(8,128)(2,1)} %bitcast.76), custom_call_target="tpu_custom_call" | custom-call | tf_op jit(solution)/shard_map/leave/pallas_call | solution.py:712
  678.4 2.2 fusion.3
  680.6 0.7 constant_dynamic-update-slice_fusion.3
  681.3 0.7 constant_dynamic-update-slice_fusion.2
  682.0 0.7 pad.4
  682.7 20.4 %sum_everywhere.1 = f32[2,152,128]{2,1,0:T(8,128)} custom-call(f32[2,152,128]{2,1,0:T(8,128)} %bitcast.84), custom_call_target="tpu_custom_call" | custom-call | tf_op jit(solution)/shard_map/sum_everywhere/pallas_call | solution.py:474
  703.2 2.3 slice.57
  705.5 0.7 slice_reduce_fusion
  706.2 1.3 sort.15
  707.5 0.6 fusion.14
  708.1 0.6 compare_select_fusion
  708.7 0.6 dynamic-slice_sqrt_fusion
  709.3 0.9 slice.63
  710.2 0.7 reshape.226
  711.0 0.8 multiply_multiply_fusion
  711.8 0.7 broadcast_bitcast_fusion
  712.5 1.3 fusion.19
  713.8 1.3 fusion.20
  715.1 1.8 multiply_convert_fusion.1
  716.9 2.5 fusion.18
  719.5 1.7 fusion.5
  721.2 1.0 convert_bitcast_fusion
  722.2 1.0 copy.49
  723.2 4.8 copy.62
  728.0 2.1 copy.63
  730.1 1.6 copy-done.7
  731.7 2.0 copy.64
  (98 shorter events, 3.2 us)
Async XLA Ops:
  7.2 149.4 %all-gather.2.cloned.1.call-start = ((), (), s32[]{:S(2)}) async-start(), calls=%async_computation.3 | async-start | bytes 1310720 | tf_op jit(solution)/shard_map/all_gather | solution.py:2017
  8.5 0.5 copy-start.31
  9.0 0.6 copy-start.24
  13.6 142.9 %copy-start.19 = (s32[1024]{0:T(1024)S(1)}, s32[1024]{0:T(1024)}, u32[]{:S(2)}) copy-start(s32[1024]{0:T(1024)} %param.20) | copy-start | bytes 12292
  182.5 24.3 %copy-start.2 = (bf16[128,2048]{1,0:T(8,128)(2,1)S(1)}, bf16[128,2048]{1,0:T(8,128)(2,1)}, u32[]{:S(2)}) copy-start(bf16[128,2048]{1,0:T(8,128)(2,1)} %param.17) | copy-start | bytes 1572868
  182.5 26.8 %copy-start.13 = (f32[2048]{0:T(1024)S(1)}, f32[2048]{0:T(1024)}, u32[]{:S(2)}) copy-start(f32[2048]{0:T(1024)} %param.23) | copy-start | bytes 24580
  206.8 3.5 copy-start.11
  206.8 4.3 copy-start.16
  208.3 1.0 copy-start
  208.3 4.1 copy-start.33
  208.4 1.0 copy-start.21
  209.5 0.8 copy-start.4
  210.5 0.6 copy-start.12
  210.6 1.9 copy-start.20
  210.6 1.8 copy-start.27
  211.2 0.6 copy-start.17
  211.2 11.5 %copy-start.28 = (f32[128]{0:T(128)}, f32[128]{0:T(128)S(1)}, u32[]{:S(2)}) copy-start(f32[128]{0:T(128)S(1)} %get-tuple-element.180) | copy-start | bytes 1540
  212.4 10.3 %all-to-all-start = ((f32[32,1,128]{2,1,0:T(1,128)}), f32[32,1,128]{2,1,0:T(1,128)S(1)}, u32[]{:S(2)}, u32[]{:S(2)}) async-start(f32[32,1,128]{2,1,0:T(1,128)} %bitcast.10), calls=%async_computation | async-start | bytes 32768 | tf_op jit(solution)/shard_map/all_to_all | solution.py:1815
  410.5 121.5 %all-to-all-start.1 = ((f32[32,1,128]{2,1,0:T(1,128)}), f32[32,1,128]{2,1,0:T(1,128)}, u32[]{:S(2)}, u32[]{:S(2)}) async-start(f32[32,1,128]{2,1,0:T(1,128)} %bitcast.17), calls=%async_computation.1 | async-start | bytes 32768 | tf_op jit(solution)/shard_map/all_to_all | solution.py:1823
  419.2 301.9 %reduce-scatter.2.cloned.1.call-start = ((), (), s32[]{:S(2)}) async-start(), calls=%async_computation.4 | async-start | bytes 1310720 | tf_op jit(solution)/shard_map/reduce_scatter | solution.py:2062
  532.0 9.1 %copy-start.34 = (f32[128]{0:T(128)S(1)}, f32[128]{0:T(128)}, u32[]{:S(2)}) copy-start(f32[128]{0:T(128)} %copy-done.33) | copy-start | bytes 1540
  532.0 9.1 %copy-start.1 = (f32[128,2048]{1,0:T(8,128)S(1)}, f32[128,2048]{1,0:T(8,128)}, u32[]{:S(2)}) copy-start(f32[128,2048]{1,0:T(8,128)} %copy-done) | copy-start | bytes 3145732
  532.0 9.1 %copy-start.5 = (bf16[128,2048]{1,0:T(8,128)(2,1)S(1)}, bf16[128,2048]{1,0:T(8,128)(2,1)}, u32[]{:S(2)}) copy-start(bf16[128,2048]{1,0:T(8,128)(2,1)} %param.18) | copy-start | bytes 1572868
  532.0 9.1 %copy-start.14 = (f32[2048]{0:T(1024)S(1)}, f32[2048]{0:T(1024)}, u32[]{:S(2)}) copy-start(f32[2048]{0:T(1024)} %param.23) | copy-start | bytes 24580
  532.1 9.1 %copy-start.22 = (f32[128]{0:T(128)S(1)}, f32[128]{0:T(128)}, u32[]{:S(2)}) copy-start(f32[128]{0:T(128)} %copy-done.21) | copy-start | bytes 1540
  541.2 25.0 %copy-start.29 = (f32[128]{0:T(128)}, f32[128]{0:T(128)S(1)}, u32[]{:S(2)}) copy-start(f32[128]{0:T(128)S(1)} %multiply_multiply_fusion.1) | copy-start | bytes 1540
  602.8 75.6 %copy-start.3 = (bf16[128,2048]{1,0:T(8,128)(2,1)S(1)}, bf16[128,2048]{1,0:T(8,128)(2,1)}, u32[]{:S(2)}) copy-start(bf16[128,2048]{1,0:T(8,128)(2,1)} %param.17) | copy-start | bytes 1572868
  602.8 75.6 %copy-start.15 = (f32[2048]{0:T(1024)S(1)}, f32[2048]{0:T(1024)}, u32[]{:S(2)}) copy-start(f32[2048]{0:T(1024)} %param.22) | copy-start | bytes 24580
  602.8 75.6 %copy-start.25 = (f32[128]{0:T(128)S(1)}, f32[128]{0:T(128)}, u32[]{:S(2)}) copy-start(f32[128]{0:T(128)} %copy-done.24) | copy-start | bytes 1540
  602.8 77.7 %copy-start.18 = (f32[2048]{0:T(1024)S(1)}, f32[2048]{0:T(1024)}, u32[]{:S(2)}) copy-start(f32[2048]{0:T(1024)} %get-tuple-element.176) | copy-start | bytes 24580
  602.8 79.2 %copy-start.32 = (f32[64]{0:T(128)S(1)}, f32[64]{0:T(128)}, u32[]{:S(2)}) copy-start(f32[64]{0:T(128)} %reshape.223) | copy-start | bytes 772
  678.4 36.7 %copy-start.10 = (bf16[512,256]{1,0:T(8,128)(2,1)S(1)}, bf16[512,256]{1,0:T(8,128)(2,1)}, u32[]{:S(2)}) copy-start(bf16[512,256]{1,0:T(8,128)(2,1)} %param.27) | copy-start | bytes 786436
  708.7 0.6 copy-start.35
  710.9 8.5 %copy-start.6 = (f32[4,2,16,2048]{3,2,1,0:T(8,128)S(1)}, f32[4,2,16,2048]{3,2,1,0:T(8,128)}, u32[]{:S(2)}) copy-start(f32[4,2,16,2048]{3,2,1,0:T(8,128)} %get-tuple-element.65) | copy-start | bytes 3145732
  710.9 8.5 %copy-start.9 = (f32[2,64,2048]{2,1,0:T(8,128)S(1)}, f32[2,64,2048]{2,1,0:T(8,128)}, u32[]{:S(2)}) copy-start(f32[2,64,2048]{2,1,0:T(8,128)} %get-tuple-element.53) | copy-start | bytes 3145732
  710.9 8.5 %copy-start.23 = (f32[128]{0:T(128)S(1)}, f32[128]{0:T(128)}, u32[]{:S(2)}) copy-start(f32[128]{0:T(128)} %copy-done.21) | copy-start | bytes 1540
  710.9 8.5 %copy-start.26 = (f32[128]{0:T(128)S(1)}, f32[128]{0:T(128)}, u32[]{:S(2)}) copy-start(f32[128]{0:T(128)} %copy-done.24) | copy-start | bytes 1540
  710.9 8.5 %copy-start.30 = (f32[128]{0:T(128)S(1)}, f32[128]{0:T(128)}, u32[]{:S(2)}) copy-start(f32[128]{0:T(128)} %copy-done.29) | copy-start | bytes 1540
  723.2 4.8 copy-start.8
  728.0 3.7 copy-start.7
Sparse Core Ops, SparseCore 0:
  129.3 27.2 all-gather.1
  602.9 42.3 reduce-scatter.1

commit v7 on v6

--- a/solution.py
+++ b/solution.py
@@ -1394,6 +1394,12 @@
     return values * cosine + pltpu.roll(values, values.shape[-1] // 2, 1) * sine
 
 
+def greet_chain(n_z):
+    z = lax.axis_index("gx")
+    g = lax.axis_index("gy")
+    barrier_with([(z < n_z - 1, {"gx": z + 1, "gy": g}), (z > 0, {"gx": z - 1, "gy": g})])
+
+
 def attend_kernel(
     heads,
     pieces,
@@ -1413,7 +1419,17 @@
     mixed_ref,
     totals_ref,
     peaks_ref,
+    full_out,
+    chain_send,
+    chain_recv,
+    chain_local,
 ):
+    n_z = lax.axis_size("gx")
+    greet_chain(n_z)
+    start, relays, finish = chain_gather(
+        n_z, out_weight_ref, full_out, chain_send, chain_recv, chain_local
+    )
+    start()
     f32, bf16 = jnp.float32, jnp.bfloat16
     dot = partial(lax.dot_general, preferred_element_type=f32)
     plain = (((1,), (0,)), ((), ()))
@@ -1437,6 +1453,9 @@
                 turned = turn(normed * gain[...], cosine_ref[at, :], sine_ref[at, :])
                 where = source * local + h * HD
                 ready_ref[at, where : where + HD] = turned.astype(bf16)
+
+        if source < len(relays) - 1:
+            relays[source]()
 
     ready_ref[:, 2 * local :] = dot(acts_ref[...], weight_ref[:, 2 * local :], plain).astype(bf16)
     lanes = lax.broadcasted_iota(jnp.int32, (block, HD), 1)
@@ -1462,24 +1481,31 @@
             peaks_ref[h : h + 1, :] = jnp.maximum(peaks_ref[h : h + 1, :], top)
         totals_ref[at, :] = kept
 
+    for relay in relays[min(2, len(relays) - 1) :]:
+        relay()
+    finish()
     rows = part_ref.shape[3]
-
-    @pl.loop(0, out_weight_ref.shape[1] // block)
+    per_owner = out_weight_ref.shape[1] // block
+
+    @pl.loop(0, n_z * per_owner)
     def _(t):
         cols = pl.ds(pl.multiple_of(t * block, block), block)
-        sent = dot(mixed_ref[...], out_weight_ref[:, cols], plain).astype(bf16)
+        inside = pl.ds(pl.multiple_of(lax.rem(t, per_owner) * block, block), block)
+        sent = dot(mixed_ref[...], full_out[lax.div(t, per_owner), :, inside], plain).astype(bf16)
         sent = sent.reshape(span, pieces, 2, rows, block)
         for p in range(pieces):
             part_ref[p, :, :, :, cols] = sent[:, p]
 
 
-def attend(acts, weights, out_weight, query_gain, key_gain, tables, docs, pieces=4):
+def attend(acts, weights, out_weight, query_gain, key_gain, tables, docs, collective_id, pieces=4):
     length, width = acts.shape
     local = weights.shape[1] // 3
     heads = local // HD
     span = lax.axis_size("gy")
+    n_z = lax.axis_size("gx")
     rows = length // (span * pieces * 2)
     f32, bf16 = jnp.float32, jnp.bfloat16
+    dma = pltpu.SemaphoreType.DMA
     vmem = pl.BlockSpec(memory_space=pltpu.VMEM)
     return pl.pallas_call(
         partial(attend_kernel, heads, pieces),
@@ -1491,10 +1517,14 @@
             jax.ShapeDtypeStruct((length, local), bf16),
             jax.ShapeDtypeStruct((length, HD), f32),
             jax.ShapeDtypeStruct((8, HD), f32),
+            jax.ShapeDtypeStruct((n_z,) + out_weight.shape, bf16),
         ),
         in_specs=[vmem] * 9,
-        out_specs=(vmem,) * 7,
-        compiler_params=pltpu.CompilerParams(vmem_limit_bytes=60 << 20),
+        out_specs=(vmem,) * 8,
+        scratch_shapes=[dma((2 * n_z,)), dma((n_z,)), dma],
+        compiler_params=pltpu.CompilerParams(
+            collective_id=collective_id, has_side_effects=True, vmem_limit_bytes=60 << 20
+        ),
         name="attend",
     )(
         acts,
@@ -1527,7 +1557,7 @@
     weight_hbm,
     part_ref,
     weight_part,
-    out_part,
+    out_sum,
     gain_ref,
     acts_ref,
     weight_ref,
@@ -1536,8 +1566,19 @@
     turned,
     key_sum,
     value_sum,
+    sums,
+    from_low,
+    from_high,
     copy_sem,
+    chain_send,
+    low_recv,
+    high_recv,
 ):
+    n_z = lax.axis_size("gx")
+    greet_chain(n_z)
+    start, relays, finish = chain_scatter(
+        n_z, sums, out_sum, from_low, from_high, chain_send, low_recv, high_recv
+    )
     f32, bf16 = jnp.float32, jnp.bfloat16
     dot = partial(lax.dot_general, preferred_element_type=f32)
     plain = (((1,), (0,)), ((), ()))
@@ -1555,13 +1596,22 @@
     ]
     for copy in copies:
         copy.start()
-    grad_mixed[...] = dot(grad_ref[...], out_weight_ref[...], last_dims).astype(bf16)
+    owned = width // n_z
 
     @pl.loop(0, width // block)
     def _(t):
         cols = pl.ds(pl.multiple_of(t * block, block), block)
-        out_part[cols, :] = dot(grad_ref[:, cols], mixed_ref[...], first_dims).astype(bf16)
-
+        inside = pl.ds(pl.multiple_of(lax.rem(t, owned // block) * block, block), block)
+        sums[lax.div(t, owned // block), inside, :] = dot(
+            grad_ref[:, cols], mixed_ref[...], first_dims
+        ).astype(bf16)
+
+    start()
+    total = dot(grad_ref[:, :owned], out_weight_ref[0], last_dims)
+    for owner in range(1, n_z):
+        cols = slice(owner * owned, (owner + 1) * owned)
+        total = total + dot(grad_ref[:, cols], out_weight_ref[owner], last_dims)
+    grad_mixed[...] = total.astype(bf16)
     gain_ref[...] = jnp.zeros_like(gain_ref)
     for h in range(heads):
         cols = slice(h * HD, (h + 1) * HD)
@@ -1607,6 +1657,12 @@
 
         where = 2 * local + h * HD
         grad_heads[:, where : where + HD] = value_sum[...].astype(bf16)
+        if h < len(relays) - 1:
+            relays[h]()
+
+    for relay in relays[min(heads, len(relays) - 1) :]:
+        relay()
+    finish()
 
     for copy in copies:
         copy.wait()
@@ -1622,9 +1678,21 @@
 
 
 def attend_back(
-    seq_grad, out_weight, saved, query_gain, key_gain, tables, docs, acts, weights, pieces=4
+    seq_grad,
+    saved,
+    query_gain,
+    key_gain,
+    tables,
+    docs,
+    acts,
+    weights,
+    collective_id,
+    pieces=4,
 ):
-    query_raw, key_raw, ready, mixed, totals = saved
+    query_raw, key_raw, ready, mixed, totals, out_weight = saved
+    n_z = lax.axis_size("gx")
+    dma = pltpu.SemaphoreType.DMA
+    block = (n_z, acts.shape[1] // n_z, query_raw.shape[1])
     length, width = seq_grad.shape
     local = query_raw.shape[1]
     heads = local // HD
@@ -1638,7 +1706,7 @@
         out_shape=(
             jax.ShapeDtypeStruct((pieces, span, 2, rows, width), bf16),
             jax.ShapeDtypeStruct((width, 3 * local), bf16),
-            jax.ShapeDtypeStruct((width, local), bf16),
+            jax.ShapeDtypeStruct(block[1:], f32),
             jax.ShapeDtypeStruct((8, HD), f32),
         ),
         in_specs=[vmem] * 13 + [hbm] * 2,
@@ -1651,9 +1719,17 @@
             pltpu.VMEM((length, HD), f32),
             pltpu.VMEM((length, HD), f32),
             pltpu.VMEM((length, HD), f32),
-            pltpu.SemaphoreType.DMA((2,)),
+            pltpu.VMEM(block, bf16),
+            pltpu.VMEM(block, bf16),
+            pltpu.VMEM(block, bf16),
+            dma((2,)),
+            dma((n_z,)),
+            dma((n_z,)),
+            dma((n_z,)),
         ],
-        compiler_params=pltpu.CompilerParams(vmem_limit_bytes=60 << 20),
+        compiler_params=pltpu.CompilerParams(
+            collective_id=collective_id, has_side_effects=True, vmem_limit_bytes=60 << 20
+        ),
         name="attend_back",
     )(
         seq_grad,
@@ -1834,8 +1910,9 @@
 
 
 def plain_attention(
-    seq_acts, full_in, out_rows, query_gain, key_gain, doc_ids
+    seq_acts, full_in, out_weight, query_gain, key_gain, doc_ids
 ):
+    out_rows = lax.all_gather(out_weight, "gx", axis=1, tiled=True)
     local_width = full_in.shape[1] // 3
     length = seq_acts.shape[0]
     local_heads = local_width // HD
@@ -1944,13 +2021,16 @@
             tiled=True,
         ).astype(jnp.float32)
         grad_acts = lax.psum_scatter(acts_part, "gy", scatter_dimension=0, tiled=True)
-        return grad_acts.astype(jnp.float32), in_sum, out_part, query_gain_part, key_gain_part
+        out_sum = lax.psum_scatter(
+            out_part.astype(jnp.bfloat16), "gx", scatter_dimension=0, tiled=True
+        ).astype(jnp.float32)
+        return grad_acts.astype(jnp.float32), in_sum, out_sum, query_gain_part, key_gain_part
 
     return attended, jnp.max(peak_blocks, axis=0), back
 
 
 def kernel_attention(
-    seq_acts, full_in, out_rows, query_gain, key_gain, doc_ids
+    seq_acts, full_in, out_weight, query_gain, key_gain, doc_ids
 ):
     length = seq_acts.shape[0]
     halfway = HD // 2
@@ -1967,19 +2047,20 @@
         jnp.broadcast_to(doc_ids[:, None], (length, HD)),
         jnp.broadcast_to(doc_ids[None, :], (8, length)),
     )
-    part, *saved, peaks = attend(
-        seq_acts, full_in, out_rows, query_gain, key_gain, tables, docs
-    )
+    part, *saved, peaks, out_rows = attend(
+        seq_acts, full_in, out_weight, query_gain, key_gain, tables, docs, 10
+    )
+    saved.append(out_rows)
     attended = scatter_plane(part, 3)
     heads = full_in.shape[1] // (3 * HD)
 
     def back(grad_resid):
         seq_grad = all_gather(grad_resid.astype(jnp.bfloat16), False, 1)
-        part, weight_part, out_part, gains = attend_back(
-            seq_grad, out_rows, saved, query_gain, key_gain, tables, docs, seq_acts, full_in
+        part, weight_part, out_sum, gains = attend_back(
+            seq_grad, saved, query_gain, key_gain, tables, docs, seq_acts, full_in, 11
         )
         grad_acts, in_sum = leave(part, weight_part, 7)
-        return grad_acts, in_sum, out_part, gains[0], gains[1]
+        return grad_acts, in_sum, out_sum, gains[0], gains[1]
 
     return attended, peaks[:heads, 0], back
 
@@ -2013,13 +2094,11 @@
     else:
         seq_acts = lax.all_gather(acts_low, "gy", axis=0, tiled=True)
         full_in = lax.all_gather(in_weights, "gx", axis=0, tiled=True)
-    seq_acts, full_in, out_weight = lax.optimization_barrier((seq_acts, full_in, out_weight))
-    out_rows = lax.all_gather(out_weight, "gx", axis=1, tiled=True)
     local_width = query_weight.shape[1]
     local_heads = local_width // HD
     attention = kernel_attention if by_kernels else plain_attention
     attended, own_peaks, attention_back = attention(
-        seq_acts, full_in, out_rows, query_gain, key_gain, doc_ids
+        seq_acts, full_in, out_weight, query_gain, key_gain, doc_ids
     )
     start_head = lax.axis_index("gy") * local_heads
     peak_slots = lax.dynamic_update_slice(
@@ -2055,13 +2134,10 @@
     grad_moe_in = grad_moe_in + contract_cols(grad_logits_low, router_weight)
     grad_resid_norm, moe_gain_part = moe_pull(grad_moe_in)
     grad_resid = grad_out + grad_resid_norm
-    grad_acts, in_sum, out_part, query_gain_part, key_gain_part = attention_back(grad_resid)
+    grad_acts, in_sum, out_sum, query_gain_part, key_gain_part = attention_back(grad_resid)
     query_sum = in_sum[:, :local_width]
     key_sum = in_sum[:, local_width : 2 * local_width]
     value_sum = in_sum[:, 2 * local_width :]
-    out_sum_rows = lax.psum_scatter(
-        out_part.astype(jnp.bfloat16), "gx", scatter_dimension=0, tiled=True
-    ).astype(jnp.float32)
     norm_input_grad, attn_gain_part = norm_pull(grad_acts)
     input_grad = grad_resid + norm_input_grad
     small = (
@@ -2096,7 +2172,7 @@
         query_sum,
         key_sum,
         value_sum,
-        out_sum_rows.T,
+        out_sum.T,
         router_grad,
         gate_part[None],
         up_part[None],

time: 742 us -> 704 us (0.949)
  waiting for transfers between devices: 30 us -> 6.04 us
  between operations: 15.2 us -> 1.89 us
    all_gather x1 -> x0, waiting for transfers between devices: 23.4 us -> none  [local(): out_rows = lax.all_gather(out_weight, 'gx', axis=1, tiled=True)]
    pallas_call x1, Pallas kernels: 75.5 us -> 60.4 us  [leave(): pl.pallas_call(partial(leave_kernel, pieces, rows), out_shape=(jax.ShapeD...]
    pallas_call x1, Pallas kernels: 24.3 us -> 34.2 us  [attend(): pl.pallas_call(partial(attend_kernel, heads, pieces), out_shape=(jax.Shap...]
    pallas_call x1, Pallas kernels: 36.6 us -> 45.6 us  [attend_back(): pl.pallas_call(partial(attend_back_kernel, heads, pieces), out_shape=(jax...]
  transfers between devices with their start and end apart: 4 -> 2, of which waited for: 2 -> 1; matrix products, arithmetic and copies ran while one was open for 4% -> 0% of each run, Pallas kernels for 28% -> 16%
where the time goes in v7:
time: 704 us; the launch traced here: 703 us
  Pallas kernels  618 us (88%)
  local copies, waits for them, and re-layouts  32 us (5%)
  other arithmetic  30.5 us (4%)
  starting transfers between devices  11.3 us (2%)
    pallas_call x1, Pallas kernels, run_experts(): pl.pallas_call(partial(expert_kernel, n_z, span), out_shape=(jax.ShapeDty...  183 us
    pallas_call x1, Pallas kernels, enter(): pl.pallas_call(partial(enter_kernel, n_z, span), out_shape=(jax.ShapeDtyp...  115 us
    pallas_call x1, Pallas kernels, pull_experts(): pl.pallas_call(partial(pull_kernel, n_i, rows), out_shape=(jax.ShapeDtype...  111 us
    pallas_call x1, Pallas kernels, leave(): pl.pallas_call(partial(leave_kernel, pieces, rows), out_shape=(jax.ShapeD...  60.4 us
    pallas_call x1, Pallas kernels, attend_back(): pl.pallas_call(partial(attend_back_kernel, heads, pieces), out_shape=(jax...  45.6 us
    pallas_call x1, Pallas kernels, attend(): pl.pallas_call(partial(attend_kernel, heads, pieces), out_shape=(jax.Shap...  34.2 us
    pallas_call x1, Pallas kernels, all_gather(): pl.pallas_call(partial(gather_kernel, n_z, span), out_shape=jax.ShapeDtyp...  23.8 us
    pallas_call x1, Pallas kernels, scatter_plane(): pl.pallas_call(partial(scatter_kernel, False, pieces, rows), out_shape=ja...  23.3 us
  transfers between devices with their start and end apart: 2, of which 1 were waited for; matrix products, arithmetic and copies ran while one was open for 0% of the time, Pallas kernels for 16%

profile of v7, /device:TPU:0, one launch (start us, length us, event | category | flops | bytes accessed | tf_op | source)
XLA Modules:
  0.0 703.1 jit_solution(7426605539362258135)
XLA Ops:
  0.7 1.3 fusion.6
  2.0 0.5 copy-done.29
  2.5 2.0 fusion.11
  4.5 2.0 fusion.2
  6.6 0.9 pad_maximum_fusion.weight_ref
  7.5 1.3 pad_maximum_fusion.1
  8.8 115.5 %enter.1 = (bf16[8,2,64,2048]{3,2,1,0:T(8,128)(2,1)}, bf16[4,512,768]{2,1,0:T(8,128)(2,1)}, bf16[32,2,64,2048]{3,2,1,0:T(8,128)(2,1)}) custom-call(bf16[2,64,2048]{2,1,0:T(8,128)(2,1)} %bitcast.77, bf16[512,768]{1,0:T(8,128)(2,1)} %pad_maximum_fusion.weight_ref, bf16[2,64,2048]{2,1,0:T(8,128)(2,1)} %bitcast.71), custom_call_target="tpu_custom_call" | custom-call | tf_op jit(solution)/shard_map/enter/pallas_call | solution.py:541
  124.3 0.6 broadcast_in_dim.112.col_docs
  124.9 1.0 broadcast_in_dim.111.row_docs
  125.9 34.2 %attend.1 = (bf16[4,8,2,16,2048]{4,3,2,1,0:T(8,128)(2,1)}, f32[1024,256]{1,0:T(8,128)}, f32[1024,256]{1,0:T(8,128)}, bf16[1024,768]{1,0:T(8,128)(2,1)}, bf16[102...) custom-call(bf16[1024,2048]{1,0:T(8,128)(2,1)} %bitcast.60, ...), custom_call_target="tpu_custom_call" | custom-call | tf_op jit(solution)/shard_map/attend/pallas_call | solution.py:1510
  160.2 23.3 %scatter_plane.1 = f32[4,2,16,2048]{3,2,1,0:T(8,128)} custom-call(bf16[4,8,2,16,2048]{4,3,2,1,0:T(8,128)(2,1)} %get-tuple-element.46.part_ref), custom_call_target="tpu_custom_call" | custom-call | tf_op jit(solution)/shard_map/scatter_plane/pallas_call | solution.py:383
  183.6 1.5 multiply_reduce_fusion.2
  185.1 0.9 copy-done
  186.2 0.8 copy-done.4
  187.3 0.6 copy-done.14
  188.0 0.5 copy-done.19
  188.5 0.6 broadcast_in_dim.116
  189.1 2.6 all-to-all-start
  191.7 0.5 multiply_divide_fusion
  192.8 6.0 all-to-all-done
  198.8 1.9 broadcast_in_dim.118.share_ref
  200.8 183.1 %experts.1 = (bf16[4096,2048]{1,0:T(8,128)(2,1)}, bf16[4096,1024]{1,0:T(8,128)(2,1)}, f32[4096,128]{1,0:T(8,128)}, f32[512,2048]{1,0:T(8,128)}, f32[2,64,2048]{2,1,0:T(8,128)}) custom-call(bf16[2,64,2048]{2,1,0:T(8,128)(2,1)} %bitcast.70, bf16[4096,2048]{1,0:T(8,128)(2,1)} %bitcast.63, f32[4096,128]{1,0:T(8,128)} %broadcast_in_dim.118.share_ref, ...), custom_call_target="tpu_custom_call" | custom-call | tf_op jit(solution)/shard_map/experts/pallas_call | solution.py:1133
  383.9 2.8 reduce_sum.162
  386.7 8.7 %all-to-all-start.1 = ((f32[32,1,128]{2,1,0:T(1,128)}), f32[32,1,128]{2,1,0:T(1,128)}, u32[]{:S(2)}, u32[]{:S(2)}) async-start(f32[32,1,128]{2,1,0:T(1,128)} %bitcast.17), calls=%async_computation.1 | async-start | bytes 32768 | tf_op jit(solution)/shard_map/all_to_all | solution.py:1899
  395.4 0.8 slice_reduce_fusion.1
  397.0 0.6 reshape.223
  397.6 111.1 %pull_experts.1 = (f32[2,64,2048]{2,1,0:T(8,128)}, f32[2048,512]{1,0:T(8,128)}, f32[2048,512]{1,0:T(8,128)}) custom-call(bf16[4096,2048]{1,0:T(8,128)(2,1)} %get-tuple-element.49.all_ref, bf16[4096,1024]{1,0:T(8,128)(2,1)} %get-tuple-element.50.pair_ref, bf16[2048,512]{1,0:T(8,128)(2,1)} %bitcast.67, bf16[2048,512]{1,0:T(8,128)(2,1)} %bitcast.69), custom_call_target="tpu_custom_call" | custom-call | tf_op jit(solution)/shard_map/pull_experts/pallas_call | solution.py:1358
  508.8 0.9 reduce_sum.163
  509.7 0.7 select_reduce_fusion.3
  510.4 0.7 multiply_reduce_fusion.4
  511.1 0.7 divide_add_fusion
  511.8 0.7 select_reduce_fusion.2
  512.5 0.7 multiply_reduce_fusion.3
  513.2 0.7 multiply_convert_fusion.3
  513.9 1.2 convolution_bitcast_fusion
  515.2 2.1 multiply_reduce_fusion
  517.4 1.2 fusion.17
  518.5 23.8 %gather_plane.1 = bf16[8,2,64,2048]{3,2,1,0:T(8,128)(2,1)} custom-call(bf16[2,64,2048]{2,1,0:T(8,128)(2,1)} %bitcast.78), custom_call_target="tpu_custom_call" | custom-call | tf_op jit(solution)/shard_map/gather_plane/pallas_call | solution.py:229
  542.4 45.6 %attend_back.1 = (bf16[4,8,2,16,2048]{4,3,2,1,0:T(8,128)(2,1)}, bf16[2048,768]{1,0:T(8,128)(2,1)}, f32[512,256]{1,0:T(8,128)}, f32[8,128]{1,0:T(8,128)}) custom-call(bf16[1024,2048]{1,0:T(8,128)(2,1)} %bitcast.62, bf16[4,256,512]{2,1,0:T(8,128)(2,1)} %get-tuple-element.53.out_weight_ref, bf16[1024,256]{1,0:T(8,128)(2,1)} %get-tuple-element.54.mixed_ref, ...), custom_call_target="tpu_custom_call" | custom-call | tf_op jit(solution)/shard_map/attend_back/pallas_call | solution.py:1704
  588.1 60.4 %leave.1 = (f32[4,2,16,2048]{3,2,1,0:T(8,128)}, f32[512,768]{1,0:T(8,128)}) custom-call(bf16[4,8,2,16,2048]{4,3,2,1,0:T(8,128)(2,1)} %get-tuple-element.59.part_ref, bf16[4,512,768]{2,1,0:T(8,128)(2,1)} %bitcast.75), custom_call_target="tpu_custom_call" | custom-call | tf_op jit(solution)/shard_map/leave/pallas_call | solution.py:712
  648.6 2.1 fusion.3
  650.7 0.7 constant_dynamic-update-slice_fusion.3
  651.4 0.7 constant_dynamic-update-slice_fusion.2
  652.1 0.7 pad.4
  652.8 20.6 %sum_everywhere.1 = f32[2,152,128]{2,1,0:T(8,128)} custom-call(f32[2,152,128]{2,1,0:T(8,128)} %bitcast.83), custom_call_target="tpu_custom_call" | custom-call | tf_op jit(solution)/shard_map/sum_everywhere/pallas_call | solution.py:474
  673.5 1.3 fusion.19
  674.7 1.3 fusion.20
  676.0 0.9 slice.63
  677.0 2.3 slice.57
  679.3 2.6 fusion.18
  681.8 0.5 multiply_multiply_fusion
  682.4 0.7 reshape.226
  683.0 2.0 copy.49
  685.1 0.7 slice_reduce_fusion
  685.8 1.3 sort.15
  687.1 0.6 fusion.14
  687.7 0.6 compare_select_fusion
  688.5 1.8 multiply_convert_fusion.1
  690.3 3.3 fusion.5
  693.7 2.1 copy.62
  695.8 1.6 copy-done.7
  697.4 2.1 copy.63
  699.5 1.6 copy-done.6
  701.1 2.0 copy.64
  (91 shorter events, 1.6 us)
Async XLA Ops:
  0.7 5.9 copy-start.9
  0.7 5.9 copy-start.11
  0.7 5.9 copy-start.12
  2.0 0.5 copy-start.29
  2.5 2.0 copy-start.24
  6.6 117.8 %copy-start.20 = (s32[1024]{0:T(1024)S(1)}, s32[1024]{0:T(1024)}, u32[]{:S(2)}) copy-start(s32[1024]{0:T(1024)} %param.20) | copy-start | bytes 12292
  160.2 23.4 %copy-start.2 = (bf16[128,2048]{1,0:T(8,128)(2,1)S(1)}, bf16[128,2048]{1,0:T(8,128)(2,1)}, u32[]{:S(2)}) copy-start(bf16[128,2048]{1,0:T(8,128)(2,1)} %param.17) | copy-start | bytes 1572868
  160.2 25.8 %copy-start.15 = (f32[2048]{0:T(1024)S(1)}, f32[2048]{0:T(1024)}, u32[]{:S(2)}) copy-start(f32[2048]{0:T(1024)} %param.23) | copy-start | bytes 24580
  183.6 3.4 copy-start.13
  183.6 4.3 copy-start.18
  185.1 1.0 copy-start
  185.1 4.1 copy-start.33
  185.1 0.9 copy-start.22
  186.2 0.8 copy-start.4
  187.2 0.6 copy-start.14
  187.3 1.9 copy-start.21
  187.9 11.0 %copy-start.26 = (f32[128]{0:T(128)}, f32[128]{0:T(128)S(1)}, u32[]{:S(2)}) copy-start(f32[128]{0:T(128)S(1)} %fusion.13) | copy-start | bytes 1540
  187.9 0.6 copy-start.19
  187.9 10.9 %copy-start.27 = (f32[128]{0:T(128)}, f32[128]{0:T(128)S(1)}, u32[]{:S(2)}) copy-start(f32[128]{0:T(128)S(1)} %get-tuple-element.176) | copy-start | bytes 1540
  189.1 9.7 %all-to-all-start = ((f32[32,1,128]{2,1,0:T(1,128)}), f32[32,1,128]{2,1,0:T(1,128)S(1)}, u32[]{:S(2)}, u32[]{:S(2)}) async-start(f32[32,1,128]{2,1,0:T(1,128)} %bitcast.10), calls=%async_computation | async-start | bytes 32768 | tf_op jit(solution)/shard_map/all_to_all | solution.py:1891
  386.7 122.1 %all-to-all-start.1 = ((f32[32,1,128]{2,1,0:T(1,128)}), f32[32,1,128]{2,1,0:T(1,128)}, u32[]{:S(2)}, u32[]{:S(2)}) async-start(f32[32,1,128]{2,1,0:T(1,128)} %bitcast.17), calls=%async_computation.1 | async-start | bytes 32768 | tf_op jit(solution)/shard_map/all_to_all | solution.py:1899
  508.8 8.6 %copy-start.34 = (f32[128]{0:T(128)S(1)}, f32[128]{0:T(128)}, u32[]{:S(2)}) copy-start(f32[128]{0:T(128)} %copy-done.33) | copy-start | bytes 1540
  508.8 8.6 %copy-start.1 = (f32[128,2048]{1,0:T(8,128)S(1)}, f32[128,2048]{1,0:T(8,128)}, u32[]{:S(2)}) copy-start(f32[128,2048]{1,0:T(8,128)} %copy-done) | copy-start | bytes 3145732
  508.8 8.6 %copy-start.5 = (bf16[128,2048]{1,0:T(8,128)(2,1)S(1)}, bf16[128,2048]{1,0:T(8,128)(2,1)}, u32[]{:S(2)}) copy-start(bf16[128,2048]{1,0:T(8,128)(2,1)} %param.18) | copy-start | bytes 1572868
  508.8 8.6 %copy-start.16 = (f32[2048]{0:T(1024)S(1)}, f32[2048]{0:T(1024)}, u32[]{:S(2)}) copy-start(f32[2048]{0:T(1024)} %param.23) | copy-start | bytes 24580
  508.8 8.6 %copy-start.23 = (f32[128]{0:T(128)S(1)}, f32[128]{0:T(128)}, u32[]{:S(2)}) copy-start(f32[128]{0:T(128)} %copy-done.22) | copy-start | bytes 1540
  517.3 25.1 %copy-start.28 = (f32[128]{0:T(128)}, f32[128]{0:T(128)S(1)}, u32[]{:S(2)}) copy-start(f32[128]{0:T(128)S(1)} %multiply_multiply_fusion.1) | copy-start | bytes 1540
  588.1 60.5 %copy-start.3 = (bf16[128,2048]{1,0:T(8,128)(2,1)S(1)}, bf16[128,2048]{1,0:T(8,128)(2,1)}, u32[]{:S(2)}) copy-start(bf16[128,2048]{1,0:T(8,128)(2,1)} %param.17) | copy-start | bytes 1572868
  588.1 60.5 %copy-start.17 = (f32[2048]{0:T(1024)S(1)}, f32[2048]{0:T(1024)}, u32[]{:S(2)}) copy-start(f32[2048]{0:T(1024)} %param.22) | copy-start | bytes 24580
  588.1 60.5 %copy-start.25 = (f32[128]{0:T(128)S(1)}, f32[128]{0:T(128)}, u32[]{:S(2)}) copy-start(f32[128]{0:T(128)} %copy-done.24) | copy-start | bytes 1540
  588.1 64.0 %copy-start.32 = (f32[64]{0:T(128)S(1)}, f32[64]{0:T(128)}, u32[]{:S(2)}) copy-start(f32[64]{0:T(128)} %reshape.223) | copy-start | bytes 772
  673.4 15.0 %copy-start.10 = (bf16[512,256]{1,0:T(8,128)(2,1)S(1)}, bf16[512,256]{1,0:T(8,128)(2,1)}, u32[]{:S(2)}) copy-start(bf16[512,256]{1,0:T(8,128)(2,1)} %param.27) | copy-start | bytes 786436
  679.3 2.6 copy-start.30
  679.3 2.6 copy-start.31
  688.3 5.4 copy-start.35
  690.3 3.3 copy-start.8
  693.7 3.7 copy-start.7
  697.4 3.7 copy-start.6

commit v8 on v7

--- a/solution.py
+++ b/solution.py
@@ -142,8 +142,11 @@
     for d in range(1, n_z):
         items += [(z >= d, z - d, -d), (z < n_z - d, z + d, d)]
 
-    def first(item):
-        ok, owner, d = item
+    upward = [always(item[0], z < n_z - 1) for item in items]
+    downward = [always(item[0], z > 0) for item in items]
+
+    def first(i):
+        ok, owner, d = items[i]
         b = owner * span + g
         if d == 0:
             local.start()
@@ -154,9 +157,9 @@
             source = out_ref.at[b]
         for h in range(2):
             if n_z > 1 and d <= 0:
-                send(always(ok, z < n_z - 1), source.at[h], b, h, above)
+                send(upward[i], source.at[h], b, h, above)
             if n_z > 1 and d >= 0:
-                send(always(ok, z > 0), source.at[h], b, h, below)
+                send(downward[i], source.at[h], b, h, below)
         send(ok, source.at[0], b, 0, x_peer)
         send(ok, source.at[1], b, 1, y_peer)
         send(ok, source.at[1], b, 1, x_peer)
@@ -183,7 +186,7 @@
 
     def step(i):
         if i < n:
-            first(items[i])
+            first(i)
         if 1 <= i <= n:
             second(items[i - 1])
         if i >= 2:
@@ -254,7 +257,7 @@
 
 
 def scatter_kernel(chain, n_i, rows, part_ref, out_ref, held, from_core, from_a, from_b, from_z,
-                   load_sem, core_send, a_send, b_send, z_send, core_recv, a_recv, b_recv, z_recv, beside=None):
+                   load_sem, core_send, a_send, b_send, z_send, core_recv, a_recv, b_recv, z_recv, beside=None, parts=None):
     z = lax.axis_index("gx"); g = lax.axis_index("gy")
     flip_x = g + 2 - 4 * ((g // 2) % 2)
     flip_y = g + 4 - 8 * ((g // 4) % 2)
@@ -269,7 +272,8 @@
     if beside:
         n_z = lax.axis_size("gx")
         partners += [(z < n_z - 1, {"gx": z + 1, "gy": g}), (z > 0, {"gx": z - 1, "gy": g})]
-    barrier_with(partners)
+    if parts is None:
+        barrier_with(partners)
     if beside:
         beside[0]()
     mesh_id = pl.DeviceIdType.MESH
@@ -311,10 +315,11 @@
         it = item(i)
         return remote(held.at[it, 3], from_z.at[it], z_send.at[i], z_recv.at[it], core)
 
-    for i in range(n_i):
-        for q in range(4):
-            core_copy(i, q).start()
-            load(i, q).start()
+    def begin():
+        for i in range(n_i):
+            for q in range(4):
+                core_copy(i, q).start()
+                load(i, q).start()
 
     def stage_a(i):
         it = item(i)
@@ -357,56 +362,40 @@
                     rows,
                 )
 
+    def step(i):
+        if i < n_i:
+            stage_a(i)
+        if 0 <= i - 1 < n_i:
+            stage_b(i - 1)
+        if 0 <= i - 2 < n_i:
+            stage_c(i - 2)
+        if chain and 0 <= i - 2 < n_i:
+            stage_d(i - 2)
+
+    def finish():
+        for i in range(n_i):
+            for q in range(4):
+                core_copy(i, q).wait_send()
+            for k in range(4):
+                a_copy(i, k).wait_send()
+            for h in range(2):
+                b_copy(i, h).wait_send()
+            if chain and i < n_i - 1:
+                z_copy(i).wait_send()
+
+    if parts is not None:
+        parts.extend([begin] + [partial(step, i) for i in range(n_i + 2)] + [finish])
+        return
+    begin()
     for i in range(n_i + 2):
-        if i < n_i: stage_a(i)
-        if 0 <= i - 1 < n_i: stage_b(i - 1)
-        if 0 <= i - 2 < n_i: stage_c(i - 2)
-        if chain and 0 <= i - 2 < n_i: stage_d(i - 2)
+        step(i)
         if beside and i == n_i:
             beside[1][0]()
     if beside:
         for relay in beside[1][1:]:
             relay()
         beside[2]()
-    for i in range(n_i):
-        for q in range(4): core_copy(i, q).wait_send()
-        for k in range(4): a_copy(i, k).wait_send()
-        for h in range(2): b_copy(i, h).wait_send()
-        if chain and i < n_i - 1: z_copy(i).wait_send()
-
-
-def scatter_plane(part, collective_id):
-    span = lax.axis_size("gy")
-    pieces, _, _, rows, cols = part.shape
-    dma = pltpu.SemaphoreType.DMA
-    half = (rows, cols)
-    out = pl.pallas_call(
-        partial(scatter_kernel, False, pieces, rows),
-        out_shape=jax.ShapeDtypeStruct((pieces, 2, rows, cols), jnp.float32),
-        in_specs=[pl.BlockSpec(memory_space=pl.ANY)],
-        out_specs=pl.BlockSpec(memory_space=pltpu.VMEM),
-        scratch_shapes=[
-            pltpu.VMEM((pieces, 4, 2) + half, jnp.bfloat16),
-            pltpu.VMEM((pieces, 4, 2) + half, jnp.bfloat16),
-            pltpu.VMEM((pieces, 2, 2) + half, jnp.bfloat16),
-            pltpu.VMEM((pieces, 2) + half, jnp.bfloat16),
-            pltpu.VMEM((1, 2, 16, 128), jnp.bfloat16),
-            dma((pieces, 4)),
-            dma((pieces, 4)),
-            dma((pieces, 4)),
-            dma((pieces, 2)),
-            dma((pieces,)),
-            dma((pieces, 4)),
-            dma((pieces, 2, 2)),
-            dma((pieces, 2)),
-            dma((pieces,)),
-        ],
-        compiler_params=pltpu.CompilerParams(
-            collective_id=collective_id, has_side_effects=True, vmem_limit_bytes=60 << 20
-        ),
-        name="scatter_plane",
-    )(part)
-    return out.reshape(pieces * 2 * rows, cols)
+    finish()
 
 
 def sum_kernel(n_z, bits, vec_ref, out_ref, held, arrived, from_z, send_sem, z_send, recv_sem, z_recv):
@@ -489,83 +478,6 @@
         name="sum_everywhere",
     )(padded)
     return out.reshape(-1)[:length]
-
-
-def enter_kernel(
-    n_z,
-    span,
-    acts_ref,
-    weight_ref,
-    cot_ref,
-    seq_ref,
-    full_ref,
-    all_cot_ref,
-    send_sem,
-    recv_sem,
-    local_sem,
-    chain_send,
-    chain_recv,
-    chain_local,
-    cot_send,
-    cot_recv,
-    cot_local,
-):
-    greet(n_z)
-    start, relays, end_chain = chain_gather(
-        n_z, weight_ref, full_ref, chain_send, chain_recv, chain_local
-    )
-    near, end_near = gather_steps(1, span, acts_ref, seq_ref, send_sem, recv_sem, local_sem)
-    far, end_far = gather_steps(n_z, span, cot_ref, all_cot_ref, cot_send, cot_recv, cot_local)
-    start()
-    near[0]()
-    far[0]()
-    near[1]()
-    near[2]()
-    for k, step in enumerate(far[1:]):
-        if k % 2 == 0 and k // 2 < len(relays):
-            relays[k // 2]()
-        step()
-    for relay in relays[len(far) // 2 :]:
-        relay()
-    end_chain()
-    end_near()
-    end_far()
-
-
-def enter(acts, weights, cotangent, collective_id):
-    n_z = lax.axis_size("gx")
-    span = lax.axis_size("gy")
-    rows, cols = acts.shape
-    dma = pltpu.SemaphoreType.DMA
-    half = (2, rows // 2, cols)
-    seq, full, all_cot = pl.pallas_call(
-        partial(enter_kernel, n_z, span),
-        out_shape=(
-            jax.ShapeDtypeStruct((span,) + half, acts.dtype),
-            jax.ShapeDtypeStruct((n_z,) + weights.shape, weights.dtype),
-            jax.ShapeDtypeStruct((n_z * span,) + half, cotangent.dtype),
-        ),
-        in_specs=[pl.BlockSpec(memory_space=pltpu.VMEM)] * 3,
-        out_specs=(pl.BlockSpec(memory_space=pl.ANY),) * 3,
-        scratch_shapes=[
-            dma((24,)),
-            dma((span, 2)),
-            dma,
-            dma((2 * n_z,)),
-            dma((n_z,)),
-            dma,
-            dma((24 * (2 * n_z - 1),)),
-            dma((n_z * span, 2)),
-            dma,
-        ],
-        compiler_params=pltpu.CompilerParams(collective_id=collective_id, has_side_effects=True),
-        name="enter",
-    )(acts.reshape(half), weights, cotangent.reshape(half))
-    return (
-        seq.reshape(span * rows, cols),
-        full.reshape(n_z * weights.shape[0], weights.shape[1]),
-        all_cot.reshape(n_z * span * rows, cols),
-    )
 
 
 def chain_scatter(n_z, part_ref, out_ref, from_low, from_high, send_sem, low_recv, high_recv):
@@ -754,7 +666,8 @@
                   gate_val, up_val, scaled, scaled_t, down_t,
                   held, from_core, from_a, from_b, from_z,
                   send_sem, recv_sem, local_sem, fetch_sem, store_sem,
-                  core_send, a_send, b_send, z_send, core_recv, a_recv, b_recv, z_recv):
+                  core_send, a_send, b_send, z_send, core_recv, a_recv, b_recv, z_recv,
+                  shares_in, dots_own, share_send, share_recv, dots_send, dots_recv):
     z = lax.axis_index("gx")
     g = lax.axis_index("gy")
     rows = own_ref.shape[1]
@@ -790,8 +703,72 @@
                 jnp.logical_and(owner > z, z > 0),
             )
         )
-    along = [{"gx": lax.rem(z + j, n_z), "gy": g} for j in range(1, n_z)]
-    barrier_with([(z >= 0, peer) for peer in (core, x_peer, y_peer, *along)])
+    devices = n_z * span
+    rank = z * span + g
+
+    def device(number):
+        return {"gx": lax.div(number, span), "gy": lax.rem(number, span)}
+
+    barrier = pltpu.get_barrier_semaphore()
+
+    @pl.loop(1, devices)
+    def _(j):
+        pl.semaphore_signal(
+            barrier,
+            inc=1,
+            device_id=device(lax.rem(rank + j, devices)),
+            device_id_type=pl.DeviceIdType.MESH,
+        )
+
+    pl.semaphore_wait(barrier, devices - 1)
+
+    def share_copy(number):
+        return pltpu.make_async_remote_copy(
+            src_ref=share_ref.at[number],
+            dst_ref=shares_in.at[rank],
+            send_sem=share_send.at[number],
+            recv_sem=share_recv.at[rank],
+            device_id=device(number),
+            device_id_type=pl.DeviceIdType.MESH,
+        )
+
+    def share_arrival(number):
+        return pltpu.make_async_remote_copy(
+            src_ref=share_ref.at[number],
+            dst_ref=shares_in.at[number],
+            send_sem=share_send.at[number],
+            recv_sem=share_recv.at[number],
+            device_id=core,
+            device_id_type=pl.DeviceIdType.MESH,
+        )
+
+    def dots_copy(number):
+        return pltpu.make_async_remote_copy(
+            src_ref=dots_own.at[number],
+            dst_ref=dots_ref.at[rank],
+            send_sem=dots_send.at[number],
+            recv_sem=dots_recv.at[rank],
+            device_id=device(number),
+            device_id_type=pl.DeviceIdType.MESH,
+        )
+
+    def dots_arrival(number):
+        return pltpu.make_async_remote_copy(
+            src_ref=dots_own.at[number],
+            dst_ref=dots_ref.at[number],
+            send_sem=dots_send.at[number],
+            recv_sem=dots_recv.at[number],
+            device_id=core,
+            device_id_type=pl.DeviceIdType.MESH,
+        )
+
+    def for_others(action):
+        @pl.loop(1, devices)
+        def _(j):
+            action(lax.rem(rank + j, devices))
+
+    for_others(lambda number: share_copy(number).start())
+    shares_in[rank] = share_ref[rank]
 
     def at(owner, gg, h):
         return pl.ds(pl.multiple_of((owner * span + gg) * block + h * rows, rows), rows)
@@ -866,6 +843,12 @@
             for item in locals_:
                 item.wait()
 
+    def owner_of(s):
+        if isinstance(s, int):
+            return order[s // 2]
+        k = lax.div(s, 2)
+        return sum((k == j).astype(jnp.int32) * order[j] for j in range(n_z))
+
     def place(s):
         k, side = (s // 2, s % 2) if isinstance(s, int) else (lax.div(s, 2), lax.rem(s, 2))
         if isinstance(s, int):
@@ -882,18 +865,16 @@
         return [
             pltpu.make_async_copy(source.at[place(s)], target.at[slot], fetch_sem.at[j, slot])
             for j, (source, target) in enumerate(
-                ((all_ref, moe_buf), (cot_ref, cot_buf), (share_ref, share_buf))
+                ((all_ref, moe_buf), (cot_ref, cot_buf))
             )
         ]
 
     def stores(s):
         slot = parity(s)
-        pairs = ((dots_buf, dots_ref), (pair_stage, pair_ref))
         return [
             pltpu.make_async_copy(
-                pairs[j][0].at[slot], pairs[j][1].at[place(s)], store_sem.at[j, slot]
+                pair_stage.at[slot], pair_ref.at[place(s)], store_sem.at[0, slot]
             )
-            for j in range(2)
         ]
 
     f32 = jnp.float32
@@ -1017,11 +998,13 @@
     complete(0)
     for item in fetches(0):
         item.start()
+    for_others(lambda number: share_arrival(number).wait_recv())
 
     @pl.loop(0, steps)
     def _(s):
         slot = lax.rem(s, 2)
-        moe, cot, share = moe_buf.at[slot], cot_buf.at[slot], share_buf.at[slot]
+        moe, cot, share = moe_buf.at[slot], cot_buf.at[slot], share_buf
+        first_device = owner_of(s) * span + slot * (span // 2)
         for item in fetches(s):
             item.wait()
 
@@ -1030,6 +1013,9 @@
             for item in stores(s - 2):
                 item.wait()
 
+        for j in range(span // 2):
+            column = jnp.broadcast_to(shares_in[first_device + j], (block, block)).T
+            share[j * block : (j + 1) * block, :] = column
         wide = jnp.concatenate([share[...]] * (tile // share.shape[1]), axis=1)
 
         @pl.loop(0, half_width // tile)
@@ -1053,7 +1039,7 @@
             )
 
         events(s, 2)
-        dots_buf[slot] = jnp.zeros(dots_buf.shape[1:], f32)
+        dots_buf[...] = jnp.zeros(dots_buf.shape, f32)
 
         @pl.loop(0, half_width // tile)
         def _(t):
@@ -1065,7 +1051,7 @@
             silu = gated * sig
             product = pulled * (silu * lifted)
             lanes = share.shape[1]
-            dots_buf[slot] = dots_buf[slot] + sum(
+            dots_buf[...] = dots_buf[...] + sum(
                 product[:, j * lanes : (j + 1) * lanes] for j in range(tile // lanes)
             )
             pulled = pulled * wide
@@ -1077,6 +1063,18 @@
 
         for item in stores(s):
             item.start()
+        for j in range(span // 2):
+            number = first_device + j
+            rows_of = dots_buf[j * block : (j + 1) * block, :]
+            dots_own[number] = jnp.sum(rows_of.T, axis=0, keepdims=True)
+
+        for j in range(span // 2):
+            number = first_device + j
+
+            @pl.when(number != rank)
+            def _():
+                dots_copy(number).start()
+
         events(s, 3)
         events(s, 4)
 
@@ -1116,6 +1114,10 @@
             z_copy(k).wait_send()
     for ok, make, k in sends:
         run_if(ok, lambda make=make: make().wait_send())
+    dots_ref[rank] = dots_own[rank]
+    for_others(lambda number: dots_arrival(number).wait_recv())
+    for_others(lambda number: share_copy(number).wait_send())
+    for_others(lambda number: dots_copy(number).wait_send())
 
 
 def run_experts(moe_in, all_cot, shares, gate_w, up_w, down_w, collective_id):
@@ -1125,7 +1127,8 @@
     half = down_w.shape[0]
     total = n_z * span * rows
     step = span * rows // 2
-    lanes = shares.shape[1]
+    lanes = 128
+    devices = n_z * span
     bf16, f32 = jnp.bfloat16, jnp.float32
     dma = pltpu.SemaphoreType.DMA
     vmem = pl.BlockSpec(memory_space=pltpu.VMEM)
@@ -1135,18 +1138,18 @@
         out_shape=(
             jax.ShapeDtypeStruct((total, width), bf16),
             jax.ShapeDtypeStruct((total, 2 * half), bf16),
-            jax.ShapeDtypeStruct((total, lanes), f32),
+            jax.ShapeDtypeStruct((devices, 1, rows), f32),
             jax.ShapeDtypeStruct((half, width), f32),
             jax.ShapeDtypeStruct((2, rows // 2, width), f32),
         ),
-        in_specs=[vmem, hbm, hbm, vmem, vmem, vmem],
-        out_specs=(hbm, hbm, hbm, vmem, vmem),
+        in_specs=[vmem, hbm, vmem, vmem, vmem, vmem],
+        out_specs=(hbm, hbm, vmem, vmem, vmem),
         scratch_shapes=[
             pltpu.VMEM((2, step, width), bf16),
             pltpu.VMEM((2, step, width), bf16),
-            pltpu.VMEM((2, step, lanes), f32),
+            pltpu.VMEM((step, lanes), f32),
             pltpu.VMEM((2, step, 2 * half), bf16),
-            pltpu.VMEM((2, step, lanes), f32),
+            pltpu.VMEM((step, lanes), f32),
             pltpu.VMEM((step, half), f32),
             pltpu.VMEM((step, half), f32),
             pltpu.VMEM((step, half), bf16),
@@ -1170,6 +1173,12 @@
             dma((n_z, 2, 2)),
             dma((n_z, 2)),
             dma((n_z,)),
+            pltpu.VMEM((devices, 1, rows), f32),
+            pltpu.VMEM((devices, 1, rows), f32),
+            dma((devices,)),
+            dma((devices,)),
+            dma((devices,)),
+            dma((devices,)),
         ],
         compiler_params=pltpu.CompilerParams(
             collective_id=collective_id, has_side_effects=True, vmem_limit_bytes=67043328
@@ -1403,45 +1412,132 @@
 def attend_kernel(
     heads,
     pieces,
-    acts_ref,
-    weight_ref,
-    out_weight_ref,
+    own_acts,
+    own_weight,
+    own_out_weight,
+    own_cot,
     query_gain,
     key_gain,
     cosine_ref,
     sine_ref,
     row_docs,
     col_docs,
-    part_ref,
+    attended_ref,
+    acts_out,
+    weight_out,
+    full_out,
+    all_cot,
     query_raw,
     key_raw,
     ready_ref,
     mixed_ref,
     totals_ref,
     peaks_ref,
-    full_out,
-    chain_send,
-    chain_recv,
-    chain_local,
+    part_ref,
+    held,
+    from_core,
+    from_a,
+    from_b,
+    from_z,
+    near_send,
+    near_recv,
+    near_local,
+    far_send,
+    far_recv,
+    far_local,
+    in_send,
+    in_recv,
+    in_local,
+    out_send,
+    out_recv,
+    out_local,
+    load_sem,
+    core_send,
+    a_send,
+    b_send,
+    z_send,
+    core_recv,
+    a_recv,
+    b_recv,
+    z_recv,
 ):
     n_z = lax.axis_size("gx")
-    greet_chain(n_z)
-    start, relays, finish = chain_gather(
-        n_z, out_weight_ref, full_out, chain_send, chain_recv, chain_local
-    )
-    start()
+    span = lax.axis_size("gy")
+    greet(n_z)
+    in_start, in_relays, in_finish = chain_gather(
+        n_z, own_weight, weight_out, in_send, in_recv, in_local
+    )
+    out_start, out_relays, out_finish = chain_gather(
+        n_z, own_out_weight, full_out, out_send, out_recv, out_local
+    )
+    near, near_finish = gather_steps(1, span, own_acts, acts_out, near_send, near_recv, near_local)
+    far, far_finish = gather_steps(n_z, span, own_cot, all_cot, far_send, far_recv, far_local)
+    back = []
+    scatter_kernel(
+        False,
+        pieces,
+        part_ref.shape[3],
+        part_ref,
+        attended_ref,
+        held,
+        from_core,
+        from_a,
+        from_b,
+        from_z,
+        load_sem,
+        core_send,
+        a_send,
+        b_send,
+        z_send,
+        core_recv,
+        a_recv,
+        b_recv,
+        z_recv,
+        parts=back,
+    )
     f32, bf16 = jnp.float32, jnp.bfloat16
     dot = partial(lax.dot_general, preferred_element_type=f32)
     plain = (((1,), (0,)), ((), ()))
     last_dims = (((1,), (1,)), ((), ()))
-    length = acts_ref.shape[0]
-    span = part_ref.shape[1]
+    length = query_raw.shape[0]
+    width = acts_out.shape[3]
     local = heads * HD
     block = 256
     scale = HD ** (-0.5)
 
+    in_start()
+    near[0]()
+    far[0]()
+    near[1]()
+    near[2]()
+    later = far[1:]
+    for relay in in_relays:
+        relay()
+        for step in later[:1]:
+            step()
+        later = later[1:]
+    out_start()
+    in_finish()
+    near_finish()
+    waiting = [list(out_relays), list(later)]
+
+    def pull(which):
+        if waiting[which]:
+            waiting[which].pop(0)()
+
+    def project(source):
+        cols = slice(source * local, (source + 1) * local)
+        acts = acts_out[...].reshape(length, width)
+        total = jnp.zeros((length, local), f32)
+        depth = own_weight.shape[0]
+        for owner in range(n_z):
+            total = total + dot(
+                acts[:, owner * depth : (owner + 1) * depth], weight_out[owner, :, cols], plain
+            )
+        return total
+
     for source, raw, gain in ((0, query_raw, query_gain), (1, key_raw, key_gain)):
-        raw[...] = dot(acts_ref[...], weight_ref[:, source * local : (source + 1) * local], plain)
+        raw[...] = project(source)
         for h in range(heads):
             cols = slice(h * HD, (h + 1) * HD)
 
@@ -1454,15 +1550,14 @@
                 where = source * local + h * HD
                 ready_ref[at, where : where + HD] = turned.astype(bf16)
 
-        if source < len(relays) - 1:
-            relays[source]()
-
-    ready_ref[:, 2 * local :] = dot(acts_ref[...], weight_ref[:, 2 * local :], plain).astype(bf16)
+        pull(source)
+
+    ready_ref[:, 2 * local :] = project(2).astype(bf16)
+    pull(0)
     lanes = lax.broadcasted_iota(jnp.int32, (block, HD), 1)
     peaks_ref[...] = jnp.full(peaks_ref.shape, NEGATIVE, f32)
 
-    @pl.loop(0, length // block)
-    def _(t):
+    def mix(t):
         at = pl.ds(pl.multiple_of(t * block, block), block)
         same = row_docs[at, :1] == col_docs[:1, :]
         kept = jnp.zeros((block, HD), f32)
@@ -1481,11 +1576,19 @@
             peaks_ref[h : h + 1, :] = jnp.maximum(peaks_ref[h : h + 1, :], top)
         totals_ref[at, :] = kept
 
-    for relay in relays[min(2, len(relays) - 1) :]:
+    blocks = length // block
+    for quarter in range(2):
+
+        @pl.loop(quarter * blocks // 2, (quarter + 1) * blocks // 2)
+        def _(t):
+            mix(t)
+
+        pull(1)
+    for relay in waiting[0]:
         relay()
-    finish()
+    out_finish()
     rows = part_ref.shape[3]
-    per_owner = out_weight_ref.shape[1] // block
+    per_owner = own_out_weight.shape[1] // block
 
     @pl.loop(0, n_z * per_owner)
     def _(t):
@@ -1496,44 +1599,98 @@
         for p in range(pieces):
             part_ref[p, :, :, :, cols] = sent[:, p]
 
-
-def attend(acts, weights, out_weight, query_gain, key_gain, tables, docs, collective_id, pieces=4):
-    length, width = acts.shape
+    for step in back[:-1]:
+        step()
+        pull(1)
+    for step in waiting[1]:
+        step()
+    back[-1]()
+    far_finish()
+
+
+def attend(
+    acts, weights, out_weight, cot, query_gain, key_gain, tables, docs, collective_id, pieces=4
+):
+    tokens, width = acts.shape
     local = weights.shape[1] // 3
     heads = local // HD
+    n_z = lax.axis_size("gx")
     span = lax.axis_size("gy")
-    n_z = lax.axis_size("gx")
-    rows = length // (span * pieces * 2)
+    length = span * tokens
+    rows = tokens // (pieces * 2)
+    half = (2, tokens // 2, width)
+    piece = (rows, width)
     f32, bf16 = jnp.float32, jnp.bfloat16
     dma = pltpu.SemaphoreType.DMA
     vmem = pl.BlockSpec(memory_space=pltpu.VMEM)
-    return pl.pallas_call(
+    hbm = pl.BlockSpec(memory_space=pl.ANY)
+    attended, seq, full, full_out, all_cot, *saved, peaks = pl.pallas_call(
         partial(attend_kernel, heads, pieces),
         out_shape=(
-            jax.ShapeDtypeStruct((pieces, span, 2, rows, width), bf16),
+            jax.ShapeDtypeStruct((pieces, 2) + piece, f32),
+            jax.ShapeDtypeStruct((span,) + half, bf16),
+            jax.ShapeDtypeStruct((n_z,) + weights.shape, bf16),
+            jax.ShapeDtypeStruct((n_z,) + out_weight.shape, bf16),
+            jax.ShapeDtypeStruct((n_z * span,) + half, bf16),
             jax.ShapeDtypeStruct((length, local), f32),
             jax.ShapeDtypeStruct((length, local), f32),
             jax.ShapeDtypeStruct((length, 3 * local), bf16),
             jax.ShapeDtypeStruct((length, local), bf16),
             jax.ShapeDtypeStruct((length, HD), f32),
             jax.ShapeDtypeStruct((8, HD), f32),
-            jax.ShapeDtypeStruct((n_z,) + out_weight.shape, bf16),
         ),
-        in_specs=[vmem] * 9,
-        out_specs=(vmem,) * 8,
-        scratch_shapes=[dma((2 * n_z,)), dma((n_z,)), dma],
+        in_specs=[vmem] * 10,
+        out_specs=(vmem, vmem, vmem, vmem, hbm) + (vmem,) * 6,
+        scratch_shapes=[
+            pltpu.VMEM((pieces, span, 2) + piece, bf16),
+            pltpu.VMEM((pieces, 4, 2) + piece, bf16),
+            pltpu.VMEM((pieces, 4, 2) + piece, bf16),
+            pltpu.VMEM((pieces, 2, 2) + piece, bf16),
+            pltpu.VMEM((pieces, 2) + piece, bf16),
+            pltpu.VMEM((1, 2, 16, 128), bf16),
+            dma((24,)),
+            dma((span, 2)),
+            dma,
+            dma((24 * (2 * n_z - 1),)),
+            dma((n_z * span, 2)),
+            dma,
+            dma((2 * n_z,)),
+            dma((n_z,)),
+            dma,
+            dma((2 * n_z,)),
+            dma((n_z,)),
+            dma,
+            dma((pieces, 4)),
+            dma((pieces, 4)),
+            dma((pieces, 4)),
+            dma((pieces, 2)),
+            dma((pieces,)),
+            dma((pieces, 4)),
+            dma((pieces, 2, 2)),
+            dma((pieces, 2)),
+            dma((pieces,)),
+        ],
         compiler_params=pltpu.CompilerParams(
             collective_id=collective_id, has_side_effects=True, vmem_limit_bytes=60 << 20
         ),
         name="attend",
     )(
-        acts,
+        acts.reshape(half),
         weights,
         out_weight,
+        cot.reshape(half),
         query_gain.reshape(1, HD),
         key_gain.reshape(1, HD),
         *tables,
         *docs,
+    )
+    return (
+        attended.reshape(tokens, width),
+        seq.reshape(length, width),
+        full.reshape(n_z * weights.shape[0], weights.shape[1]),
+        all_cot.reshape(n_z * span * tokens, width),
+        (*saved, full_out),
+        peaks,
     )
 
 
@@ -1883,35 +2040,26 @@
 def dense_experts(
     moe_in, all_cot, expert_ids, gate_share, gate_weight, up_weight, down_weight
 ):
-    everyone = ("gx", "gy")
     devices = lax.axis_size("gx") * lax.axis_size("gy")
     experts = devices // 2
     matches = expert_ids[:, :, None] == jnp.arange(experts, dtype=jnp.int32)[None, None, :]
     dense_gates = jnp.sum(jnp.where(matches, gate_share[:, :, None], 0.0), axis=1)
-    own_gate = lax.all_to_all(
-        jnp.repeat(dense_gates.T, 2, axis=0), everyone, split_axis=0, concat_axis=0, tiled=True
-    ).reshape(-1)
-    shares = jnp.broadcast_to(own_gate[:, None], (own_gate.shape[0], 128))
+    shares = jnp.repeat(dense_gates.T, 2, axis=0)[:, None, :]
     all_moe, pair, gate_dots, down_part, moe_out = run_experts(
         moe_in, all_cot, shares, gate_weight[0], up_weight[0], down_weight[0], 8
     )
     moe_out = moe_out.reshape(moe_in.shape)
-    dots_back = lax.all_to_all(
-        jnp.sum(gate_dots, axis=-1).reshape(devices, -1),
-        everyone,
-        split_axis=0,
-        concat_axis=0,
-        tiled=True,
-    )
-    dots_experts = dots_back.reshape(experts, 2, -1).sum(axis=1).T
+    dots_experts = gate_dots.reshape(experts, 2, -1).sum(axis=1).T
     grad_gates = jnp.sum(jnp.where(matches, dots_experts[:, None, :], 0.0), axis=-1)
     grad_moe_in, gate_part, up_part = pull_experts(all_moe, pair, gate_weight[0], up_weight[0], 9)
     return moe_out, grad_gates, grad_moe_in, gate_part, up_part, down_part
 
 
 def plain_attention(
-    seq_acts, full_in, out_weight, query_gain, key_gain, doc_ids
+    acts, in_weights, out_weight, query_gain, key_gain, doc_ids, cotangent
 ):
+    seq_acts = lax.all_gather(acts, "gy", axis=0, tiled=True)
+    full_in = lax.all_gather(in_weights, "gx", axis=0, tiled=True)
     out_rows = lax.all_gather(out_weight, "gx", axis=1, tiled=True)
     local_width = full_in.shape[1] // 3
     length = seq_acts.shape[0]
@@ -2026,13 +2174,13 @@
         ).astype(jnp.float32)
         return grad_acts.astype(jnp.float32), in_sum, out_sum, query_gain_part, key_gain_part
 
-    return attended, jnp.max(peak_blocks, axis=0), back
+    return attended, jnp.max(peak_blocks, axis=0), None, back
 
 
 def kernel_attention(
-    seq_acts, full_in, out_weight, query_gain, key_gain, doc_ids
+    acts, in_weights, out_weight, query_gain, key_gain, doc_ids, cotangent
 ):
-    length = seq_acts.shape[0]
+    length = doc_ids.shape[0]
     halfway = HD // 2
     frequency = jnp.exp(
         jnp.arange(halfway, dtype=jnp.float32) * (-2.0 * jnp.log(10000.0) / HD)
@@ -2047,12 +2195,10 @@
         jnp.broadcast_to(doc_ids[:, None], (length, HD)),
         jnp.broadcast_to(doc_ids[None, :], (8, length)),
     )
-    part, *saved, peaks, out_rows = attend(
-        seq_acts, full_in, out_weight, query_gain, key_gain, tables, docs, 10
-    )
-    saved.append(out_rows)
-    attended = scatter_plane(part, 3)
-    heads = full_in.shape[1] // (3 * HD)
+    attended, seq_acts, full_in, all_cot, saved, peaks = attend(
+        acts, in_weights, out_weight, cotangent, query_gain, key_gain, tables, docs, 10
+    )
+    heads = in_weights.shape[1] // (3 * HD)
 
     def back(grad_resid):
         seq_grad = all_gather(grad_resid.astype(jnp.bfloat16), False, 1)
@@ -2062,7 +2208,7 @@
         grad_acts, in_sum = leave(part, weight_part, 7)
         return grad_acts, in_sum, out_sum, gains[0], gains[1]
 
-    return attended, peaks[:heads, 0], back
+    return attended, peaks[:heads, 0], all_cot, back
 
 
 def local(
@@ -2089,16 +2235,11 @@
     acts_low = acts_float.astype(jnp.bfloat16)
     in_weights = jnp.concatenate([query_weight, key_weight, value_weight], axis=1)
     by_kernels = lax.axis_size("gy") == 8
-    if by_kernels:
-        seq_acts, full_in, all_cot = enter(acts_low, in_weights, cotangent, 6)
-    else:
-        seq_acts = lax.all_gather(acts_low, "gy", axis=0, tiled=True)
-        full_in = lax.all_gather(in_weights, "gx", axis=0, tiled=True)
     local_width = query_weight.shape[1]
     local_heads = local_width // HD
     attention = kernel_attention if by_kernels else plain_attention
-    attended, own_peaks, attention_back = attention(
-        seq_acts, full_in, out_weight, query_gain, key_gain, doc_ids
+    attended, own_peaks, all_cot, attention_back = attention(
+        acts_low, in_weights, out_weight, query_gain, key_gain, doc_ids, cotangent
     )
     start_head = lax.axis_index("gy") * local_heads
     peak_slots = lax.dynamic_update_slice(

time: 704 us -> 666 us (0.946)
  Pallas kernels: 618 us -> 606 us
  starting transfers between devices: 11.3 us -> 0 us
  other arithmetic: 30.5 us -> 23 us
    pallas_call x2 -> x0, Pallas kernels: 139 us -> none  [the longest x1 115 us: enter(): pl.pallas_call(partial(enter_kernel, n_z, span), out_shape=(jax.ShapeDtyp...]
    pallas_call x1, Pallas kernels: 34.2 us -> 153 us  [attend(): pl.pallas_call(partial(attend_kernel, heads, pieces), out_shape=(jax.Shap...]
    all_to_all x2 -> x0, starting transfers between devices: 11.3 us -> none  [the longest x1 8.67 us: dense_experts(): lax.all_to_all(jnp.sum(gate_dots, axis=-1).reshape(devices, -1), everyone...]
  transfers between devices with their start and end apart: 2 -> 0, of which waited for: 1 -> 0; matrix products, arithmetic and copies ran while one was open for 0% -> 0% of each run, Pallas kernels for 16% -> 0%
where the time goes in v8:
time: 666 us; the launch traced here: 665 us
  Pallas kernels  606 us (91%)
  local copies, waits for them, and re-layouts  30.9 us (5%)
  other arithmetic  23 us (3%)
    pallas_call x1, Pallas kernels, run_experts(): pl.pallas_call(partial(expert_kernel, n_z, span), out_shape=(jax.ShapeDty...  190 us
    pallas_call x1, Pallas kernels, attend(): pl.pallas_call(partial(attend_kernel, heads, pieces), out_shape=(jax.Shap...  153 us
    pallas_call x1, Pallas kernels, pull_experts(): pl.pallas_call(partial(pull_kernel, n_i, rows), out_shape=(jax.ShapeDtype...  114 us
    pallas_call x1, Pallas kernels, leave(): pl.pallas_call(partial(leave_kernel, pieces, rows), out_shape=(jax.ShapeD...  59.9 us
    pallas_call x1, Pallas kernels, attend_back(): pl.pallas_call(partial(attend_back_kernel, heads, pieces), out_shape=(jax...  45.5 us
    pallas_call x1, Pallas kernels, all_gather(): pl.pallas_call(partial(gather_kernel, n_z, span), out_shape=jax.ShapeDtyp...  23.5 us
    pallas_call x1, Pallas kernels, sum_everywhere(): pl.pallas_call(partial(sum_kernel, n_z, bits), out_shape=jax.ShapeDtypeSt...  21.1 us
    unnamed x82, local copies, waits for them, and re-layouts  16.2 us

profile of v8, /device:TPU:0, one launch (start us, length us, event | category | flops | bytes accessed | tf_op | source)
XLA Modules:
  0.0 665.4 jit_solution(1927593696735579495)
XLA Ops:
  1.3 1.2 fusion.6
  2.5 0.6 copy-done.29
  3.1 0.5 iota.28
  3.7 1.3 broadcast_in_dim.105.col_docs
  5.0 1.7 broadcast_in_dim.104.row_docs
  6.7 2.0 fusion.2
  8.7 2.0 pad_maximum_fusion.own_weight
  10.7 2.0 fusion.11
  12.7 0.0 copy-start.2
  12.7 1.3 pad_maximum_fusion.1
  14.0 152.6 %attend.1 = (f32[4,2,16,2048]{3,2,1,0:T(8,128)}, bf16[8,2,64,2048]{3,2,1,0:T(8,128)(2,1)}, bf16[4,512,768]{2,1,0:T(8,128)(2,1)}, bf16[4,256,512]{2,1,0:T(8,128)(...) custom-call(bf16[2,64,2048]{2,1,0:T(8,128)(2,1)} %bitcast.74, ...), custom_call_target="tpu_custom_call" | custom-call | tf_op jit(solution)/shard_map/attend/pallas_call | solution.py:1627
  166.6 0.8 slice_reduce_fusion.1
  167.4 0.2 dynamic_update_slice.3
  167.6 0.6 reshape.212
  168.2 1.4 multiply_reduce_fusion.2
  169.7 0.9 copy-done
  170.6 0.2 multiply_convert_fusion
  170.8 0.8 copy-done.4
  171.6 0.3 fusion.21
  171.8 0.0 copy-start.15
  171.9 0.5 multiply_divide_fusion
  172.4 0.0 copy-done.15
  172.5 0.5 multiply_divide_fusion.1
  173.1 0.0 copy-done.21
  173.1 0.6 broadcast_in_dim.109
  173.7 189.5 %experts.1 = (bf16[4096,2048]{1,0:T(8,128)(2,1)}, bf16[4096,1024]{1,0:T(8,128)(2,1)}, f32[32,1,128]{2,1,0:T(1,128)}, f32[512,2048]{1,0:T(8,128)}, f32[2,64,2048]{2,1,0:T(8,128)}) custom-call(bf16[2,64,2048]{2,1,0:T(8,128)(2,1)} %bitcast.64, bf16[4096,2048]{1,0:T(8,128)(2,1)} %bitcast.58, f32[32,1,128]{2,1,0:T(1,128)} %bitcast.83, ...), custom_call_target="tpu_custom_call" | custom-call | tf_op jit(solution)/shard_map/experts/pallas_call | solution.py:1136
  363.3 0.7 reduce_sum.154
  364.0 0.7 select_reduce_fusion.3
  364.7 0.7 multiply_reduce_fusion.4
  365.4 0.7 divide_add_fusion
  366.1 0.7 select_reduce_fusion.2
  366.8 0.7 multiply_reduce_fusion.3
  367.5 0.7 multiply_convert_fusion.3
  368.3 1.2 convolution_bitcast_fusion
  369.5 0.7 copy.45
  370.2 113.8 %pull_experts.1 = (f32[2,64,2048]{2,1,0:T(8,128)}, f32[2048,512]{1,0:T(8,128)}, f32[2048,512]{1,0:T(8,128)}) custom-call(bf16[4096,2048]{1,0:T(8,128)(2,1)} %get-tuple-element.47.all_ref, bf16[4096,1024]{1,0:T(8,128)(2,1)} %get-tuple-element.48.pair_ref, bf16[2048,512]{1,0:T(8,128)(2,1)} %bitcast.61, bf16[2048,512]{1,0:T(8,128)(2,1)} %bitcast.63), custom_call_target="tpu_custom_call" | custom-call | tf_op jit(solution)/shard_map/pull_experts/pallas_call | solution.py:1367
  484.1 2.2 multiply_reduce_fusion
  486.4 1.2 fusion.17
  487.5 23.5 %gather_plane.1 = bf16[8,2,64,2048]{3,2,1,0:T(8,128)(2,1)} custom-call(bf16[2,64,2048]{2,1,0:T(8,128)(2,1)} %bitcast.73), custom_call_target="tpu_custom_call" | custom-call | tf_op jit(solution)/shard_map/gather_plane/pallas_call | solution.py:232
  511.0 45.5 %attend_back.1 = (bf16[4,8,2,16,2048]{4,3,2,1,0:T(8,128)(2,1)}, bf16[2048,768]{1,0:T(8,128)(2,1)}, f32[512,256]{1,0:T(8,128)}, f32[8,128]{1,0:T(8,128)}) custom-call(bf16[1024,2048]{1,0:T(8,128)(2,1)} %bitcast.59, bf16[4,256,512]{2,1,0:T(8,128)(2,1)} %get-tuple-element.51.out_weight_ref, bf16[1024,256]{1,0:T(8,128)(2,1)} %get-tuple-element.52.mixed_ref, ...), custom_call_target="tpu_custom_call" | custom-call | tf_op jit(solution)/shard_map/attend_back/pallas_call | solution.py:1861
  556.6 59.9 %leave.1 = (f32[4,2,16,2048]{3,2,1,0:T(8,128)}, f32[512,768]{1,0:T(8,128)}) custom-call(bf16[4,8,2,16,2048]{4,3,2,1,0:T(8,128)(2,1)} %get-tuple-element.59.part_ref, bf16[4,512,768]{2,1,0:T(8,128)(2,1)} %bitcast.71), custom_call_target="tpu_custom_call" | custom-call | tf_op jit(solution)/shard_map/leave/pallas_call | solution.py:624
  616.5 2.7 fusion.18
  619.2 0.4 fusion.3
  619.7 1.7 fusion.5
  621.4 0.7 constant_dynamic-update-slice_fusion.3
  622.1 0.7 constant_dynamic-update-slice_fusion.2
  622.9 0.7 pad.4
  623.6 21.1 %sum_everywhere.1 = f32[2,152,128]{2,1,0:T(8,128)} custom-call(f32[2,152,128]{2,1,0:T(8,128)} %bitcast.79), custom_call_target="tpu_custom_call" | custom-call | tf_op jit(solution)/shard_map/sum_everywhere/pallas_call | solution.py:463
  644.7 1.3 fusion.19
  646.0 1.3 fusion.20
  647.3 0.9 slice.63
  648.2 0.7 reshape.215
  648.9 1.0 copy.44
  649.9 1.3 slice.57
  651.2 1.3 sort.15
  652.5 0.6 fusion.14
  653.1 0.6 compare_select_fusion
  653.8 0.1 dynamic-slice_sqrt_fusion
  653.8 0.1 broadcast_bitcast_fusion
  653.9 0.9 multiply_convert_fusion.1
  654.8 4.8 copy.56
  659.6 2.1 copy.57
  661.8 1.6 copy-done.7
  663.3 2.0 copy.58
  (83 shorter events, 0.4 us)
Async XLA Ops:
  2.5 0.6 copy-start.29
  3.1 3.5 copy-start.25
  12.7 155.5 %copy-start.2 = (bf16[128,2048]{1,0:T(8,128)(2,1)S(1)}, bf16[128,2048]{1,0:T(8,128)(2,1)}, u32[]{:S(2)}) copy-start(bf16[128,2048]{1,0:T(8,128)(2,1)} %param.17) | copy-start | bytes 1572868
  14.0 156.6 %copy-start.16 = (f32[2048]{0:T(1024)S(1)}, f32[2048]{0:T(1024)}, u32[]{:S(2)}) copy-start(f32[2048]{0:T(1024)} %param.23) | copy-start | bytes 24580
  14.0 157.6 %copy-start.14 = (bf16[2048,16]{0,1:T(8,128)(2,1)S(1)}, bf16[2048,16]{0,1:T(8,128)(2,1)}, u32[]{:S(2)}) copy-start(bf16[2048,16]{0,1:T(8,128)(2,1)} %param.30) | copy-start | bytes 196612
  166.6 5.8 copy-start.19
  169.6 1.0 copy-start
  169.6 4.1 copy-start.32
  170.6 3.1 copy-start.23
  170.8 0.8 copy-start.4
  171.8 0.6 copy-start.15
  171.8 1.9 copy-start.22
  171.9 1.8 copy-start.27
  172.5 0.5 copy-start.28
  172.5 0.6 copy-start.21
  368.3 1.9 copy-start.20
  484.0 2.3 copy-start.33
  484.0 2.3 copy-start.1
  484.0 2.3 copy-start.5
  484.1 2.3 copy-start.17
  484.1 2.3 copy-start.24
  616.4 2.8 copy-start.3
  616.5 2.8 copy-start.6
  616.5 2.7 copy-start.18
  616.5 2.7 copy-start.26
  616.5 3.1 copy-start.30
  616.5 3.2 copy-start.9
  619.7 3.2 copy-start.13
  619.7 3.2 copy-start.31
  619.7 29.2 %copy-start.12 = (f32[512,256]{1,0:T(8,128)S(1)}, f32[512,256]{1,0:T(8,128)}, u32[]{:S(2)}) copy-start(f32[512,256]{1,0:T(8,128)} %get-tuple-element.65) | copy-start | bytes 1572868
  621.4 29.8 %copy-start.35 = (s32[16]{0:T(128)S(1)}, s32[16]{0:T(128)}, u32[]{:S(2)}) copy-start(s32[16]{0:T(128)} %iota.28) | copy-start | bytes 196
  621.4 32.5 %copy-start.10 = (bf16[512,256]{1,0:T(8,128)(2,1)S(1)}, bf16[512,256]{1,0:T(8,128)(2,1)}, u32[]{:S(2)}) copy-start(bf16[512,256]{1,0:T(8,128)(2,1)} %param.27) | copy-start | bytes 786436
  621.4 32.5 %copy-start.11 = (bf16[512,256]{1,0:T(8,128)(2,1)S(1)}, bf16[512,256]{1,0:T(8,128)(2,1)}, u32[]{:S(2)}) copy-start(bf16[512,256]{1,0:T(8,128)(2,1)} %param.26) | copy-start | bytes 786436
  653.7 5.9 copy-start.34
  654.8 4.8 copy-start.8
  659.6 3.7 copy-start.7

commit v9 on v8

--- a/solution.py
+++ b/solution.py
@@ -108,12 +108,12 @@
     first_z = z if n_z > 1 else 0
     sends = []
 
-    def send(ok, source, b, h, peer):
+    def send(ok, b, h, peer, own=False):
         k = len(sends)
 
         def make():
             return pltpu.make_async_remote_copy(
-                src_ref=source,
+                src_ref=own_ref.at[h] if own else out_ref.at[b, h],
                 dst_ref=out_ref.at[b, h],
                 send_sem=send_sem.at[k],
                 recv_sem=recv_sem.at[b, h],
@@ -145,42 +145,40 @@
     upward = [always(item[0], z < n_z - 1) for item in items]
     downward = [always(item[0], z > 0) for item in items]
 
+    near_b = [owner * span + g for _, owner, _ in items]
+    x_b = [owner * span + flip_x for _, owner, _ in items]
+    y_b = [owner * span + flip_y for _, owner, _ in items]
+    both_b = [owner * span + flip_both for _, owner, _ in items]
+
     def first(i):
-        ok, owner, d = items[i]
-        b = owner * span + g
-        if d == 0:
+        ok, _, d = items[i]
+        b = near_b[i]
+        own = d == 0
+        if own:
             local.start()
-            source = own_ref
         else:
             arrive(ok, b, 0)
             arrive(ok, b, 1)
-            source = out_ref.at[b]
         for h in range(2):
             if n_z > 1 and d <= 0:
-                send(upward[i], source.at[h], b, h, above)
+                send(upward[i], b, h, above, own)
             if n_z > 1 and d >= 0:
-                send(downward[i], source.at[h], b, h, below)
-        send(ok, source.at[0], b, 0, x_peer)
-        send(ok, source.at[1], b, 1, y_peer)
-        send(ok, source.at[1], b, 1, x_peer)
-        send(ok, source.at[0], b, 0, y_peer)
-        send(ok, source.at[0], b, 0, core)
-        send(ok, source.at[1], b, 1, core)
-
-    def second(item):
-        ok, owner, _ = item
-        for side, h, peer in ((flip_x, 0, y_peer), (flip_y, 1, x_peer)):
-            b = owner * span + side
+                send(downward[i], b, h, below, own)
+        for h, peer in ((0, x_peer), (1, y_peer), (1, x_peer), (0, y_peer), (0, core), (1, core)):
+            send(ok, b, h, peer, own)
+
+    def second(i):
+        ok = items[i][0]
+        for b, h, peer in ((x_b[i], 0, y_peer), (y_b[i], 1, x_peer)):
             arrive(ok, b, h)
-            send(ok, out_ref.at[b, h], b, h, peer)
-            send(ok, out_ref.at[b, h], b, h, core)
-
-    def third(item):
-        ok, owner, _ = item
-        for side, h in ((flip_both, 0), (flip_both, 1), (flip_y, 0), (flip_x, 1)):
-            b = owner * span + side
+            send(ok, b, h, peer)
+            send(ok, b, h, core)
+
+    def third(i):
+        ok = items[i][0]
+        for b, h in ((both_b[i], 0), (both_b[i], 1), (y_b[i], 0), (x_b[i], 1)):
             arrive(ok, b, h)
-            send(ok, out_ref.at[b, h], b, h, core)
+            send(ok, b, h, core)
 
     n = len(items)
 
@@ -188,9 +186,9 @@
         if i < n:
             first(i)
         if 1 <= i <= n:
-            second(items[i - 1])
+            second(i - 1)
         if i >= 2:
-            third(items[i - 2])
+            third(i - 2)
 
     def finish():
         for ok, owner, _ in items:
@@ -213,32 +211,6 @@
     if n_z > 1:
         peers += [(z < n_z - 1, {"gx": z + 1, "gy": g}), (z > 0, {"gx": z - 1, "gy": g})]
     barrier_with(peers)
-
-
-def gather_kernel(n_z, span, own_ref, out_ref, send_sem, recv_sem, local_sem):
-    greet(n_z)
-    steps, finish = gather_steps(n_z, span, own_ref, out_ref, send_sem, recv_sem, local_sem)
-    for step in steps:
-        step()
-    finish()
-
-
-def all_gather(block, both, collective_id):
-    n_z = lax.axis_size("gx") if both else 1
-    span = lax.axis_size("gy")
-    rows, cols = block.shape
-    own = block.reshape(2, rows // 2, cols)
-    n_sends = (2 * n_z - 1) * 24
-    out = pl.pallas_call(
-        partial(gather_kernel, n_z, span),
-        out_shape=jax.ShapeDtypeStruct((n_z * span, 2, rows // 2, cols), block.dtype),
-        in_specs=[pl.BlockSpec(memory_space=pltpu.VMEM)],
-        out_specs=pl.BlockSpec(memory_space=pl.ANY),
-        scratch_shapes=[pltpu.SemaphoreType.DMA((n_sends,)), pltpu.SemaphoreType.DMA((n_z * span, 2)), pltpu.SemaphoreType.DMA],
-        compiler_params=pltpu.CompilerParams(collective_id=collective_id, has_side_effects=True),
-        name="gather_all" if both else "gather_plane",
-    )(own)
-    return out.reshape(n_z * span * rows, cols)
 
 
 def add_into(dst, parts, rows):
@@ -398,18 +370,15 @@
     finish()
 
 
-def sum_kernel(n_z, bits, vec_ref, out_ref, held, arrived, from_z, send_sem, z_send, recv_sem, z_recv):
+def sum_steps(n_z, bits, vec_ref, out_ref, held, arrived, from_z, send_sem, z_send, recv_sem, z_recv):
     z = lax.axis_index("gx")
     g = lax.axis_index("gy")
-    half = vec_ref.shape[1]
     side = lax.rem(g, 2)
-    core = {"gx": z, "gy": g + 1 - 2 * (g % 2)}
     peers = [
         {"gx": z, "gy": g + bit - 2 * bit * ((g // bit) % 2)}
-        for bit in (2**power for power in range(1, bits))
+        for bit in (2**power for power in range(bits))
     ]
     others = [{"gx": lax.rem(z + j, n_z), "gy": g} for j in range(1, n_z)]
-    barrier_with([(z >= 0, peer) for peer in (core, *peers, *others)])
 
     def remote(src, dst, ssem, rsem, peer):
         return pltpu.make_async_remote_copy(
@@ -421,63 +390,90 @@
             device_id_type=pl.DeviceIdType.MESH,
         )
 
-    first = remote(vec_ref.at[1 - side], arrived.at[0], send_sem.at[0], recv_sem.at[0], core)
-    first.start()
-    first.wait()
-    held[0] = vec_ref[side] + arrived[0]
-    for k, peer in enumerate(peers, 1):
-        step = remote(held.at[k - 1], arrived.at[k], send_sem.at[k], recv_sem.at[k], peer)
-        step.start()
-        step.wait()
-        held[k] = held[k - 1] + arrived[k]
-    copies = [
-        remote(held.at[bits - 1], from_z.at[j], z_send.at[j], z_recv.at[j], peer)
-        for j, peer in enumerate(others)
+    def hop(k):
+        source = vec_ref.at[1 - side] if k == 0 else held.at[k - 1]
+        return remote(source, arrived.at[k], send_sem.at[k], recv_sem.at[k], peers[k])
+
+    def across(j):
+        return remote(held.at[bits - 1], from_z.at[j], z_send.at[j], z_recv.at[j], others[j])
+
+    def back():
+        return remote(held.at[bits], arrived.at[bits], send_sem.at[bits], recv_sem.at[bits], peers[0])
+
+    def onward(k):
+        hop(k).wait()
+        held[k] = (vec_ref[side] if k == 0 else held[k - 1]) + arrived[k]
+        if k + 1 < bits:
+            hop(k + 1).start()
+        else:
+            for j in range(n_z - 1):
+                across(j).start()
+
+    def gather():
+        for j in range(n_z - 1):
+            across(j).wait()
+        total = jnp.zeros_like(held[0])
+        for owner in range(n_z):
+            term = held[bits - 1]
+            for j in range(1, n_z):
+                term = jnp.where(lax.rem(z - j + n_z, n_z) == owner, from_z[j - 1], term)
+            total = total + term
+        held[bits] = total
+        back().start()
+        out_ref[side] = total
+
+    def finish():
+        back().wait()
+        out_ref[1 - side] = arrived[bits]
+
+    return [lambda: hop(0).start()] + [partial(onward, k) for k in range(bits)] + [gather, finish]
+
+
+def sum_kernel(n_z, bits, *refs):
+    z = lax.axis_index("gx")
+    g = lax.axis_index("gy")
+    peers = [
+        {"gx": z, "gy": g + bit - 2 * bit * ((g // bit) % 2)}
+        for bit in (2**power for power in range(bits))
     ]
-    for copy in copies:
-        copy.start()
-    for copy in copies:
-        copy.wait()
-    total = jnp.zeros_like(held[0])
-    for owner in range(n_z):
-        term = held[bits - 1]
-        for j in range(1, n_z):
-            term = jnp.where(lax.rem(z - j + n_z, n_z) == owner, from_z[j - 1], term)
-        total = total + term
-    held[bits] = total
-    last = remote(held.at[bits], arrived.at[bits], send_sem.at[bits], recv_sem.at[bits], core)
-    last.start()
-    out_ref[side] = total
-    last.wait()
-    out_ref[1 - side] = arrived[bits]
+    peers += [{"gx": lax.rem(z + j, n_z), "gy": g} for j in range(1, n_z)]
+    barrier_with([(z >= 0, peer) for peer in peers])
+    for step in sum_steps(n_z, bits, *refs):
+        step()
+
+
+def folded(vector):
+    rows = -(-vector.shape[0] // (128 * 16)) * 8
+    return jnp.pad(vector, (0, 2 * rows * 128 - vector.shape[0])).reshape(2, rows, 128)
+
+
+def sum_scratch(n_z, bits, rows):
+    dma = pltpu.SemaphoreType.DMA
+    return [
+        pltpu.VMEM((bits + 1, rows, 128), jnp.float32),
+        pltpu.VMEM((bits + 1, rows, 128), jnp.float32),
+        pltpu.VMEM((n_z - 1, rows, 128), jnp.float32),
+        dma((bits + 1,)),
+        dma((n_z - 1,)),
+        dma((bits + 1,)),
+        dma((n_z - 1,)),
+    ]
 
 
 def sum_everywhere(vector, collective_id):
     n_z = lax.axis_size("gx")
     bits = lax.axis_size("gy").bit_length() - 1
-    lanes = 128
-    length = vector.shape[0]
-    rows = -(-length // (lanes * 16)) * 8
-    padded = jnp.pad(vector, (0, 2 * rows * lanes - length)).reshape(2, rows, lanes)
-    dma = pltpu.SemaphoreType.DMA
+    halves = folded(vector)
     out = pl.pallas_call(
         partial(sum_kernel, n_z, bits),
-        out_shape=jax.ShapeDtypeStruct((2, rows, lanes), jnp.float32),
+        out_shape=jax.ShapeDtypeStruct(halves.shape, jnp.float32),
         in_specs=[pl.BlockSpec(memory_space=pltpu.VMEM)],
         out_specs=pl.BlockSpec(memory_space=pltpu.VMEM),
-        scratch_shapes=[
-            pltpu.VMEM((bits + 1, rows, lanes), jnp.float32),
-            pltpu.VMEM((bits + 1, rows, lanes), jnp.float32),
-            pltpu.VMEM((n_z - 1, rows, lanes), jnp.float32),
-            dma((bits + 1,)),
-            dma((n_z - 1,)),
-            dma((bits + 1,)),
-            dma((n_z - 1,)),
-        ],
+        scratch_shapes=sum_scratch(n_z, bits, halves.shape[1]),
         compiler_params=pltpu.CompilerParams(collective_id=collective_id, has_side_effects=True),
         name="sum_everywhere",
-    )(padded)
-    return out.reshape(-1)[:length]
+    )(halves)
+    return out.reshape(-1)[: vector.shape[0]]
 
 
 def chain_scatter(n_z, part_ref, out_ref, from_low, from_high, send_sem, low_recv, high_recv):
@@ -547,117 +543,6 @@
             run_if(z != dest, lambda dest=dest: up(dest).wait_send())
 
     return start, [partial(relay, time) for time in range(1, n_z)], finish
-
-
-def leave_kernel(
-    n_i,
-    rows,
-    part_ref,
-    weight_ref,
-    out_ref,
-    weight_out,
-    held,
-    from_core,
-    from_a,
-    from_b,
-    from_z,
-    sums,
-    from_low,
-    from_high,
-    load_sem,
-    core_send,
-    a_send,
-    b_send,
-    z_send,
-    core_recv,
-    a_recv,
-    b_recv,
-    z_recv,
-    copy_sem,
-    chain_send,
-    low_recv,
-    high_recv,
-):
-    n_z = lax.axis_size("gx")
-    copy = pltpu.make_async_copy(weight_ref, sums, copy_sem)
-    copy.start()
-    chain = chain_scatter(
-        n_z, sums, weight_out, from_low, from_high, chain_send, low_recv, high_recv
-    )
-
-    def start():
-        copy.wait()
-        chain[0]()
-
-    scatter_kernel(
-        False,
-        n_i,
-        rows,
-        part_ref,
-        out_ref,
-        held,
-        from_core,
-        from_a,
-        from_b,
-        from_z,
-        load_sem,
-        core_send,
-        a_send,
-        b_send,
-        z_send,
-        core_recv,
-        a_recv,
-        b_recv,
-        z_recv,
-        (start, chain[1], chain[2]),
-    )
-
-
-def leave(part, weight_part, collective_id):
-    n_z = lax.axis_size("gx")
-    span = lax.axis_size("gy")
-    pieces, _, _, rows, cols = part.shape
-    total = span * pieces * 2 * rows
-    half = (rows, cols)
-    dma = pltpu.SemaphoreType.DMA
-    block = (weight_part.shape[0] // n_z, weight_part.shape[1])
-    out, sums = pl.pallas_call(
-        partial(leave_kernel, pieces, rows),
-        out_shape=(
-            jax.ShapeDtypeStruct((pieces, 2, rows, cols), jnp.float32),
-            jax.ShapeDtypeStruct(block, jnp.float32),
-        ),
-        in_specs=[pl.BlockSpec(memory_space=pl.ANY)] * 2,
-        out_specs=(pl.BlockSpec(memory_space=pltpu.VMEM),) * 2,
-        scratch_shapes=[
-            pltpu.VMEM((pieces, 4, 2) + half, jnp.bfloat16),
-            pltpu.VMEM((pieces, 4, 2) + half, jnp.bfloat16),
-            pltpu.VMEM((pieces, 2, 2) + half, jnp.bfloat16),
-            pltpu.VMEM((pieces, 2) + half, jnp.bfloat16),
-            pltpu.VMEM((1, 2, 16, 128), jnp.bfloat16),
-            pltpu.VMEM((n_z,) + block, jnp.bfloat16),
-            pltpu.VMEM((n_z,) + block, jnp.bfloat16),
-            pltpu.VMEM((n_z,) + block, jnp.bfloat16),
-            dma((pieces, 4)),
-            dma((pieces, 4)),
-            dma((pieces, 4)),
-            dma((pieces, 2)),
-            dma((pieces,)),
-            dma((pieces, 4)),
-            dma((pieces, 2, 2)),
-            dma((pieces, 2)),
-            dma((pieces,)),
-            dma,
-            dma((n_z,)),
-            dma((n_z,)),
-            dma((n_z,)),
-        ],
-        compiler_params=pltpu.CompilerParams(
-            collective_id=collective_id, has_side_effects=True, vmem_limit_bytes=60 << 20
-        ),
-        name="leave",
-    )(part, weight_part.reshape((n_z,) + block))
-    return out.reshape(total // span, cols), sums
 
 
 def expert_kernel(n_z, span, own_ref, cot_ref, share_ref, gate_ref, up_ref, down_ref,
@@ -1403,25 +1288,28 @@
     return values * cosine + pltpu.roll(values, values.shape[-1] // 2, 1) * sine
 
 
-def greet_chain(n_z):
-    z = lax.axis_index("gx")
-    g = lax.axis_index("gy")
-    barrier_with([(z < n_z - 1, {"gx": z + 1, "gy": g}), (z > 0, {"gx": z - 1, "gy": g})])
+def spread_docs(docs_ref, row_docs, col_docs):
+    lanes = docs_ref.shape[1]
+    for j in range(docs_ref.shape[0]):
+        line = docs_ref[j : j + 1, :].astype(jnp.float32)
+        row_docs[j * lanes : (j + 1) * lanes, :] = jnp.broadcast_to(line, (lanes, lanes)).T
+        col_docs[:, j * lanes : (j + 1) * lanes] = jnp.broadcast_to(line, (8, lanes))
 
 
 def attend_kernel(
     heads,
     pieces,
     own_acts,
-    own_weight,
+    query_weight,
+    key_weight,
+    value_weight,
     own_out_weight,
     own_cot,
     query_gain,
     key_gain,
     cosine_ref,
     sine_ref,
-    row_docs,
-    col_docs,
+    docs_ref,
     attended_ref,
     acts_out,
     weight_out,
@@ -1433,6 +1321,9 @@
     mixed_ref,
     totals_ref,
     peaks_ref,
+    own_weight,
+    row_docs,
+    col_docs,
     part_ref,
     held,
     from_core,
@@ -1463,6 +1354,8 @@
 ):
     n_z = lax.axis_size("gx")
     span = lax.axis_size("gy")
+    for j, item in enumerate((query_weight, key_weight, value_weight)):
+        own_weight[:, j * item.shape[1] : (j + 1) * item.shape[1]] = item[...]
     greet(n_z)
     in_start, in_relays, in_finish = chain_gather(
         n_z, own_weight, weight_out, in_send, in_recv, in_local
@@ -1508,6 +1401,7 @@
     in_start()
     near[0]()
     far[0]()
+    spread_docs(docs_ref, row_docs, col_docs)
     near[1]()
     near[2]()
     later = far[1:]
@@ -1577,13 +1471,14 @@
         totals_ref[at, :] = kept
 
     blocks = length // block
-    for quarter in range(2):
-
-        @pl.loop(quarter * blocks // 2, (quarter + 1) * blocks // 2)
-        def _(t):
-            mix(t)
-
-        pull(1)
+    between = waiting[1].pop(0) if waiting[1] else lambda: None
+
+    @pl.loop(0, blocks)
+    def _(t):
+        mix(t)
+        pl.when(t == blocks // 2 - 1)(between)
+
+    pull(1)
     for relay in waiting[0]:
         relay()
     out_finish()
@@ -1612,7 +1507,7 @@
     acts, weights, out_weight, cot, query_gain, key_gain, tables, docs, collective_id, pieces=4
 ):
     tokens, width = acts.shape
-    local = weights.shape[1] // 3
+    depth, local = weights[0].shape
     heads = local // HD
     n_z = lax.axis_size("gx")
     span = lax.axis_size("gy")
@@ -1629,7 +1524,7 @@
         out_shape=(
             jax.ShapeDtypeStruct((pieces, 2) + piece, f32),
             jax.ShapeDtypeStruct((span,) + half, bf16),
-            jax.ShapeDtypeStruct((n_z,) + weights.shape, bf16),
+            jax.ShapeDtypeStruct((n_z, depth, 3 * local), bf16),
             jax.ShapeDtypeStruct((n_z,) + out_weight.shape, bf16),
             jax.ShapeDtypeStruct((n_z * span,) + half, bf16),
             jax.ShapeDtypeStruct((length, local), f32),
@@ -1639,9 +1534,12 @@
             jax.ShapeDtypeStruct((length, HD), f32),
             jax.ShapeDtypeStruct((8, HD), f32),
         ),
-        in_specs=[vmem] * 10,
+        in_specs=[vmem] * 11,
         out_specs=(vmem, vmem, vmem, vmem, hbm) + (vmem,) * 6,
         scratch_shapes=[
+            pltpu.VMEM((depth, 3 * local), bf16),
+            pltpu.VMEM((length, 128), f32),
+            pltpu.VMEM((8, length), f32),
             pltpu.VMEM((pieces, span, 2) + piece, bf16),
             pltpu.VMEM((pieces, 4, 2) + piece, bf16),
             pltpu.VMEM((pieces, 4, 2) + piece, bf16),
@@ -1676,18 +1574,18 @@
         name="attend",
     )(
         acts.reshape(half),
-        weights,
+        *weights,
         out_weight,
         cot.reshape(half),
         query_gain.reshape(1, HD),
         key_gain.reshape(1, HD),
         *tables,
-        *docs,
+        docs,
     )
     return (
         attended.reshape(tokens, width),
         seq.reshape(length, width),
-        full.reshape(n_z * weights.shape[0], weights.shape[1]),
+        full.reshape(n_z * depth, 3 * local),
         all_cot.reshape(n_z * span * tokens, width),
         (*saved, full_out),
         peaks,
@@ -1697,7 +1595,7 @@
 def attend_back_kernel(
     heads,
     pieces,
-    grad_ref,
+    own_grad,
     out_weight_ref,
     mixed_ref,
     ready_ref,
@@ -1708,67 +1606,150 @@
     key_gain,
     cosine_ref,
     sine_ref,
+    docs_ref,
+    small_ref,
+    acts_hbm,
+    weight_hbm,
+    grad_acts,
+    weight_sum,
+    out_sum,
+    gain_ref,
+    small_sum,
     row_docs,
     col_docs,
-    acts_hbm,
-    weight_hbm,
+    seq_ref,
     part_ref,
-    weight_part,
-    out_sum,
-    gain_ref,
     acts_ref,
     weight_ref,
     grad_mixed,
     grad_heads,
+    one_head,
     turned,
     key_sum,
     value_sum,
-    sums,
-    from_low,
-    from_high,
+    out_sums,
+    out_low,
+    out_high,
+    in_sums,
+    in_low,
+    in_high,
+    held,
+    from_core,
+    from_a,
+    from_b,
+    from_z,
     copy_sem,
-    chain_send,
-    low_recv,
-    high_recv,
+    near_send,
+    near_recv,
+    near_local,
+    out_send,
+    out_low_recv,
+    out_high_recv,
+    in_send,
+    in_low_recv,
+    in_high_recv,
+    load_sem,
+    core_send,
+    a_send,
+    b_send,
+    z_send,
+    core_recv,
+    a_recv,
+    b_recv,
+    z_recv,
+    *small_scratch,
 ):
     n_z = lax.axis_size("gx")
-    greet_chain(n_z)
-    start, relays, finish = chain_scatter(
-        n_z, sums, out_sum, from_low, from_high, chain_send, low_recv, high_recv
+    span = lax.axis_size("gy")
+    z = lax.axis_index("gx")
+    g = lax.axis_index("gy")
+    peers = [{"gx": z, "gy": g + bit - 2 * bit * ((g // bit) % 2)} for bit in (1, 2, 4)]
+    peers += [{"gx": lax.rem(z + j, n_z), "gy": g} for j in range(1, n_z)]
+    barrier_with([(z >= 0, peer) for peer in peers])
+    out_start, out_relays, out_finish = chain_scatter(
+        n_z, out_sums, out_sum, out_low, out_high, out_send, out_low_recv, out_high_recv
+    )
+    chains = [
+        chain_scatter(
+            n_z,
+            in_sums.at[h],
+            weight_sum.at[h],
+            in_low.at[h],
+            in_high.at[h],
+            in_send.at[h],
+            in_low_recv.at[h],
+            in_high_recv.at[h],
+        )
+        for h in range(heads)
+    ]
+    near, near_finish = gather_steps(1, span, own_grad, seq_ref, near_send, near_recv, near_local)
+    small = sum_steps(n_z, span.bit_length() - 1, small_ref, small_sum, *small_scratch)
+    back = []
+    scatter_kernel(
+        False,
+        pieces,
+        part_ref.shape[3],
+        part_ref,
+        grad_acts,
+        held,
+        from_core,
+        from_a,
+        from_b,
+        from_z,
+        load_sem,
+        core_send,
+        a_send,
+        b_send,
+        z_send,
+        core_recv,
+        a_recv,
+        b_recv,
+        z_recv,
+        parts=back,
     )
     f32, bf16 = jnp.float32, jnp.bfloat16
     dot = partial(lax.dot_general, preferred_element_type=f32)
     plain = (((1,), (0,)), ((), ()))
     last_dims = (((1,), (1,)), ((), ()))
     first_dims = (((0,), (0,)), ((), ()))
-    length, width = grad_ref.shape
-    span = part_ref.shape[1]
+    length, local = query_raw.shape
+    width = acts_ref.shape[1]
     rows = part_ref.shape[3]
-    local = heads * HD
     block = 256
     scale = HD ** (-0.5)
     copies = [
         pltpu.make_async_copy(acts_hbm, acts_ref, copy_sem.at[0]),
         pltpu.make_async_copy(weight_hbm, weight_ref, copy_sem.at[1]),
     ]
+    near[0]()
+    small[0]()
+    spread_docs(docs_ref, row_docs, col_docs)
     for copy in copies:
         copy.start()
+    near[1]()
+    small[1]()
+    near[2]()
+    small[2]()
+    near_finish()
     owned = width // n_z
 
     @pl.loop(0, width // block)
     def _(t):
         cols = pl.ds(pl.multiple_of(t * block, block), block)
         inside = pl.ds(pl.multiple_of(lax.rem(t, owned // block) * block, block), block)
-        sums[lax.div(t, owned // block), inside, :] = dot(
-            grad_ref[:, cols], mixed_ref[...], first_dims
+        grad = seq_ref[:, :, :, cols].reshape(length, block)
+        out_sums[lax.div(t, owned // block), inside, :] = dot(
+            grad, mixed_ref[...], first_dims
         ).astype(bf16)
 
-    start()
-    total = dot(grad_ref[:, :owned], out_weight_ref[0], last_dims)
-    for owner in range(1, n_z):
+    out_start()
+    total = jnp.zeros((length, local), f32)
+    for owner in range(n_z):
         cols = slice(owner * owned, (owner + 1) * owned)
-        total = total + dot(grad_ref[:, cols], out_weight_ref[owner], last_dims)
+        grad = seq_ref[:, :, :, cols].reshape(length, owned)
+        total = total + dot(grad, out_weight_ref[owner], last_dims)
     grad_mixed[...] = total.astype(bf16)
+    small[3]()
     gain_ref[...] = jnp.zeros_like(gain_ref)
     for h in range(heads):
         cols = slice(h * HD, (h + 1) * HD)
@@ -1811,31 +1792,58 @@
                 )
                 where = source * local + h * HD
                 grad_heads[at, where : where + HD] = pulled.astype(bf16)
+                one_head[at, source * HD : (source + 1) * HD] = pulled.astype(bf16)
 
         where = 2 * local + h * HD
         grad_heads[:, where : where + HD] = value_sum[...].astype(bf16)
-        if h < len(relays) - 1:
-            relays[h]()
-
-    for relay in relays[min(heads, len(relays) - 1) :]:
-        relay()
-    finish()
-
-    for copy in copies:
-        copy.wait()
+        one_head[:, 2 * HD :] = value_sum[...].astype(bf16)
+        if h == 0:
+            for copy in copies:
+                copy.wait()
+            for relay in out_relays:
+                relay()
+            out_finish()
+            small[4]()
+        else:
+            chains[h - 1][1][0]()
+
+        @pl.loop(0, width // block)
+        def _(t):
+            cols = pl.ds(pl.multiple_of(t * block, block), block)
+            inside = pl.ds(pl.multiple_of(lax.rem(t, owned // block) * block, block), block)
+            in_sums[h, lax.div(t, owned // block), inside, :] = dot(
+                acts_ref[:, cols], one_head[...], first_dims
+            ).astype(bf16)
+
+        chains[h][0]()
+
+    for chain in chains[:-1]:
+        for relay in chain[1][1:2]:
+            relay()
 
     @pl.loop(0, width // block)
     def _(t):
         cols = pl.ds(pl.multiple_of(t * block, block), block)
-        weight_part[cols, :] = dot(acts_ref[:, cols], grad_heads[...], first_dims).astype(bf16)
         sent = dot(grad_heads[...], weight_ref[cols, :], last_dims).astype(bf16)
         sent = sent.reshape(span, pieces, 2, rows, block)
         for p in range(pieces):
             part_ref[p, :, :, :, cols] = sent[:, p]
 
+    small[5]()
+    waiting = [relay for chain in chains[:-1] for relay in chain[1][2:]] + list(chains[-1][1])
+    for i, step in enumerate(back[:-1]):
+        step()
+        if i % 2 == 0 and waiting:
+            waiting.pop(0)()
+    for relay in waiting:
+        relay()
+    for chain in chains:
+        chain[2]()
+    back[-1]()
+
 
 def attend_back(
-    seq_grad,
+    grad,
     saved,
     query_gain,
     key_gain,
@@ -1843,53 +1851,89 @@
     docs,
     acts,
     weights,
+    small,
     collective_id,
     pieces=4,
 ):
     query_raw, key_raw, ready, mixed, totals, out_weight = saved
     n_z = lax.axis_size("gx")
+    span = lax.axis_size("gy")
+    bits = span.bit_length() - 1
+    tokens, width = grad.shape
+    length, local = query_raw.shape
+    heads = local // HD
+    rows = tokens // (pieces * 2)
+    halves = folded(small)
+    half = (2, tokens // 2, width)
+    piece = (rows, width)
+    out_block = (n_z, width // n_z, local)
+    in_block = (heads, n_z, width // n_z, 3 * HD)
+    f32, bf16 = jnp.float32, jnp.bfloat16
     dma = pltpu.SemaphoreType.DMA
-    block = (n_z, acts.shape[1] // n_z, query_raw.shape[1])
-    length, width = seq_grad.shape
-    local = query_raw.shape[1]
-    heads = local // HD
-    span = lax.axis_size("gy")
-    rows = length // (span * pieces * 2)
-    f32, bf16 = jnp.float32, jnp.bfloat16
     vmem = pl.BlockSpec(memory_space=pltpu.VMEM)
     hbm = pl.BlockSpec(memory_space=pl.ANY)
-    return pl.pallas_call(
+    grad_acts, weight_sum, out_sum, gains, small_sum = pl.pallas_call(
         partial(attend_back_kernel, heads, pieces),
         out_shape=(
-            jax.ShapeDtypeStruct((pieces, span, 2, rows, width), bf16),
-            jax.ShapeDtypeStruct((width, 3 * local), bf16),
-            jax.ShapeDtypeStruct(block[1:], f32),
+            jax.ShapeDtypeStruct((pieces, 2) + piece, f32),
+            jax.ShapeDtypeStruct((heads,) + in_block[2:], f32),
+            jax.ShapeDtypeStruct(out_block[1:], f32),
             jax.ShapeDtypeStruct((8, HD), f32),
+            jax.ShapeDtypeStruct(halves.shape, f32),
         ),
         in_specs=[vmem] * 13 + [hbm] * 2,
-        out_specs=(vmem,) * 4,
+        out_specs=(vmem,) * 5,
         scratch_shapes=[
+            pltpu.VMEM((length, 128), f32),
+            pltpu.VMEM((8, length), f32),
+            pltpu.VMEM((span,) + half, bf16),
+            pltpu.VMEM((pieces, span, 2) + piece, bf16),
             pltpu.VMEM((length, width), bf16),
             pltpu.VMEM((width, 3 * local), bf16),
             pltpu.VMEM((length, local), bf16),
             pltpu.VMEM((length, 3 * local), bf16),
+            pltpu.VMEM((length, 3 * HD), bf16),
             pltpu.VMEM((length, HD), f32),
             pltpu.VMEM((length, HD), f32),
             pltpu.VMEM((length, HD), f32),
-            pltpu.VMEM(block, bf16),
-            pltpu.VMEM(block, bf16),
-            pltpu.VMEM(block, bf16),
+            pltpu.VMEM(out_block, bf16),
+            pltpu.VMEM(out_block, bf16),
+            pltpu.VMEM(out_block, bf16),
+            pltpu.VMEM(in_block, bf16),
+            pltpu.VMEM(in_block, bf16),
+            pltpu.VMEM(in_block, bf16),
+            pltpu.VMEM((pieces, 4, 2) + piece, bf16),
+            pltpu.VMEM((pieces, 4, 2) + piece, bf16),
+            pltpu.VMEM((pieces, 2, 2) + piece, bf16),
+            pltpu.VMEM((pieces, 2) + piece, bf16),
+            pltpu.VMEM((1, 2, 16, 128), bf16),
             dma((2,)),
+            dma((24,)),
+            dma((span, 2)),
+            dma,
             dma((n_z,)),
             dma((n_z,)),
             dma((n_z,)),
-        ],
+            dma((heads, n_z)),
+            dma((heads, n_z)),
+            dma((heads, n_z)),
+            dma((pieces, 4)),
+            dma((pieces, 4)),
+            dma((pieces, 4)),
+            dma((pieces, 2)),
+            dma((pieces,)),
+            dma((pieces, 4)),
+            dma((pieces, 2, 2)),
+            dma((pieces, 2)),
+            dma((pieces,)),
+        ]
+        + sum_scratch(n_z, bits, halves.shape[1]),
         compiler_params=pltpu.CompilerParams(
-            collective_id=collective_id, has_side_effects=True, vmem_limit_bytes=60 << 20
+            collective_id=collective_id, has_side_effects=True, vmem_limit_bytes=67043328
         ),
         name="attend_back",
     )(
-        seq_grad,
+        grad.reshape(half),
         out_weight,
         mixed,
         ready,
@@ -1899,10 +1943,28 @@
         query_gain.reshape(1, HD),
         key_gain.reshape(1, HD),
         *tables,
-        *docs,
+        docs,
+        halves,
         acts,
         weights,
     )
+    weight_sum = weight_sum.reshape(heads, -1, 3, HD).transpose(1, 2, 0, 3)
+    return (
+        grad_acts.reshape(tokens, width),
+        weight_sum.reshape(-1, 3 * local),
+        out_sum,
+        gains,
+        small_sum.reshape(-1)[: small.shape[0]],
+    )
+
+
+def flat(parts):
+    return jnp.concatenate([part.reshape(-1) for part in parts])
+
+
+def unflat(vector, parts):
+    ends = accumulate(part.size for part in parts)
+    return [vector[end - part.size : end].reshape(part.shape) for end, part in zip(ends, parts)]
 
 
 def norm_rows(values, gain_row):
@@ -2059,7 +2121,7 @@
     acts, in_weights, out_weight, query_gain, key_gain, doc_ids, cotangent
 ):
     seq_acts = lax.all_gather(acts, "gy", axis=0, tiled=True)
-    full_in = lax.all_gather(in_weights, "gx", axis=0, tiled=True)
+    full_in = lax.all_gather(jnp.concatenate(in_weights, axis=1), "gx", axis=0, tiled=True)
     out_rows = lax.all_gather(out_weight, "gx", axis=1, tiled=True)
     local_width = full_in.shape[1] // 3
     length = seq_acts.shape[0]
@@ -2114,7 +2176,7 @@
         tiled=True,
     )
 
-    def back(grad_resid):
+    def back(grad_resid, small):
         seq_grad = lax.all_gather(grad_resid.astype(jnp.bfloat16), "gy", axis=0, tiled=True)
         grad_mixed = contract_cols(seq_grad, out_rows).astype(jnp.bfloat16)
         out_part = contract_rows(seq_grad, mixed_seq)
@@ -2172,7 +2234,7 @@
         out_sum = lax.psum_scatter(
             out_part.astype(jnp.bfloat16), "gx", scatter_dimension=0, tiled=True
         ).astype(jnp.float32)
-        return grad_acts.astype(jnp.float32), in_sum, out_sum, query_gain_part, key_gain_part
+        return grad_acts.astype(jnp.float32), in_sum, out_sum, query_gain_part, key_gain_part, sum_everywhere(small, 12)
 
     return attended, jnp.max(peak_blocks, axis=0), None, back
 
@@ -2191,22 +2253,26 @@
         jnp.concatenate([cosine, cosine], axis=1),
         jnp.concatenate([-sine, sine], axis=1),
     )
-    docs = (
-        jnp.broadcast_to(doc_ids[:, None], (length, HD)),
-        jnp.broadcast_to(doc_ids[None, :], (8, length)),
-    )
+    docs = doc_ids.reshape(-1, 128)
     attended, seq_acts, full_in, all_cot, saved, peaks = attend(
         acts, in_weights, out_weight, cotangent, query_gain, key_gain, tables, docs, 10
     )
-    heads = in_weights.shape[1] // (3 * HD)
-
-    def back(grad_resid):
-        seq_grad = all_gather(grad_resid.astype(jnp.bfloat16), False, 1)
-        part, weight_part, out_sum, gains = attend_back(
-            seq_grad, saved, query_gain, key_gain, tables, docs, seq_acts, full_in, 11
-        )
-        grad_acts, in_sum = leave(part, weight_part, 7)
-        return grad_acts, in_sum, out_sum, gains[0], gains[1]
+    heads = in_weights[0].shape[1] // HD
+
+    def back(grad_resid, small):
+        grad_acts, in_sum, out_sum, gains, small_sum = attend_back(
+            grad_resid.astype(jnp.bfloat16),
+            saved,
+            query_gain,
+            key_gain,
+            tables,
+            docs,
+            seq_acts,
+            full_in,
+            small,
+            11,
+        )
+        return grad_acts, in_sum, out_sum, gains[0], gains[1], small_sum
 
     return attended, peaks[:heads, 0], all_cot, back
 
@@ -2233,7 +2299,7 @@
     inputs = tokens.astype(jnp.float32)
     acts_float, norm_pull = jax.vjp(norm_rows, inputs, attn_gain)
     acts_low = acts_float.astype(jnp.bfloat16)
-    in_weights = jnp.concatenate([query_weight, key_weight, value_weight], axis=1)
+    in_weights = (query_weight, key_weight, value_weight)
     by_kernels = lax.axis_size("gy") == 8
     local_width = query_weight.shape[1]
     local_heads = local_width // HD
@@ -2275,25 +2341,18 @@
     grad_moe_in = grad_moe_in + contract_cols(grad_logits_low, router_weight)
     grad_resid_norm, moe_gain_part = moe_pull(grad_moe_in)
     grad_resid = grad_out + grad_resid_norm
-    grad_acts, in_sum, out_sum, query_gain_part, key_gain_part = attention_back(grad_resid)
+    early = (moe_gain_part, router_part.T, peak_slots)
+    grad_acts, in_sum, out_sum, query_gain_part, key_gain_part, early_sum = attention_back(
+        grad_resid, flat(early)
+    )
+    moe_gain_grad, router_flat, peaks = unflat(early_sum, early)
     query_sum = in_sum[:, :local_width]
     key_sum = in_sum[:, local_width : 2 * local_width]
     value_sum = in_sum[:, 2 * local_width :]
     norm_input_grad, attn_gain_part = norm_pull(grad_acts)
     input_grad = grad_resid + norm_input_grad
-    small = (
-        attn_gain_part,
-        moe_gain_part,
-        query_gain_part,
-        key_gain_part,
-        router_part.T,
-        peak_slots,
-    )
-    summed = sum_everywhere(jnp.concatenate([part.reshape(-1) for part in small]), 5)
-    ends = list(accumulate(part.size for part in small))
-    attn_gain_grad, moe_gain_grad, query_gain_grad, key_gain_grad, router_flat, peaks = (
-        summed[end - part.size : end].reshape(part.shape) for end, part in zip(ends, small)
-    )
+    late = (attn_gain_part, query_gain_part, key_gain_part)
+    attn_gain_grad, query_gain_grad, key_gain_grad = unflat(sum_everywhere(flat(late), 5), late)
     router_grad = router_flat.T
     peak_global = jnp.max(peaks, axis=0)
     ranked = -jnp.sort(-peak_global)

time: 666 us -> 646 us (0.970)
  Pallas kernels: 606 us -> 586 us
    pallas_call x2 -> x0, Pallas kernels: 83.4 us -> none  [the longest x1 59.9 us: leave(): pl.pallas_call(partial(leave_kernel, pieces, rows), out_shape=(jax.ShapeD...]
    pallas_call x1, Pallas kernels: 45.5 us -> 115 us  [attend_back(): pl.pallas_call(partial(attend_back_kernel, heads, pieces), out_shape=(jax...]
    unnamed x82 -> x76, local copies, waits for them, and re-layouts: 16.2 us -> 17.7 us
where the time goes in v9:
time: 646 us; the launch traced here: 645 us
  Pallas kernels  586 us (91%)
  local copies, waits for them, and re-layouts  27 us (4%)
  other arithmetic  26.9 us (4%)
    pallas_call x1, Pallas kernels, run_experts(): pl.pallas_call(partial(expert_kernel, n_z, span), out_shape=(jax.ShapeDty...  190 us
    pallas_call x1, Pallas kernels, attend(): pl.pallas_call(partial(attend_kernel, heads, pieces), out_shape=(jax.Shap...  153 us
    pallas_call x1, Pallas kernels, attend_back(): pl.pallas_call(partial(attend_back_kernel, heads, pieces), out_shape=(jax...  115 us
    pallas_call x1, Pallas kernels, pull_experts(): pl.pallas_call(partial(pull_kernel, n_i, rows), out_shape=(jax.ShapeDtype...  114 us
    unnamed x76, local copies, waits for them, and re-layouts  17.7 us
    pallas_call x1, Pallas kernels, sum_everywhere(): pl.pallas_call(partial(sum_kernel, n_z, bits), out_shape=jax.ShapeDtypeSt...  15 us

profile of v9, /device:TPU:0, one launch (start us, length us, event | category | flops | bytes accessed | tf_op | source)
XLA Modules:
  0.0 645.2 jit_solution(4275744080425337194)
XLA Ops:
  1.3 1.2 fusion.6
  2.5 0.6 copy-done.29
  3.1 0.5 iota.28
  3.7 2.0 fusion.2
  5.7 2.0 fusion.11
  7.7 1.3 pad_maximum_fusion
  9.0 152.5 %attend.1 = (f32[4,2,16,2048]{3,2,1,0:T(8,128)}, bf16[8,2,64,2048]{3,2,1,0:T(8,128)(2,1)}, bf16[4,512,768]{2,1,0:T(8,128)(2,1)}, bf16[4,256,512]{2,1,0:T(8,128)(...) custom-call(bf16[2,64,2048]{2,1,0:T(8,128)(2,1)} %bitcast.82, ...), custom_call_target="tpu_custom_call" | custom-call | tf_op jit(solution)/shard_map/attend/pallas_call | solution.py:1522
  161.5 0.8 slice_reduce_fusion.1
  162.3 0.2 dynamic_update_slice.3
  162.5 0.6 reshape.216
  163.1 1.4 multiply_reduce_fusion.2
  164.6 0.9 copy-done
  165.5 0.2 multiply_convert_fusion
  165.7 0.8 copy-done.4
  166.5 0.3 fusion.20
  166.7 0.0 copy-start.15
  166.8 0.5 multiply_divide_fusion
  167.3 0.0 copy-done.15
  167.4 0.5 multiply_divide_fusion.1
  168.0 0.0 copy-done.20
  168.0 0.6 broadcast_in_dim.95
  168.6 189.7 %experts.1 = (bf16[4096,2048]{1,0:T(8,128)(2,1)}, bf16[4096,1024]{1,0:T(8,128)(2,1)}, f32[32,1,128]{2,1,0:T(1,128)}, f32[512,2048]{1,0:T(8,128)}, f32[2,64,2048]{2,1,0:T(8,128)}) custom-call(bf16[2,64,2048]{2,1,0:T(8,128)(2,1)} %bitcast.71, bf16[4096,2048]{1,0:T(8,128)(2,1)} %bitcast.66, f32[32,1,128]{2,1,0:T(1,128)} %bitcast.88, ...), custom_call_target="tpu_custom_call" | custom-call | tf_op jit(solution)/shard_map/experts/pallas_call | solution.py:1021
  358.3 0.7 reduce_sum.154
  359.1 0.7 select_reduce_fusion.3
  359.8 0.7 multiply_reduce_fusion.4
  360.5 0.7 divide_add_fusion
  361.1 0.7 select_reduce_fusion.2
  361.8 0.7 multiply_reduce_fusion.3
  362.6 0.7 multiply_convert_fusion.3
  363.3 1.2 convolution_bitcast_fusion
  364.6 0.7 copy.65
  365.3 113.7 %pull_experts.1 = (f32[2,64,2048]{2,1,0:T(8,128)}, f32[2048,512]{1,0:T(8,128)}, f32[2048,512]{1,0:T(8,128)}) custom-call(bf16[4096,2048]{1,0:T(8,128)(2,1)} %get-tuple-element.46.all_ref, bf16[4096,1024]{1,0:T(8,128)(2,1)} %get-tuple-element.47.pair_ref, bf16[2048,512]{1,0:T(8,128)(2,1)} %bitcast.68, bf16[2048,512]{1,0:T(8,128)(2,1)} %bitcast.70), custom_call_target="tpu_custom_call" | custom-call | tf_op jit(solution)/shard_map/pull_experts/pallas_call | solution.py:1252
  479.1 2.2 multiply_reduce_fusion
  481.4 0.8 select_maximum_fusion
  482.2 1.2 fusion.17
  483.4 114.9 %attend_back.1 = (f32[4,2,16,2048]{3,2,1,0:T(8,128)}, f32[2,512,384]{2,1,0:T(8,128)}, f32[512,256]{1,0:T(8,128)}, f32[8,128]{1,0:T(8,128)}, f32[2,144,128]{2,1,0:T(8,128)}) custom-call(bf16[2,64,2048]{2,1,0:T(8,128)(2,1)} %bitcast.81, bf16[4,256,512]{2,1,0:T(8,128)(2,1)} %get-tuple-element.50.out_weight_ref, bf16[1024,256]{1,0:T(8,128)(2,1)} %get-tuple-element.51.mixed_ref, ...), custom_call_target="tpu_custom_call" | custom-call | tf_op jit(solution)/shard_map/attend_back/pallas_call | solution.py:1875
  598.3 0.8 slice_bitcast_fusion.3
  599.1 1.3 slice.68
  600.4 1.8 fusion.3
  602.1 0.7 multiply_multiply_fusion
  602.8 4.2 fusion.5
  607.0 0.6 select_maximum_fusion.2
  607.6 15.0 %sum_everywhere.1 = f32[2,16,128]{2,1,0:T(8,128)} custom-call(f32[2,16,128]{2,1,0:T(8,128)} %bitcast.89), custom_call_target="tpu_custom_call" | custom-call | tf_op jit(solution)/shard_map/sum_everywhere/pallas_call | solution.py:467
  622.6 1.3 fusion.19
  623.9 1.3 slice_bitcast_fusion.1
  625.2 0.7 slice_bitcast_fusion
  625.9 1.0 copy.64
  626.9 0.3 slice.66
  627.3 1.3 sort.15
  628.6 0.6 fusion.14
  629.2 0.6 compare_select_fusion
  629.8 0.1 dynamic-slice_sqrt_fusion
  629.9 0.1 broadcast_bitcast_fusion
  630.0 0.9 multiply_convert_fusion.1
  630.9 0.5 copy.59
  631.4 0.2 copy.60
  631.6 0.1 fusion.18
  631.7 1.0 copy.63
  632.7 1.0 copy.62
  633.7 1.0 copy.61
  634.7 4.8 copy.71
  639.5 2.1 copy.72
  641.7 1.6 copy-done.6
  643.2 2.0 copy.73
  (76 shorter events, 0.3 us)
Async XLA Ops:
  2.5 0.6 copy-start.29
  3.1 2.6 copy-start.24
  7.7 155.4 %copy-start.2 = (bf16[128,2048]{1,0:T(8,128)(2,1)S(1)}, bf16[128,2048]{1,0:T(8,128)(2,1)}, u32[]{:S(2)}) copy-start(bf16[128,2048]{1,0:T(8,128)(2,1)} %param.17) | copy-start | bytes 1572868
  9.0 156.5 %copy-start.16 = (f32[2048]{0:T(1024)S(1)}, f32[2048]{0:T(1024)}, u32[]{:S(2)}) copy-start(f32[2048]{0:T(1024)} %param.23) | copy-start | bytes 24580
  9.0 157.5 %copy-start.14 = (bf16[2048,16]{0,1:T(8,128)(2,1)S(1)}, bf16[2048,16]{0,1:T(8,128)(2,1)}, u32[]{:S(2)}) copy-start(bf16[2048,16]{0,1:T(8,128)(2,1)} %param.30) | copy-start | bytes 196612
  161.5 5.8 copy-start.18
  164.6 1.0 copy-start
  164.6 4.1 copy-start.30
  165.5 3.1 copy-start.22
  165.7 0.8 copy-start.4
  166.7 0.6 copy-start.15
  166.8 1.9 copy-start.21
  166.8 1.8 copy-start.25
  167.4 0.5 copy-start.26
  167.4 0.6 copy-start.20
  363.3 1.9 copy-start.19
  479.0 2.3 copy-start.31
  479.0 2.4 copy-start.13
  479.0 2.4 copy-start.28
  479.0 3.1 copy-start.1
  479.0 3.1 copy-start.5
  479.1 3.1 copy-start.17
  479.1 3.1 copy-start.23
  481.3 2.0 copy-start.3
  481.4 2.0 copy-start.27
  602.8 22.4 %copy-start.11 = (f32[2,144,128]{2,1,0:T(8,128)S(1)}, f32[2,144,128]{2,1,0:T(8,128)}, u32[]{:S(2)}) copy-start(f32[2,144,128]{2,1,0:T(8,128)} %get-tuple-element.61) | copy-start | bytes 442372
  602.8 23.1 %copy-start.12 = (f32[512,256]{1,0:T(8,128)S(1)}, f32[512,256]{1,0:T(8,128)}, u32[]{:S(2)}) copy-start(f32[512,256]{1,0:T(8,128)} %get-tuple-element.63) | copy-start | bytes 1572868
  602.8 24.5 %copy-start.33 = (s32[16]{0:T(128)S(1)}, s32[16]{0:T(128)}, u32[]{:S(2)}) copy-start(s32[16]{0:T(128)} %iota.28) | copy-start | bytes 196
  607.0 23.0 %copy-start.9 = (bf16[512,256]{1,0:T(8,128)(2,1)S(1)}, bf16[512,256]{1,0:T(8,128)(2,1)}, u32[]{:S(2)}) copy-start(bf16[512,256]{1,0:T(8,128)(2,1)} %query_weight.1) | copy-start | bytes 786436
  607.0 23.0 %copy-start.10 = (bf16[512,256]{1,0:T(8,128)(2,1)S(1)}, bf16[512,256]{1,0:T(8,128)(2,1)}, u32[]{:S(2)}) copy-start(bf16[512,256]{1,0:T(8,128)(2,1)} %key_weight.1) | copy-start | bytes 786436
  607.0 23.9 %copy-start.8 = (f32[2,512,384]{2,1,0:T(8,128)S(1)}, f32[2,512,384]{2,1,0:T(8,128)}, u32[]{:S(2)}) copy-start(f32[2,512,384]{2,1,0:T(8,128)} %get-tuple-element.62) | copy-start | bytes 4718596
  629.8 1.8 copy-start.32
  634.7 4.8 copy-start.7
  639.5 3.7 copy-start.6

commit v10 on v9

--- a/solution.py
+++ b/solution.py
@@ -849,9 +849,9 @@
 
     backs = (
         (stage_core, lambda k: 2 * k + 1, 2),
-        (stage_a, lambda k: 2 * k + 2, 2),
-        (stage_b, lambda k: 2 * k + 3, 2),
-        (stage_c, lambda k: 2 * k + 4, 1),
+        (stage_a, lambda k: 2 * k + 1, 4),
+        (stage_b, lambda k: 2 * k + 2, 4),
+        (stage_c, lambda k: 2 * k + 3, 4),
     )
 
     def events(s, phase):
@@ -1604,6 +1604,7 @@
     totals_ref,
     query_gain,
     key_gain,
+    attn_gain,
     cosine_ref,
     sine_ref,
     docs_ref,
@@ -1611,10 +1612,15 @@
     acts_hbm,
     weight_hbm,
     grad_acts,
+    query_sum,
+    key_sum_out,
+    value_sum_out,
+    out_sum,
+    small_sum,
+    late_sum,
     weight_sum,
-    out_sum,
     gain_ref,
-    small_sum,
+    late_ref,
     row_docs,
     col_docs,
     seq_ref,
@@ -1683,7 +1689,10 @@
         for h in range(heads)
     ]
     near, near_finish = gather_steps(1, span, own_grad, seq_ref, near_send, near_recv, near_local)
-    small = sum_steps(n_z, span.bit_length() - 1, small_ref, small_sum, *small_scratch)
+    bits = span.bit_length() - 1
+    half_scratch = len(small_scratch) // 2
+    small = sum_steps(n_z, bits, small_ref, small_sum, *small_scratch[:half_scratch])
+    late = sum_steps(n_z, bits, late_ref, late_sum, *small_scratch[half_scratch:])
     back = []
     scatter_kernel(
         False,
@@ -1751,6 +1760,7 @@
     grad_mixed[...] = total.astype(bf16)
     small[3]()
     gain_ref[...] = jnp.zeros_like(gain_ref)
+    late_ref[...] = jnp.zeros_like(late_ref)
     for h in range(heads):
         cols = slice(h * HD, (h + 1) * HD)
         key = ready_ref[:, local + h * HD : local + (h + 1) * HD]
@@ -1824,21 +1834,33 @@
     @pl.loop(0, width // block)
     def _(t):
         cols = pl.ds(pl.multiple_of(t * block, block), block)
-        sent = dot(grad_heads[...], weight_ref[cols, :], last_dims).astype(bf16)
-        sent = sent.reshape(span, pieces, 2, rows, block)
+        pulled = dot(grad_heads[...], weight_ref[cols, :], last_dims)
+        gained = jnp.sum(pulled * acts_ref[:, cols].astype(f32), axis=0, keepdims=True)
+        gained = gained / attn_gain[:, cols]
+        for j in range(block // 128):
+            late_ref[0, pl.ds(t * (block // 128) + j, 1), :] = gained[:, j * 128 : (j + 1) * 128]
+        sent = pulled.astype(bf16).reshape(span, pieces, 2, rows, block)
         for p in range(pieces):
             part_ref[p, :, :, :, cols] = sent[:, p]
 
+    late_ref[1, :8, :] = gain_ref[...]
     small[5]()
     waiting = [relay for chain in chains[:-1] for relay in chain[1][2:]] + list(chains[-1][1])
     for i, step in enumerate(back[:-1]):
         step()
+        if i < len(late) - 2:
+            late[i]()
         if i % 2 == 0 and waiting:
             waiting.pop(0)()
     for relay in waiting:
         relay()
     for chain in chains:
         chain[2]()
+    for step in late[min(len(late) - 2, len(back) - 1) :]:
+        step()
+    for h in range(heads):
+        for j, target in enumerate((query_sum, key_sum_out, value_sum_out)):
+            target[:, h * HD : (h + 1) * HD] = weight_sum[h, :, j * HD : (j + 1) * HD]
     back[-1]()
 
 
@@ -1847,6 +1869,7 @@
     saved,
     query_gain,
     key_gain,
+    attn_gain,
     tables,
     docs,
     acts,
@@ -1872,18 +1895,24 @@
     dma = pltpu.SemaphoreType.DMA
     vmem = pl.BlockSpec(memory_space=pltpu.VMEM)
     hbm = pl.BlockSpec(memory_space=pl.ANY)
-    grad_acts, weight_sum, out_sum, gains, small_sum = pl.pallas_call(
+    late_shape = (2, -(-width // (128 * 8)) * 8, 128)
+    grad_acts, *in_sums, out_sum, small_sum, late_sum = pl.pallas_call(
         partial(attend_back_kernel, heads, pieces),
         out_shape=(
             jax.ShapeDtypeStruct((pieces, 2) + piece, f32),
-            jax.ShapeDtypeStruct((heads,) + in_block[2:], f32),
+            jax.ShapeDtypeStruct((in_block[2], local), f32),
+            jax.ShapeDtypeStruct((in_block[2], local), f32),
+            jax.ShapeDtypeStruct((in_block[2], local), f32),
             jax.ShapeDtypeStruct(out_block[1:], f32),
-            jax.ShapeDtypeStruct((8, HD), f32),
             jax.ShapeDtypeStruct(halves.shape, f32),
+            jax.ShapeDtypeStruct(late_shape, f32),
         ),
-        in_specs=[vmem] * 13 + [hbm] * 2,
-        out_specs=(vmem,) * 5,
+        in_specs=[vmem] * 14 + [hbm] * 2,
+        out_specs=(vmem,) * 7,
         scratch_shapes=[
+            pltpu.VMEM((heads,) + in_block[2:], f32),
+            pltpu.VMEM((8, HD), f32),
+            pltpu.VMEM(late_shape, f32),
             pltpu.VMEM((length, 128), f32),
             pltpu.VMEM((8, length), f32),
             pltpu.VMEM((span,) + half, bf16),
@@ -1927,7 +1956,8 @@
             dma((pieces, 2)),
             dma((pieces,)),
         ]
-        + sum_scratch(n_z, bits, halves.shape[1]),
+        + sum_scratch(n_z, bits, halves.shape[1])
+        + sum_scratch(n_z, bits, late_shape[1]),
         compiler_params=pltpu.CompilerParams(
             collective_id=collective_id, has_side_effects=True, vmem_limit_bytes=67043328
         ),
@@ -1942,19 +1972,19 @@
         totals,
         query_gain.reshape(1, HD),
         key_gain.reshape(1, HD),
+        attn_gain.reshape(1, width),
         *tables,
         docs,
         halves,
         acts,
         weights,
     )
-    weight_sum = weight_sum.reshape(heads, -1, 3, HD).transpose(1, 2, 0, 3)
     return (
         grad_acts.reshape(tokens, width),
-        weight_sum.reshape(-1, 3 * local),
+        in_sums,
         out_sum,
-        gains,
         small_sum.reshape(-1)[: small.shape[0]],
+        (late_sum[0].reshape(-1)[:width], late_sum[1, 0], late_sum[1, 1]),
     )
 
 
@@ -2118,7 +2148,7 @@
 
 
 def plain_attention(
-    acts, in_weights, out_weight, query_gain, key_gain, doc_ids, cotangent
+    acts, in_weights, out_weight, query_gain, key_gain, attn_gain, doc_ids, cotangent
 ):
     seq_acts = lax.all_gather(acts, "gy", axis=0, tiled=True)
     full_in = lax.all_gather(jnp.concatenate(in_weights, axis=1), "gx", axis=0, tiled=True)
@@ -2234,13 +2264,15 @@
         out_sum = lax.psum_scatter(
             out_part.astype(jnp.bfloat16), "gx", scatter_dimension=0, tiled=True
         ).astype(jnp.float32)
-        return grad_acts.astype(jnp.float32), in_sum, out_sum, query_gain_part, key_gain_part, sum_everywhere(small, 12)
+        in_sums = (in_sum[:, :local_width], in_sum[:, local_width : 2 * local_width], in_sum[:, 2 * local_width :])
+        gain_parts = (None, query_gain_part, key_gain_part)
+        return grad_acts.astype(jnp.float32), in_sums, out_sum, sum_everywhere(small, 12), gain_parts
 
     return attended, jnp.max(peak_blocks, axis=0), None, back
 
 
 def kernel_attention(
-    acts, in_weights, out_weight, query_gain, key_gain, doc_ids, cotangent
+    acts, in_weights, out_weight, query_gain, key_gain, attn_gain, doc_ids, cotangent
 ):
     length = doc_ids.shape[0]
     halfway = HD // 2
@@ -2260,11 +2292,12 @@
     heads = in_weights[0].shape[1] // HD
 
     def back(grad_resid, small):
-        grad_acts, in_sum, out_sum, gains, small_sum = attend_back(
+        return attend_back(
             grad_resid.astype(jnp.bfloat16),
             saved,
             query_gain,
             key_gain,
+            attn_gain,
             tables,
             docs,
             seq_acts,
@@ -2272,7 +2305,6 @@
             small,
             11,
         )
-        return grad_acts, in_sum, out_sum, gains[0], gains[1], small_sum
 
     return attended, peaks[:heads, 0], all_cot, back
 
@@ -2305,7 +2337,7 @@
     local_heads = local_width // HD
     attention = kernel_attention if by_kernels else plain_attention
     attended, own_peaks, all_cot, attention_back = attention(
-        acts_low, in_weights, out_weight, query_gain, key_gain, doc_ids, cotangent
+        acts_low, in_weights, out_weight, query_gain, key_gain, attn_gain, doc_ids, cotangent
     )
     start_head = lax.axis_index("gy") * local_heads
     peak_slots = lax.dynamic_update_slice(
@@ -2342,17 +2374,15 @@
     grad_resid_norm, moe_gain_part = moe_pull(grad_moe_in)
     grad_resid = grad_out + grad_resid_norm
     early = (moe_gain_part, router_part.T, peak_slots)
-    grad_acts, in_sum, out_sum, query_gain_part, key_gain_part, early_sum = attention_back(
-        grad_resid, flat(early)
-    )
+    grad_acts, in_sums, out_sum, early_sum, late = attention_back(grad_resid, flat(early))
+    query_sum, key_sum, value_sum = in_sums
     moe_gain_grad, router_flat, peaks = unflat(early_sum, early)
-    query_sum = in_sum[:, :local_width]
-    key_sum = in_sum[:, local_width : 2 * local_width]
-    value_sum = in_sum[:, 2 * local_width :]
     norm_input_grad, attn_gain_part = norm_pull(grad_acts)
     input_grad = grad_resid + norm_input_grad
-    late = (attn_gain_part, query_gain_part, key_gain_part)
-    attn_gain_grad, query_gain_grad, key_gain_grad = unflat(sum_everywhere(flat(late), 5), late)
+    if late[0] is None:
+        late = (attn_gain_part, *late[1:])
+        late = unflat(sum_everywhere(flat(late), 5), late)
+    attn_gain_grad, query_gain_grad, key_gain_grad = late
     router_grad = router_flat.T
     peak_global = jnp.max(peaks, axis=0)
     ranked = -jnp.sort(-peak_global)

time: 646 us -> 624 us (0.966)
  Pallas kernels: 586 us -> 567 us
    pallas_call x1 -> x0, Pallas kernels: 15 us -> none  [sum_everywhere(): pl.pallas_call(partial(sum_kernel, n_z, bits), out_shape=jax.ShapeDtypeSt...]
    pallas_call x1, Pallas kernels: 190 us -> 181 us  [run_experts(): pl.pallas_call(partial(expert_kernel, n_z, span), out_shape=(jax.ShapeDty...]
    unnamed x76 -> x72, local copies, waits for them, and re-layouts: 17.7 us -> 15.9 us
where the time goes in v10:
time: 624 us; the launch traced here: 623 us
  Pallas kernels  567 us (91%)
  other arithmetic  29.2 us (5%)
  local copies, waits for them, and re-layouts  21.5 us (3%)
    pallas_call x1, Pallas kernels, run_experts(): pl.pallas_call(partial(expert_kernel, n_z, span), out_shape=(jax.ShapeDty...  181 us
    pallas_call x1, Pallas kernels, attend(): pl.pallas_call(partial(attend_kernel, heads, pieces), out_shape=(jax.Shap...  153 us
    pallas_call x1, Pallas kernels, attend_back(): pl.pallas_call(partial(attend_back_kernel, heads, pieces), out_shape=(jax...  118 us
    pallas_call x1, Pallas kernels, pull_experts(): pl.pallas_call(partial(pull_kernel, n_i, rows), out_shape=(jax.ShapeDtype...  116 us
    unnamed x72, local copies, waits for them, and re-layouts  15.9 us

profile of v10, /device:TPU:0, one launch (start us, length us, event | category | flops | bytes accessed | tf_op | source)
XLA Modules:
  0.0 623.0 jit_solution(10041890801756129225)
XLA Ops:
  1.3 1.2 fusion.2
  2.6 0.5 copy-done.28
  3.0 0.5 iota.28
  3.6 2.1 fusion.4
  5.7 2.0 fusion.9
  7.6 0.0 copy-start.17
  7.6 1.3 pad_maximum_fusion
  9.0 152.5 %attend.1 = (f32[4,2,16,2048]{3,2,1,0:T(8,128)}, bf16[8,2,64,2048]{3,2,1,0:T(8,128)(2,1)}, bf16[4,512,768]{2,1,0:T(8,128)(2,1)}, bf16[4,256,512]{2,1,0:T(8,128)(...) custom-call(bf16[2,64,2048]{2,1,0:T(8,128)(2,1)} %bitcast.74, ...), custom_call_target="tpu_custom_call" | custom-call | tf_op jit(solution)/shard_map/attend/pallas_call | solution.py:1522
  161.5 0.8 slice_reduce_fusion.1
  162.3 0.2 dynamic_update_slice.3
  162.5 0.6 reshape.201
  163.1 1.4 multiply_reduce_fusion.2
  164.5 0.9 copy-done
  165.5 0.2 multiply_convert_fusion
  165.6 0.0 copy-start.4
  165.7 0.8 copy-done.4
  166.4 0.3 fusion.16
  166.7 0.0 copy-start.16
  166.7 0.0 copy-start.21
  166.8 0.5 multiply_divide_fusion
  167.3 0.0 copy-done.16
  167.4 0.0 copy-start.20
  167.4 0.5 multiply_divide_fusion.1
  167.9 0.0 copy-done.20
  168.0 0.6 broadcast_in_dim.97
  168.6 181.0 %experts.1 = (bf16[4096,2048]{1,0:T(8,128)(2,1)}, bf16[4096,1024]{1,0:T(8,128)(2,1)}, f32[32,1,128]{2,1,0:T(1,128)}, f32[512,2048]{1,0:T(8,128)}, f32[2,64,2048]{2,1,0:T(8,128)}) custom-call(bf16[2,64,2048]{2,1,0:T(8,128)(2,1)} %bitcast.65, bf16[4096,2048]{1,0:T(8,128)(2,1)} %bitcast.60, f32[32,1,128]{2,1,0:T(1,128)} %bitcast.81, ...), custom_call_target="tpu_custom_call" | custom-call | tf_op jit(solution)/shard_map/experts/pallas_call | solution.py:1021
  349.6 0.7 reduce_sum.143
  350.4 0.7 select_reduce_fusion.3
  351.1 0.7 multiply_reduce_fusion.4
  351.8 0.7 divide_add_fusion
  352.5 0.7 select_reduce_fusion.2
  353.2 0.7 multiply_reduce_fusion.3
  353.9 0.7 multiply_convert_fusion.3
  354.7 1.2 convolution_bitcast_fusion
  355.9 0.7 copy.45
  356.6 115.9 %pull_experts.1 = (f32[2,64,2048]{2,1,0:T(8,128)}, f32[2048,512]{1,0:T(8,128)}, f32[2048,512]{1,0:T(8,128)}) custom-call(bf16[4096,2048]{1,0:T(8,128)(2,1)} %get-tuple-element.48.all_ref, bf16[4096,1024]{1,0:T(8,128)(2,1)} %get-tuple-element.49.pair_ref, bf16[2048,512]{1,0:T(8,128)(2,1)} %bitcast.62, bf16[2048,512]{1,0:T(8,128)(2,1)} %bitcast.64), custom_call_target="tpu_custom_call" | custom-call | tf_op jit(solution)/shard_map/pull_experts/pallas_call | solution.py:1252
  472.5 2.2 multiply_reduce_fusion
  474.7 0.7 multiply_multiply_fusion.1
  475.4 1.6 select_maximum_fusion
  477.0 2.3 fusion.15
  479.3 117.6 %attend_back.1 = (f32[4,2,16,2048]{3,2,1,0:T(8,128)}, f32[512,256]{1,0:T(8,128)}, f32[512,256]{1,0:T(8,128)}, f32[512,256]{1,0:T(8,128)}, f32[512,256]{1,0:T(8,1...) custom-call(bf16[2,64,2048]{2,1,0:T(8,128)(2,1)} %bitcast.73, bf16[4,256,512]{2,1,0:T(8,128)(2,1)} %get-tuple-element.52.out_weight_ref, ...), custom_call_target="tpu_custom_call" | custom-call | tf_op jit(solution)/shard_map/attend_back/pallas_call | solution.py:1899
  596.9 1.6 fusion.5
  598.5 0.7 multiply_multiply_fusion
  599.2 4.2 fusion.1
  603.5 0.5 slice_bitcast_fusion.2
  604.0 0.6 slice_bitcast_fusion.1
  604.6 0.6 slice.40
  605.2 0.7 slice_bitcast_fusion
  605.9 1.0 copy.44
  606.9 0.3 slice.38
  607.3 1.3 sort.15
  608.6 0.6 fusion.12
  609.2 0.9 compare_select_fusion
  610.1 0.1 dynamic-slice_sqrt_fusion
  610.2 0.1 broadcast_bitcast_fusion
  610.3 0.9 multiply_convert_fusion.1
  611.2 0.8 copy.54
  612.0 0.8 copy.55
  612.8 0.8 copy.56
  613.6 2.1 copy.57
  615.7 1.6 copy-done.6
  617.3 2.1 copy.58
  619.4 1.6 copy-done.5
  621.0 2.0 copy.59
  (66 shorter events, 0.3 us)
Async XLA Ops:
  2.5 0.5 copy-start.28
  2.6 5.1 copy-start.26
  3.6 159.5 %copy-start.2 = (bf16[128,2048]{1,0:T(8,128)(2,1)S(1)}, bf16[128,2048]{1,0:T(8,128)(2,1)}, u32[]{:S(2)}) copy-start(bf16[128,2048]{1,0:T(8,128)(2,1)} %param.17) | copy-start | bytes 1572868
  7.6 157.8 %copy-start.17 = (f32[2048]{0:T(1024)S(1)}, f32[2048]{0:T(1024)}, u32[]{:S(2)}) copy-start(f32[2048]{0:T(1024)} %param.23) | copy-start | bytes 24580
  9.0 157.5 %copy-start.15 = (bf16[2048,16]{0,1:T(8,128)(2,1)S(1)}, bf16[2048,16]{0,1:T(8,128)(2,1)}, u32[]{:S(2)}) copy-start(bf16[2048,16]{0,1:T(8,128)(2,1)} %param.30) | copy-start | bytes 196612
  9.0 158.4 %copy-start.18 = (s32[128,8]{0,1:T(8,128)S(1)}, s32[128,8]{0,1:T(8,128)}, u32[]{:S(2)}) copy-start(s32[128,8]{0,1:T(8,128)} %param.19) | copy-start | bytes 12292
  164.5 1.0 copy-start
  164.5 4.1 copy-start.29
  165.5 3.1 copy-start.22
  165.6 0.8 copy-start.4
  166.7 0.6 copy-start.16
  166.7 1.9 copy-start.21
  166.7 1.8 copy-start.24
  167.4 0.5 copy-start.25
  167.4 0.6 copy-start.20
  354.6 1.9 copy-start.19
  472.4 4.5 copy-start.1
  474.7 4.6 copy-start.3
  475.4 3.9 copy-start.27
  596.9 6.6 %copy-start.23 = (f32[2,16,128]{2,1,0:T(8,128)S(1)}, f32[2,16,128]{2,1,0:T(8,128)}, u32[]{:S(2)}) copy-start(f32[2,16,128]{2,1,0:T(8,128)} %get-tuple-element.62) | copy-start | bytes 49156
  596.9 7.7 %copy-start.10 = (f32[2,144,128]{2,1,0:T(8,128)S(1)}, f32[2,144,128]{2,1,0:T(8,128)}, u32[]{:S(2)}) copy-start(f32[2,144,128]{2,1,0:T(8,128)} %get-tuple-element.63) | copy-start | bytes 442372
  596.9 9.0 %copy-start.14 = (f32[512,256]{1,0:T(8,128)S(1)}, f32[512,256]{1,0:T(8,128)}, u32[]{:S(2)}) copy-start(f32[512,256]{1,0:T(8,128)} %get-tuple-element.67) | copy-start | bytes 1572868
  599.2 8.1 %copy-start.31 = (s32[16]{0:T(128)S(1)}, s32[16]{0:T(128)}, u32[]{:S(2)}) copy-start(s32[16]{0:T(128)} %iota.28) | copy-start | bytes 196
  599.2 11.1 %copy-start.8 = (bf16[512,256]{1,0:T(8,128)(2,1)S(1)}, bf16[512,256]{1,0:T(8,128)(2,1)}, u32[]{:S(2)}) copy-start(bf16[512,256]{1,0:T(8,128)(2,1)} %query_weight.1) | copy-start | bytes 786436
  599.2 11.1 %copy-start.9 = (bf16[512,256]{1,0:T(8,128)(2,1)S(1)}, bf16[512,256]{1,0:T(8,128)(2,1)}, u32[]{:S(2)}) copy-start(bf16[512,256]{1,0:T(8,128)(2,1)} %key_weight.1) | copy-start | bytes 786436
  599.2 12.0 %copy-start.13 = (f32[512,256]{1,0:T(8,128)S(1)}, f32[512,256]{1,0:T(8,128)}, u32[]{:S(2)}) copy-start(f32[512,256]{1,0:T(8,128)} %get-tuple-element.183) | copy-start | bytes 1572868
  603.4 8.5 %copy-start.12 = (f32[512,256]{1,0:T(8,128)S(1)}, f32[512,256]{1,0:T(8,128)}, u32[]{:S(2)}) copy-start(f32[512,256]{1,0:T(8,128)} %get-tuple-element.184) | copy-start | bytes 1572868
  603.5 9.3 %copy-start.11 = (f32[512,256]{1,0:T(8,128)S(1)}, f32[512,256]{1,0:T(8,128)}, u32[]{:S(2)}) copy-start(f32[512,256]{1,0:T(8,128)} %get-tuple-element.185) | copy-start | bytes 1572868
  608.5 5.0 copy-start.7
  610.1 5.6 copy-start.30
  613.6 3.7 copy-start.6
  617.3 3.7 copy-start.5

commit v11 on v10

--- a/solution.py
+++ b/solution.py
@@ -1163,7 +1163,7 @@
 
     def accumulate(i):
         moe, pair = moe_buf.at[i % 2], pair_buf.at[i % 2]
-        tile = 256
+        tile = 512
 
         @pl.loop(0, width // tile)
         def _(t):
@@ -1221,12 +1221,12 @@
             multiply(t)
         if 0 <= t - 1 < n_i:
             stage_a(t - 1)
-        if 0 <= t - 2 < n_i:
-            stage_b(t - 2)
         if 0 <= t - 1 < n_i:
             accumulate(t - 1)
-        if 0 <= t - 3 < n_i:
-            stage_c(t - 3)
+        if 0 <= t - 1 < n_i:
+            stage_b(t - 1)
+        if 0 <= t - 2 < n_i:
+            stage_c(t - 2)
     for i in range(n_i):
         for q in range(4):
             core_copy(i, q).wait_send()

time: 624 us -> 615 us (0.986)
  Pallas kernels: 567 us -> 558 us
    pallas_call x1, Pallas kernels: 116 us -> 109 us  [pull_experts(): pl.pallas_call(partial(pull_kernel, n_i, rows), out_shape=(jax.ShapeDtype...]
where the time goes in v11:
time: 615 us; the launch traced here: 614 us
  Pallas kernels  558 us (91%)
  other arithmetic  29.2 us (5%)
  local copies, waits for them, and re-layouts  21.5 us (3%)
    pallas_call x1, Pallas kernels, run_experts(): pl.pallas_call(partial(expert_kernel, n_z, span), out_shape=(jax.ShapeDty...  181 us
    pallas_call x1, Pallas kernels, attend(): pl.pallas_call(partial(attend_kernel, heads, pieces), out_shape=(jax.Shap...  153 us
    pallas_call x1, Pallas kernels, attend_back(): pl.pallas_call(partial(attend_back_kernel, heads, pieces), out_shape=(jax...  115 us
    pallas_call x1, Pallas kernels, pull_experts(): pl.pallas_call(partial(pull_kernel, n_i, rows), out_shape=(jax.ShapeDtype...  109 us
    unnamed x72, local copies, waits for them, and re-layouts  15.9 us

profile of v11, /device:TPU:0, one launch (start us, length us, event | category | flops | bytes accessed | tf_op | source)
XLA Modules:
  0.0 614.1 jit_solution(17635851100715414621)
XLA Ops:
  1.3 1.2 fusion.2
  2.6 0.5 copy-done.28
  3.0 0.5 iota.28
  3.6 2.1 fusion.4
  5.7 2.0 fusion.9
  7.6 1.3 pad_maximum_fusion
  9.0 152.5 %attend.1 = (f32[4,2,16,2048]{3,2,1,0:T(8,128)}, bf16[8,2,64,2048]{3,2,1,0:T(8,128)(2,1)}, bf16[4,512,768]{2,1,0:T(8,128)(2,1)}, bf16[4,256,512]{2,1,0:T(8,128)(...) custom-call(bf16[2,64,2048]{2,1,0:T(8,128)(2,1)} %bitcast.74, ...), custom_call_target="tpu_custom_call" | custom-call | tf_op jit(solution)/shard_map/attend/pallas_call | solution.py:1522
  161.5 0.8 slice_reduce_fusion.1
  162.3 0.2 dynamic_update_slice.3
  162.5 0.6 reshape.201
  163.1 1.4 multiply_reduce_fusion.2
  164.5 0.0 copy-start.29
  164.5 0.9 copy-done
  165.5 0.2 multiply_convert_fusion
  165.7 0.8 copy-done.4
  166.4 0.3 fusion.16
  166.7 0.0 copy-start.16
  166.8 0.5 multiply_divide_fusion
  167.3 0.0 copy-done.16
  167.4 0.5 multiply_divide_fusion.1
  167.9 0.0 copy-done.20
  168.0 0.6 broadcast_in_dim.97
  168.6 181.0 %experts.1 = (bf16[4096,2048]{1,0:T(8,128)(2,1)}, bf16[4096,1024]{1,0:T(8,128)(2,1)}, f32[32,1,128]{2,1,0:T(1,128)}, f32[512,2048]{1,0:T(8,128)}, f32[2,64,2048]{2,1,0:T(8,128)}) custom-call(bf16[2,64,2048]{2,1,0:T(8,128)(2,1)} %bitcast.65, bf16[4096,2048]{1,0:T(8,128)(2,1)} %bitcast.60, f32[32,1,128]{2,1,0:T(1,128)} %bitcast.81, ...), custom_call_target="tpu_custom_call" | custom-call | tf_op jit(solution)/shard_map/experts/pallas_call | solution.py:1021
  349.6 0.7 reduce_sum.143
  350.4 0.7 select_reduce_fusion.3
  351.1 0.7 multiply_reduce_fusion.4
  351.8 0.7 divide_add_fusion
  352.5 0.7 select_reduce_fusion.2
  353.2 0.7 multiply_reduce_fusion.3
  353.9 0.7 multiply_convert_fusion.3
  354.7 1.2 convolution_bitcast_fusion
  355.9 0.7 copy.45
  356.6 109.4 %pull_experts.1 = (f32[2,64,2048]{2,1,0:T(8,128)}, f32[2048,512]{1,0:T(8,128)}, f32[2048,512]{1,0:T(8,128)}) custom-call(bf16[4096,2048]{1,0:T(8,128)(2,1)} %get-tuple-element.48.all_ref, bf16[4096,1024]{1,0:T(8,128)(2,1)} %get-tuple-element.49.pair_ref, bf16[2048,512]{1,0:T(8,128)(2,1)} %bitcast.62, bf16[2048,512]{1,0:T(8,128)(2,1)} %bitcast.64), custom_call_target="tpu_custom_call" | custom-call | tf_op jit(solution)/shard_map/pull_experts/pallas_call | solution.py:1252
  466.0 2.2 multiply_reduce_fusion
  468.2 0.0 copy-start.3
  468.2 0.7 multiply_multiply_fusion.1
  468.9 1.6 select_maximum_fusion
  470.5 2.3 fusion.15
  472.8 115.2 %attend_back.1 = (f32[4,2,16,2048]{3,2,1,0:T(8,128)}, f32[512,256]{1,0:T(8,128)}, f32[512,256]{1,0:T(8,128)}, f32[512,256]{1,0:T(8,128)}, f32[512,256]{1,0:T(8,1...) custom-call(bf16[2,64,2048]{2,1,0:T(8,128)(2,1)} %bitcast.73, bf16[4,256,512]{2,1,0:T(8,128)(2,1)} %get-tuple-element.52.out_weight_ref, ...), custom_call_target="tpu_custom_call" | custom-call | tf_op jit(solution)/shard_map/attend_back/pallas_call | solution.py:1899
  588.1 1.6 fusion.5
  589.7 0.7 multiply_multiply_fusion
  590.4 0.0 copy-start.9
  590.4 4.2 fusion.1
  594.6 0.5 slice_bitcast_fusion.2
  595.1 0.6 slice_bitcast_fusion.1
  595.7 0.6 slice.40
  596.4 0.7 slice_bitcast_fusion
  597.0 1.0 copy.44
  598.0 0.3 slice.38
  598.4 1.3 sort.15
  599.7 0.6 fusion.12
  600.3 0.9 compare_select_fusion
  601.3 0.0 copy-start.30
  601.3 0.1 dynamic-slice_sqrt_fusion
  601.4 0.1 broadcast_bitcast_fusion
  601.4 0.9 multiply_convert_fusion.1
  602.3 0.8 copy.54
  603.1 0.8 copy.55
  603.9 0.8 copy.56
  604.7 2.1 copy.57
  606.9 1.6 copy-done.6
  608.4 2.1 copy.58
  610.6 1.6 copy-done.5
  612.1 2.0 copy.59
  (66 shorter events, 0.3 us)
Async XLA Ops:
  2.5 0.5 copy-start.28
  2.6 5.1 copy-start.26
  3.6 159.5 %copy-start.2 = (bf16[128,2048]{1,0:T(8,128)(2,1)S(1)}, bf16[128,2048]{1,0:T(8,128)(2,1)}, u32[]{:S(2)}) copy-start(bf16[128,2048]{1,0:T(8,128)(2,1)} %param.17) | copy-start | bytes 1572868
  7.6 157.8 %copy-start.17 = (f32[2048]{0:T(1024)S(1)}, f32[2048]{0:T(1024)}, u32[]{:S(2)}) copy-start(f32[2048]{0:T(1024)} %param.23) | copy-start | bytes 24580
  9.0 157.5 %copy-start.15 = (bf16[2048,16]{0,1:T(8,128)(2,1)S(1)}, bf16[2048,16]{0,1:T(8,128)(2,1)}, u32[]{:S(2)}) copy-start(bf16[2048,16]{0,1:T(8,128)(2,1)} %param.30) | copy-start | bytes 196612
  9.0 158.4 %copy-start.18 = (s32[128,8]{0,1:T(8,128)S(1)}, s32[128,8]{0,1:T(8,128)}, u32[]{:S(2)}) copy-start(s32[128,8]{0,1:T(8,128)} %param.19) | copy-start | bytes 12292
  164.5 1.0 copy-start
  164.5 4.1 copy-start.29
  165.5 3.1 copy-start.22
  165.6 0.8 copy-start.4
  166.7 0.6 copy-start.16
  166.7 1.9 copy-start.21
  166.7 1.8 copy-start.24
  167.4 0.5 copy-start.25
  167.4 0.6 copy-start.20
  354.6 1.9 copy-start.19
  465.9 4.6 copy-start.1
  468.2 4.6 copy-start.3
  468.9 3.9 copy-start.27
  588.0 6.6 %copy-start.23 = (f32[2,16,128]{2,1,0:T(8,128)S(1)}, f32[2,16,128]{2,1,0:T(8,128)}, u32[]{:S(2)}) copy-start(f32[2,16,128]{2,1,0:T(8,128)} %get-tuple-element.62) | copy-start | bytes 49156
  588.0 7.7 %copy-start.10 = (f32[2,144,128]{2,1,0:T(8,128)S(1)}, f32[2,144,128]{2,1,0:T(8,128)}, u32[]{:S(2)}) copy-start(f32[2,144,128]{2,1,0:T(8,128)} %get-tuple-element.63) | copy-start | bytes 442372
  588.0 9.0 %copy-start.14 = (f32[512,256]{1,0:T(8,128)S(1)}, f32[512,256]{1,0:T(8,128)}, u32[]{:S(2)}) copy-start(f32[512,256]{1,0:T(8,128)} %get-tuple-element.67) | copy-start | bytes 1572868
  590.4 8.1 %copy-start.31 = (s32[16]{0:T(128)S(1)}, s32[16]{0:T(128)}, u32[]{:S(2)}) copy-start(s32[16]{0:T(128)} %iota.28) | copy-start | bytes 196
  590.4 11.1 %copy-start.8 = (bf16[512,256]{1,0:T(8,128)(2,1)S(1)}, bf16[512,256]{1,0:T(8,128)(2,1)}, u32[]{:S(2)}) copy-start(bf16[512,256]{1,0:T(8,128)(2,1)} %query_weight.1) | copy-start | bytes 786436
  590.4 11.1 %copy-start.9 = (bf16[512,256]{1,0:T(8,128)(2,1)S(1)}, bf16[512,256]{1,0:T(8,128)(2,1)}, u32[]{:S(2)}) copy-start(bf16[512,256]{1,0:T(8,128)(2,1)} %key_weight.1) | copy-start | bytes 786436
  590.4 12.0 %copy-start.13 = (f32[512,256]{1,0:T(8,128)S(1)}, f32[512,256]{1,0:T(8,128)}, u32[]{:S(2)}) copy-start(f32[512,256]{1,0:T(8,128)} %get-tuple-element.183) | copy-start | bytes 1572868
  594.6 8.5 %copy-start.12 = (f32[512,256]{1,0:T(8,128)S(1)}, f32[512,256]{1,0:T(8,128)}, u32[]{:S(2)}) copy-start(f32[512,256]{1,0:T(8,128)} %get-tuple-element.184) | copy-start | bytes 1572868
  594.6 9.3 %copy-start.11 = (f32[512,256]{1,0:T(8,128)S(1)}, f32[512,256]{1,0:T(8,128)}, u32[]{:S(2)}) copy-start(f32[512,256]{1,0:T(8,128)} %get-tuple-element.185) | copy-start | bytes 1572868
  599.7 5.0 copy-start.7
  601.3 5.6 copy-start.30
  604.7 3.7 copy-start.6
  608.4 3.7 copy-start.5

commit v12 on v11

--- a/solution.py
+++ b/solution.py
@@ -1221,12 +1221,11 @@
             multiply(t)
         if 0 <= t - 1 < n_i:
             stage_a(t - 1)
+        if 0 <= t - 2 < n_i:
+            stage_c(t - 2)
         if 0 <= t - 1 < n_i:
             accumulate(t - 1)
-        if 0 <= t - 1 < n_i:
             stage_b(t - 1)
-        if 0 <= t - 2 < n_i:
-            stage_c(t - 2)
     for i in range(n_i):
         for q in range(4):
             core_copy(i, q).wait_send()

time: 615 us -> 608 us (0.989)
    pallas_call x1, Pallas kernels: 109 us -> 102 us  [pull_experts(): pl.pallas_call(partial(pull_kernel, n_i, rows), out_shape=(jax.ShapeDtype...]
where the time goes in v12:
time: 608 us
  Pallas kernels  552 us (91%)
  other arithmetic  29.2 us (5%)
  local copies, waits for them, and re-layouts  21.5 us (4%)
    pallas_call x1, Pallas kernels, run_experts(): pl.pallas_call(partial(expert_kernel, n_z, span), out_shape=(jax.ShapeDty...  181 us
    pallas_call x1, Pallas kernels, attend(): pl.pallas_call(partial(attend_kernel, heads, pieces), out_shape=(jax.Shap...  153 us
    pallas_call x1, Pallas kernels, attend_back(): pl.pallas_call(partial(attend_back_kernel, heads, pieces), out_shape=(jax...  116 us
    pallas_call x1, Pallas kernels, pull_experts(): pl.pallas_call(partial(pull_kernel, n_i, rows), out_shape=(jax.ShapeDtype...  102 us
    unnamed x72, local copies, waits for them, and re-layouts  15.9 us

profile of v12, /device:TPU:0, one launch (start us, length us, event | category | flops | bytes accessed | tf_op | source)
XLA Modules:
  0.0 607.5 jit_solution(16929934819682513469)
XLA Ops:
  1.3 1.2 fusion.2
  2.6 0.5 copy-done.28
  3.0 0.5 iota.28
  3.6 2.1 fusion.4
  5.7 2.0 fusion.9
  7.6 0.0 copy-start.17
  7.6 1.3 pad_maximum_fusion
  9.0 152.5 %attend.1 = (f32[4,2,16,2048]{3,2,1,0:T(8,128)}, bf16[8,2,64,2048]{3,2,1,0:T(8,128)(2,1)}, bf16[4,512,768]{2,1,0:T(8,128)(2,1)}, bf16[4,256,512]{2,1,0:T(8,128)(...) custom-call(bf16[2,64,2048]{2,1,0:T(8,128)(2,1)} %bitcast.74, ...), custom_call_target="tpu_custom_call" | custom-call | tf_op jit(solution)/shard_map/attend/pallas_call | solution.py:1521
  161.5 0.8 slice_reduce_fusion.1
  162.3 0.2 dynamic_update_slice.3
  162.5 0.6 reshape.201
  163.1 1.4 multiply_reduce_fusion.2
  164.5 0.0 copy-start.29
  164.5 0.9 copy-done
  165.5 0.2 multiply_convert_fusion
  165.6 0.0 copy-start.4
  165.7 0.8 copy-done.4
  166.4 0.3 fusion.16
  166.7 0.0 copy-start.16
  166.8 0.5 multiply_divide_fusion
  167.3 0.0 copy-done.16
  167.4 0.5 multiply_divide_fusion.1
  167.9 0.0 copy-done.20
  168.0 0.6 broadcast_in_dim.97
  168.6 181.0 %experts.1 = (bf16[4096,2048]{1,0:T(8,128)(2,1)}, bf16[4096,1024]{1,0:T(8,128)(2,1)}, f32[32,1,128]{2,1,0:T(1,128)}, f32[512,2048]{1,0:T(8,128)}, f32[2,64,2048]{2,1,0:T(8,128)}) custom-call(bf16[2,64,2048]{2,1,0:T(8,128)(2,1)} %bitcast.65, bf16[4096,2048]{1,0:T(8,128)(2,1)} %bitcast.60, f32[32,1,128]{2,1,0:T(1,128)} %bitcast.81, ...), custom_call_target="tpu_custom_call" | custom-call | tf_op jit(solution)/shard_map/experts/pallas_call | solution.py:1021
  349.6 0.7 reduce_sum.143
  350.4 0.7 select_reduce_fusion.3
  351.1 0.7 multiply_reduce_fusion.4
  351.8 0.7 divide_add_fusion
  352.5 0.7 select_reduce_fusion.2
  353.2 0.7 multiply_reduce_fusion.3
  353.9 0.7 multiply_convert_fusion.3
  354.7 1.2 convolution_bitcast_fusion
  355.9 0.7 copy.45
  356.6 101.6 %pull_experts.1 = (f32[2,64,2048]{2,1,0:T(8,128)}, f32[2048,512]{1,0:T(8,128)}, f32[2048,512]{1,0:T(8,128)}) custom-call(bf16[4096,2048]{1,0:T(8,128)(2,1)} %get-tuple-element.48.all_ref, bf16[4096,1024]{1,0:T(8,128)(2,1)} %get-tuple-element.49.pair_ref, bf16[2048,512]{1,0:T(8,128)(2,1)} %bitcast.62, bf16[2048,512]{1,0:T(8,128)(2,1)} %bitcast.64), custom_call_target="tpu_custom_call" | custom-call | tf_op jit(solution)/shard_map/pull_experts/pallas_call | solution.py:1251
  458.2 2.2 multiply_reduce_fusion
  460.5 0.0 copy-start.3
  460.5 0.7 multiply_multiply_fusion.1
  461.2 1.6 select_maximum_fusion
  462.8 2.3 fusion.15
  465.0 116.3 %attend_back.1 = (f32[4,2,16,2048]{3,2,1,0:T(8,128)}, f32[512,256]{1,0:T(8,128)}, f32[512,256]{1,0:T(8,128)}, f32[512,256]{1,0:T(8,128)}, f32[512,256]{1,0:T(8,1...) custom-call(bf16[2,64,2048]{2,1,0:T(8,128)(2,1)} %bitcast.73, bf16[4,256,512]{2,1,0:T(8,128)(2,1)} %get-tuple-element.52.out_weight_ref, ...), custom_call_target="tpu_custom_call" | custom-call | tf_op jit(solution)/shard_map/attend_back/pallas_call | solution.py:1898
  581.4 1.6 fusion.5
  583.1 0.7 multiply_multiply_fusion
  583.8 4.2 fusion.1
  588.0 0.5 slice_bitcast_fusion.2
  588.5 0.6 slice_bitcast_fusion.1
  589.1 0.6 slice.40
  589.8 0.7 slice_bitcast_fusion
  590.4 1.0 copy.44
  591.4 0.3 slice.38
  591.8 1.3 sort.15
  593.1 0.6 fusion.12
  593.7 0.9 compare_select_fusion
  594.7 0.1 dynamic-slice_sqrt_fusion
  594.7 0.1 broadcast_bitcast_fusion
  594.8 0.9 multiply_convert_fusion.1
  595.7 0.8 copy.54
  596.5 0.8 copy.55
  597.3 0.8 copy.56
  598.1 2.1 copy.57
  600.2 1.6 copy-done.6
  601.8 2.1 copy.58
  603.9 1.6 copy-done.5
  605.5 2.0 copy.59
  (66 shorter events, 0.3 us)
Async XLA Ops:
  2.5 0.5 copy-start.28
  2.6 5.1 copy-start.26
  3.6 159.5 %copy-start.2 = (bf16[128,2048]{1,0:T(8,128)(2,1)S(1)}, bf16[128,2048]{1,0:T(8,128)(2,1)}, u32[]{:S(2)}) copy-start(bf16[128,2048]{1,0:T(8,128)(2,1)} %param.17) | copy-start | bytes 1572868
  7.6 157.8 %copy-start.17 = (f32[2048]{0:T(1024)S(1)}, f32[2048]{0:T(1024)}, u32[]{:S(2)}) copy-start(f32[2048]{0:T(1024)} %param.23) | copy-start | bytes 24580
  9.0 157.5 %copy-start.15 = (bf16[2048,16]{0,1:T(8,128)(2,1)S(1)}, bf16[2048,16]{0,1:T(8,128)(2,1)}, u32[]{:S(2)}) copy-start(bf16[2048,16]{0,1:T(8,128)(2,1)} %param.30) | copy-start | bytes 196612
  9.0 158.4 %copy-start.18 = (s32[128,8]{0,1:T(8,128)S(1)}, s32[128,8]{0,1:T(8,128)}, u32[]{:S(2)}) copy-start(s32[128,8]{0,1:T(8,128)} %param.19) | copy-start | bytes 12292
  164.5 1.0 copy-start
  164.5 4.1 copy-start.29
  165.5 3.1 copy-start.22
  165.6 0.8 copy-start.4
  166.7 0.6 copy-start.16
  166.7 1.9 copy-start.21
  166.7 1.8 copy-start.24
  167.4 0.5 copy-start.25
  167.4 0.6 copy-start.20
  354.6 1.9 copy-start.19
  458.2 4.6 copy-start.1
  460.5 4.6 copy-start.3
  461.2 3.9 copy-start.27
  581.4 6.6 %copy-start.23 = (f32[2,16,128]{2,1,0:T(8,128)S(1)}, f32[2,16,128]{2,1,0:T(8,128)}, u32[]{:S(2)}) copy-start(f32[2,16,128]{2,1,0:T(8,128)} %get-tuple-element.62) | copy-start | bytes 49156
  581.4 7.7 %copy-start.10 = (f32[2,144,128]{2,1,0:T(8,128)S(1)}, f32[2,144,128]{2,1,0:T(8,128)}, u32[]{:S(2)}) copy-start(f32[2,144,128]{2,1,0:T(8,128)} %get-tuple-element.63) | copy-start | bytes 442372
  581.4 9.0 %copy-start.14 = (f32[512,256]{1,0:T(8,128)S(1)}, f32[512,256]{1,0:T(8,128)}, u32[]{:S(2)}) copy-start(f32[512,256]{1,0:T(8,128)} %get-tuple-element.67) | copy-start | bytes 1572868
  583.7 8.1 %copy-start.31 = (s32[16]{0:T(128)S(1)}, s32[16]{0:T(128)}, u32[]{:S(2)}) copy-start(s32[16]{0:T(128)} %iota.28) | copy-start | bytes 196
  583.7 11.1 %copy-start.8 = (bf16[512,256]{1,0:T(8,128)(2,1)S(1)}, bf16[512,256]{1,0:T(8,128)(2,1)}, u32[]{:S(2)}) copy-start(bf16[512,256]{1,0:T(8,128)(2,1)} %query_weight.1) | copy-start | bytes 786436
  583.8 11.1 %copy-start.9 = (bf16[512,256]{1,0:T(8,128)(2,1)S(1)}, bf16[512,256]{1,0:T(8,128)(2,1)}, u32[]{:S(2)}) copy-start(bf16[512,256]{1,0:T(8,128)(2,1)} %key_weight.1) | copy-start | bytes 786436
  583.8 12.0 %copy-start.13 = (f32[512,256]{1,0:T(8,128)S(1)}, f32[512,256]{1,0:T(8,128)}, u32[]{:S(2)}) copy-start(f32[512,256]{1,0:T(8,128)} %get-tuple-element.183) | copy-start | bytes 1572868
  588.0 8.5 %copy-start.12 = (f32[512,256]{1,0:T(8,128)S(1)}, f32[512,256]{1,0:T(8,128)}, u32[]{:S(2)}) copy-start(f32[512,256]{1,0:T(8,128)} %get-tuple-element.184) | copy-start | bytes 1572868
  588.0 9.3 %copy-start.11 = (f32[512,256]{1,0:T(8,128)S(1)}, f32[512,256]{1,0:T(8,128)}, u32[]{:S(2)}) copy-start(f32[512,256]{1,0:T(8,128)} %get-tuple-element.185) | copy-start | bytes 1572868
  593.1 5.0 copy-start.7
  594.6 5.6 copy-start.30
  598.1 3.7 copy-start.6
  601.8 3.7 copy-start.5
